TPU v7x, 256 devices: a whole 4x4x8 slice. The times are simulated.
256 devices in a mesh: gz: 64 (over z, x, core), gx: 4 (over y).
Axes of the slice: x: 4, y: 4, z: 8, core: 2. Of those that a mesh axis runs over, the one named last changes fastest.
Arguments:
- d_field: float32 [3, 512, 128, 128], P(None, 'gz', 'gx'), may hold values from -6 to 6
- e_field: float32 [3, 512, 128, 128], P(None, 'gz', 'gx'), may hold values from -6 to 6
- h_field: float32 [3, 512, 128, 128], P(None, 'gz', 'gx'), may hold values from -6 to 6
- permittivity: float32 [512, 128, 128], P('gz', 'gx'), may hold values from 1 to 4
- kerr_coeff: float32 [512, 128, 128], P('gz', 'gx'), may hold values from 0.05 to 0.3
- classes: int32 [2, 128, 128], P(None, 'gx'), may hold values from 0 to 7
- eps_table: float32 [8], replicated, may hold values from 1 to 6
- chi_table: float32 [8], replicated, may hold values from 0.02 to 0.4
Outputs:
- d_out: float32 [3, 512, 128, 128], P(None, 'gz', 'gx')
- e_out: float32 [3, 512, 128, 128], P(None, 'gz', 'gx')
- h_out: float32 [3, 512, 128, 128], P(None, 'gz', 'gx')
- eps_out: float32 [512, 128, 128], P('gz', 'gx')
- chi_out: float32 [512, 128, 128], P('gz', 'gx')
All inputs are finite; a program needn't handle non-finite values.
Results may differ from a plain program's by a relative error of at most 0.00002.
Values sent between devices are 32-bit elements; how exact they have to be, the bound alone decides.
No kernel may reach another device: no remote copies, remote signals or barrier semaphores. Data moves between devices by JAX's collectives and lax.ppermute only.
A program may use at most 64 MiB of HBM per device.

v0:
```python
import jax
import jax.numpy as jnp
from jax import lax
from jax.sharding import PartitionSpec as P

STEPS = 4
KERR = 3
ADVANCE = 2


courant = 0.5


def passed_along(shard, axis, by):
    devices = lax.axis_size(axis)
    pairs = [(i, i + by) for i in range(devices) if 0 <= i + by < devices]
    return lax.ppermute(shard, axis, pairs)


def ahead_y(values):
    zeros = jnp.zeros_like(values[..., 0:1])
    return jnp.concatenate([values[..., 1:], zeros], axis=-1)


def behind_y(values):
    zeros = jnp.zeros_like(values[..., 0:1])
    return jnp.concatenate([zeros, values[..., :-1]], axis=-1)


def curl_ahead(field, next_z, next_x):
    curl_x = ahead_y(field[2]) - field[2] - (next_z[1] - field[1])
    curl_y = next_z[0] - field[0] - (next_x[1] - field[2])
    curl_z = next_x[0] - field[1] - (ahead_y(field[0]) - field[0])
    return jnp.stack([curl_x, curl_y, curl_z])


def curl_behind(field, prev_z, prev_x):
    curl_x = field[2] - behind_y(field[2]) - (field[1] - prev_z[1])
    curl_y = field[0] - prev_z[0] - (field[2] - prev_x[1])
    curl_z = field[1] - prev_x[0] - (field[0] - behind_y(field[0]))
    return jnp.stack([curl_x, curl_y, curl_z])


def lookup(classes, table):
    labels = jnp.arange(table.shape[0], dtype=jnp.int32).reshape(-1, 1, 1, 1)
    picked = jnp.where(classes[None] == labels, table.reshape(-1, 1, 1, 1), jnp.float32(0.0))
    return jnp.sum(picked, axis=0)


def on_device(d_field, e_field, h_field, permittivity, kerr_coeff, classes, eps_table, chi_table):
    is_last = lax.axis_index("gz") == lax.axis_size("gz") - 1
    displace, electric, magnetic = (d_field, e_field, h_field)
    for sweep in range(STEPS):
        plane = passed_along(electric[0:2, 0:1], "gz", -1)
        next_z = jnp.concatenate([electric[0:2, 1:], plane], axis=1)
        row_in = passed_along(electric[1:3, :, 0:1], "gx", -1)
        next_x = jnp.concatenate([electric[1:3, :, 1:], row_in], axis=2)
        magnetic = magnetic - courant * curl_ahead(electric, next_z, next_x)
        plane = passed_along(magnetic[0:2, -1:], "gz", 1)
        prev_z = jnp.concatenate([plane, magnetic[0:2, :-1]], axis=1)
        row_in = passed_along(magnetic[1:3, :, -1:], "gx", 1)
        prev_x = jnp.concatenate([row_in, magnetic[1:3, :, :-1]], axis=2)
        displace = displace + courant * curl_behind(magnetic, prev_z, prev_x)
        for inner in range(KERR):
            energy = (
                electric[0] * electric[0] + electric[1] * electric[1] + electric[2] * electric[2]
            )
            electric = displace / (permittivity + kerr_coeff * energy)[None]
    d_in, e_in, h_in, eps_in, chi_in = passed_along(
        (
            displace[:, 0:ADVANCE],
            electric[:, 0:ADVANCE],
            magnetic[:, 0:ADVANCE],
            permittivity[0:ADVANCE],
            kerr_coeff[0:ADVANCE],
        ),
        "gz",
        -1,
    )
    eps_in = jnp.where(is_last, lookup(classes, eps_table), eps_in)
    chi_in = jnp.where(is_last, lookup(classes, chi_table), chi_in)
    d_out = jnp.concatenate([displace[:, ADVANCE:], d_in], axis=1)
    e_out = jnp.concatenate([electric[:, ADVANCE:], e_in], axis=1)
    h_out = jnp.concatenate([magnetic[:, ADVANCE:], h_in], axis=1)
    eps_out = jnp.concatenate([permittivity[ADVANCE:], eps_in], axis=0)
    chi_out = jnp.concatenate([kerr_coeff[ADVANCE:], chi_in], axis=0)
    return (d_out, e_out, h_out, eps_out, chi_out)


def solution(mesh):
    placed = (
        P(None, "gz", "gx", None),
        P(None, "gz", "gx", None),
        P(None, "gz", "gx", None),
        P("gz", "gx", None),
        P("gz", "gx", None),
        P(None, "gx", None),
        P(),
        P(),
    )
    return jax.shard_map(
        on_device,
        mesh=mesh,
        in_specs=placed,
        out_specs=(
            P(None, "gz", "gx", None),
            P(None, "gz", "gx", None),
            P(None, "gz", "gx", None),
            P("gz", "gx", None),
            P("gz", "gx", None),
        ),
        check_vma=False,
    )
```

profile of v0, /device:TPU:111, one launch (start us, length us, event | category | flops | bytes accessed | tf_op | source)
XLA Modules:
  0.0 100.0 jit_solution(183929014449383360)
XLA Ops:
  1.5 2.6 %collective-permute-start = (f32[2,1,32,128]{3,2,1,0:T(8,128)S(1)}, f32[2,1,32,128]{3,2,1,0:T(8,128)S(1)}, u32[]{:S(2)}, u32[]{:S(2)}) collective-permute-start(f32[2,1,32,128]{3,2,1,0:T(8,128)S(1)} %slice.505), channel_id=1, source_target_pairs={{4,0},{8,4},{12,8},{16,12},{20,16},{24,20},{28,24},{32,28},{36,32}... | collective-permute-start | bytes 98312 | tf_op jit(solution)/shard_map/ppermute | solution.py:17
  4.9 2.1 %collective-permute-start.1 = (f32[2,8,1,128]{3,2,1,0:T(1,128)S(1)}, f32[2,8,1,128]{3,2,1,0:T(1,128)S(1)}, u32[]{:S(2)}, u32[]{:S(2)}) collective-permute-start(f32[2,8,1,128]{3,2,1,0:T(1,128)S(1)} %slice.511), channel_id=1, source_target_pairs={{1,0},{2,1},{3,2},{5,4},{6,5},{7,6},{9,8},{10,9},{11,10},{13,12},{... | collective-permute-start | bytes 24584 | tf_op jit(solution)/shard_map/ppermute | solution.py:17
  7.0 1.0 slice.504
  8.0 1.3 %collective-permute-done.1 = f32[2,8,1,128]{3,2,1,0:T(1,128)S(1)} collective-permute-done((f32[2,8,1,128]{3,2,1,0:T(1,128)S(1)}, f32[2,8,1,128]{3,2,1,0:T(1,128)S(1)}, u32[]{:S(2)}, u32[]{:S(2)}) %collective-permute-start.1) | collective-permute-done | bytes 8224 | tf_op jit(solution)/shard_map/ppermute | solution.py:17
  11.3 0.9 copy-done.3
  12.2 6.7 %collective-permute-start.2 = (f32[2,1,32,128]{3,2,1,0:T(8,128)S(1)}, f32[2,1,32,128]{3,2,1,0:T(8,128)S(1)}, u32[]{:S(2)}, u32[]{:S(2)}) collective-permute-start(f32[2,1,32,128]{3,2,1,0:T(8,128)S(1)} %slice.649), channel_id=1, source_target_pairs={{0,4},{4,8},{8,12},{12,16},{16,20},{20,24},{24,28},{28,32},{32,36}... | collective-permute-start | bytes 98312 | tf_op jit(solution)/shard_map/ppermute | solution.py:17
  19.0 3.2 %collective-permute-start.3 = (f32[2,8,1,128]{3,2,1,0:T(1,128)S(1)}, f32[2,8,1,128]{3,2,1,0:T(1,128)S(1)}, u32[]{:S(2)}, u32[]{:S(2)}) collective-permute-start(f32[2,8,1,128]{3,2,1,0:T(1,128)S(1)} %slice.654), channel_id=1, source_target_pairs={{0,1},{1,2},{2,3},{4,5},{5,6},{6,7},{8,9},{9,10},{10,11},{12,13},{... | collective-permute-start | bytes 24584 | tf_op jit(solution)/shard_map/ppermute | solution.py:17
  22.2 1.1 %collective-permute-done.3 = f32[2,8,1,128]{3,2,1,0:T(1,128)S(1)} collective-permute-done((f32[2,8,1,128]{3,2,1,0:T(1,128)S(1)}, f32[2,8,1,128]{3,2,1,0:T(1,128)S(1)}, u32[]{:S(2)}, u32[]{:S(2)}) %collective-permute-start.3) | collective-permute-done | bytes 8224 | tf_op jit(solution)/shard_map/ppermute | solution.py:17
  24.7 1.9 %collective-permute-start.4 = (f32[2,1,32,128]{3,2,1,0:T(8,128)S(1)}, f32[2,1,32,128]{3,2,1,0:T(8,128)S(1)}, u32[]{:S(2)}, u32[]{:S(2)}) collective-permute-start(f32[2,1,32,128]{3,2,1,0:T(8,128)S(1)} %slice.668), channel_id=1, source_target_pairs={{4,0},{8,4},{12,8},{16,12},{20,16},{24,20},{28,24},{32,28},{36,32}... | collective-permute-start | bytes 98312 | tf_op jit(solution)/shard_map/ppermute | solution.py:17
  26.7 1.9 %collective-permute-start.5 = (f32[2,8,1,128]{3,2,1,0:T(1,128)S(1)}, f32[2,8,1,128]{3,2,1,0:T(1,128)S(1)}, u32[]{:S(2)}, u32[]{:S(2)}) collective-permute-start(f32[2,8,1,128]{3,2,1,0:T(1,128)S(1)} %slice.674), channel_id=1, source_target_pairs={{1,0},{2,1},{3,2},{5,4},{6,5},{7,6},{9,8},{10,9},{11,10},{13,12},{... | collective-permute-start | bytes 24584 | tf_op jit(solution)/shard_map/ppermute | solution.py:17
  28.6 1.9 %collective-permute-start.19 = (f32[2,32,128]{2,1,0:T(8,128)S(1)}, f32[2,32,128]{2,1,0:T(8,128)S(1)}, u32[]{:S(2)}, u32[]{:S(2)}) collective-permute-start(f32[2,32,128]{2,1,0:T(8,128)S(1)} %slice.637), channel_id=1, source_target_pairs={{4,0},{8,4},{12,8},{16,12},{20,16},{24,20},{28,24},{32,28},{36,32}... | collective-permute-start | bytes 98312 | tf_op jit(solution)/shard_map/ppermute | solution.py:17
  30.6 1.9 %collective-permute-start.20 = (f32[2,32,128]{2,1,0:T(8,128)S(1)}, f32[2,32,128]{2,1,0:T(8,128)S(1)}, u32[]{:S(2)}, u32[]{:S(2)}) collective-permute-start(f32[2,32,128]{2,1,0:T(8,128)S(1)} %slice.639), channel_id=1, source_target_pairs={{4,0},{8,4},{12,8},{16,12},{20,16},{24,20},{28,24},{32,28},{36,32}... | collective-permute-start | bytes 98312 | tf_op jit(solution)/shard_map/ppermute | solution.py:17
  33.9 6.3 %collective-permute-start.6 = (f32[2,1,32,128]{3,2,1,0:T(8,128)S(1)}, f32[2,1,32,128]{3,2,1,0:T(8,128)S(1)}, u32[]{:S(2)}, u32[]{:S(2)}) collective-permute-start(f32[2,1,32,128]{3,2,1,0:T(8,128)S(1)} %slice.681), channel_id=1, source_target_pairs={{0,4},{4,8},{8,12},{12,16},{16,20},{20,24},{24,28},{28,32},{32,36}... | collective-permute-start | bytes 98312 | tf_op jit(solution)/shard_map/ppermute | solution.py:17
  40.2 3.6 %collective-permute-start.7 = (f32[2,8,1,128]{3,2,1,0:T(1,128)S(1)}, f32[2,8,1,128]{3,2,1,0:T(1,128)S(1)}, u32[]{:S(2)}, u32[]{:S(2)}) collective-permute-start(f32[2,8,1,128]{3,2,1,0:T(1,128)S(1)} %slice.686), channel_id=1, source_target_pairs={{0,1},{1,2},{2,3},{4,5},{5,6},{6,7},{8,9},{9,10},{10,11},{12,13},{... | collective-permute-start | bytes 24584 | tf_op jit(solution)/shard_map/ppermute | solution.py:17
  45.1 1.9 %collective-permute-start.8 = (f32[2,1,32,128]{3,2,1,0:T(8,128)S(1)}, f32[2,1,32,128]{3,2,1,0:T(8,128)S(1)}, u32[]{:S(2)}, u32[]{:S(2)}) collective-permute-start(f32[2,1,32,128]{3,2,1,0:T(8,128)S(1)} %slice.700), channel_id=1, source_target_pairs={{4,0},{8,4},{12,8},{16,12},{20,16},{24,20},{28,24},{32,28},{36,32}... | collective-permute-start | bytes 98312 | tf_op jit(solution)/shard_map/ppermute | solution.py:17
  47.0 1.9 %collective-permute-start.9 = (f32[2,8,1,128]{3,2,1,0:T(1,128)S(1)}, f32[2,8,1,128]{3,2,1,0:T(1,128)S(1)}, u32[]{:S(2)}, u32[]{:S(2)}) collective-permute-start(f32[2,8,1,128]{3,2,1,0:T(1,128)S(1)} %slice.706), channel_id=1, source_target_pairs={{1,0},{2,1},{3,2},{5,4},{6,5},{7,6},{9,8},{10,9},{11,10},{13,12},{... | collective-permute-start | bytes 24584 | tf_op jit(solution)/shard_map/ppermute | solution.py:17
  49.1 2.6 %collective-permute-done.9 = f32[2,8,1,128]{3,2,1,0:T(1,128)S(1)} collective-permute-done((f32[2,8,1,128]{3,2,1,0:T(1,128)S(1)}, f32[2,8,1,128]{3,2,1,0:T(1,128)S(1)}, u32[]{:S(2)}, u32[]{:S(2)}) %collective-permute-start.9) | collective-permute-done | bytes 8224 | tf_op jit(solution)/shard_map/ppermute | solution.py:17
  51.7 2.0 %collective-permute-done.8 = f32[2,1,32,128]{3,2,1,0:T(8,128)S(1)} collective-permute-done((f32[2,1,32,128]{3,2,1,0:T(8,128)S(1)}, f32[2,1,32,128]{3,2,1,0:T(8,128)S(1)}, u32[]{:S(2)}, u32[]{:S(2)}) %collective-permute-start.8) | collective-permute-done | bytes 32800 | tf_op jit(solution)/shard_map/ppermute | solution.py:17
  54.3 5.9 %collective-permute-start.10 = (f32[2,1,32,128]{3,2,1,0:T(8,128)S(1)}, f32[2,1,32,128]{3,2,1,0:T(8,128)S(1)}, u32[]{:S(2)}, u32[]{:S(2)}) collective-permute-start(f32[2,1,32,128]{3,2,1,0:T(8,128)S(1)} %slice.713), channel_id=1, source_target_pairs={{0,4},{4,8},{8,12},{12,16},{16,20},{20,24},{24,28},{28,32},{32,36}... | collective-permute-start | bytes 98312 | tf_op jit(solution)/shard_map/ppermute | solution.py:17
  60.2 3.6 %collective-permute-start.11 = (f32[2,8,1,128]{3,2,1,0:T(1,128)S(1)}, f32[2,8,1,128]{3,2,1,0:T(1,128)S(1)}, u32[]{:S(2)}, u32[]{:S(2)}) collective-permute-start(f32[2,8,1,128]{3,2,1,0:T(1,128)S(1)} %slice.718), channel_id=1, source_target_pairs={{0,1},{1,2},{2,3},{4,5},{5,6},{6,7},{8,9},{9,10},{10,11},{12,13},{... | collective-permute-start | bytes 24584 | tf_op jit(solution)/shard_map/ppermute | solution.py:17
  65.1 1.9 %collective-permute-start.12 = (f32[2,1,32,128]{3,2,1,0:T(8,128)S(1)}, f32[2,1,32,128]{3,2,1,0:T(8,128)S(1)}, u32[]{:S(2)}, u32[]{:S(2)}) collective-permute-start(f32[2,1,32,128]{3,2,1,0:T(8,128)S(1)} %slice.732), channel_id=1, source_target_pairs={{4,0},{8,4},{12,8},{16,12},{20,16},{24,20},{28,24},{32,28},{36,32}... | collective-permute-start | bytes 98312 | tf_op jit(solution)/shard_map/ppermute | solution.py:17
  67.1 1.9 %collective-permute-start.13 = (f32[2,8,1,128]{3,2,1,0:T(1,128)S(1)}, f32[2,8,1,128]{3,2,1,0:T(1,128)S(1)}, u32[]{:S(2)}, u32[]{:S(2)}) collective-permute-start(f32[2,8,1,128]{3,2,1,0:T(1,128)S(1)} %slice.738), channel_id=1, source_target_pairs={{1,0},{2,1},{3,2},{5,4},{6,5},{7,6},{9,8},{10,9},{11,10},{13,12},{... | collective-permute-start | bytes 24584 | tf_op jit(solution)/shard_map/ppermute | solution.py:17
  69.7 2.0 %collective-permute-done.13 = f32[2,8,1,128]{3,2,1,0:T(1,128)S(1)} collective-permute-done((f32[2,8,1,128]{3,2,1,0:T(1,128)S(1)}, f32[2,8,1,128]{3,2,1,0:T(1,128)S(1)}, u32[]{:S(2)}, u32[]{:S(2)}) %collective-permute-start.13) | collective-permute-done | bytes 8224 | tf_op jit(solution)/shard_map/ppermute | solution.py:17
  71.7 2.0 %collective-permute-done.12 = f32[2,1,32,128]{3,2,1,0:T(8,128)S(1)} collective-permute-done((f32[2,1,32,128]{3,2,1,0:T(8,128)S(1)}, f32[2,1,32,128]{3,2,1,0:T(8,128)S(1)}, u32[]{:S(2)}, u32[]{:S(2)}) %collective-permute-start.12) | collective-permute-done | bytes 32800 | tf_op jit(solution)/shard_map/ppermute | solution.py:17
  74.4 5.9 %collective-permute-start.14 = (f32[2,1,32,128]{3,2,1,0:T(8,128)S(1)}, f32[2,1,32,128]{3,2,1,0:T(8,128)S(1)}, u32[]{:S(2)}, u32[]{:S(2)}) collective-permute-start(f32[2,1,32,128]{3,2,1,0:T(8,128)S(1)} %slice.745), channel_id=1, source_target_pairs={{0,4},{4,8},{8,12},{12,16},{16,20},{20,24},{24,28},{28,32},{32,36}... | collective-permute-start | bytes 98312 | tf_op jit(solution)/shard_map/ppermute | solution.py:17
  80.3 3.6 %collective-permute-start.15 = (f32[2,8,1,128]{3,2,1,0:T(1,128)S(1)}, f32[2,8,1,128]{3,2,1,0:T(1,128)S(1)}, u32[]{:S(2)}, u32[]{:S(2)}) collective-permute-start(f32[2,8,1,128]{3,2,1,0:T(1,128)S(1)} %slice.750), channel_id=1, source_target_pairs={{0,1},{1,2},{2,3},{4,5},{5,6},{6,7},{8,9},{9,10},{10,11},{12,13},{... | collective-permute-start | bytes 24584 | tf_op jit(solution)/shard_map/ppermute | solution.py:17
  84.6 1.9 %collective-permute-start.18 = (f32[3,2,32,128]{3,2,1,0:T(8,128)S(1)}, f32[3,2,32,128]{3,2,1,0:T(8,128)S(1)}, u32[]{:S(2)}, u32[]{:S(2)}) collective-permute-start(f32[3,2,32,128]{3,2,1,0:T(8,128)S(1)} %slice.766), channel_id=1, source_target_pairs={{4,0},{8,4},{12,8},{16,12},{20,16},{24,20},{28,24},{32,28},{36,32}... | collective-permute-start | bytes 294920 | tf_op jit(solution)/shard_map/ppermute | solution.py:17
  87.9 2.0 %collective-permute-start.16 = (f32[3,2,32,128]{3,2,1,0:T(8,128)S(1)}, f32[3,2,32,128]{3,2,1,0:T(8,128)S(1)}, u32[]{:S(2)}, u32[]{:S(2)}) collective-permute-start(f32[3,2,32,128]{3,2,1,0:T(8,128)S(1)} %slice.756), channel_id=1, source_target_pairs={{4,0},{8,4},{12,8},{16,12},{20,16},{24,20},{28,24},{32,28},{36,32}... | collective-permute-start | bytes 294920 | tf_op jit(solution)/shard_map/ppermute | solution.py:17
  89.9 1.9 %collective-permute-start.17 = (f32[3,2,32,128]{3,2,1,0:T(8,128)S(1)}, f32[3,2,32,128]{3,2,1,0:T(8,128)S(1)}, u32[]{:S(2)}, u32[]{:S(2)}) collective-permute-start(f32[3,2,32,128]{3,2,1,0:T(8,128)S(1)} %slice.764), channel_id=1, source_target_pairs={{4,0},{8,4},{12,8},{16,12},{20,16},{24,20},{28,24},{32,28},{36,32}... | collective-permute-start | bytes 294920 | tf_op jit(solution)/shard_map/ppermute | solution.py:17
  91.8 2.0 %collective-permute-done.18 = f32[3,2,32,128]{3,2,1,0:T(8,128)S(1)} collective-permute-done((f32[3,2,32,128]{3,2,1,0:T(8,128)S(1)}, f32[3,2,32,128]{3,2,1,0:T(8,128)S(1)}, u32[]{:S(2)}, u32[]{:S(2)}) %collective-permute-start.18) | collective-permute-done | bytes 98336 | tf_op jit(solution)/shard_map/ppermute | solution.py:17
  94.7 2.6 %collective-permute-done.16 = f32[3,2,32,128]{3,2,1,0:T(8,128)S(1)} collective-permute-done((f32[3,2,32,128]{3,2,1,0:T(8,128)S(1)}, f32[3,2,32,128]{3,2,1,0:T(8,128)S(1)}, u32[]{:S(2)}, u32[]{:S(2)}) %collective-permute-start.16) | collective-permute-done | bytes 98336 | tf_op jit(solution)/shard_map/ppermute | solution.py:17
  98.0 1.2 %collective-permute-done.17 = f32[3,2,32,128]{3,2,1,0:T(8,128)S(1)} collective-permute-done((f32[3,2,32,128]{3,2,1,0:T(8,128)S(1)}, f32[3,2,32,128]{3,2,1,0:T(8,128)S(1)}, u32[]{:S(2)}, u32[]{:S(2)}) %collective-permute-start.17) | collective-permute-done | bytes 98336 | tf_op jit(solution)/shard_map/ppermute | solution.py:17
  (132 shorter events, 15.0 us)
Async XLA Ops:
  0.6 7.3 %copy-start.4 = (f32[3,8,32,128]{3,2,1,0:T(8,128)S(1)}, f32[3,8,32,128]{3,2,1,0:T(8,128)}, u32[]{:S(2)}) copy-start(f32[3,8,32,128]{3,2,1,0:T(8,128)} %param.9) | copy-start | bytes 1179652
  1.5 8.5 %collective-permute-start = (f32[2,1,32,128]{3,2,1,0:T(8,128)S(1)}, f32[2,1,32,128]{3,2,1,0:T(8,128)S(1)}, u32[]{:S(2)}, u32[]{:S(2)}) collective-permute-start(f32[2,1,32,128]{3,2,1,0:T(8,128)S(1)} %slice.505), channel_id=1, source_target_pairs={{4,0},{8,4},{12,8},{16,12},{20,16},{24,20},{28,24},{32,28},{36,32}... | collective-permute-start | bytes 98312 | tf_op jit(solution)/shard_map/ppermute | solution.py:17
  4.9 4.4 %collective-permute-start.1 = (f32[2,8,1,128]{3,2,1,0:T(1,128)S(1)}, f32[2,8,1,128]{3,2,1,0:T(1,128)S(1)}, u32[]{:S(2)}, u32[]{:S(2)}) collective-permute-start(f32[2,8,1,128]{3,2,1,0:T(1,128)S(1)} %slice.511), channel_id=1, source_target_pairs={{1,0},{2,1},{3,2},{5,4},{6,5},{7,6},{9,8},{10,9},{11,10},{13,12},{... | collective-permute-start | bytes 24584 | tf_op jit(solution)/shard_map/ppermute | solution.py:17
  11.1 1.0 copy-start.3
  12.2 11.1 %collective-permute-start.2 = (f32[2,1,32,128]{3,2,1,0:T(8,128)S(1)}, f32[2,1,32,128]{3,2,1,0:T(8,128)S(1)}, u32[]{:S(2)}, u32[]{:S(2)}) collective-permute-start(f32[2,1,32,128]{3,2,1,0:T(8,128)S(1)} %slice.649), channel_id=1, source_target_pairs={{0,4},{4,8},{8,12},{12,16},{16,20},{20,24},{24,28},{28,32},{32,36}... | collective-permute-start | bytes 98312 | tf_op jit(solution)/shard_map/ppermute | solution.py:17
  19.0 4.4 %collective-permute-start.3 = (f32[2,8,1,128]{3,2,1,0:T(1,128)S(1)}, f32[2,8,1,128]{3,2,1,0:T(1,128)S(1)}, u32[]{:S(2)}, u32[]{:S(2)}) collective-permute-start(f32[2,8,1,128]{3,2,1,0:T(1,128)S(1)} %slice.654), channel_id=1, source_target_pairs={{0,1},{1,2},{2,3},{4,5},{5,6},{6,7},{8,9},{9,10},{10,11},{12,13},{... | collective-permute-start | bytes 24584 | tf_op jit(solution)/shard_map/ppermute | solution.py:17
  23.4 1.0 copy-start.6
  24.7 8.6 %collective-permute-start.4 = (f32[2,1,32,128]{3,2,1,0:T(8,128)S(1)}, f32[2,1,32,128]{3,2,1,0:T(8,128)S(1)}, u32[]{:S(2)}, u32[]{:S(2)}) collective-permute-start(f32[2,1,32,128]{3,2,1,0:T(8,128)S(1)} %slice.668), channel_id=1, source_target_pairs={{4,0},{8,4},{12,8},{16,12},{20,16},{24,20},{28,24},{32,28},{36,32}... | collective-permute-start | bytes 98312 | tf_op jit(solution)/shard_map/ppermute | solution.py:17
  26.7 5.9 %collective-permute-start.5 = (f32[2,8,1,128]{3,2,1,0:T(1,128)S(1)}, f32[2,8,1,128]{3,2,1,0:T(1,128)S(1)}, u32[]{:S(2)}, u32[]{:S(2)}) collective-permute-start(f32[2,8,1,128]{3,2,1,0:T(1,128)S(1)} %slice.674), channel_id=1, source_target_pairs={{1,0},{2,1},{3,2},{5,4},{6,5},{7,6},{9,8},{10,9},{11,10},{13,12},{... | collective-permute-start | bytes 24584 | tf_op jit(solution)/shard_map/ppermute | solution.py:17
  28.6 20.3 %collective-permute-start.19 = (f32[2,32,128]{2,1,0:T(8,128)S(1)}, f32[2,32,128]{2,1,0:T(8,128)S(1)}, u32[]{:S(2)}, u32[]{:S(2)}) collective-permute-start(f32[2,32,128]{2,1,0:T(8,128)S(1)} %slice.637), channel_id=1, source_target_pairs={{4,0},{8,4},{12,8},{16,12},{20,16},{24,20},{28,24},{32,28},{36,32}... | collective-permute-start | bytes 98312 | tf_op jit(solution)/shard_map/ppermute | solution.py:17
  30.6 33.2 %collective-permute-start.20 = (f32[2,32,128]{2,1,0:T(8,128)S(1)}, f32[2,32,128]{2,1,0:T(8,128)S(1)}, u32[]{:S(2)}, u32[]{:S(2)}) collective-permute-start(f32[2,32,128]{2,1,0:T(8,128)S(1)} %slice.639), channel_id=1, source_target_pairs={{4,0},{8,4},{12,8},{16,12},{20,16},{24,20},{28,24},{32,28},{36,32}... | collective-permute-start | bytes 98312 | tf_op jit(solution)/shard_map/ppermute | solution.py:17
  33.8 10.0 %copy-start.7 = (s32[2,32,128]{2,1,0:T(8,128)S(1)}, s32[2,32,128]{2,1,0:T(8,128)}, u32[]{:S(2)}) copy-start(s32[2,32,128]{2,1,0:T(8,128)} %param.13) | copy-start | bytes 98308
  33.8 10.0 %copy-start.8 = (f32[8]{0:T(128)S(1)}, f32[8]{0:T(128)}, u32[]{:S(2)}) copy-start(f32[8]{0:T(128)} %param.15) | copy-start | bytes 100
  33.8 10.0 %copy-start.9 = (f32[8]{0:T(128)S(1)}, f32[8]{0:T(128)}, u32[]{:S(2)}) copy-start(f32[8]{0:T(128)} %param.14) | copy-start | bytes 100
  33.9 10.7 %collective-permute-start.6 = (f32[2,1,32,128]{3,2,1,0:T(8,128)S(1)}, f32[2,1,32,128]{3,2,1,0:T(8,128)S(1)}, u32[]{:S(2)}, u32[]{:S(2)}) collective-permute-start(f32[2,1,32,128]{3,2,1,0:T(8,128)S(1)} %slice.681), channel_id=1, source_target_pairs={{0,4},{4,8},{8,12},{12,16},{16,20},{20,24},{24,28},{28,32},{32,36}... | collective-permute-start | bytes 98312 | tf_op jit(solution)/shard_map/ppermute | solution.py:17
  40.2 4.4 %collective-permute-start.7 = (f32[2,8,1,128]{3,2,1,0:T(1,128)S(1)}, f32[2,8,1,128]{3,2,1,0:T(1,128)S(1)}, u32[]{:S(2)}, u32[]{:S(2)}) collective-permute-start(f32[2,8,1,128]{3,2,1,0:T(1,128)S(1)} %slice.686), channel_id=1, source_target_pairs={{0,1},{1,2},{2,3},{4,5},{5,6},{6,7},{8,9},{9,10},{10,11},{12,13},{... | collective-permute-start | bytes 24584 | tf_op jit(solution)/shard_map/ppermute | solution.py:17
  45.1 8.6 %collective-permute-start.8 = (f32[2,1,32,128]{3,2,1,0:T(8,128)S(1)}, f32[2,1,32,128]{3,2,1,0:T(8,128)S(1)}, u32[]{:S(2)}, u32[]{:S(2)}) collective-permute-start(f32[2,1,32,128]{3,2,1,0:T(8,128)S(1)} %slice.700), channel_id=1, source_target_pairs={{4,0},{8,4},{12,8},{16,12},{20,16},{24,20},{28,24},{32,28},{36,32}... | collective-permute-start | bytes 98312 | tf_op jit(solution)/shard_map/ppermute | solution.py:17
  47.0 4.7 %collective-permute-start.9 = (f32[2,8,1,128]{3,2,1,0:T(1,128)S(1)}, f32[2,8,1,128]{3,2,1,0:T(1,128)S(1)}, u32[]{:S(2)}, u32[]{:S(2)}) collective-permute-start(f32[2,8,1,128]{3,2,1,0:T(1,128)S(1)} %slice.706), channel_id=1, source_target_pairs={{1,0},{2,1},{3,2},{5,4},{6,5},{7,6},{9,8},{10,9},{11,10},{13,12},{... | collective-permute-start | bytes 24584 | tf_op jit(solution)/shard_map/ppermute | solution.py:17
  54.3 10.3 %collective-permute-start.10 = (f32[2,1,32,128]{3,2,1,0:T(8,128)S(1)}, f32[2,1,32,128]{3,2,1,0:T(8,128)S(1)}, u32[]{:S(2)}, u32[]{:S(2)}) collective-permute-start(f32[2,1,32,128]{3,2,1,0:T(8,128)S(1)} %slice.713), channel_id=1, source_target_pairs={{0,4},{4,8},{8,12},{12,16},{16,20},{20,24},{24,28},{28,32},{32,36}... | collective-permute-start | bytes 98312 | tf_op jit(solution)/shard_map/ppermute | solution.py:17
  60.2 4.4 %collective-permute-start.11 = (f32[2,8,1,128]{3,2,1,0:T(1,128)S(1)}, f32[2,8,1,128]{3,2,1,0:T(1,128)S(1)}, u32[]{:S(2)}, u32[]{:S(2)}) collective-permute-start(f32[2,8,1,128]{3,2,1,0:T(1,128)S(1)} %slice.718), channel_id=1, source_target_pairs={{0,1},{1,2},{2,3},{4,5},{5,6},{6,7},{8,9},{9,10},{10,11},{12,13},{... | collective-permute-start | bytes 24584 | tf_op jit(solution)/shard_map/ppermute | solution.py:17
  65.0 4.0 %slice-start = ((f32[8,32,128]{2,1,0:T(8,128)}), f32[6,32,128]{2,1,0:T(8,128)S(1)}, s32[]{:S(2)}) async-start(f32[8,32,128]{2,1,0:T(8,128)} %param.11), calls=%async_computation | async-start | bytes 196608 | tf_op jit(solution)/shard_map/slice | solution.py:85
  65.1 8.6 %collective-permute-start.12 = (f32[2,1,32,128]{3,2,1,0:T(8,128)S(1)}, f32[2,1,32,128]{3,2,1,0:T(8,128)S(1)}, u32[]{:S(2)}, u32[]{:S(2)}) collective-permute-start(f32[2,1,32,128]{3,2,1,0:T(8,128)S(1)} %slice.732), channel_id=1, source_target_pairs={{4,0},{8,4},{12,8},{16,12},{20,16},{24,20},{28,24},{32,28},{36,32}... | collective-permute-start | bytes 98312 | tf_op jit(solution)/shard_map/ppermute | solution.py:17
  67.1 4.7 %collective-permute-start.13 = (f32[2,8,1,128]{3,2,1,0:T(1,128)S(1)}, f32[2,8,1,128]{3,2,1,0:T(1,128)S(1)}, u32[]{:S(2)}, u32[]{:S(2)}) collective-permute-start(f32[2,8,1,128]{3,2,1,0:T(1,128)S(1)} %slice.738), channel_id=1, source_target_pairs={{1,0},{2,1},{3,2},{5,4},{6,5},{7,6},{9,8},{10,9},{11,10},{13,12},{... | collective-permute-start | bytes 24584 | tf_op jit(solution)/shard_map/ppermute | solution.py:17
  74.1 9.8 %slice-start.1 = ((f32[8,32,128]{2,1,0:T(8,128)}), f32[6,32,128]{2,1,0:T(8,128)S(1)}, s32[]{:S(2)}) async-start(f32[8,32,128]{2,1,0:T(8,128)} %param.12), calls=%async_computation.1 | async-start | bytes 196608 | tf_op jit(solution)/shard_map/slice | solution.py:86
  74.3 12.3 %copy-start.2 = (f32[3,8,32,128]{3,2,1,0:T(8,128)}, f32[3,8,32,128]{3,2,1,0:T(8,128)S(1)}, u32[]{:S(2)}) copy-start(f32[3,8,32,128]{3,2,1,0:T(8,128)S(1)} %fusion.6) | copy-start | bytes 1179652
  74.4 12.2 %collective-permute-start.14 = (f32[2,1,32,128]{3,2,1,0:T(8,128)S(1)}, f32[2,1,32,128]{3,2,1,0:T(8,128)S(1)}, u32[]{:S(2)}, u32[]{:S(2)}) collective-permute-start(f32[2,1,32,128]{3,2,1,0:T(8,128)S(1)} %slice.745), channel_id=1, source_target_pairs={{0,4},{4,8},{8,12},{12,16},{16,20},{20,24},{24,28},{28,32},{32,36}... | collective-permute-start | bytes 98312 | tf_op jit(solution)/shard_map/ppermute | solution.py:17
  80.3 6.3 %collective-permute-start.15 = (f32[2,8,1,128]{3,2,1,0:T(1,128)S(1)}, f32[2,8,1,128]{3,2,1,0:T(1,128)S(1)}, u32[]{:S(2)}, u32[]{:S(2)}) collective-permute-start(f32[2,8,1,128]{3,2,1,0:T(1,128)S(1)} %slice.750), channel_id=1, source_target_pairs={{0,1},{1,2},{2,3},{4,5},{5,6},{6,7},{8,9},{9,10},{10,11},{12,13},{... | collective-permute-start | bytes 24584 | tf_op jit(solution)/shard_map/ppermute | solution.py:17
  84.6 9.3 %collective-permute-start.18 = (f32[3,2,32,128]{3,2,1,0:T(8,128)S(1)}, f32[3,2,32,128]{3,2,1,0:T(8,128)S(1)}, u32[]{:S(2)}, u32[]{:S(2)}) collective-permute-start(f32[3,2,32,128]{3,2,1,0:T(8,128)S(1)} %slice.766), channel_id=1, source_target_pairs={{4,0},{8,4},{12,8},{16,12},{20,16},{24,20},{28,24},{32,28},{36,32}... | collective-permute-start | bytes 294920 | tf_op jit(solution)/shard_map/ppermute | solution.py:17
  87.9 6.0 %slice-start.2 = ((f32[3,8,32,128]{3,2,1,0:T(8,128)}), f32[3,6,32,128]{3,2,1,0:T(8,128)S(1)}, s32[]{:S(2)}) async-start(f32[3,8,32,128]{3,2,1,0:T(8,128)} %copy-done.2), calls=%async_computation.2 | async-start | bytes 589824 | tf_op jit(solution)/shard_map/slice | solution.py:84
  87.9 9.4 %collective-permute-start.16 = (f32[3,2,32,128]{3,2,1,0:T(8,128)S(1)}, f32[3,2,32,128]{3,2,1,0:T(8,128)S(1)}, u32[]{:S(2)}, u32[]{:S(2)}) collective-permute-start(f32[3,2,32,128]{3,2,1,0:T(8,128)S(1)} %slice.756), channel_id=1, source_target_pairs={{4,0},{8,4},{12,8},{16,12},{20,16},{24,20},{28,24},{32,28},{36,32}... | collective-permute-start | bytes 294920 | tf_op jit(solution)/shard_map/ppermute | solution.py:17
  89.9 9.3 %collective-permute-start.17 = (f32[3,2,32,128]{3,2,1,0:T(8,128)S(1)}, f32[3,2,32,128]{3,2,1,0:T(8,128)S(1)}, u32[]{:S(2)}, u32[]{:S(2)}) collective-permute-start(f32[3,2,32,128]{3,2,1,0:T(8,128)S(1)} %slice.764), channel_id=1, source_target_pairs={{4,0},{8,4},{12,8},{16,12},{20,16},{24,20},{28,24},{32,28},{36,32}... | collective-permute-start | bytes 294920 | tf_op jit(solution)/shard_map/ppermute | solution.py:17
  94.7 4.5 %slice-start.3 = ((f32[3,8,32,128]{3,2,1,0:T(8,128)}), f32[3,6,32,128]{3,2,1,0:T(8,128)S(1)}, s32[]{:S(2)}) async-start(f32[3,8,32,128]{3,2,1,0:T(8,128)} %copy-done.5), calls=%async_computation.3 | async-start | bytes 589824 | tf_op jit(solution)/shard_map/slice | solution.py:83
  (3 other events, 2.6 us)
where the time goes:
time: 101 us; the launch traced here: 100 us
  starting transfers between devices  64.7 us (64%)
  waiting for transfers between devices  19.5 us (19%)
  local copies, waits for them, and re-layouts  7.12 us (7%)
  other arithmetic  7 us (7%)
  between operations  1.59 us (2%)
    ppermute x21, starting transfers between devices, passed_along(): return lax.ppermute(shard, axis, pairs)  64.7 us
    ppermute x21, waiting for transfers between devices, passed_along(): return lax.ppermute(shard, axis, pairs)  19.5 us
    unnamed x20, local copies, waits for them, and re-layouts  3.28 us
  transfers between devices with their start and end apart: 21, of which 13 were waited for; matrix products, arithmetic and copies ran while one was open for 7% of the time, Pallas kernels for 0%

commit v1 on v0

v1 whole, which is shorter than its diff:
```python
import jax
import jax.numpy as jnp
from jax import lax
from jax.experimental import pallas as pl
from jax.experimental.pallas import tpu as pltpu
from jax.sharding import PartitionSpec as P

STEPS = 4
KERR = 3
ADVANCE = 2
HALF = 0.5

D, E, H, EPS, CHI = 0, 3, 6, 9, 10
NZL, NXL, NY = 8, 32, 128
XH = 4
ROWS = NXL + 2 * XH

ZHI = {(c, p): c * 5 + p for c in range(11) for p in range(5)}
ZHI.update({(E, 5): 55, (E + 1, 5): 56})
ZLO = {}
for _c in (D, D + 1, D + 2, H, H + 1, H + 2, E, E + 1, E + 2, EPS, CHI):
    ZLO[(_c, 7)] = len(ZLO)
for _c in (E, E + 1, E + 2, H, H + 1):
    ZLO[(_c, 6)] = len(ZLO)

VM = pl.BlockSpec(memory_space=pltpu.VMEM)
ANY = pl.BlockSpec(memory_space=pltpu.HBM)
SM = pl.BlockSpec(memory_space=pltpu.SMEM)


def shape(*dims):
    return jax.ShapeDtypeStruct(dims, jnp.float32)


def pack_zhi(d, e, h, eps, chi, out, sems):
    moves = []
    for base, ref in ((D, d), (E, e), (H, h)):
        for c in range(3):
            moves.append((ref.at[c, pl.ds(0, 5)], out.at[pl.ds((base + c) * 5, 5)]))
    moves.append((eps.at[pl.ds(0, 5)], out.at[pl.ds(EPS * 5, 5)]))
    moves.append((chi.at[pl.ds(0, 5)], out.at[pl.ds(CHI * 5, 5)]))
    for c in range(2):
        moves.append((e.at[c, pl.ds(5, 1)], out.at[pl.ds(55 + c, 1)]))
    copies = [pltpu.make_async_copy(a, b, sems.at[i]) for i, (a, b) in enumerate(moves)]
    for c in copies:
        c.start()
    for c in copies:
        c.wait()


def pick(d, e, h, eps, chi, comp, plane):
    if comp < E:
        return d[comp, plane]
    if comp < H:
        return e[comp - E, plane]
    if comp < EPS:
        return h[comp - H, plane]
    return eps[plane] if comp == EPS else chi[plane]


def pack_rest(d, e, h, eps, chi, xhi, xlo, zlo):
    for comp in range(11):
        for plane in range(NZL):
            v = pick(d, e, h, eps, chi, comp, plane)
            xhi[comp, plane] = v[0:XH]
            xlo[comp, plane] = v[NXL - XH :]
    for (comp, plane), i in ZLO.items():
        zlo[i] = pick(d, e, h, eps, chi, comp, plane)


def pack_corners(xhi, xlo, xt, czhi, czlo):
    for comp in range(11):
        for plane in range(NZL):
            t = jnp.concatenate([xhi[comp, plane], xlo[comp, plane]], axis=0)
            xt[comp, plane] = t
            if (comp, plane) in ZHI:
                czhi[ZHI[(comp, plane)]] = t
            if (comp, plane) in ZLO:
                czlo[ZLO[(comp, plane)]] = t


def advance(d, e, h, eps, chi, xt, zhi, zlo, czhi, czlo, classes, eps_table, chi_table, d_out, e_out, h_out, eps_out, chi_out, ds, es, hs):
    gz, gx = lax.axis_index("gz"), lax.axis_index("gx")
    last_z = gz == lax.axis_size("gz") - 1
    up = jnp.where(last_z, 0.0, 1.0).astype(jnp.float32)
    down = jnp.where(gz == 0, 0.0, 1.0).astype(jnp.float32)
    right = jnp.where(gx == lax.axis_size("gx") - 1, 0.0, 1.0).astype(jnp.float32)
    left = jnp.where(gx == 0, 0.0, 1.0).astype(jnp.float32)
    row = lax.broadcasted_iota(jnp.int32, (8, NY), 0)
    lane = lax.broadcasted_iota(jnp.int32, (ROWS, NY), 1)
    edge = jnp.where(row < XH, right, left)
    last_y, first_y = lane == NY - 1, lane == 0

    def inside(plane):
        return up if plane >= NZL else (down if plane < 0 else None)

    def factor(plane):
        z = inside(plane)
        main = jnp.full((NXL, NY), HALF, jnp.float32)
        tile = edge * HALF
        if z is not None:
            main, tile = main * z, tile * z
        return jnp.concatenate([main, tile], axis=0)

    def start(comp, plane):
        if plane >= NZL:
            i = ZHI[(comp, plane - NZL)]
            return jnp.concatenate([zhi[i], czhi[i]], axis=0)
        if plane < 0:
            i = ZLO[(comp, plane + NZL)]
            return jnp.concatenate([zlo[i], czlo[i]], axis=0)
        return jnp.concatenate([pick(d, e, h, eps, chi, comp, plane), xt[comp, plane]], axis=0)

    def medium(plane):
        a, b = start(EPS, plane), start(CHI, plane)
        z = inside(plane)
        if z is None:
            fill = jnp.concatenate([jnp.zeros((NXL, NY), jnp.float32), 1.0 - edge], axis=0)
        else:
            fill = jnp.concatenate([jnp.full((NXL, NY), 1.0 - z, jnp.float32), 1.0 - edge * z], axis=0)
        return a + fill, b

    def get(step, comp, plane):
        if step == 0:
            return start(comp, plane)
        ref, c = ((ds, comp), (es, comp - E), (hs, comp - H))[comp // 3]
        return ref[c, plane + 2]

    def next_y(v):
        return jnp.where(last_y, 0.0, pltpu.roll(v, NY - 1, 1))

    def prev_y(v):
        return jnp.where(first_y, 0.0, pltpu.roll(v, 1, 1))

    def next_x(v):
        return pltpu.roll(v, ROWS - 1, 0)

    def prev_x(v):
        return pltpu.roll(v, 1, 0)

    for n in range(1, STEPS + 1):
        for plane in range(n - 3, 14 - n):
            f = factor(plane)
            ex, ey, ez = (get(n - 1, E + c, plane) for c in range(3))
            exn, eyn = (get(n - 1, E + c, plane + 1) for c in range(2))
            below = plane == n - 3
            hx = get(n - 1, H, plane) - f * ((next_y(ez) - ez) - (eyn - ey))
            hy = get(n - 1, H + 1, plane) - f * ((exn - ex) - (next_x(ez) - ez))
            hs[0, plane + 2] = hx
            hs[1, plane + 2] = hy
            if below:
                continue
            hz = get(n - 1, H + 2, plane) - f * ((next_x(ey) - ey) - (next_y(ex) - ex))
            hs[2, plane + 2] = hz
            hxp, hyp = hs[0, plane + 1], hs[1, plane + 1]
            dx = get(n - 1, D, plane) + f * ((hz - prev_y(hz)) - (hy - hyp))
            dy = get(n - 1, D + 1, plane) + f * ((hx - hxp) - (hz - prev_x(hz)))
            dz = get(n - 1, D + 2, plane) + f * ((hy - prev_x(hy)) - (hx - prev_y(hx)))
            eps_p, chi_p = medium(plane)
            last = n == STEPS
            if last:
                dx, dy, dz, ex, ey, ez, eps_p, chi_p = (v[:NXL] for v in (dx, dy, dz, ex, ey, ez, eps_p, chi_p))
            inverse = 1.0 / (eps_p + chi_p * (ex * ex + ey * ey + ez * ez))
            squares = chi_p * (dx * dx + dy * dy + dz * dz)
            for _ in range(KERR - 1):
                inverse = 1.0 / (eps_p + squares * (inverse * inverse))
            if last:
                o = plane - ADVANCE
                for c, (dv, hv) in enumerate(((dx, hx), (dy, hy), (dz, hz))):
                    d_out[c, o] = dv
                    e_out[c, o] = dv * inverse
                    h_out[c, o] = hv[:NXL]
            else:
                for c, dv in enumerate((dx, dy, dz)):
                    ds[c, plane + 2] = dv
                    es[c, plane + 2] = dv * inverse

    for ref, comp, out, table in ((eps, EPS, eps_out, eps_table), (chi, CHI, chi_out, chi_table)):
        for plane in range(ADVANCE, NZL):
            out[plane - ADVANCE] = ref[plane]
        for k in range(ADVANCE):
            picked = jnp.zeros((NXL, NY), jnp.float32)
            for label in range(table.shape[0]):
                picked = jnp.where(classes[k] == label, table[label], picked)
            out[NZL - ADVANCE + k] = jnp.where(last_z, picked, zhi[ZHI[(comp, k)]])


def passed_along(shard, axis, by):
    devices = lax.axis_size(axis)
    pairs = [(i, i + by) for i in range(devices) if 0 <= i + by < devices]
    return lax.ppermute(shard, axis, pairs)


def on_device(d_field, e_field, h_field, permittivity, kerr_coeff, classes, eps_table, chi_table):
    fields = (d_field, e_field, h_field, permittivity, kerr_coeff)
    zhi = pl.pallas_call(
        pack_zhi,
        out_shape=shape(57, NXL, NY),
        in_specs=[ANY] * 5,
        out_specs=VM,
        scratch_shapes=[pltpu.SemaphoreType.DMA((13,))],
        name="pack_zhi", compiler_params=pltpu.CompilerParams(vmem_limit_bytes=4 << 20),
    )(*fields)
    zhi = passed_along(zhi, "gz", -1)
    xhi, xlo, zlo = pl.pallas_call(
        pack_rest,
        out_shape=(shape(11, NZL, XH, NY), shape(11, NZL, XH, NY), shape(16, NXL, NY)),
        in_specs=[VM] * 5,
        out_specs=(VM, VM, VM),
        name="pack_rest", compiler_params=pltpu.CompilerParams(vmem_limit_bytes=8 << 20),
    )(*fields)
    xhi = passed_along(xhi, "gx", -1)
    xlo = passed_along(xlo, "gx", 1)
    zlo = passed_along(zlo, "gz", 1)
    xt, czhi, czlo = pl.pallas_call(
        pack_corners,
        out_shape=(shape(11, NZL, 8, NY), shape(57, 8, NY), shape(16, 8, NY)),
        in_specs=[VM] * 2,
        out_specs=(VM, VM, VM),
        name="pack_corners", compiler_params=pltpu.CompilerParams(vmem_limit_bytes=8 << 20),
    )(xhi, xlo)
    czhi = passed_along(czhi, "gz", -1)
    czlo = passed_along(czlo, "gz", 1)
    state = pltpu.VMEM((3, 16, ROWS, NY), jnp.float32)
    field = shape(3, NZL, NXL, NY)
    medium = shape(NZL, NXL, NY)
    return pl.pallas_call(
        advance,
        out_shape=(field, field, field, medium, medium),
        in_specs=[VM] * 11 + [SM, SM],
        out_specs=(VM,) * 5,
        scratch_shapes=[state, state, state],
        name="advance", compiler_params=pltpu.CompilerParams(vmem_limit_bytes=24 << 20),
    )(*fields, xt, zhi, zlo, czhi, czlo, classes, eps_table, chi_table)


def solution(mesh):
    placed = (
        P(None, "gz", "gx", None),
        P(None, "gz", "gx", None),
        P(None, "gz", "gx", None),
        P("gz", "gx", None),
        P("gz", "gx", None),
        P(None, "gx", None),
        P(),
        P(),
    )
    return jax.shard_map(
        on_device,
        mesh=mesh,
        in_specs=placed,
        out_specs=placed[:5],
        check_vma=False,
    )
```

time: 101 us -> 40 us (0.40)
  the two profiles are of different devices: /device:TPU:111 before, /device:TPU:128 now
where the time goes in v1:
time: 40 us; the launch traced here: 39.6 us
  starting transfers between devices  19.3 us (48%)
  waiting for transfers between devices  8.02 us (20%)
  Pallas kernels  6.61 us (17%)
  local copies, waits for them, and re-layouts  4.82 us (12%)
  between operations  0.82 us (2%)
    ppermute x6, starting transfers between devices, passed_along(): return lax.ppermute(shard, axis, pairs)  19.3 us
    ppermute x6, waiting for transfers between devices, passed_along(): return lax.ppermute(shard, axis, pairs)  8.02 us
    pallas_call x1, Pallas kernels, on_device(): pl.pallas_call(advance, out_shape=(field, field, field, medium, medium),...  5.14 us
    unnamed x26, local copies, waits for them, and re-layouts  4.82 us
    pallas_call x1, Pallas kernels, on_device(): pl.pallas_call(pack_zhi, out_shape=shape(57, NXL, NY), in_specs=[ANY] * 5...  1.35 us
  transfers between devices with their start and end apart: 6, of which 2 were waited for; matrix products, arithmetic and copies ran while one was open for 0% of the time, Pallas kernels for 0%

profile of v1, /device:TPU:128, one launch (start us, length us, event | category | flops | bytes accessed | tf_op | source)
XLA Modules:
  0.0 39.6 jit_solution(12649581749556405429)
XLA Ops:
  0.6 0.0 copy-start
  0.6 1.0 %copy-done = f32[3,8,32,128]{3,2,1,0:T(8,128)S(1)} copy-done((f32[3,8,32,128]{3,2,1,0:T(8,128)S(1)}, f32[3,8,32,128]{3,2,1,0:T(8,128)}, u32[]{:S(2)}) %copy-start) | copy-done | bytes 393240
  1.6 1.0 %copy-done.2 = f32[3,8,32,128]{3,2,1,0:T(8,128)S(1)} copy-done((f32[3,8,32,128]{3,2,1,0:T(8,128)S(1)}, f32[3,8,32,128]{3,2,1,0:T(8,128)}, u32[]{:S(2)}) %copy-start.2) | copy-done | bytes 393240
  2.6 1.0 %copy-done.4 = f32[3,8,32,128]{3,2,1,0:T(8,128)S(1)} copy-done((f32[3,8,32,128]{3,2,1,0:T(8,128)S(1)}, f32[3,8,32,128]{3,2,1,0:T(8,128)}, u32[]{:S(2)}) %copy-start.4) | copy-done | bytes 393240
  3.6 0.9 %copy-done.6 = f32[8,32,128]{2,1,0:T(8,128)S(1)} copy-done((f32[8,32,128]{2,1,0:T(8,128)S(1)}, f32[8,32,128]{2,1,0:T(8,128)}, u32[]{:S(2)}) %copy-start.6) | copy-done | bytes 131096
  4.5 0.9 %copy-done.8 = f32[8,32,128]{2,1,0:T(8,128)S(1)} copy-done((f32[8,32,128]{2,1,0:T(8,128)S(1)}, f32[8,32,128]{2,1,0:T(8,128)}, u32[]{:S(2)}) %copy-start.8) | copy-done | bytes 131096
  5.4 0.0 copy-start.9
  5.5 1.3 %pack_zhi.1 = f32[57,32,128]{2,1,0:T(8,128)S(1)} custom-call(f32[3,8,32,128]{3,2,1,0:T(8,128)S(1)} %copy-done, f32[3,8,32,128]{3,2,1,0:T(8,128)S(1)} %copy-done.2, f32[3,8,32,128]{3,2,1,0:T(8,128)S(1)} %copy-done.4, f32[8,32,128]{2,1,0:T(8,128)S(1)} %copy-done.6, f32[8,32,128]{2,1,0:T(8,128)S(1)} %copy-done.8), custom_call_target="tpu_custom_call" | custom-call | tf_op jit(solution)/shard_map/pack_zhi/pallas_call | solution.py:196
  6.8 3.7 %collective-permute-start.2 = (f32[57,32,128]{2,1,0:T(8,128)S(1)}, f32[57,32,128]{2,1,0:T(8,128)S(1)}, u32[]{:S(2)}, u32[]{:S(2)}) collective-permute-start(f32[57,32,128]{2,1,0:T(8,128)S(1)} %pack_zhi.1), channel_id=1, source_target_pairs={{4,0},{8,4},{12,8},{16,12},{20,16},{24,20},{28,24},{32,28},{36,32}... | collective-permute-start | bytes 2801672 | tf_op jit(solution)/shard_map/ppermute | solution.py:191
  10.5 0.0 copy-done.1
  10.5 0.0 copy-done.3
  10.5 0.0 copy-done.5
  10.5 0.0 copy-done.7
  10.5 0.0 copy-done.9
  10.5 0.1 pack_rest.1
  10.6 1.3 %collective-permute-start = (f32[11,8,4,128]{3,2,1,0:T(4,128)S(1)}, f32[11,8,4,128]{3,2,1,0:T(4,128)S(1)}, u32[]{:S(2)}, u32[]{:S(2)}) collective-permute-start(f32[11,8,4,128]{3,2,1,0:T(4,128)S(1)} %get-tuple-element.11), channel_id=1, source_target_pairs={{1,0},{2,1},{3,2},{5,4},{6,5},{7,6},{9,8},{10,9},{11,10},{13,12},{... | collective-permute-start | bytes 540680 | tf_op jit(solution)/shard_map/ppermute | solution.py:191
  11.9 4.6 %collective-permute-start.1 = (f32[11,8,4,128]{3,2,1,0:T(4,128)S(1)}, f32[11,8,4,128]{3,2,1,0:T(4,128)S(1)}, u32[]{:S(2)}, u32[]{:S(2)}) collective-permute-start(f32[11,8,4,128]{3,2,1,0:T(4,128)S(1)} %get-tuple-element.12), channel_id=1, source_target_pairs={{0,1},{1,2},{2,3},{4,5},{5,6},{6,7},{8,9},{9,10},{10,11},{12,13},{... | collective-permute-start | bytes 540680 | tf_op jit(solution)/shard_map/ppermute | solution.py:191
  16.5 0.0 copy-start.10
  16.5 1.9 %collective-permute-start.3 = (f32[16,32,128]{2,1,0:T(8,128)S(1)}, f32[16,32,128]{2,1,0:T(8,128)S(1)}, u32[]{:S(2)}, u32[]{:S(2)}) collective-permute-start(f32[16,32,128]{2,1,0:T(8,128)S(1)} %get-tuple-element.14), channel_id=1, source_target_pairs={{0,4},{4,8},{8,12},{12,16},{16,20},{20,24},{24,28},{28,32},{32,36}... | collective-permute-start | bytes 786440 | tf_op jit(solution)/shard_map/ppermute | solution.py:191
  18.4 0.0 collective-permute-done.xhi
  18.4 1.0 %collective-permute-done.1.xlo = f32[11,8,4,128]{3,2,1,0:T(4,128)S(1)} collective-permute-done((f32[11,8,4,128]{3,2,1,0:T(4,128)S(1)}, f32[11,8,4,128]{3,2,1,0:T(4,128)S(1)}, u32[]{:S(2)}, u32[]{:S(2)}) %collective-permute-start.1) | collective-permute-done | bytes 180256 | tf_op jit(solution)/shard_map/ppermute | solution.py:191
  19.4 0.1 pack_corners.1
  19.5 5.9 %collective-permute-start.4 = (f32[57,8,128]{2,1,0:T(8,128)S(1)}, f32[57,8,128]{2,1,0:T(8,128)S(1)}, u32[]{:S(2)}, u32[]{:S(2)}) collective-permute-start(f32[57,8,128]{2,1,0:T(8,128)S(1)} %get-tuple-element.15), channel_id=1, source_target_pairs={{4,0},{8,4},{12,8},{16,12},{20,16},{24,20},{28,24},{32,28},{36,32}... | collective-permute-start | bytes 700424 | tf_op jit(solution)/shard_map/ppermute | solution.py:191
  25.5 0.0 copy-start.11
  25.5 0.0 copy-start.12
  25.5 1.9 %collective-permute-start.5 = (f32[16,8,128]{2,1,0:T(8,128)S(1)}, f32[16,8,128]{2,1,0:T(8,128)S(1)}, u32[]{:S(2)}, u32[]{:S(2)}) collective-permute-start(f32[16,8,128]{2,1,0:T(8,128)S(1)} %get-tuple-element.16), channel_id=1, source_target_pairs={{0,4},{4,8},{8,12},{12,16},{16,20},{20,24},{24,28},{28,32},{32,36}... | collective-permute-start | bytes 196616 | tf_op jit(solution)/shard_map/ppermute | solution.py:191
  27.4 7.0 %collective-permute-done.5.czlo = f32[16,8,128]{2,1,0:T(8,128)S(1)} collective-permute-done((f32[16,8,128]{2,1,0:T(8,128)S(1)}, f32[16,8,128]{2,1,0:T(8,128)S(1)}, u32[]{:S(2)}, u32[]{:S(2)}) %collective-permute-start.5) | collective-permute-done | bytes 65568 | tf_op jit(solution)/shard_map/ppermute | solution.py:191
  34.4 0.0 collective-permute-done.3.zlo
  34.4 0.0 collective-permute-done.4.czhi
  34.4 0.0 collective-permute-done.2.zhi
  34.4 0.0 copy-done.10
  34.4 5.1 %advance.1 = (f32[3,8,32,128]{3,2,1,0:T(8,128)}, f32[3,8,32,128]{3,2,1,0:T(8,128)}, f32[3,8,32,128]{3,2,1,0:T(8,128)}, f32[8,32,128]{2,1,0:T(8,128)}, f32[8,32,128]{2,1,0:T(8,128)}) custom-call(f32[3,8,32,128]{3,2,1,0:T(8,128)S(1)} %copy-done.1, f32[3,8,32,128]{3,2,1,0:T(8,128)S(1)} %copy-done.3, f32[3,8,32,128]{3,2,1,0:T(8,128)S(1)} %copy-done.5, ...), custom_call_target="tpu_custom_call" | custom-call | tf_op jit(solution)/shard_map/advance/pallas_call | solution.py:227
  (10 shorter events, 0.0 us)
Async XLA Ops:
  0.6 1.0 %copy-start = (f32[3,8,32,128]{3,2,1,0:T(8,128)S(1)}, f32[3,8,32,128]{3,2,1,0:T(8,128)}, u32[]{:S(2)}) copy-start(f32[3,8,32,128]{3,2,1,0:T(8,128)} %d.5) | copy-start | bytes 1179652
  1.6 1.0 %copy-start.2 = (f32[3,8,32,128]{3,2,1,0:T(8,128)S(1)}, f32[3,8,32,128]{3,2,1,0:T(8,128)}, u32[]{:S(2)}) copy-start(f32[3,8,32,128]{3,2,1,0:T(8,128)} %e.5) | copy-start | bytes 1179652
  2.6 1.0 %copy-start.4 = (f32[3,8,32,128]{3,2,1,0:T(8,128)S(1)}, f32[3,8,32,128]{3,2,1,0:T(8,128)}, u32[]{:S(2)}) copy-start(f32[3,8,32,128]{3,2,1,0:T(8,128)} %h.5) | copy-start | bytes 1179652
  3.6 0.9 %copy-start.6 = (f32[8,32,128]{2,1,0:T(8,128)S(1)}, f32[8,32,128]{2,1,0:T(8,128)}, u32[]{:S(2)}) copy-start(f32[8,32,128]{2,1,0:T(8,128)} %eps.5) | copy-start | bytes 393220
  4.5 0.9 %copy-start.8 = (f32[8,32,128]{2,1,0:T(8,128)S(1)}, f32[8,32,128]{2,1,0:T(8,128)}, u32[]{:S(2)}) copy-start(f32[8,32,128]{2,1,0:T(8,128)} %chi.5) | copy-start | bytes 393220
  5.4 5.0 %copy-start.1 = (f32[3,8,32,128]{3,2,1,0:T(8,128)S(1)}, f32[3,8,32,128]{3,2,1,0:T(8,128)}, u32[]{:S(2)}) copy-start(f32[3,8,32,128]{3,2,1,0:T(8,128)} %d.5) | copy-start | bytes 1179652
  5.4 5.0 %copy-start.3 = (f32[3,8,32,128]{3,2,1,0:T(8,128)S(1)}, f32[3,8,32,128]{3,2,1,0:T(8,128)}, u32[]{:S(2)}) copy-start(f32[3,8,32,128]{3,2,1,0:T(8,128)} %e.5) | copy-start | bytes 1179652
  5.4 5.1 %copy-start.5 = (f32[3,8,32,128]{3,2,1,0:T(8,128)S(1)}, f32[3,8,32,128]{3,2,1,0:T(8,128)}, u32[]{:S(2)}) copy-start(f32[3,8,32,128]{3,2,1,0:T(8,128)} %h.5) | copy-start | bytes 1179652
  5.4 5.1 %copy-start.7 = (f32[8,32,128]{2,1,0:T(8,128)S(1)}, f32[8,32,128]{2,1,0:T(8,128)}, u32[]{:S(2)}) copy-start(f32[8,32,128]{2,1,0:T(8,128)} %eps.5) | copy-start | bytes 393220
  5.4 5.1 %copy-start.9 = (f32[8,32,128]{2,1,0:T(8,128)S(1)}, f32[8,32,128]{2,1,0:T(8,128)}, u32[]{:S(2)}) copy-start(f32[8,32,128]{2,1,0:T(8,128)} %chi.5) | copy-start | bytes 393220
  6.8 27.6 %collective-permute-start.2 = (f32[57,32,128]{2,1,0:T(8,128)S(1)}, f32[57,32,128]{2,1,0:T(8,128)S(1)}, u32[]{:S(2)}, u32[]{:S(2)}) collective-permute-start(f32[57,32,128]{2,1,0:T(8,128)S(1)} %pack_zhi.1), channel_id=1, source_target_pairs={{4,0},{8,4},{12,8},{16,12},{20,16},{24,20},{28,24},{32,28},{36,32}... | collective-permute-start | bytes 2801672 | tf_op jit(solution)/shard_map/ppermute | solution.py:191
  10.6 7.8 %collective-permute-start = (f32[11,8,4,128]{3,2,1,0:T(4,128)S(1)}, f32[11,8,4,128]{3,2,1,0:T(4,128)S(1)}, u32[]{:S(2)}, u32[]{:S(2)}) collective-permute-start(f32[11,8,4,128]{3,2,1,0:T(4,128)S(1)} %get-tuple-element.11), channel_id=1, source_target_pairs={{1,0},{2,1},{3,2},{5,4},{6,5},{7,6},{9,8},{10,9},{11,10},{13,12},{... | collective-permute-start | bytes 540680 | tf_op jit(solution)/shard_map/ppermute | solution.py:191
  11.9 7.5 %collective-permute-start.1 = (f32[11,8,4,128]{3,2,1,0:T(4,128)S(1)}, f32[11,8,4,128]{3,2,1,0:T(4,128)S(1)}, u32[]{:S(2)}, u32[]{:S(2)}) collective-permute-start(f32[11,8,4,128]{3,2,1,0:T(4,128)S(1)} %get-tuple-element.12), channel_id=1, source_target_pairs={{0,1},{1,2},{2,3},{4,5},{5,6},{6,7},{8,9},{9,10},{10,11},{12,13},{... | collective-permute-start | bytes 540680 | tf_op jit(solution)/shard_map/ppermute | solution.py:191
  16.5 17.9 %copy-start.10 = (s32[2,32,128]{2,1,0:T(8,128)S(1)}, s32[2,32,128]{2,1,0:T(8,128)}, u32[]{:S(2)}) copy-start(s32[2,32,128]{2,1,0:T(8,128)} %classes.1) | copy-start | bytes 98308
  16.5 17.9 %collective-permute-start.3 = (f32[16,32,128]{2,1,0:T(8,128)S(1)}, f32[16,32,128]{2,1,0:T(8,128)S(1)}, u32[]{:S(2)}, u32[]{:S(2)}) collective-permute-start(f32[16,32,128]{2,1,0:T(8,128)S(1)} %get-tuple-element.14), channel_id=1, source_target_pairs={{0,4},{4,8},{8,12},{12,16},{16,20},{20,24},{24,28},{28,32},{32,36}... | collective-permute-start | bytes 786440 | tf_op jit(solution)/shard_map/ppermute | solution.py:191
  19.5 14.9 %collective-permute-start.4 = (f32[57,8,128]{2,1,0:T(8,128)S(1)}, f32[57,8,128]{2,1,0:T(8,128)S(1)}, u32[]{:S(2)}, u32[]{:S(2)}) collective-permute-start(f32[57,8,128]{2,1,0:T(8,128)S(1)} %get-tuple-element.15), channel_id=1, source_target_pairs={{4,0},{8,4},{12,8},{16,12},{20,16},{24,20},{28,24},{32,28},{36,32}... | collective-permute-start | bytes 700424 | tf_op jit(solution)/shard_map/ppermute | solution.py:191
  25.5 9.0 %copy-start.11 = (f32[8]{0:T(128)S(1)}, f32[8]{0:T(128)}, u32[]{:S(2)}) copy-start(f32[8]{0:T(128)} %eps_table.1) | copy-start | bytes 100
  25.5 9.0 %copy-start.12 = (f32[8]{0:T(128)S(1)}, f32[8]{0:T(128)}, u32[]{:S(2)}) copy-start(f32[8]{0:T(128)} %chi_table.1) | copy-start | bytes 100
  25.5 8.9 %collective-permute-start.5 = (f32[16,8,128]{2,1,0:T(8,128)S(1)}, f32[16,8,128]{2,1,0:T(8,128)S(1)}, u32[]{:S(2)}, u32[]{:S(2)}) collective-permute-start(f32[16,8,128]{2,1,0:T(8,128)S(1)} %get-tuple-element.16), channel_id=1, source_target_pairs={{0,4},{4,8},{8,12},{12,16},{16,20},{20,24},{24,28},{28,32},{32,36}... | collective-permute-start | bytes 196616 | tf_op jit(solution)/shard_map/ppermute | solution.py:191

commit v2 on v0

v2 whole, which is shorter than its diff:
```python
import functools

import jax
import jax.numpy as jnp
from jax import lax
from jax.experimental import pallas as pl
from jax.experimental.pallas import tpu as pltpu
from jax.sharding import PartitionSpec as P

STEPS = 4
KERR = 3
ADVANCE = 2
HALF = 0.5

D, E, H, EPS, CHI = 0, 3, 6, 9, 10
ALL = range(11)
NZL, NXL, NY = 8, 32, 128
XH = 4
ROWS = NXL + 2 * XH
EDGE = 24

HI = [(c, p) for p in range(3) for c in ALL]
LO = [(c, 7) for c in ALL] + [(H, 6), (H + 1, 6)]
HI_AT = {k: i for i, k in enumerate(HI)}
LO_AT = {k: i for i, k in enumerate(LO)}
NS = len(HI)

VM = pl.BlockSpec(memory_space=pltpu.VMEM)
HBM = pl.BlockSpec(memory_space=pltpu.HBM)
SM = pl.BlockSpec(memory_space=pltpu.SMEM)


def shape(*dims):
    return jax.ShapeDtypeStruct(dims, jnp.float32)


def rows(*parts):
    return jnp.concatenate(parts, axis=0)


def scalar(condition):
    return jnp.where(condition, 1.0, 0.0).astype(jnp.float32)


def position():
    gz, gx = lax.axis_index("gz"), lax.axis_index("gx")
    return gz, gx, lax.axis_size("gz") - 1, lax.axis_size("gx") - 1


def halo_row():
    return lax.broadcasted_iota(jnp.int32, (8, NY), 0)


def inside_x():
    _, gx, _, last = position()
    return jnp.where(halo_row() < XH, scalar(gx != last), scalar(gx != 0))


class Grid:
    def __init__(self, size, factor, fill):
        self.size, self.factor, self.fill = size, factor, fill
        self.where, self.level = {}, {}
        lane = lax.broadcasted_iota(jnp.int32, (size, NY), 1)
        self.last_y, self.first_y = lane == NY - 1, lane == 0

    def hold(self, comp, plane, read, level=0):
        self.where[(comp, plane)] = read
        self.level[(comp, plane)] = level

    def get(self, comp, plane, level=None):
        assert level is None or self.level[(comp, plane)] == level, (comp, plane)
        return self.where[(comp, plane)]()

    def put(self, ref, index, comp, plane, value, level):
        ref[index] = value
        self.hold(comp, plane, lambda: ref[index], level)

    def next_y(self, v):
        return jnp.where(self.last_y, 0.0, pltpu.roll(v, NY - 1, 1))

    def prev_y(self, v):
        return jnp.where(self.first_y, 0.0, pltpu.roll(v, 1, 1))

    def next_x(self, v):
        return pltpu.roll(v, self.size - 1, 0)

    def prev_x(self, v):
        return pltpu.roll(v, 1, 0)

    def step_h(self, n, p, comps, put):
        f = self.factor(p)
        ex, ey, ez = (self.get(E + c, p, n - 1) for c in range(3))
        new = {}
        if 0 in comps:
            eyn = self.get(E + 1, p + 1, n - 1)
            new[0] = (self.next_y(ez) - ez) - (eyn - ey)
        if 1 in comps:
            exn = self.get(E, p + 1, n - 1)
            new[1] = (exn - ex) - (self.next_x(ez) - ez)
        if 2 in comps:
            new[2] = (self.next_x(ey) - ey) - (self.next_y(ex) - ex)
        for c, curl in new.items():
            put(H + c, p, self.get(H + c, p, n - 1) - f * curl, n)

    def step_de(self, n, p, put):
        f = self.factor(p)
        hx, hy, hz = (self.get(H + c, p, n) for c in range(3))
        hxp, hyp = (self.get(H + c, p - 1, n) for c in range(2))
        dx = self.get(D, p, n - 1) + f * ((hz - self.prev_y(hz)) - (hy - hyp))
        dy = self.get(D + 1, p, n - 1) + f * ((hx - hxp) - (hz - self.prev_x(hz)))
        dz = self.get(D + 2, p, n - 1) + f * ((hy - self.prev_x(hy)) - (hx - self.prev_y(hx)))
        ex, ey, ez = (self.get(E + c, p, n - 1) for c in range(3))
        eps, chi = self.get(EPS, p), self.get(CHI, p)
        fill = self.fill(p)
        if fill is not None:
            eps = eps + fill
        if n == STEPS:
            dx, dy, dz, ex, ey, ez, eps, chi = (v[:NXL] for v in (dx, dy, dz, ex, ey, ez, eps, chi))
        inverse = 1.0 / (eps + chi * (ex * ex + ey * ey + ez * ez))
        squares = chi * (dx * dx + dy * dy + dz * dz)
        for _ in range(KERR - 1):
            inverse = 1.0 / (eps + squares * (inverse * inverse))
        for c, v in enumerate((dx, dy, dz)):
            put(D + c, p, v, n)
            put(E + c, p, v * inverse, n)

    def sweep(self, n, h_planes, de_planes, put):
        for p in range(-2, 11):
            if p in h_planes:
                self.step_h(n, p, range(3), put)
            if p in de_planes:
                self.step_de(n, p, put)


def own(fields, comp, plane):
    d, e, h, eps, chi = fields
    if comp < E:
        return d[comp, plane]
    if comp < H:
        return e[comp - E, plane]
    if comp < EPS:
        return h[comp - H, plane]
    return eps[plane] if comp == EPS else chi[plane]


def load(d, e, h, eps, chi, dv, ev, hv, epsv, chiv, ya, yb, sems):
    moves = [(a.at[c], b.at[c]) for a, b in ((d, dv), (e, ev), (h, hv)) for c in range(3)] + [(eps, epsv), (chi, chiv)]
    copies = [pltpu.make_async_copy(a, b, sems.at[i]) for i, (a, b) in enumerate(moves)]
    for c in copies:
        c.start()
    _, gx, _, last = position()
    even = lax.rem(gx, 2) == 0
    keep = scalar(jnp.logical_and(gx != 0, gx != last))
    for comp in ALL:
        copies[comp].wait()
        for plane in range(NZL):
            v = own((dv, ev, hv, epsv, chiv), comp, plane)
            low, high = v[:XH], v[NXL - XH :]
            ya[comp, plane] = jnp.where(even, high, low)
            yb[comp, plane] = jnp.where(even, low, high) * keep


def early(grid, put):
    grid.sweep(1, range(0, 5), range(1, 5), put)
    grid.sweep(2, range(1, 4), range(2, 4), put)
    grid.sweep(3, range(2, 3), (), put)


def sent(grid, side, i):
    comp, plane = side[i]
    return grid.get(comp, plane)


def inner(d, e, h, eps, chi, fd, fe, fh, lo, out):
    fields = (d, e, h, eps, chi)
    grid = Grid(NXL, lambda p: HALF, lambda p: None)
    for comp in ALL:
        for p in range(NZL):
            grid.hold(comp, p, functools.partial(own, fields, comp, p))
    grid.step_h(1, 6, range(2), lambda c, p, v, n: grid.put(lo, c - H, c, p, v, n))

    def put(c, p, v, n):
        ref = (fd, fe, fh)[c // 3]
        grid.put(ref, (c % 3, p), c, p, v, n)

    early(grid, put)
    gz, _, last, _ = position()
    first_core = lax.rem(gz, 2) == 0
    keep = scalar(jnp.logical_and(gz != 0, gz != last))
    half = halo_row() < XH
    for i in range(NS):
        v = sent(grid, HI, i)
        if i < len(LO):
            v = jnp.where(first_core, v, sent(grid, LO, i))
        v = v * keep
        out[i, 0:8] = jnp.where(half, v[24:32], v[0:8])
        out[i, 8:24] = v[8:24]


def edges(d, e, h, eps, chi, id_, ie, ih, ilo, ra, rb, xt, fd, fe, fh, flo, cross, chip, sd, se, sh, slo):
    fields = (d, e, h, eps, chi)
    _, gx, _, _ = position()
    even = lax.rem(gx, 2) == 0
    for comp in ALL:
        for p in range(NZL):
            a, b = ra[comp, p], rb[comp, p]
            xt[comp, p] = rows(jnp.where(even, a, b), jnp.where(even, b, a))
    edge = inside_x()
    f = rows(jnp.full((8, NY), HALF), edge * HALF, jnp.full((8, NY), HALF))
    none = jnp.zeros((8, NY), jnp.float32)
    fill = rows(none, 1.0 - edge, none)
    grid = Grid(EDGE, lambda p: f, lambda p: fill)

    def read(comp, p):
        v = own(fields, comp, p)
        return rows(v[24:32], xt[comp, p], v[0:8])

    for comp in ALL:
        for p in range(NZL):
            grid.hold(comp, p, functools.partial(read, comp, p))
    grid.step_h(1, 6, range(2), lambda c, p, v, n: grid.put(slo, c - H, c, p, v, n))

    def put(c, p, v, n):
        ref = (sd, se, sh)[c // 3]
        grid.put(ref, (c % 3, p), c, p, v, n)

    early(grid, put)
    half = halo_row() < XH

    def merged(v, w):
        return rows(jnp.where(half, w[16:24], v[0:8]), v[8:24], jnp.where(half, v[24:32], w[0:8]), w[8:16])

    whole = {}
    for (comp, p), level in grid.level.items():
        if comp < EPS and (level or comp >= H and (comp, p) in ((H, 6), (H + 1, 6))):
            if p == 6:
                v, w, ref, index = ilo[comp - H], slo[comp - H], flo, comp - H
            else:
                k = comp // 3
                index = (comp % 3, p)
                v, w, ref = (id_, ie, ih)[k][index], (sd, se, sh)[k][index], (fd, fe, fh)[k]
            ref[index] = merged(v, w)
            whole[(comp, p)] = (ref, index)

    gz, _, last, _ = position()
    first_core = lax.rem(gz, 2) == 0
    keep = scalar(jnp.logical_and(gz != 0, gz != last))

    def frame(comp, p):
        if (comp, p) in whole:
            ref, index = whole[(comp, p)]
            return ref[index]
        return rows(own(fields, comp, p), xt[comp, p])

    for i in range(NS):
        hi = frame(*HI[i])
        if i < len(LO):
            lo = frame(*LO[i])
            there, here = jnp.where(first_core, hi, lo), jnp.where(first_core, lo, hi)
        else:
            there, here = hi, hi
        chip[i] = here
        there = there * keep
        cross[i, 0:8] = jnp.where(half, there[0:8], there[24:32])
        cross[i, 8:16] = there[32:40]


def full_grid():
    gz, _, last, _ = position()
    up, down = scalar(gz != last), scalar(gz != 0)
    edge = inside_x()

    def inside(p):
        return up if p >= NZL else (down if p < 0 else None)

    def factor(p):
        z = inside(p)
        main, tile = jnp.full((NXL, NY), HALF, jnp.float32), edge * HALF
        return rows(main, tile) if z is None else rows(main * z, tile * z)

    def fill(p):
        z = inside(p)
        if z is None:
            return rows(jnp.zeros((NXL, NY), jnp.float32), 1.0 - edge)
        return rows(jnp.full((NXL, NY), 1.0 - z, jnp.float32), 1.0 - edge * z)

    return Grid(ROWS, factor, fill)


def hold_own(grid, fields, xt):
    for comp in ALL:
        for p in range(NZL):
            grid.hold(comp, p, functools.partial(lambda c, q: rows(own(fields, c, q), xt[c, q]), comp, p))


def hold_frames(grid, refs, levels):
    for k, ref in enumerate(refs):
        for p, level in levels[k].items():
            for c in range(3):
                grid.hold(3 * k + c, p, functools.partial(lambda r, a, b: r[a, b], ref, c, p), level)


EARLY = ({1: 1, 2: 2, 3: 2, 4: 1}, {1: 1, 2: 2, 3: 2, 4: 1}, {0: 1, 1: 2, 2: 3, 3: 2, 4: 1})
MIDDLE = ({3: 3, 4: 3, 5: 2, 6: 1}, {3: 3, 4: 3, 5: 2, 6: 1}, {3: 4, 4: 3, 5: 2, 6: 1})


def middle(d, e, h, eps, chi, xt, fd, fe, fh, gd, ge, gh):
    grid = full_grid()
    hold_own(grid, (d, e, h, eps, chi), xt)
    hold_frames(grid, (fd, fe, fh), EARLY)

    def put(c, p, v, n):
        grid.put((gd, ge, gh)[c // 3], (c % 3, p), c, p, v, n)

    grid.sweep(1, (5, 6), (5, 6), put)
    grid.sweep(2, (4, 5), (4, 5), put)
    grid.sweep(3, (3, 4), (3, 4), put)
    grid.sweep(4, (3,), (), put)


def finish(d, e, h, eps, chi, xt, fd, fe, fh, gd, ge, gh, ca, cb, cc, classes, eps_table, chi_table, d_out, e_out, h_out, eps_out, chi_out, sd, se, sh):
    gz, _, last, _ = position()
    first_core = lax.rem(gz, 2) == 0
    last_z = gz == last
    half = halo_row() < XH
    grid = full_grid()
    hold_own(grid, (d, e, h, eps, chi), xt)
    hold_frames(grid, (fd, fe, fh), EARLY)
    hold_frames(grid, (gd, ge, gh), MIDDLE)

    def cross(i):
        m, x = ca[i, 0:8], cb[i, 0:8]
        return rows(jnp.where(half, x, m), ca[i, 8:24], jnp.where(half, m, x), cb[i, 8:16])

    def above(i):
        return jnp.where(first_core, cc[i], cross(i))

    def below(i):
        return jnp.where(first_core, cross(i), cc[i])

    for (comp, p), i in HI_AT.items():
        level = p + 1 if H <= comp < EPS else p
        grid.hold(comp, p + NZL, functools.partial(above, i), level)
    for (comp, p), i in LO_AT.items():
        grid.hold(comp, p - NZL, functools.partial(below, i), 1 if p == 6 else 0)

    def put(c, p, v, n):
        k = c // 3
        if n == STEPS:
            o = p - ADVANCE
            if o >= 0:
                (d_out, e_out, h_out)[k][c % 3, o] = v[:NXL]
            if k < 2:
                return
        grid.put((sd, se, sh)[k], (c % 3, p + 2), c, p, v, n)

    grid.sweep(1, (-1,), (-1, 0), put)
    grid.sweep(2, (-1, 0), (0, 1), put)
    grid.sweep(3, (0, 1), (1, 2), put)
    grid.sweep(4, (1, 2), (2, 3), put)
    for c in range(3):
        h_out[c, 3 - ADVANCE] = grid.get(H + c, 3, 4)[:NXL]
    grid.sweep(1, (7,), (7, 8), put)
    grid.sweep(2, range(6, 9), range(6, 10), put)
    grid.sweep(3, range(5, 10), range(5, 11), put)
    grid.sweep(4, range(4, 10), range(4, 10), put)

    for ref, comp, out, table in ((eps, EPS, eps_out, eps_table), (chi, CHI, chi_out, chi_table)):
        for plane in range(ADVANCE, NZL):
            out[plane - ADVANCE] = ref[plane]
        for k in range(ADVANCE):
            picked = jnp.zeros((NXL, NY), jnp.float32)
            for label in range(table.shape[0]):
                picked = jnp.where(classes[k] == label, table[label], picked)
            out[NZL - ADVANCE + k] = jnp.where(last_z, picked, grid.get(comp, NZL + k)[:NXL])


def pairs(axis, first):
    n = lax.axis_size(axis)
    out = []
    for i in range(first, n, 2):
        j = (i + 1) % n
        out += [(i, j), (j, i)]
    return out


def swapped(shard, axis, first):
    return lax.ppermute(shard, axis, pairs(axis, first))


def call(body, name, inputs, out_shape, scratch=(), vmem=8, specs=None):
    return pl.pallas_call(
        body,
        out_shape=out_shape,
        in_specs=[VM] * len(inputs) if specs is None else specs,
        out_specs=jax.tree.map(lambda _: VM, out_shape),
        scratch_shapes=list(scratch),
        compiler_params=pltpu.CompilerParams(vmem_limit_bytes=vmem << 20),
        name=name,
    )(*inputs)


def on_device(d_field, e_field, h_field, permittivity, kerr_coeff, classes, eps_table, chi_table):
    field, medium = shape(3, NZL, NXL, NY), shape(NZL, NXL, NY)
    halo = shape(11, NZL, XH, NY)
    *fields, ya, yb = call(
        load,
        "load",
        [pltpu.with_memory_space_constraint(a, pltpu.HBM) for a in (d_field, e_field, h_field, permittivity, kerr_coeff)],
        (field, field, field, medium, medium, halo, halo),
        [pltpu.SemaphoreType.DMA((11,))],
        specs=[HBM] * 5,
    )
    ra, rb = swapped(ya, "gx", 0), swapped(yb, "gx", 1)
    frames = [shape(3, 5, NXL, NY)] * 3
    lo = shape(2, NXL, NY)
    *inside, za = call(inner, "inner", fields, (*frames, lo, shape(NS, 24, NY)))
    ca = swapped(za, "gz", 1)
    frames = [shape(3, 5, ROWS, NY)] * 3
    scratch = [pltpu.VMEM((3, 5, EDGE, NY), jnp.float32)] * 3 + [pltpu.VMEM((2, EDGE, NY), jnp.float32)]
    xt, *frames, _, zb, zc = call(
        edges,
        "edges",
        [*fields, *inside, ra, rb],
        (shape(11, NZL, 8, NY), *frames, shape(2, ROWS, NY), shape(NS, 16, NY), shape(NS, ROWS, NY)),
        scratch,
    )
    cb, cc = swapped(zb, "gz", 1), swapped(zc, "gz", 0)
    more = call(middle, "middle", [*fields, xt, *frames], (shape(3, 7, ROWS, NY),) * 3)
    state = pltpu.VMEM((3, 13, ROWS, NY), jnp.float32)
    inputs = [*fields, xt, *frames, *more, ca, cb, cc, classes, eps_table, chi_table]
    return call(
        finish,
        "finish",
        inputs,
        (field, field, field, medium, medium),
        [state] * 3,
        vmem=16,
        specs=[VM] * (len(inputs) - 2) + [SM, SM],
    )


def solution(mesh):
    placed = (
        P(None, "gz", "gx", None),
        P(None, "gz", "gx", None),
        P(None, "gz", "gx", None),
        P("gz", "gx", None),
        P("gz", "gx", None),
        P(None, "gx", None),
        P(),
        P(),
    )
    return jax.shard_map(
        on_device,
        mesh=mesh,
        in_specs=placed,
        out_specs=placed[:5],
        check_vma=False,
    )
```

time: 101 us -> 32.5 us (0.32)
  the two profiles are of different devices: /device:TPU:111 before, /device:TPU:24 now
where the time goes in v2:
time: 32.5 us; the launch traced here: 32.4 us
  waiting for transfers between devices  14.1 us (43%)
  starting transfers between devices  10.3 us (32%)
  Pallas kernels  6.56 us (20%)
  local copies, waits for them, and re-layouts  0.67 us (2%)
  between operations  0.66 us (2%)
    ppermute x5, waiting for transfers between devices, swapped(): return lax.ppermute(shard, axis, pairs(axis, first))  14.1 us
    ppermute x5, starting transfers between devices, swapped(): return lax.ppermute(shard, axis, pairs(axis, first))  10.3 us
    pallas_call x5, Pallas kernels, call(): pl.pallas_call(body, out_shape=out_shape, in_specs=[VM] * len(inputs) if...  6.56 us
    unnamed x6, local copies, waits for them, and re-layouts  0.67 us
  transfers between devices with their start and end apart: 5, of which 4 were waited for; matrix products, arithmetic and copies ran while one was open for 0% of the time, Pallas kernels for 3%

profile of v2, /device:TPU:24, one launch (start us, length us, event | category | flops | bytes accessed | tf_op | source)
XLA Modules:
  0.0 32.4 jit_solution(16602799406877591089)
XLA Ops:
  0.6 1.5 %load.1 = (f32[3,8,32,128]{3,2,1,0:T(8,128)S(1)}, f32[3,8,32,128]{3,2,1,0:T(8,128)S(1)}, f32[3,8,32,128]{3,2,1,0:T(8,128)S(1)}, f32[8,32,128]{2,1,0:T(8,128)S(1)...) custom-call(f32[3,8,32,128]{3,2,1,0:T(8,128)} %d.1, ...), custom_call_target="tpu_custom_call" | custom-call | tf_op jit(solution)/shard_map/load/pallas_call | solution.py:392
  2.1 0.8 %collective-permute-start = (f32[11,8,4,128]{3,2,1,0:T(4,128)S(1)}, f32[11,8,4,128]{3,2,1,0:T(4,128)S(1)}, u32[]{:S(2)}, u32[]{:S(2)}) collective-permute-start(f32[11,8,4,128]{3,2,1,0:T(4,128)S(1)} %get-tuple-element.35), channel_id=1, source_target_pairs={{0,1},{1,0},{2,3},{3,2},{4,5},{5,4},{6,7},{7,6},{8,9},{9,8},{10,11... | collective-permute-start | bytes 540680 | tf_op jit(solution)/shard_map/ppermute | solution.py:388
  3.0 1.3 %collective-permute-start.1 = (f32[11,8,4,128]{3,2,1,0:T(4,128)S(1)}, f32[11,8,4,128]{3,2,1,0:T(4,128)S(1)}, u32[]{:S(2)}, u32[]{:S(2)}) collective-permute-start(f32[11,8,4,128]{3,2,1,0:T(4,128)S(1)} %get-tuple-element.36), channel_id=1, source_target_pairs={{1,2},{2,1},{3,0},{0,3},{5,6},{6,5},{7,4},{4,7},{9,10},{10,9},{11,... | collective-permute-start | bytes 540680 | tf_op jit(solution)/shard_map/ppermute | solution.py:388
  4.3 0.4 %inner.1 = (f32[3,5,32,128]{3,2,1,0:T(8,128)S(1)}, f32[3,5,32,128]{3,2,1,0:T(8,128)S(1)}, f32[3,5,32,128]{3,2,1,0:T(8,128)S(1)}, f32[2,32,128]{2,1,0:T(8,128)S(1)}, f32[33,24,128]{2,1,0:T(8,128)S(1)}) custom-call(f32[3,8,32,128]{3,2,1,0:T(8,128)S(1)} %get-tuple-element.26.d, f32[3,8,32,128]{3,2,1,0:T(8,128)S(1)} %get-tuple-element.27.e, ...), custom_call_target="tpu_custom_call" | custom-call | tf_op jit(solution)/shard_map/inner/pallas_call | solution.py:392
  4.7 3.8 %collective-permute-done.ra = f32[11,8,4,128]{3,2,1,0:T(4,128)S(1)} collective-permute-done((f32[11,8,4,128]{3,2,1,0:T(4,128)S(1)}, f32[11,8,4,128]{3,2,1,0:T(4,128)S(1)}, u32[]{:S(2)}, u32[]{:S(2)}) %collective-permute-start) | collective-permute-done | bytes 180256 | tf_op jit(solution)/shard_map/ppermute | solution.py:388
  8.5 1.7 %collective-permute-done.1.rb = f32[11,8,4,128]{3,2,1,0:T(4,128)S(1)} collective-permute-done((f32[11,8,4,128]{3,2,1,0:T(4,128)S(1)}, f32[11,8,4,128]{3,2,1,0:T(4,128)S(1)}, u32[]{:S(2)}, u32[]{:S(2)}) %collective-permute-start.1) | collective-permute-done | bytes 180256 | tf_op jit(solution)/shard_map/ppermute | solution.py:388
  10.2 1.1 %edges.1 = (f32[11,8,8,128]{3,2,1,0:T(8,128)S(1)}, f32[3,5,40,128]{3,2,1,0:T(8,128)S(1)}, f32[3,5,40,128]{3,2,1,0:T(8,128)S(1)}, f32[3,5,40,128]{3,2,1,0:T(8,128...) custom-call(f32[3,8,32,128]{3,2,1,0:T(8,128)S(1)} %get-tuple-element.26.d, ...), custom_call_target="tpu_custom_call" | custom-call | tf_op jit(solution)/shard_map/edges/pallas_call | solution.py:392
  11.3 0.0 collective-permute-start.4
  11.3 8.2 %collective-permute-start.2 = (f32[33,24,128]{2,1,0:T(8,128)S(1)}, f32[33,24,128]{2,1,0:T(8,128)S(1)}, u32[]{:S(2)}, u32[]{:S(2)}) collective-permute-start(f32[33,24,128]{2,1,0:T(8,128)S(1)} %get-tuple-element.44), channel_id=1, source_target_pairs={{4,8},{8,4},{12,16},{16,12},{20,24},{24,20},{28,32},{32,28},{36,40... | collective-permute-start | bytes 1216520 | tf_op jit(solution)/shard_map/ppermute | solution.py:388
  19.4 0.0 collective-permute-start.3
  19.5 0.0 copy-start
  19.5 0.5 %middle.1 = (f32[3,7,40,128]{3,2,1,0:T(8,128)S(1)}, f32[3,7,40,128]{3,2,1,0:T(8,128)S(1)}, f32[3,7,40,128]{3,2,1,0:T(8,128)S(1)}) custom-call(f32[3,8,32,128]{3,2,1,0:T(8,128)S(1)} %get-tuple-element.26.d, f32[3,8,32,128]{3,2,1,0:T(8,128)S(1)} %get-tuple-element.27.e, f32[3,8,32,128]{3,2,1,0:T(8,128)S(1)} %get-tuple-element.28.h, ...), custom_call_target="tpu_custom_call" | custom-call | tf_op jit(solution)/shard_map/middle/pallas_call | solution.py:392
  20.0 5.0 %collective-permute-done.2.ca = f32[33,24,128]{2,1,0:T(8,128)S(1)} collective-permute-done((f32[33,24,128]{2,1,0:T(8,128)S(1)}, f32[33,24,128]{2,1,0:T(8,128)S(1)}, u32[]{:S(2)}, u32[]{:S(2)}) %collective-permute-start.2) | collective-permute-done | bytes 405536 | tf_op jit(solution)/shard_map/ppermute | solution.py:388
  25.0 3.6 %collective-permute-done.3.cb = f32[33,16,128]{2,1,0:T(8,128)S(1)} collective-permute-done((f32[33,16,128]{2,1,0:T(8,128)S(1)}, f32[33,16,128]{2,1,0:T(8,128)S(1)}, u32[]{:S(2)}, u32[]{:S(2)}) %collective-permute-start.3) | collective-permute-done | bytes 270368 | tf_op jit(solution)/shard_map/ppermute | solution.py:388
  28.6 0.0 collective-permute-done.4.cc
  28.7 0.0 copy-start.1
  28.7 0.0 copy-start.2
  28.7 0.0 copy-done
  28.7 0.6 %copy-done.1 = f32[8]{0:T(128)S(1)} copy-done((f32[8]{0:T(128)S(1)}, f32[8]{0:T(128)}, u32[]{:S(2)}) %copy-start.1) | copy-done | bytes 56
  29.3 0.0 copy-done.2
  29.3 3.0 %finish.1 = (f32[3,8,32,128]{3,2,1,0:T(8,128)}, f32[3,8,32,128]{3,2,1,0:T(8,128)}, f32[3,8,32,128]{3,2,1,0:T(8,128)}, f32[8,32,128]{2,1,0:T(8,128)}, f32[8,32,128]{2,1,0:T(8,128)}) custom-call(f32[3,8,32,128]{3,2,1,0:T(8,128)S(1)} %get-tuple-element.26.d, f32[3,8,32,128]{3,2,1,0:T(8,128)S(1)} %get-tuple-element.27.e, ...), custom_call_target="tpu_custom_call" | custom-call | tf_op jit(solution)/shard_map/finish/pallas_call | solution.py:392
Async XLA Ops:
  2.1 6.4 %collective-permute-start = (f32[11,8,4,128]{3,2,1,0:T(4,128)S(1)}, f32[11,8,4,128]{3,2,1,0:T(4,128)S(1)}, u32[]{:S(2)}, u32[]{:S(2)}) collective-permute-start(f32[11,8,4,128]{3,2,1,0:T(4,128)S(1)} %get-tuple-element.35), channel_id=1, source_target_pairs={{0,1},{1,0},{2,3},{3,2},{4,5},{5,4},{6,7},{7,6},{8,9},{9,8},{10,11... | collective-permute-start | bytes 540680 | tf_op jit(solution)/shard_map/ppermute | solution.py:388
  3.0 7.2 %collective-permute-start.1 = (f32[11,8,4,128]{3,2,1,0:T(4,128)S(1)}, f32[11,8,4,128]{3,2,1,0:T(4,128)S(1)}, u32[]{:S(2)}, u32[]{:S(2)}) collective-permute-start(f32[11,8,4,128]{3,2,1,0:T(4,128)S(1)} %get-tuple-element.36), channel_id=1, source_target_pairs={{1,2},{2,1},{3,0},{0,3},{5,6},{6,5},{7,4},{4,7},{9,10},{10,9},{11,... | collective-permute-start | bytes 540680 | tf_op jit(solution)/shard_map/ppermute | solution.py:388
  11.3 17.4 %collective-permute-start.4 = (f32[33,40,128]{2,1,0:T(8,128)S(1)}, f32[33,40,128]{2,1,0:T(8,128)S(1)}, u32[]{:S(2)}, u32[]{:S(2)}) collective-permute-start(f32[33,40,128]{2,1,0:T(8,128)S(1)} %get-tuple-element.46), channel_id=1, source_target_pairs={{0,4},{4,0},{8,12},{12,8},{16,20},{20,16},{24,28},{28,24},{32,36},... | collective-permute-start | bytes 2027528 | tf_op jit(solution)/shard_map/ppermute | solution.py:388
  11.3 13.8 %collective-permute-start.2 = (f32[33,24,128]{2,1,0:T(8,128)S(1)}, f32[33,24,128]{2,1,0:T(8,128)S(1)}, u32[]{:S(2)}, u32[]{:S(2)}) collective-permute-start(f32[33,24,128]{2,1,0:T(8,128)S(1)} %get-tuple-element.44), channel_id=1, source_target_pairs={{4,8},{8,4},{12,16},{16,12},{20,24},{24,20},{28,32},{32,28},{36,40... | collective-permute-start | bytes 1216520 | tf_op jit(solution)/shard_map/ppermute | solution.py:388
  19.4 9.2 %collective-permute-start.3 = (f32[33,16,128]{2,1,0:T(8,128)S(1)}, f32[33,16,128]{2,1,0:T(8,128)S(1)}, u32[]{:S(2)}, u32[]{:S(2)}) collective-permute-start(f32[33,16,128]{2,1,0:T(8,128)S(1)} %get-tuple-element.45), channel_id=1, source_target_pairs={{4,8},{8,4},{12,16},{16,12},{20,24},{24,20},{28,32},{32,28},{36,40... | collective-permute-start | bytes 811016 | tf_op jit(solution)/shard_map/ppermute | solution.py:388
  19.5 9.2 %copy-start = (s32[2,32,128]{2,1,0:T(8,128)S(1)}, s32[2,32,128]{2,1,0:T(8,128)}, u32[]{:S(2)}) copy-start(s32[2,32,128]{2,1,0:T(8,128)} %classes.1) | copy-start | bytes 98308
  28.7 0.7 %copy-start.1 = (f32[8]{0:T(128)S(1)}, f32[8]{0:T(128)}, u32[]{:S(2)}) copy-start(f32[8]{0:T(128)} %eps_table.1) | copy-start | bytes 100
  28.7 0.7 %copy-start.2 = (f32[8]{0:T(128)S(1)}, f32[8]{0:T(128)}, u32[]{:S(2)}) copy-start(f32[8]{0:T(128)} %chi_table.1) | copy-start | bytes 100

commit v3 on v2

--- a/solution.py
+++ b/solution.py
@@ -6,6 +6,7 @@
 from jax.experimental import pallas as pl
 from jax.experimental.pallas import tpu as pltpu
 from jax.sharding import PartitionSpec as P
+
 
 STEPS = 4
 KERR = 3
@@ -166,6 +167,15 @@
     grid.sweep(3, range(2, 3), (), put)
 
 
+def lookup(classes, eps_table, chi_table, eps_in, chi_in):
+    for out, table in ((eps_in, eps_table), (chi_in, chi_table)):
+        for k in range(ADVANCE):
+            picked = jnp.zeros((NXL, NY), jnp.float32)
+            for label in range(table.shape[0]):
+                picked = jnp.where(classes[k] == label, table[label], picked)
+            out[k] = picked
+
+
 def sent(grid, side, i):
     comp, plane = side[i]
     return grid.get(comp, plane)
@@ -184,15 +194,13 @@
         grid.put(ref, (c % 3, p), c, p, v, n)
 
     early(grid, put)
-    gz, _, last, _ = position()
+    gz, _, _, _ = position()
     first_core = lax.rem(gz, 2) == 0
-    keep = scalar(jnp.logical_and(gz != 0, gz != last))
     half = halo_row() < XH
     for i in range(NS):
         v = sent(grid, HI, i)
         if i < len(LO):
             v = jnp.where(first_core, v, sent(grid, LO, i))
-        v = v * keep
         out[i, 0:8] = jnp.where(half, v[24:32], v[0:8])
         out[i, 8:24] = v[8:24]
 
@@ -242,9 +250,8 @@
             ref[index] = merged(v, w)
             whole[(comp, p)] = (ref, index)
 
-    gz, _, last, _ = position()
+    gz, _, _, _ = position()
     first_core = lax.rem(gz, 2) == 0
-    keep = scalar(jnp.logical_and(gz != 0, gz != last))
 
     def frame(comp, p):
         if (comp, p) in whole:
@@ -260,7 +267,6 @@
         else:
             there, here = hi, hi
         chip[i] = here
-        there = there * keep
         cross[i, 0:8] = jnp.where(half, there[0:8], there[24:32])
         cross[i, 8:16] = there[32:40]
 
@@ -318,7 +324,7 @@
     grid.sweep(4, (3,), (), put)
 
 
-def finish(d, e, h, eps, chi, xt, fd, fe, fh, gd, ge, gh, ca, cb, cc, classes, eps_table, chi_table, d_out, e_out, h_out, eps_out, chi_out, sd, se, sh):
+def finish(d, e, h, eps, chi, xt, fd, fe, fh, gd, ge, gh, ca, cb, cc, eps_in, chi_in, d_out, e_out, h_out, eps_out, chi_out, sd, se, sh):
     gz, _, last, _ = position()
     first_core = lax.rem(gz, 2) == 0
     last_z = gz == last
@@ -365,30 +371,31 @@
     grid.sweep(3, range(5, 10), range(5, 11), put)
     grid.sweep(4, range(4, 10), range(4, 10), put)
 
-    for ref, comp, out, table in ((eps, EPS, eps_out, eps_table), (chi, CHI, chi_out, chi_table)):
+    for ref, comp, out, new in ((eps, EPS, eps_out, eps_in), (chi, CHI, chi_out, chi_in)):
         for plane in range(ADVANCE, NZL):
             out[plane - ADVANCE] = ref[plane]
         for k in range(ADVANCE):
-            picked = jnp.zeros((NXL, NY), jnp.float32)
-            for label in range(table.shape[0]):
-                picked = jnp.where(classes[k] == label, table[label], picked)
-            out[NZL - ADVANCE + k] = jnp.where(last_z, picked, grid.get(comp, NZL + k)[:NXL])
-
-
-def pairs(axis, first):
-    n = lax.axis_size(axis)
-    out = []
-    for i in range(first, n, 2):
-        j = (i + 1) % n
-        out += [(i, j), (j, i)]
-    return out
+            out[NZL - ADVANCE + k] = jnp.where(last_z, new[k], grid.get(comp, NZL + k)[:NXL])
 
 
 def swapped(shard, axis, first):
-    return lax.ppermute(shard, axis, pairs(axis, first))
-
-
-def call(body, name, inputs, out_shape, scratch=(), vmem=8, specs=None):
+    n = {a: lax.axis_size(a) for a in ("gz", "gx")}
+    moves = []
+    for z in range(n["gz"]):
+        for x in range(n["gx"]):
+            at = z if axis == "gz" else x
+            to = at + 1 if at % 2 == first else at - 1
+            if 0 <= to < n[axis]:
+                other = (to, x) if axis == "gz" else (z, to)
+            elif axis == "gx":
+                other = (z ^ 1, x)
+            else:
+                continue
+            moves.append((z * n["gx"] + x, other[0] * n["gx"] + other[1]))
+    return lax.ppermute(shard, ("gz", "gx"), moves)
+
+
+def call(body, inputs, out_shape, scratch=(), vmem=8, specs=None):
     return pl.pallas_call(
         body,
         out_shape=out_shape,
@@ -396,7 +403,6 @@
         out_specs=jax.tree.map(lambda _: VM, out_shape),
         scratch_shapes=list(scratch),
         compiler_params=pltpu.CompilerParams(vmem_limit_bytes=vmem << 20),
-        name=name,
     )(*inputs)
 
 
@@ -405,7 +411,6 @@
     halo = shape(11, NZL, XH, NY)
     *fields, ya, yb = call(
         load,
-        "load",
         [pltpu.with_memory_space_constraint(a, pltpu.HBM) for a in (d_field, e_field, h_field, permittivity, kerr_coeff)],
         (field, field, field, medium, medium, halo, halo),
         [pltpu.SemaphoreType.DMA((11,))],
@@ -414,30 +419,22 @@
     ra, rb = swapped(ya, "gx", 0), swapped(yb, "gx", 1)
     frames = [shape(3, 5, NXL, NY)] * 3
     lo = shape(2, NXL, NY)
-    *inside, za = call(inner, "inner", fields, (*frames, lo, shape(NS, 24, NY)))
+    *inside, za = call(inner, fields, (*frames, lo, shape(NS, 24, NY)))
     ca = swapped(za, "gz", 1)
+    coming = call(lookup, [classes, eps_table, chi_table], (shape(ADVANCE, NXL, NY),) * 2, specs=[VM, SM, SM])
     frames = [shape(3, 5, ROWS, NY)] * 3
     scratch = [pltpu.VMEM((3, 5, EDGE, NY), jnp.float32)] * 3 + [pltpu.VMEM((2, EDGE, NY), jnp.float32)]
     xt, *frames, _, zb, zc = call(
         edges,
-        "edges",
         [*fields, *inside, ra, rb],
         (shape(11, NZL, 8, NY), *frames, shape(2, ROWS, NY), shape(NS, 16, NY), shape(NS, ROWS, NY)),
         scratch,
     )
     cb, cc = swapped(zb, "gz", 1), swapped(zc, "gz", 0)
-    more = call(middle, "middle", [*fields, xt, *frames], (shape(3, 7, ROWS, NY),) * 3)
+    more = call(middle, [*fields, xt, *frames], (shape(3, 7, ROWS, NY),) * 3)
     state = pltpu.VMEM((3, 13, ROWS, NY), jnp.float32)
-    inputs = [*fields, xt, *frames, *more, ca, cb, cc, classes, eps_table, chi_table]
-    return call(
-        finish,
-        "finish",
-        inputs,
-        (field, field, field, medium, medium),
-        [state] * 3,
-        vmem=16,
-        specs=[VM] * (len(inputs) - 2) + [SM, SM],
-    )
+    inputs = [*fields, xt, *frames, *more, ca, cb, cc, *coming]
+    return call(finish, inputs, (field, field, field, medium, medium), [state] * 3, vmem=16)
 
 
 def solution(mesh):

time: 32.5 us -> 29.7 us (0.914)
  the two profiles are of different devices: /device:TPU:24 before, /device:TPU:111 now
where the time goes in v3:
time: 29.7 us; the launch traced here: 29.4 us
  starting transfers between devices  12.9 us (43%)
  waiting for transfers between devices  9.17 us (31%)
  Pallas kernels  6.63 us (22%)
  between operations  0.7 us (2%)
    ppermute x5, starting transfers between devices, swapped(): return lax.ppermute(shard, ('gz', 'gx'), moves)  12.9 us
    ppermute x5, waiting for transfers between devices, swapped(): return lax.ppermute(shard, ('gz', 'gx'), moves)  9.17 us
    pallas_call x6, Pallas kernels, call(): pl.pallas_call(body, out_shape=out_shape, in_specs=[VM] * len(inputs) if...  6.63 us
  transfers between devices with their start and end apart: 5, of which 4 were waited for; matrix products, arithmetic and copies ran while one was open for 0% of the time, Pallas kernels for 5%

profile of v3, /device:TPU:111, one launch (start us, length us, event | category | flops | bytes accessed | tf_op | source)
XLA Modules:
  0.0 29.4 jit_solution(5808929670478923260)
XLA Ops:
  0.6 1.5 %shard_map.119 = (f32[3,8,32,128]{3,2,1,0:T(8,128)S(1)}, f32[3,8,32,128]{3,2,1,0:T(8,128)S(1)}, f32[3,8,32,128]{3,2,1,0:T(8,128)S(1)}, f32[8,32,128]{2,1,0:T(8,1...) custom-call(f32[3,8,32,128]{3,2,1,0:T(8,128)} %d.1, ...), custom_call_target="tpu_custom_call" | custom-call | tf_op jit(solution)/shard_map/pallas_call | solution.py:399
  2.1 0.3 collective-permute-start
  2.4 2.1 %collective-permute-start.1 = (f32[11,8,4,128]{3,2,1,0:T(4,128)S(1)}, f32[11,8,4,128]{3,2,1,0:T(4,128)S(1)}, u32[]{:S(2)}, u32[]{:S(2)}) collective-permute-start(f32[11,8,4,128]{3,2,1,0:T(4,128)S(1)} %get-tuple-element.38), channel_id=1, source_target_pairs={{0,4},{1,2},{2,1},{3,7},{4,0},{5,6},{6,5},{7,3},{8,12},{9,10},{10,... | collective-permute-start | bytes 540680 | tf_op jit(solution)/shard_map/ppermute | solution.py:395
  4.5 0.4 %shard_map.120 = (f32[3,5,32,128]{3,2,1,0:T(8,128)S(1)}, f32[3,5,32,128]{3,2,1,0:T(8,128)S(1)}, f32[3,5,32,128]{3,2,1,0:T(8,128)S(1)}, f32[2,32,128]{2,1,0:T(8,128)S(1)}, f32[33,24,128]{2,1,0:T(8,128)S(1)}) custom-call(f32[3,8,32,128]{3,2,1,0:T(8,128)S(1)} %get-tuple-element.28.d, f32[3,8,32,128]{3,2,1,0:T(8,128)S(1)} %get-tuple-element.29.e, ...), custom_call_target="tpu_custom_call" | custom-call | tf_op jit(solution)/shard_map/pallas_call | solution.py:399
  5.0 2.7 %collective-permute-done.ra = f32[11,8,4,128]{3,2,1,0:T(4,128)S(1)} collective-permute-done((f32[11,8,4,128]{3,2,1,0:T(4,128)S(1)}, f32[11,8,4,128]{3,2,1,0:T(4,128)S(1)}, u32[]{:S(2)}, u32[]{:S(2)}) %collective-permute-start) | collective-permute-done | bytes 180256 | tf_op jit(solution)/shard_map/ppermute | solution.py:395
  7.7 0.8 %collective-permute-done.1.rb = f32[11,8,4,128]{3,2,1,0:T(4,128)S(1)} collective-permute-done((f32[11,8,4,128]{3,2,1,0:T(4,128)S(1)}, f32[11,8,4,128]{3,2,1,0:T(4,128)S(1)}, u32[]{:S(2)}, u32[]{:S(2)}) %collective-permute-start.1) | collective-permute-done | bytes 180256 | tf_op jit(solution)/shard_map/ppermute | solution.py:395
  8.5 0.0 copy-start
  8.5 1.1 %shard_map.121 = (f32[11,8,8,128]{3,2,1,0:T(8,128)S(1)}, f32[3,5,40,128]{3,2,1,0:T(8,128)S(1)}, f32[3,5,40,128]{3,2,1,0:T(8,128)S(1)}, f32[3,5,40,128]{3,2,1,0:T...) custom-call(f32[3,8,32,128]{3,2,1,0:T(8,128)S(1)} %get-tuple-element.28.d, ...), custom_call_target="tpu_custom_call" | custom-call | tf_op jit(solution)/shard_map/pallas_call | solution.py:399
  9.6 1.5 %collective-permute-start.4 = (f32[33,40,128]{2,1,0:T(8,128)S(1)}, f32[33,40,128]{2,1,0:T(8,128)S(1)}, u32[]{:S(2)}, u32[]{:S(2)}) collective-permute-start(f32[33,40,128]{2,1,0:T(8,128)S(1)} %get-tuple-element.48), channel_id=1, source_target_pairs={{0,4},{1,5},{2,6},{3,7},{4,0},{5,1},{6,2},{7,3},{8,12},{9,13},{10,... | collective-permute-start | bytes 2027528 | tf_op jit(solution)/shard_map/ppermute | solution.py:395
  11.1 0.0 copy-start.1
  11.1 0.0 copy-start.2
  11.1 4.7 %collective-permute-start.2 = (f32[33,24,128]{2,1,0:T(8,128)S(1)}, f32[33,24,128]{2,1,0:T(8,128)S(1)}, u32[]{:S(2)}, u32[]{:S(2)}) collective-permute-start(f32[33,24,128]{2,1,0:T(8,128)S(1)} %get-tuple-element.46), channel_id=1, source_target_pairs={{4,8},{5,9},{6,10},{7,11},{8,4},{9,5},{10,6},{11,7},{12,16},{13,17... | collective-permute-start | bytes 1216520 | tf_op jit(solution)/shard_map/ppermute | solution.py:395
  15.8 4.3 %collective-permute-start.3 = (f32[33,16,128]{2,1,0:T(8,128)S(1)}, f32[33,16,128]{2,1,0:T(8,128)S(1)}, u32[]{:S(2)}, u32[]{:S(2)}) collective-permute-start(f32[33,16,128]{2,1,0:T(8,128)S(1)} %get-tuple-element.47), channel_id=1, source_target_pairs={{4,8},{5,9},{6,10},{7,11},{8,4},{9,5},{10,6},{11,7},{12,16},{13,17... | collective-permute-start | bytes 811016 | tf_op jit(solution)/shard_map/ppermute | solution.py:395
  20.1 0.0 copy-done
  20.2 0.0 copy-done.1
  20.2 0.0 copy-done.2
  20.2 0.6 %shard_map.123 = (f32[2,32,128]{2,1,0:T(8,128)S(1)}, f32[2,32,128]{2,1,0:T(8,128)S(1)}) custom-call(s32[2,32,128]{2,1,0:T(8,128)S(1)} %copy-done, f32[8]{0:T(128)S(1)} %copy-done.1, f32[8]{0:T(128)S(1)} %copy-done.2), custom_call_target="tpu_custom_call" | custom-call | tf_op jit(solution)/shard_map/pallas_call | solution.py:399
  20.8 0.5 %shard_map.122 = (f32[3,7,40,128]{3,2,1,0:T(8,128)S(1)}, f32[3,7,40,128]{3,2,1,0:T(8,128)S(1)}, f32[3,7,40,128]{3,2,1,0:T(8,128)S(1)}) custom-call(f32[3,8,32,128]{3,2,1,0:T(8,128)S(1)} %get-tuple-element.28.d, f32[3,8,32,128]{3,2,1,0:T(8,128)S(1)} %get-tuple-element.29.e, f32[3,8,32,128]{3,2,1,0:T(8,128)S(1)} %get-tuple-element.30.h, ...), custom_call_target="tpu_custom_call" | custom-call | tf_op jit(solution)/shard_map/pallas_call | solution.py:399
  21.3 2.5 %collective-permute-done.2.ca = f32[33,24,128]{2,1,0:T(8,128)S(1)} collective-permute-done((f32[33,24,128]{2,1,0:T(8,128)S(1)}, f32[33,24,128]{2,1,0:T(8,128)S(1)}, u32[]{:S(2)}, u32[]{:S(2)}) %collective-permute-start.2) | collective-permute-done | bytes 405536 | tf_op jit(solution)/shard_map/ppermute | solution.py:395
  23.8 3.1 %collective-permute-done.3.cb = f32[33,16,128]{2,1,0:T(8,128)S(1)} collective-permute-done((f32[33,16,128]{2,1,0:T(8,128)S(1)}, f32[33,16,128]{2,1,0:T(8,128)S(1)}, u32[]{:S(2)}, u32[]{:S(2)}) %collective-permute-start.3) | collective-permute-done | bytes 270368 | tf_op jit(solution)/shard_map/ppermute | solution.py:395
  26.9 0.0 collective-permute-done.4.cc
  26.9 2.5 %shard_map.124 = (f32[3,8,32,128]{3,2,1,0:T(8,128)}, f32[3,8,32,128]{3,2,1,0:T(8,128)}, f32[3,8,32,128]{3,2,1,0:T(8,128)}, f32[8,32,128]{2,1,0:T(8,128)}, f32[8,32,128]{2,1,0:T(8,128)}) custom-call(f32[3,8,32,128]{3,2,1,0:T(8,128)S(1)} %get-tuple-element.28.d, f32[3,8,32,128]{3,2,1,0:T(8,128)S(1)} %get-tuple-element.29.e, ...), custom_call_target="tpu_custom_call" | custom-call | tf_op jit(solution)/shard_map/pallas_call | solution.py:399
Async XLA Ops:
  2.1 5.5 %collective-permute-start = (f32[11,8,4,128]{3,2,1,0:T(4,128)S(1)}, f32[11,8,4,128]{3,2,1,0:T(4,128)S(1)}, u32[]{:S(2)}, u32[]{:S(2)}) collective-permute-start(f32[11,8,4,128]{3,2,1,0:T(4,128)S(1)} %get-tuple-element.37), channel_id=1, source_target_pairs={{0,1},{1,0},{2,3},{3,2},{4,5},{5,4},{6,7},{7,6},{8,9},{9,8},{10,11... | collective-permute-start | bytes 540680 | tf_op jit(solution)/shard_map/ppermute | solution.py:395
  2.4 6.1 %collective-permute-start.1 = (f32[11,8,4,128]{3,2,1,0:T(4,128)S(1)}, f32[11,8,4,128]{3,2,1,0:T(4,128)S(1)}, u32[]{:S(2)}, u32[]{:S(2)}) collective-permute-start(f32[11,8,4,128]{3,2,1,0:T(4,128)S(1)} %get-tuple-element.38), channel_id=1, source_target_pairs={{0,4},{1,2},{2,1},{3,7},{4,0},{5,6},{6,5},{7,3},{8,12},{9,10},{10,... | collective-permute-start | bytes 540680 | tf_op jit(solution)/shard_map/ppermute | solution.py:395
  8.5 11.6 %copy-start = (s32[2,32,128]{2,1,0:T(8,128)S(1)}, s32[2,32,128]{2,1,0:T(8,128)}, u32[]{:S(2)}) copy-start(s32[2,32,128]{2,1,0:T(8,128)} %classes.1) | copy-start | bytes 98308
  9.6 17.3 %collective-permute-start.4 = (f32[33,40,128]{2,1,0:T(8,128)S(1)}, f32[33,40,128]{2,1,0:T(8,128)S(1)}, u32[]{:S(2)}, u32[]{:S(2)}) collective-permute-start(f32[33,40,128]{2,1,0:T(8,128)S(1)} %get-tuple-element.48), channel_id=1, source_target_pairs={{0,4},{1,5},{2,6},{3,7},{4,0},{5,1},{6,2},{7,3},{8,12},{9,13},{10,... | collective-permute-start | bytes 2027528 | tf_op jit(solution)/shard_map/ppermute | solution.py:395
  11.1 9.0 %copy-start.1 = (f32[8]{0:T(128)S(1)}, f32[8]{0:T(128)}, u32[]{:S(2)}) copy-start(f32[8]{0:T(128)} %eps_table.1) | copy-start | bytes 100
  11.1 9.0 %copy-start.2 = (f32[8]{0:T(128)S(1)}, f32[8]{0:T(128)}, u32[]{:S(2)}) copy-start(f32[8]{0:T(128)} %chi_table.1) | copy-start | bytes 100
  11.1 12.7 %collective-permute-start.2 = (f32[33,24,128]{2,1,0:T(8,128)S(1)}, f32[33,24,128]{2,1,0:T(8,128)S(1)}, u32[]{:S(2)}, u32[]{:S(2)}) collective-permute-start(f32[33,24,128]{2,1,0:T(8,128)S(1)} %get-tuple-element.46), channel_id=1, source_target_pairs={{4,8},{5,9},{6,10},{7,11},{8,4},{9,5},{10,6},{11,7},{12,16},{13,17... | collective-permute-start | bytes 1216520 | tf_op jit(solution)/shard_map/ppermute | solution.py:395
  15.8 11.1 %collective-permute-start.3 = (f32[33,16,128]{2,1,0:T(8,128)S(1)}, f32[33,16,128]{2,1,0:T(8,128)S(1)}, u32[]{:S(2)}, u32[]{:S(2)}) collective-permute-start(f32[33,16,128]{2,1,0:T(8,128)S(1)} %get-tuple-element.47), channel_id=1, source_target_pairs={{4,8},{5,9},{6,10},{7,11},{8,4},{9,5},{10,6},{11,7},{12,16},{13,17... | collective-permute-start | bytes 811016 | tf_op jit(solution)/shard_map/ppermute | solution.py:395

commit v4 on v3

--- a/solution.py
+++ b/solution.py
@@ -194,18 +194,20 @@
         grid.put(ref, (c % 3, p), c, p, v, n)
 
     early(grid, put)
-    gz, _, _, _ = position()
+    gz, _, last, _ = position()
     first_core = lax.rem(gz, 2) == 0
+    keep = scalar(jnp.logical_and(gz != 0, gz != last))
     half = halo_row() < XH
     for i in range(NS):
         v = sent(grid, HI, i)
         if i < len(LO):
             v = jnp.where(first_core, v, sent(grid, LO, i))
+        v = v * keep
         out[i, 0:8] = jnp.where(half, v[24:32], v[0:8])
         out[i, 8:24] = v[8:24]
 
 
-def edges(d, e, h, eps, chi, id_, ie, ih, ilo, ra, rb, xt, fd, fe, fh, flo, cross, chip, sd, se, sh, slo):
+def edges(d, e, h, eps, chi, ra, rb, xt, sd, se, sh, slo, cross):
     fields = (d, e, h, eps, chi)
     _, gx, _, _ = position()
     even = lax.rem(gx, 2) == 0
@@ -229,46 +231,44 @@
     grid.step_h(1, 6, range(2), lambda c, p, v, n: grid.put(slo, c - H, c, p, v, n))
 
     def put(c, p, v, n):
-        ref = (sd, se, sh)[c // 3]
-        grid.put(ref, (c % 3, p), c, p, v, n)
+        grid.put((sd, se, sh)[c // 3], (c % 3, p), c, p, v, n)
 
     early(grid, put)
     half = halo_row() < XH
+    gz, _, last, _ = position()
+    first_core = lax.rem(gz, 2) == 0
+    keep = scalar(jnp.logical_and(gz != 0, gz != last))
+    for i in range(NS):
+        v = sent(grid, HI, i)
+        if i < len(LO):
+            v = jnp.where(first_core, v, sent(grid, LO, i))
+        v = v * keep
+        cross[i, 0:8] = jnp.where(half, v[16:24], v[0:8])
+        cross[i, 8:16] = v[8:16]
+
+
+def merge(d, e, h, eps, chi, id_, ie, ih, ilo, sd, se, sh, slo, xt, fd, fe, fh, chip):
+    fields = (d, e, h, eps, chi)
+    half = halo_row() < XH
 
     def merged(v, w):
         return rows(jnp.where(half, w[16:24], v[0:8]), v[8:24], jnp.where(half, v[24:32], w[0:8]), w[8:16])
 
-    whole = {}
-    for (comp, p), level in grid.level.items():
-        if comp < EPS and (level or comp >= H and (comp, p) in ((H, 6), (H + 1, 6))):
-            if p == 6:
-                v, w, ref, index = ilo[comp - H], slo[comp - H], flo, comp - H
-            else:
-                k = comp // 3
-                index = (comp % 3, p)
-                v, w, ref = (id_, ie, ih)[k][index], (sd, se, sh)[k][index], (fd, fe, fh)[k]
-            ref[index] = merged(v, w)
-            whole[(comp, p)] = (ref, index)
-
+    grid = Grid(ROWS, None, None)
+    hold_own(grid, fields, xt)
+    for k, (v, w, ref) in enumerate(((id_, sd, fd), (ie, se, fe), (ih, sh, fh))):
+        for p in EARLY[k]:
+            for c in range(3):
+                grid.put(ref, (c, p), 3 * k + c, p, merged(v[c, p], w[c, p]), 1)
+    for c in range(2):
+        grid.hold(H + c, 6, functools.partial(lambda a: merged(ilo[a], slo[a]), c))
     gz, _, _, _ = position()
     first_core = lax.rem(gz, 2) == 0
-
-    def frame(comp, p):
-        if (comp, p) in whole:
-            ref, index = whole[(comp, p)]
-            return ref[index]
-        return rows(own(fields, comp, p), xt[comp, p])
-
     for i in range(NS):
-        hi = frame(*HI[i])
+        v = sent(grid, HI, i)
         if i < len(LO):
-            lo = frame(*LO[i])
-            there, here = jnp.where(first_core, hi, lo), jnp.where(first_core, lo, hi)
-        else:
-            there, here = hi, hi
-        chip[i] = here
-        cross[i, 0:8] = jnp.where(half, there[0:8], there[24:32])
-        cross[i, 8:16] = there[32:40]
+            v = jnp.where(first_core, sent(grid, LO, i), v)
+        chip[i] = v
 
 
 def full_grid():
@@ -324,58 +324,108 @@
     grid.sweep(4, (3,), (), put)
 
 
-def finish(d, e, h, eps, chi, xt, fd, fe, fh, gd, ge, gh, ca, cb, cc, eps_in, chi_in, d_out, e_out, h_out, eps_out, chi_out, sd, se, sh):
-    gz, _, last, _ = position()
-    first_core = lax.rem(gz, 2) == 0
-    last_z = gz == last
+def complete(own_refs, xt, frames, more, above, below, scratch, outs, sems, coming):
+    fields = own_refs
+    grid = full_grid()
+    hold_own(grid, fields, xt)
+    hold_frames(grid, frames, EARLY)
+    hold_frames(grid, more, MIDDLE)
+    for side, at, shift in ((above, HI_AT, NZL), (below, LO_AT, -NZL)):
+        if side is not None:
+            for (comp, p), i in at.items():
+                level = (p + (H <= comp < EPS)) if shift > 0 else int(p == 6)
+                grid.hold(comp, p + shift, functools.partial(side, i), level)
+    state, staged = scratch[:3], scratch[3:6]
+    copies = []
+
+    def send(o):
+        for k in range(3):
+            copies.append(pltpu.make_async_copy(staged[k].at[:, pl.ds(o, 1)], outs[k].at[:, pl.ds(o, 1)], sems.at[k, o]))
+            copies[-1].start()
+
+    def put(c, p, v, n):
+        k = c // 3
+        if n == STEPS and p >= ADVANCE:
+            staged[k][c % 3, p - ADVANCE] = v[:NXL]
+        if n < STEPS or k == 2:
+            grid.put(state[k], (c % 3, p + 2), c, p, v, n)
+
+    def last_sweep(h_planes, de_planes):
+        for p in sorted(set(h_planes) | set(de_planes)):
+            if p in h_planes:
+                grid.step_h(STEPS, p, range(3), put)
+            if p in de_planes:
+                if p not in h_planes:
+                    for c in range(3):
+                        staged[2][c, p - ADVANCE] = grid.get(H + c, p, STEPS)[:NXL]
+                grid.step_de(STEPS, p, put)
+                send(p - ADVANCE)
+
+    if below is not None:
+        grid.sweep(1, (-1,), (-1, 0), put)
+        grid.sweep(2, (-1, 0), (0, 1), put)
+        grid.sweep(3, (0, 1), (1, 2), put)
+        last_sweep((1, 2), (2, 3))
+    if above is not None:
+        for k, (comp, new) in enumerate(((EPS, coming and coming[0]), (CHI, coming and coming[1]))):
+            for o in range(ADVANCE):
+                v = grid.get(comp, NZL + o)[:NXL]
+                if new is not None:
+                    gz, _, last, _ = position()
+                    v = jnp.where(gz == last, new[o], v)
+                scratch[6 + k][o] = v
+            copies.append(pltpu.make_async_copy(scratch[6 + k], outs[3 + k].at[pl.ds(NZL - ADVANCE, ADVANCE)], sems.at[3, k]))
+            copies[-1].start()
+        grid.sweep(1, (7,), (7, 8), put)
+        grid.sweep(2, range(6, 9), range(6, 10), put)
+        grid.sweep(3, range(5, 10), range(5, 11), put)
+        last_sweep(range(4, 10), range(4, 10))
+    for c in copies:
+        c.wait()
+
+
+def near(d, e, h, eps, chi, xt, fd, fe, fh, gd, ge, gh, cc, d_out, e_out, h_out, eps_out, chi_out, *rest):
+    *scratch, sems = rest
+    fields, frames, more = (d, e, h, eps, chi), (fd, fe, fh), (gd, ge, gh)
+    outs = (d_out, e_out, h_out, eps_out, chi_out)
+    gz, _, _, _ = position()
+    keep = NZL - ADVANCE
+    media = [
+        pltpu.make_async_copy(a.at[pl.ds(ADVANCE, keep)], b.at[pl.ds(0, keep)], sems.at[3, 2 + k])
+        for k, (a, b) in enumerate(((eps, eps_out), (chi, chi_out)))
+    ]
+    for c in media:
+        c.start()
+
+    @pl.when(lax.rem(gz, 2) == 0)
+    def _():
+        complete(fields, xt, frames, more, lambda i: cc[i], None, scratch, outs, sems, None)
+
+    @pl.when(lax.rem(gz, 2) == 1)
+    def _():
+        complete(fields, xt, frames, more, None, lambda i: cc[i], scratch, outs, sems, None)
+
+    for c in media:
+        c.wait()
+
+
+def far(d, e, h, eps, chi, xt, fd, fe, fh, gd, ge, gh, ca, cb, eps_in, chi_in, *rest):
+    outs, scratch, sems = rest[5:10], rest[10:-1], rest[-1]
+    fields, frames, more = (d, e, h, eps, chi), (fd, fe, fh), (gd, ge, gh)
     half = halo_row() < XH
-    grid = full_grid()
-    hold_own(grid, (d, e, h, eps, chi), xt)
-    hold_frames(grid, (fd, fe, fh), EARLY)
-    hold_frames(grid, (gd, ge, gh), MIDDLE)
+    gz, _, _, _ = position()
 
     def cross(i):
         m, x = ca[i, 0:8], cb[i, 0:8]
         return rows(jnp.where(half, x, m), ca[i, 8:24], jnp.where(half, m, x), cb[i, 8:16])
 
-    def above(i):
-        return jnp.where(first_core, cc[i], cross(i))
-
-    def below(i):
-        return jnp.where(first_core, cross(i), cc[i])
-
-    for (comp, p), i in HI_AT.items():
-        level = p + 1 if H <= comp < EPS else p
-        grid.hold(comp, p + NZL, functools.partial(above, i), level)
-    for (comp, p), i in LO_AT.items():
-        grid.hold(comp, p - NZL, functools.partial(below, i), 1 if p == 6 else 0)
-
-    def put(c, p, v, n):
-        k = c // 3
-        if n == STEPS:
-            o = p - ADVANCE
-            if o >= 0:
-                (d_out, e_out, h_out)[k][c % 3, o] = v[:NXL]
-            if k < 2:
-                return
-        grid.put((sd, se, sh)[k], (c % 3, p + 2), c, p, v, n)
-
-    grid.sweep(1, (-1,), (-1, 0), put)
-    grid.sweep(2, (-1, 0), (0, 1), put)
-    grid.sweep(3, (0, 1), (1, 2), put)
-    grid.sweep(4, (1, 2), (2, 3), put)
-    for c in range(3):
-        h_out[c, 3 - ADVANCE] = grid.get(H + c, 3, 4)[:NXL]
-    grid.sweep(1, (7,), (7, 8), put)
-    grid.sweep(2, range(6, 9), range(6, 10), put)
-    grid.sweep(3, range(5, 10), range(5, 11), put)
-    grid.sweep(4, range(4, 10), range(4, 10), put)
-
-    for ref, comp, out, new in ((eps, EPS, eps_out, eps_in), (chi, CHI, chi_out, chi_in)):
-        for plane in range(ADVANCE, NZL):
-            out[plane - ADVANCE] = ref[plane]
-        for k in range(ADVANCE):
-            out[NZL - ADVANCE + k] = jnp.where(last_z, new[k], grid.get(comp, NZL + k)[:NXL])
+    @pl.when(lax.rem(gz, 2) == 0)
+    def _():
+        complete(fields, xt, frames, more, None, cross, scratch, outs, sems, None)
+
+    @pl.when(lax.rem(gz, 2) == 1)
+    def _():
+        complete(fields, xt, frames, more, cross, None, scratch, outs, sems, (eps_in, chi_in))
 
 
 def swapped(shard, axis, first):
@@ -387,20 +437,19 @@
             to = at + 1 if at % 2 == first else at - 1
             if 0 <= to < n[axis]:
                 other = (to, x) if axis == "gz" else (z, to)
-            elif axis == "gx":
-                other = (z ^ 1, x)
             else:
-                continue
+                other = (z ^ 1, x) if axis == "gx" else (z, x ^ 1)
             moves.append((z * n["gx"] + x, other[0] * n["gx"] + other[1]))
     return lax.ppermute(shard, ("gz", "gx"), moves)
 
 
-def call(body, inputs, out_shape, scratch=(), vmem=8, specs=None):
+def call(body, inputs, out_shape, scratch=(), vmem=8, specs=None, out=VM, aliases=None):
     return pl.pallas_call(
         body,
         out_shape=out_shape,
         in_specs=[VM] * len(inputs) if specs is None else specs,
-        out_specs=jax.tree.map(lambda _: VM, out_shape),
+        out_specs=jax.tree.map(lambda _: out, out_shape),
+        input_output_aliases=aliases or {},
         scratch_shapes=list(scratch),
         compiler_params=pltpu.CompilerParams(vmem_limit_bytes=vmem << 20),
     )(*inputs)
@@ -422,19 +471,32 @@
     *inside, za = call(inner, fields, (*frames, lo, shape(NS, 24, NY)))
     ca = swapped(za, "gz", 1)
     coming = call(lookup, [classes, eps_table, chi_table], (shape(ADVANCE, NXL, NY),) * 2, specs=[VM, SM, SM])
+    thin = [shape(3, 5, EDGE, NY)] * 3
+    xt, *outside, zb = call(
+        edges, [*fields, ra, rb], (shape(11, NZL, 8, NY), *thin, shape(2, EDGE, NY), shape(NS, 16, NY))
+    )
+    cb = swapped(zb, "gz", 1)
     frames = [shape(3, 5, ROWS, NY)] * 3
-    scratch = [pltpu.VMEM((3, 5, EDGE, NY), jnp.float32)] * 3 + [pltpu.VMEM((2, EDGE, NY), jnp.float32)]
-    xt, *frames, _, zb, zc = call(
-        edges,
-        [*fields, *inside, ra, rb],
-        (shape(11, NZL, 8, NY), *frames, shape(2, ROWS, NY), shape(NS, 16, NY), shape(NS, ROWS, NY)),
+    *frames, zc = call(merge, [*fields, *inside, *outside, xt], (*frames, shape(NS, ROWS, NY)))
+    cc = swapped(zc, "gz", 0)
+    more = call(middle, [*fields, xt, *frames], (shape(3, 7, ROWS, NY),) * 3)
+    scratch = [pltpu.VMEM((3, 13, ROWS, NY), jnp.float32)] * 3 + [pltpu.VMEM((3, NZL, NXL, NY), jnp.float32)] * 3
+    scratch += [pltpu.VMEM((ADVANCE, NXL, NY), jnp.float32)] * 2 + [pltpu.SemaphoreType.DMA((4, NZL))]
+    given = [*fields, xt, *frames, *more]
+    results = (field, field, field, medium, medium)
+    outs = call(near, [*given, cc], results, scratch, vmem=16, out=HBM)
+    given += [ca, cb, *coming]
+    n = len(given)
+    return call(
+        far,
+        [*given, *outs],
+        results,
         scratch,
+        vmem=16,
+        specs=[VM] * n + [HBM] * 5,
+        out=HBM,
+        aliases={n + k: k for k in range(5)},
     )
-    cb, cc = swapped(zb, "gz", 1), swapped(zc, "gz", 0)
-    more = call(middle, [*fields, xt, *frames], (shape(3, 7, ROWS, NY),) * 3)
-    state = pltpu.VMEM((3, 13, ROWS, NY), jnp.float32)
-    inputs = [*fields, xt, *frames, *more, ca, cb, cc, *coming]
-    return call(finish, inputs, (field, field, field, medium, medium), [state] * 3, vmem=16)
 
 
 def solution(mesh):

time: 29.7 us -> 26.6 us (0.90)
  starting transfers between devices: 12.9 us -> 9.07 us
  Pallas kernels: 6.63 us -> 7.19 us
    ppermute x5, starting transfers between devices: 12.9 us -> 9.07 us  [swapped(): return lax.ppermute(shard, ('gz', 'gx'), moves)]
    pallas_call x6 -> x8, Pallas kernels: 6.63 us -> 7.19 us  [call(): pl.pallas_call(body, out_shape=out_shape, in_specs=[VM] * len(inputs) if...]
  transfers between devices with their start and end apart: 5 -> 5, of which waited for: 4 -> 4; matrix products, arithmetic and copies ran while one was open for 0% -> 0% of each run, Pallas kernels for 5% -> 12%
where the time goes in v4:
time: 26.6 us; the launch traced here: 26.3 us
  waiting for transfers between devices  9.36 us (35%)
  starting transfers between devices  9.07 us (34%)
  Pallas kernels  7.19 us (27%)
  between operations  0.7 us (3%)
    ppermute x5, waiting for transfers between devices, swapped(): return lax.ppermute(shard, ('gz', 'gx'), moves)  9.36 us
    ppermute x5, starting transfers between devices, swapped(): return lax.ppermute(shard, ('gz', 'gx'), moves)  9.07 us
    pallas_call x8, Pallas kernels, call(): pl.pallas_call(body, out_shape=out_shape, in_specs=[VM] * len(inputs) if...  7.19 us
  transfers between devices with their start and end apart: 5, of which 4 were waited for; matrix products, arithmetic and copies ran while one was open for 0% of the time, Pallas kernels for 12%

profile of v4, /device:TPU:111, one launch (start us, length us, event | category | flops | bytes accessed | tf_op | source)
XLA Modules:
  0.0 26.3 jit_solution(10286956195485921463)
XLA Ops:
  0.6 1.5 %shard_map.119 = (f32[3,8,32,128]{3,2,1,0:T(8,128)S(1)}, f32[3,8,32,128]{3,2,1,0:T(8,128)S(1)}, f32[3,8,32,128]{3,2,1,0:T(8,128)S(1)}, f32[8,32,128]{2,1,0:T(8,1...) custom-call(f32[3,8,32,128]{3,2,1,0:T(8,128)} %d.1, ...), custom_call_target="tpu_custom_call" | custom-call | tf_op jit(solution)/shard_map/pallas_call | solution.py:447
  2.1 0.3 collective-permute-start
  2.4 2.1 %collective-permute-start.1 = (f32[11,8,4,128]{3,2,1,0:T(4,128)S(1)}, f32[11,8,4,128]{3,2,1,0:T(4,128)S(1)}, u32[]{:S(2)}, u32[]{:S(2)}) collective-permute-start(f32[11,8,4,128]{3,2,1,0:T(4,128)S(1)} %get-tuple-element.43), channel_id=1, source_target_pairs={{0,4},{1,2},{2,1},{3,7},{4,0},{5,6},{6,5},{7,3},{8,12},{9,10},{10,... | collective-permute-start | bytes 540680 | tf_op jit(solution)/shard_map/ppermute | solution.py:443
  4.5 0.4 %shard_map.121 = (f32[3,5,32,128]{3,2,1,0:T(8,128)S(1)}, f32[3,5,32,128]{3,2,1,0:T(8,128)S(1)}, f32[3,5,32,128]{3,2,1,0:T(8,128)S(1)}, f32[2,32,128]{2,1,0:T(8,128)S(1)}, f32[33,24,128]{2,1,0:T(8,128)S(1)}) custom-call(f32[3,8,32,128]{3,2,1,0:T(8,128)S(1)} %get-tuple-element.37.d, f32[3,8,32,128]{3,2,1,0:T(8,128)S(1)} %get-tuple-element.38.e, ...), custom_call_target="tpu_custom_call" | custom-call | tf_op jit(solution)/shard_map/pallas_call | solution.py:447
  5.0 2.7 %collective-permute-done.ra = f32[11,8,4,128]{3,2,1,0:T(4,128)S(1)} collective-permute-done((f32[11,8,4,128]{3,2,1,0:T(4,128)S(1)}, f32[11,8,4,128]{3,2,1,0:T(4,128)S(1)}, u32[]{:S(2)}, u32[]{:S(2)}) %collective-permute-start) | collective-permute-done | bytes 180256 | tf_op jit(solution)/shard_map/ppermute | solution.py:443
  7.7 0.8 %collective-permute-done.1.rb = f32[11,8,4,128]{3,2,1,0:T(4,128)S(1)} collective-permute-done((f32[11,8,4,128]{3,2,1,0:T(4,128)S(1)}, f32[11,8,4,128]{3,2,1,0:T(4,128)S(1)}, u32[]{:S(2)}, u32[]{:S(2)}) %collective-permute-start.1) | collective-permute-done | bytes 180256 | tf_op jit(solution)/shard_map/ppermute | solution.py:443
  8.5 0.4 %shard_map.120 = (f32[11,8,8,128]{3,2,1,0:T(8,128)S(1)}, f32[3,5,24,128]{3,2,1,0:T(8,128)S(1)}, f32[3,5,24,128]{3,2,1,0:T(8,128)S(1)}, f32[3,5,24,128]{3,2,1,0:T...) custom-call(f32[3,8,32,128]{3,2,1,0:T(8,128)S(1)} %get-tuple-element.37.d, ...), custom_call_target="tpu_custom_call" | custom-call | tf_op jit(solution)/shard_map/pallas_call | solution.py:447
  9.0 0.0 copy-start
  9.0 0.1 shard_map.122
  9.1 1.6 %collective-permute-start.4 = (f32[33,40,128]{2,1,0:T(8,128)S(1)}, f32[33,40,128]{2,1,0:T(8,128)S(1)}, u32[]{:S(2)}, u32[]{:S(2)}) collective-permute-start(f32[33,40,128]{2,1,0:T(8,128)S(1)} %get-tuple-element.63), channel_id=1, source_target_pairs={{0,4},{1,5},{2,6},{3,7},{4,0},{5,1},{6,2},{7,3},{8,12},{9,13},{10,... | collective-permute-start | bytes 2027528 | tf_op jit(solution)/shard_map/ppermute | solution.py:443
  10.7 0.0 copy-start.1
  10.7 0.0 copy-start.2
  10.7 2.8 %collective-permute-start.2 = (f32[33,24,128]{2,1,0:T(8,128)S(1)}, f32[33,24,128]{2,1,0:T(8,128)S(1)}, u32[]{:S(2)}, u32[]{:S(2)}) collective-permute-start(f32[33,24,128]{2,1,0:T(8,128)S(1)} %get-tuple-element.59), channel_id=1, source_target_pairs={{0,1},{1,0},{2,3},{3,2},{4,8},{5,9},{6,10},{7,11},{8,4},{9,5},{10,... | collective-permute-start | bytes 1216520 | tf_op jit(solution)/shard_map/ppermute | solution.py:443
  13.5 2.3 %collective-permute-start.3 = (f32[33,16,128]{2,1,0:T(8,128)S(1)}, f32[33,16,128]{2,1,0:T(8,128)S(1)}, u32[]{:S(2)}, u32[]{:S(2)}) collective-permute-start(f32[33,16,128]{2,1,0:T(8,128)S(1)} %get-tuple-element.60), channel_id=1, source_target_pairs={{0,1},{1,0},{2,3},{3,2},{4,8},{5,9},{6,10},{7,11},{8,4},{9,5},{10,... | collective-permute-start | bytes 811016 | tf_op jit(solution)/shard_map/ppermute | solution.py:443
  15.8 0.0 copy-done
  15.8 0.0 copy-done.1
  15.8 0.0 copy-done.2
  15.8 0.6 %shard_map.124 = (f32[2,32,128]{2,1,0:T(8,128)S(1)}, f32[2,32,128]{2,1,0:T(8,128)S(1)}) custom-call(s32[2,32,128]{2,1,0:T(8,128)S(1)} %copy-done, f32[8]{0:T(128)S(1)} %copy-done.1, f32[8]{0:T(128)S(1)} %copy-done.2), custom_call_target="tpu_custom_call" | custom-call | tf_op jit(solution)/shard_map/pallas_call | solution.py:447
  16.4 0.5 %shard_map.123 = (f32[3,7,40,128]{3,2,1,0:T(8,128)S(1)}, f32[3,7,40,128]{3,2,1,0:T(8,128)S(1)}, f32[3,7,40,128]{3,2,1,0:T(8,128)S(1)}) custom-call(f32[3,8,32,128]{3,2,1,0:T(8,128)S(1)} %get-tuple-element.37.d, f32[3,8,32,128]{3,2,1,0:T(8,128)S(1)} %get-tuple-element.38.e, f32[3,8,32,128]{3,2,1,0:T(8,128)S(1)} %get-tuple-element.39.h, ...), custom_call_target="tpu_custom_call" | custom-call | tf_op jit(solution)/shard_map/pallas_call | solution.py:447
  16.9 0.0 collective-permute-done.4.cc
  16.9 1.5 %shard_map.125 = (f32[3,8,32,128]{3,2,1,0:T(8,128)}, f32[3,8,32,128]{3,2,1,0:T(8,128)}, f32[3,8,32,128]{3,2,1,0:T(8,128)}, f32[8,32,128]{2,1,0:T(8,128)}, f32[8,32,128]{2,1,0:T(8,128)}) custom-call(f32[3,8,32,128]{3,2,1,0:T(8,128)S(1)} %get-tuple-element.37.d, f32[3,8,32,128]{3,2,1,0:T(8,128)S(1)} %get-tuple-element.38.e, ...), custom_call_target="tpu_custom_call" | custom-call | tf_op jit(solution)/shard_map/pallas_call | solution.py:447
  18.4 2.9 %collective-permute-done.2.ca = f32[33,24,128]{2,1,0:T(8,128)S(1)} collective-permute-done((f32[33,24,128]{2,1,0:T(8,128)S(1)}, f32[33,24,128]{2,1,0:T(8,128)S(1)}, u32[]{:S(2)}, u32[]{:S(2)}) %collective-permute-start.2) | collective-permute-done | bytes 405536 | tf_op jit(solution)/shard_map/ppermute | solution.py:443
  21.4 2.9 %collective-permute-done.3.cb = f32[33,16,128]{2,1,0:T(8,128)S(1)} collective-permute-done((f32[33,16,128]{2,1,0:T(8,128)S(1)}, f32[33,16,128]{2,1,0:T(8,128)S(1)}, u32[]{:S(2)}, u32[]{:S(2)}) %collective-permute-start.3) | collective-permute-done | bytes 270368 | tf_op jit(solution)/shard_map/ppermute | solution.py:443
  24.3 2.1 %shard_map.126 = (f32[3,8,32,128]{3,2,1,0:T(8,128)}, f32[3,8,32,128]{3,2,1,0:T(8,128)}, f32[3,8,32,128]{3,2,1,0:T(8,128)}, f32[8,32,128]{2,1,0:T(8,128)}, f32[8,32,128]{2,1,0:T(8,128)}) custom-call(f32[3,8,32,128]{3,2,1,0:T(8,128)S(1)} %get-tuple-element.37.d, ...), custom_call_target="tpu_custom_call", output_to_operand_aliasing={{0}: (16, {}), {1}: (17, {}), {2}: (18, {}), {3}: (19, {}),... | custom-call | tf_op jit(solution)/shard_map/pallas_call | solution.py:447
Async XLA Ops:
  2.1 5.5 %collective-permute-start = (f32[11,8,4,128]{3,2,1,0:T(4,128)S(1)}, f32[11,8,4,128]{3,2,1,0:T(4,128)S(1)}, u32[]{:S(2)}, u32[]{:S(2)}) collective-permute-start(f32[11,8,4,128]{3,2,1,0:T(4,128)S(1)} %get-tuple-element.42), channel_id=1, source_target_pairs={{0,1},{1,0},{2,3},{3,2},{4,5},{5,4},{6,7},{7,6},{8,9},{9,8},{10,11... | collective-permute-start | bytes 540680 | tf_op jit(solution)/shard_map/ppermute | solution.py:443
  2.4 6.1 %collective-permute-start.1 = (f32[11,8,4,128]{3,2,1,0:T(4,128)S(1)}, f32[11,8,4,128]{3,2,1,0:T(4,128)S(1)}, u32[]{:S(2)}, u32[]{:S(2)}) collective-permute-start(f32[11,8,4,128]{3,2,1,0:T(4,128)S(1)} %get-tuple-element.43), channel_id=1, source_target_pairs={{0,4},{1,2},{2,1},{3,7},{4,0},{5,6},{6,5},{7,3},{8,12},{9,10},{10,... | collective-permute-start | bytes 540680 | tf_op jit(solution)/shard_map/ppermute | solution.py:443
  9.0 6.8 %copy-start = (s32[2,32,128]{2,1,0:T(8,128)S(1)}, s32[2,32,128]{2,1,0:T(8,128)}, u32[]{:S(2)}) copy-start(s32[2,32,128]{2,1,0:T(8,128)} %classes.1) | copy-start | bytes 98308
  9.1 7.8 %collective-permute-start.4 = (f32[33,40,128]{2,1,0:T(8,128)S(1)}, f32[33,40,128]{2,1,0:T(8,128)S(1)}, u32[]{:S(2)}, u32[]{:S(2)}) collective-permute-start(f32[33,40,128]{2,1,0:T(8,128)S(1)} %get-tuple-element.63), channel_id=1, source_target_pairs={{0,4},{1,5},{2,6},{3,7},{4,0},{5,1},{6,2},{7,3},{8,12},{9,13},{10,... | collective-permute-start | bytes 2027528 | tf_op jit(solution)/shard_map/ppermute | solution.py:443
  10.7 5.1 %copy-start.1 = (f32[8]{0:T(128)S(1)}, f32[8]{0:T(128)}, u32[]{:S(2)}) copy-start(f32[8]{0:T(128)} %eps_table.1) | copy-start | bytes 100
  10.7 5.1 %copy-start.2 = (f32[8]{0:T(128)S(1)}, f32[8]{0:T(128)}, u32[]{:S(2)}) copy-start(f32[8]{0:T(128)} %chi_table.1) | copy-start | bytes 100
  10.7 10.7 %collective-permute-start.2 = (f32[33,24,128]{2,1,0:T(8,128)S(1)}, f32[33,24,128]{2,1,0:T(8,128)S(1)}, u32[]{:S(2)}, u32[]{:S(2)}) collective-permute-start(f32[33,24,128]{2,1,0:T(8,128)S(1)} %get-tuple-element.59), channel_id=1, source_target_pairs={{0,1},{1,0},{2,3},{3,2},{4,8},{5,9},{6,10},{7,11},{8,4},{9,5},{10,... | collective-permute-start | bytes 1216520 | tf_op jit(solution)/shard_map/ppermute | solution.py:443
  13.5 10.8 %collective-permute-start.3 = (f32[33,16,128]{2,1,0:T(8,128)S(1)}, f32[33,16,128]{2,1,0:T(8,128)S(1)}, u32[]{:S(2)}, u32[]{:S(2)}) collective-permute-start(f32[33,16,128]{2,1,0:T(8,128)S(1)} %get-tuple-element.60), channel_id=1, source_target_pairs={{0,1},{1,0},{2,3},{3,2},{4,8},{5,9},{6,10},{7,11},{8,4},{9,5},{10,... | collective-permute-start | bytes 811016 | tf_op jit(solution)/shard_map/ppermute | solution.py:443

commit v5 on v4

--- a/solution.py
+++ b/solution.py
@@ -20,11 +20,15 @@
 ROWS = NXL + 2 * XH
 EDGE = 24
 
-HI = [(c, p) for p in range(3) for c in ALL]
-LO = [(c, 7) for c in ALL] + [(H, 6), (H + 1, 6)]
+RAW = [(c, 0) for c in range(H)] + [(c, p) for p in range(3) for c in (EPS, CHI)]
+HI = RAW + [(H + c, 0) for c in range(3)] + [(c, p) for p in (1, 2) for c in range(EPS)]
+LO = [(c, 7) for c in ALL] + [None, (H, 6), (H + 1, 6)]
 HI_AT = {k: i for i, k in enumerate(HI)}
-LO_AT = {k: i for i, k in enumerate(LO)}
-NS = len(HI)
+LO_AT = {k: i for i, k in enumerate(LO) if k}
+NS, NR = len(HI), len(RAW)
+
+FIRST = [(c, p) for p in range(5) for c in ALL] + [(E, 5), (E + 1, 5)]
+SECOND = [(c, p) for p in (5, 6, 7) for c in ALL if (c, p) not in FIRST]
 
 VM = pl.BlockSpec(memory_space=pltpu.VMEM)
 HBM = pl.BlockSpec(memory_space=pltpu.HBM)
@@ -144,21 +148,27 @@
     return eps[plane] if comp == EPS else chi[plane]
 
 
-def load(d, e, h, eps, chi, dv, ev, hv, epsv, chiv, ya, yb, sems):
+def load(d, e, h, eps, chi, dv, ev, hv, epsv, chiv, ya, yb, yc, yd, sems):
     moves = [(a.at[c], b.at[c]) for a, b in ((d, dv), (e, ev), (h, hv)) for c in range(3)] + [(eps, epsv), (chi, chiv)]
     copies = [pltpu.make_async_copy(a, b, sems.at[i]) for i, (a, b) in enumerate(moves)]
     for c in copies:
         c.start()
-    _, gx, _, last = position()
-    even = lax.rem(gx, 2) == 0
+    gz, gx, _, last = position()
+    even, first_core = lax.rem(gx, 2) == 0, lax.rem(gz, 2) == 0
     keep = scalar(jnp.logical_and(gx != 0, gx != last))
-    for comp in ALL:
-        copies[comp].wait()
-        for plane in range(NZL):
-            v = own((dv, ev, hv, epsv, chiv), comp, plane)
+    for c in copies:
+        c.wait()
+    fields = (dv, ev, hv, epsv, chiv)
+    for units, a, b in ((FIRST, ya, yb), (SECOND, yc, yd)):
+        for i, (comp, p) in enumerate(units):
+            v = jnp.where(first_core, own(fields, comp, p), own(fields, comp, NZL - 1 - p))
             low, high = v[:XH], v[NXL - XH :]
-            ya[comp, plane] = jnp.where(even, high, low)
-            yb[comp, plane] = jnp.where(even, low, high) * keep
+            a[i] = jnp.where(even, high, low)
+            b[i] = jnp.where(even, low, high) * keep
+
+
+def mark(out):
+    out[...] = inside_x()
 
 
 def early(grid, put):
@@ -200,55 +210,81 @@
     half = halo_row() < XH
     for i in range(NS):
         v = sent(grid, HI, i)
-        if i < len(LO):
+        if i < len(LO) and LO[i]:
             v = jnp.where(first_core, v, sent(grid, LO, i))
         v = v * keep
-        out[i, 0:8] = jnp.where(half, v[24:32], v[0:8])
-        out[i, 8:24] = v[8:24]
-
-
-def edges(d, e, h, eps, chi, ra, rb, xt, sd, se, sh, slo, cross):
-    fields = (d, e, h, eps, chi)
-    _, gx, _, _ = position()
-    even = lax.rem(gx, 2) == 0
-    for comp in ALL:
-        for p in range(NZL):
-            a, b = ra[comp, p], rb[comp, p]
-            xt[comp, p] = rows(jnp.where(even, a, b), jnp.where(even, b, a))
-    edge = inside_x()
-    f = rows(jnp.full((8, NY), HALF), edge * HALF, jnp.full((8, NY), HALF))
+        out[24 * i : 24 * i + 8] = jnp.where(half, v[24:32], v[0:8])
+        out[24 * i + 8 : 24 * i + 24] = v[8:24]
+        if i < NR:
+            out[24 * NS + 8 * i : 24 * NS + 8 * i + 8] = jnp.where(half, v[0:8], v[24:32])
+
+
+def edge_grid(inside, fields, tile):
+    f = rows(jnp.full((8, NY), HALF), inside * HALF, jnp.full((8, NY), HALF))
     none = jnp.zeros((8, NY), jnp.float32)
-    fill = rows(none, 1.0 - edge, none)
+    fill = rows(none, 1.0 - inside, none)
     grid = Grid(EDGE, lambda p: f, lambda p: fill)
 
     def read(comp, p):
         v = own(fields, comp, p)
-        return rows(v[24:32], xt[comp, p], v[0:8])
+        return rows(v[24:32], tile(comp, p), v[0:8])
 
     for comp in ALL:
         for p in range(NZL):
             grid.hold(comp, p, functools.partial(read, comp, p))
-    grid.step_h(1, 6, range(2), lambda c, p, v, n: grid.put(slo, c - H, c, p, v, n))
-
-    def put(c, p, v, n):
-        grid.put((sd, se, sh)[c // 3], (c % 3, p), c, p, v, n)
-
-    early(grid, put)
+    return grid
+
+
+def joined(a, b):
+    _, gx, _, _ = position()
+    even = lax.rem(gx, 2) == 0
+    return rows(jnp.where(even, a, b), jnp.where(even, b, a))
+
+
+def edges(d, e, h, eps, chi, ra, rb, inside, cross, sd, se, sh, slo, tiles):
+    fields = (d, e, h, eps, chi)
+    gz, _, last, _ = position()
+    keep = scalar(jnp.logical_and(gz != 0, gz != last))
     half = halo_row() < XH
-    gz, _, last, _ = position()
+
+    def pack(grid, side):
+        for i, unit in enumerate(side):
+            if unit:
+                v = grid.get(*unit) * keep
+                cross[8 * i : 8 * i + 8] = v[8:16]
+                if i >= NR:
+                    at = 8 * (NS + i - NR)
+                    cross[at : at + 8] = jnp.where(half, v[16:24], v[0:8])
+
+    @pl.when(lax.rem(gz, 2) == 0)
+    def _():
+        at = {k: i for i, k in enumerate(FIRST)}
+        for i in range(len(FIRST)):
+            tiles[i] = joined(ra[i], rb[i])
+        grid = edge_grid(inside[...], fields, lambda comp, p: tiles[at[(comp, p)]])
+        early(grid, lambda c, p, v, n: grid.put((sd, se, sh)[c // 3], (c % 3, p), c, p, v, n))
+        pack(grid, HI)
+
+    @pl.when(lax.rem(gz, 2) == 1)
+    def _():
+        at = {(c, NZL - 1 - p): i for i, (c, p) in enumerate(FIRST) if p < 2}
+        for i in at.values():
+            tiles[i] = joined(ra[i], rb[i])
+        grid = edge_grid(inside[...], fields, lambda comp, p: tiles[at[(comp, p)]])
+        grid.step_h(1, 6, range(2), lambda c, p, v, n: grid.put(slo, c - H, c, p, v, n))
+        pack(grid, LO)
+
+
+def merge(d, e, h, eps, chi, id_, ie, ih, ilo, ra, rb, rc, rd, inside, xt, fd, fe, fh, chip, sd, se, sh, slo):
+    fields = (d, e, h, eps, chi)
+    gz, _, _, _ = position()
     first_core = lax.rem(gz, 2) == 0
-    keep = scalar(jnp.logical_and(gz != 0, gz != last))
-    for i in range(NS):
-        v = sent(grid, HI, i)
-        if i < len(LO):
-            v = jnp.where(first_core, v, sent(grid, LO, i))
-        v = v * keep
-        cross[i, 0:8] = jnp.where(half, v[16:24], v[0:8])
-        cross[i, 8:16] = v[8:16]
-
-
-def merge(d, e, h, eps, chi, id_, ie, ih, ilo, sd, se, sh, slo, xt, fd, fe, fh, chip):
-    fields = (d, e, h, eps, chi)
+    for units, a, b in ((FIRST, ra, rb), (SECOND, rc, rd)):
+        for i, (comp, p) in enumerate(units):
+            xt[comp, jnp.where(first_core, p, NZL - 1 - p)] = joined(a[i], b[i])
+    thin = edge_grid(inside[...], fields, lambda comp, p: xt[comp, p])
+    thin.step_h(1, 6, range(2), lambda c, p, v, n: thin.put(slo, c - H, c, p, v, n))
+    early(thin, lambda c, p, v, n: thin.put((sd, se, sh)[c // 3], (c % 3, p), c, p, v, n))
     half = halo_row() < XH
 
     def merged(v, w):
@@ -262,11 +298,9 @@
                 grid.put(ref, (c, p), 3 * k + c, p, merged(v[c, p], w[c, p]), 1)
     for c in range(2):
         grid.hold(H + c, 6, functools.partial(lambda a: merged(ilo[a], slo[a]), c))
-    gz, _, _, _ = position()
-    first_core = lax.rem(gz, 2) == 0
     for i in range(NS):
         v = sent(grid, HI, i)
-        if i < len(LO):
+        if i < len(LO) and LO[i]:
             v = jnp.where(first_core, sent(grid, LO, i), v)
         chip[i] = v
 
@@ -416,8 +450,9 @@
     gz, _, _, _ = position()
 
     def cross(i):
-        m, x = ca[i, 0:8], cb[i, 0:8]
-        return rows(jnp.where(half, x, m), ca[i, 8:24], jnp.where(half, m, x), cb[i, 8:16])
+        m = ca[24 * i : 24 * i + 8]
+        x = ca[24 * NS + 8 * i : 24 * NS + 8 * i + 8] if i < NR else cb[8 * (NS + i - NR) : 8 * (NS + i - NR) + 8]
+        return rows(jnp.where(half, x, m), ca[24 * i + 8 : 24 * i + 24], jnp.where(half, m, x), cb[8 * i : 8 * i + 8])
 
     @pl.when(lax.rem(gz, 2) == 0)
     def _():
@@ -457,27 +492,33 @@
 
 def on_device(d_field, e_field, h_field, permittivity, kerr_coeff, classes, eps_table, chi_table):
     field, medium = shape(3, NZL, NXL, NY), shape(NZL, NXL, NY)
-    halo = shape(11, NZL, XH, NY)
-    *fields, ya, yb = call(
+    one, two = shape(len(FIRST), XH, NY), shape(len(SECOND), XH, NY)
+    *fields, ya, yb, yc, yd = call(
         load,
         [pltpu.with_memory_space_constraint(a, pltpu.HBM) for a in (d_field, e_field, h_field, permittivity, kerr_coeff)],
-        (field, field, field, medium, medium, halo, halo),
+        (field, field, field, medium, medium, one, one, two, two),
         [pltpu.SemaphoreType.DMA((11,))],
         specs=[HBM] * 5,
     )
     ra, rb = swapped(ya, "gx", 0), swapped(yb, "gx", 1)
-    frames = [shape(3, 5, NXL, NY)] * 3
     lo = shape(2, NXL, NY)
-    *inside, za = call(inner, fields, (*frames, lo, shape(NS, 24, NY)))
+    *inside, za = call(inner, fields, (*[shape(3, 5, NXL, NY)] * 3, lo, shape(24 * NS + 8 * NR, NY)))
     ca = swapped(za, "gz", 1)
-    coming = call(lookup, [classes, eps_table, chi_table], (shape(ADVANCE, NXL, NY),) * 2, specs=[VM, SM, SM])
-    thin = [shape(3, 5, EDGE, NY)] * 3
-    xt, *outside, zb = call(
-        edges, [*fields, ra, rb], (shape(11, NZL, 8, NY), *thin, shape(2, EDGE, NY), shape(NS, 16, NY))
+    rc, rd = swapped(yc, "gx", 0), swapped(yd, "gx", 1)
+    (edge,) = call(mark, [], (shape(8, NY),))
+    thin = [pltpu.VMEM((3, 5, EDGE, NY), jnp.float32)] * 3 + [pltpu.VMEM((2, EDGE, NY), jnp.float32)]
+    (zb,) = call(
+        edges,
+        [*fields, ra, rb, edge],
+        (shape(8 * (NS + NS - NR), NY),),
+        [*thin, pltpu.VMEM((len(FIRST), 8, NY), jnp.float32)],
     )
     cb = swapped(zb, "gz", 1)
+    coming = call(lookup, [classes, eps_table, chi_table], (shape(ADVANCE, NXL, NY),) * 2, specs=[VM, SM, SM])
     frames = [shape(3, 5, ROWS, NY)] * 3
-    *frames, zc = call(merge, [*fields, *inside, *outside, xt], (*frames, shape(NS, ROWS, NY)))
+    xt, *frames, zc = call(
+        merge, [*fields, *inside, ra, rb, rc, rd, edge], (shape(11, NZL, 8, NY), *frames, shape(NS, ROWS, NY)), thin
+    )
     cc = swapped(zc, "gz", 0)
     more = call(middle, [*fields, xt, *frames], (shape(3, 7, ROWS, NY),) * 3)
     scratch = [pltpu.VMEM((3, 13, ROWS, NY), jnp.float32)] * 3 + [pltpu.VMEM((3, NZL, NXL, NY), jnp.float32)] * 3

time: 26.6 us -> 26.8 us (level)
  waiting for transfers between devices: 9.36 us -> 7.61 us
  starting transfers between devices: 9.07 us -> 10.7 us
    ppermute x5 -> x7, waiting for transfers between devices: 9.36 us -> 7.61 us  [swapped(): return lax.ppermute(shard, ('gz', 'gx'), moves)]
    ppermute x5 -> x7, starting transfers between devices: 9.07 us -> 10.7 us  [swapped(): return lax.ppermute(shard, ('gz', 'gx'), moves)]
    pallas_call x8 -> x9, Pallas kernels: 7.19 us -> 7.34 us  [call(): pl.pallas_call(body, out_shape=out_shape, in_specs=[VM] * len(inputs) if...]
  transfers between devices with their start and end apart: 5 -> 7, of which waited for: 4 -> 3; matrix products, arithmetic and copies ran while one was open for 0% -> 0% of each run, Pallas kernels for 12% -> 12%
where the time goes in v5:
time: 26.8 us; the launch traced here: 26.4 us
  starting transfers between devices  10.7 us (40%)
  waiting for transfers between devices  7.61 us (28%)
  Pallas kernels  7.34 us (27%)
  between operations  0.69 us (3%)
    ppermute x7, starting transfers between devices, swapped(): return lax.ppermute(shard, ('gz', 'gx'), moves)  10.7 us
    ppermute x7, waiting for transfers between devices, swapped(): return lax.ppermute(shard, ('gz', 'gx'), moves)  7.61 us
    pallas_call x9, Pallas kernels, call(): pl.pallas_call(body, out_shape=out_shape, in_specs=[VM] * len(inputs) if...  7.34 us
  transfers between devices with their start and end apart: 7, of which 3 were waited for; matrix products, arithmetic and copies ran while one was open for 0% of the time, Pallas kernels for 12%

profile of v5, /device:TPU:111, one launch (start us, length us, event | category | flops | bytes accessed | tf_op | source)
XLA Modules:
  0.0 26.4 jit_solution(18426314542872946182)
XLA Ops:
  0.6 1.6 %shard_map.119 = (f32[3,8,32,128]{3,2,1,0:T(8,128)S(1)}, f32[3,8,32,128]{3,2,1,0:T(8,128)S(1)}, f32[3,8,32,128]{3,2,1,0:T(8,128)S(1)}, f32[8,32,128]{2,1,0:T(8,1...) custom-call(f32[3,8,32,128]{3,2,1,0:T(8,128)} %d.1, ...), custom_call_target="tpu_custom_call" | custom-call | tf_op jit(solution)/shard_map/pallas_call | solution.py:482
  2.2 0.3 collective-permute-start
  2.5 2.1 %collective-permute-start.1 = (f32[57,4,128]{2,1,0:T(4,128)S(1)}, f32[57,4,128]{2,1,0:T(4,128)S(1)}, u32[]{:S(2)}, u32[]{:S(2)}) collective-permute-start(f32[57,4,128]{2,1,0:T(4,128)S(1)} %get-tuple-element.44), channel_id=1, source_target_pairs={{0,4},{1,2},{2,1},{3,7},{4,0},{5,6},{6,5},{7,3},{8,12},{9,10},{10,... | collective-permute-start | bytes 350216 | tf_op jit(solution)/shard_map/ppermute | solution.py:478
  4.6 0.1 collective-permute-start.2
  4.7 1.3 %collective-permute-start.3 = (f32[31,4,128]{2,1,0:T(4,128)S(1)}, f32[31,4,128]{2,1,0:T(4,128)S(1)}, u32[]{:S(2)}, u32[]{:S(2)}) collective-permute-start(f32[31,4,128]{2,1,0:T(4,128)S(1)} %get-tuple-element.46), channel_id=1, source_target_pairs={{0,4},{1,2},{2,1},{3,7},{4,0},{5,6},{6,5},{7,3},{8,12},{9,10},{10,... | collective-permute-start | bytes 190472 | tf_op jit(solution)/shard_map/ppermute | solution.py:478
  6.0 0.5 %shard_map.120 = (f32[3,5,32,128]{3,2,1,0:T(8,128)S(1)}, f32[3,5,32,128]{3,2,1,0:T(8,128)S(1)}, f32[3,5,32,128]{3,2,1,0:T(8,128)S(1)}, f32[2,32,128]{2,1,0:T(8,128)S(1)}, f32[888,128]{1,0:T(8,128)S(1)}) custom-call(f32[3,8,32,128]{3,2,1,0:T(8,128)S(1)} %get-tuple-element.34.d, f32[3,8,32,128]{3,2,1,0:T(8,128)S(1)} %get-tuple-element.35.e, ...), custom_call_target="tpu_custom_call" | custom-call | tf_op jit(solution)/shard_map/pallas_call | solution.py:482
  6.5 1.7 %collective-permute-done.2.rc = f32[31,4,128]{2,1,0:T(4,128)S(1)} collective-permute-done((f32[31,4,128]{2,1,0:T(4,128)S(1)}, f32[31,4,128]{2,1,0:T(4,128)S(1)}, u32[]{:S(2)}, u32[]{:S(2)}) %collective-permute-start.2) | collective-permute-done | bytes 63520 | tf_op jit(solution)/shard_map/ppermute | solution.py:478
  8.2 0.6 %collective-permute-done.3.rd = f32[31,4,128]{2,1,0:T(4,128)S(1)} collective-permute-done((f32[31,4,128]{2,1,0:T(4,128)S(1)}, f32[31,4,128]{2,1,0:T(4,128)S(1)}, u32[]{:S(2)}, u32[]{:S(2)}) %collective-permute-start.3) | collective-permute-done | bytes 63520 | tf_op jit(solution)/shard_map/ppermute | solution.py:478
  8.8 0.0 collective-permute-done.ra
  8.8 0.0 collective-permute-done.1.rb
  8.8 0.5 %shard_map.122 = (f32[11,8,8,128]{3,2,1,0:T(8,128)S(1)}, f32[3,5,40,128]{3,2,1,0:T(8,128)S(1)}, f32[3,5,40,128]{3,2,1,0:T(8,128)S(1)}, f32[3,5,40,128]{3,2,1,0:T(8,128)S(1)}, f32[33,40,128]{2,1,0:T(8,128)S(1)}) custom-call(f32[3,8,32,128]{3,2,1,0:T(8,128)S(1)} %get-tuple-element.34.d, f32[3,8,32,128]{3,2,1,0:T(8,128)S(1)} %get-tuple-element.35.e, ...), custom_call_target="tpu_custom_call" | custom-call | tf_op jit(solution)/shard_map/pallas_call | solution.py:482
  9.3 1.4 %collective-permute-start.6 = (f32[33,40,128]{2,1,0:T(8,128)S(1)}, f32[33,40,128]{2,1,0:T(8,128)S(1)}, u32[]{:S(2)}, u32[]{:S(2)}) collective-permute-start(f32[33,40,128]{2,1,0:T(8,128)S(1)} %get-tuple-element.57), channel_id=1, source_target_pairs={{0,4},{1,5},{2,6},{3,7},{4,0},{5,1},{6,2},{7,3},{8,12},{9,13},{10,... | collective-permute-start | bytes 2027528 | tf_op jit(solution)/shard_map/ppermute | solution.py:478
  10.7 0.0 copy-start
  10.7 0.0 copy-start.1
  10.7 0.0 copy-start.2
  10.7 2.8 %collective-permute-start.4 = (f32[888,128]{1,0:T(8,128)S(1)}, f32[888,128]{1,0:T(8,128)S(1)}, u32[]{:S(2)}, u32[]{:S(2)}) collective-permute-start(f32[888,128]{1,0:T(8,128)S(1)} %get-tuple-element.54), channel_id=1, source_target_pairs={{0,1},{1,0},{2,3},{3,2},{4,8},{5,9},{6,10},{7,11},{8,4},{9,5},{10,... | collective-permute-start | bytes 1363976 | tf_op jit(solution)/shard_map/ppermute | solution.py:478
  13.5 0.1 shard_map.124
  13.6 2.7 %collective-permute-start.5 = (f32[432,128]{1,0:T(8,128)S(1)}, f32[432,128]{1,0:T(8,128)S(1)}, u32[]{:S(2)}, u32[]{:S(2)}) collective-permute-start(f32[432,128]{1,0:T(8,128)S(1)} %shard_map.124), channel_id=1, source_target_pairs={{0,1},{1,0},{2,3},{3,2},{4,8},{5,9},{6,10},{7,11},{8,4},{9,5},{10,... | collective-permute-start | bytes 663560 | tf_op jit(solution)/shard_map/ppermute | solution.py:478
  16.3 0.0 copy-done
  16.4 0.0 copy-done.1
  16.4 0.0 copy-done.2
  16.4 0.6 %shard_map.125 = (f32[2,32,128]{2,1,0:T(8,128)S(1)}, f32[2,32,128]{2,1,0:T(8,128)S(1)}) custom-call(s32[2,32,128]{2,1,0:T(8,128)S(1)} %copy-done, f32[8]{0:T(128)S(1)} %copy-done.1, f32[8]{0:T(128)S(1)} %copy-done.2), custom_call_target="tpu_custom_call" | custom-call | tf_op jit(solution)/shard_map/pallas_call | solution.py:482
  16.9 0.5 %shard_map.123 = (f32[3,7,40,128]{3,2,1,0:T(8,128)S(1)}, f32[3,7,40,128]{3,2,1,0:T(8,128)S(1)}, f32[3,7,40,128]{3,2,1,0:T(8,128)S(1)}) custom-call(f32[3,8,32,128]{3,2,1,0:T(8,128)S(1)} %get-tuple-element.34.d, f32[3,8,32,128]{3,2,1,0:T(8,128)S(1)} %get-tuple-element.35.e, f32[3,8,32,128]{3,2,1,0:T(8,128)S(1)} %get-tuple-element.36.h, ...), custom_call_target="tpu_custom_call" | custom-call | tf_op jit(solution)/shard_map/pallas_call | solution.py:482
  17.5 0.0 collective-permute-done.6.cc
  17.5 1.5 %shard_map.126 = (f32[3,8,32,128]{3,2,1,0:T(8,128)}, f32[3,8,32,128]{3,2,1,0:T(8,128)}, f32[3,8,32,128]{3,2,1,0:T(8,128)}, f32[8,32,128]{2,1,0:T(8,128)}, f32[8,32,128]{2,1,0:T(8,128)}) custom-call(f32[3,8,32,128]{3,2,1,0:T(8,128)S(1)} %get-tuple-element.34.d, f32[3,8,32,128]{3,2,1,0:T(8,128)S(1)} %get-tuple-element.35.e, ...), custom_call_target="tpu_custom_call" | custom-call | tf_op jit(solution)/shard_map/pallas_call | solution.py:482
  19.0 5.3 %collective-permute-done.5.cb = f32[432,128]{1,0:T(8,128)S(1)} collective-permute-done((f32[432,128]{1,0:T(8,128)S(1)}, f32[432,128]{1,0:T(8,128)S(1)}, u32[]{:S(2)}, u32[]{:S(2)}) %collective-permute-start.5) | collective-permute-done | bytes 221216 | tf_op jit(solution)/shard_map/ppermute | solution.py:478
  24.3 0.0 collective-permute-done.4.ca
  24.3 2.1 %shard_map.127 = (f32[3,8,32,128]{3,2,1,0:T(8,128)}, f32[3,8,32,128]{3,2,1,0:T(8,128)}, f32[3,8,32,128]{3,2,1,0:T(8,128)}, f32[8,32,128]{2,1,0:T(8,128)}, f32[8,32,128]{2,1,0:T(8,128)}) custom-call(f32[3,8,32,128]{3,2,1,0:T(8,128)S(1)} %get-tuple-element.34.d, ...), custom_call_target="tpu_custom_call", output_to_operand_aliasing={{0}: (16, {}), {1}: (17, {}), {2}: (18, {}), {3}: (19, {}),... | custom-call | tf_op jit(solution)/shard_map/pallas_call | solution.py:482
  (1 shorter events, 0.0 us)
Async XLA Ops:
  2.2 6.6 %collective-permute-start = (f32[57,4,128]{2,1,0:T(4,128)S(1)}, f32[57,4,128]{2,1,0:T(4,128)S(1)}, u32[]{:S(2)}, u32[]{:S(2)}) collective-permute-start(f32[57,4,128]{2,1,0:T(4,128)S(1)} %get-tuple-element.43), channel_id=1, source_target_pairs={{0,1},{1,0},{2,3},{3,2},{4,5},{5,4},{6,7},{7,6},{8,9},{9,8},{10,11... | collective-permute-start | bytes 350216 | tf_op jit(solution)/shard_map/ppermute | solution.py:478
  2.5 6.3 %collective-permute-start.1 = (f32[57,4,128]{2,1,0:T(4,128)S(1)}, f32[57,4,128]{2,1,0:T(4,128)S(1)}, u32[]{:S(2)}, u32[]{:S(2)}) collective-permute-start(f32[57,4,128]{2,1,0:T(4,128)S(1)} %get-tuple-element.44), channel_id=1, source_target_pairs={{0,4},{1,2},{2,1},{3,7},{4,0},{5,6},{6,5},{7,3},{8,12},{9,10},{10,... | collective-permute-start | bytes 350216 | tf_op jit(solution)/shard_map/ppermute | solution.py:478
  4.6 3.6 %collective-permute-start.2 = (f32[31,4,128]{2,1,0:T(4,128)S(1)}, f32[31,4,128]{2,1,0:T(4,128)S(1)}, u32[]{:S(2)}, u32[]{:S(2)}) collective-permute-start(f32[31,4,128]{2,1,0:T(4,128)S(1)} %get-tuple-element.45), channel_id=1, source_target_pairs={{0,1},{1,0},{2,3},{3,2},{4,5},{5,4},{6,7},{7,6},{8,9},{9,8},{10,11... | collective-permute-start | bytes 190472 | tf_op jit(solution)/shard_map/ppermute | solution.py:478
  4.7 4.1 %collective-permute-start.3 = (f32[31,4,128]{2,1,0:T(4,128)S(1)}, f32[31,4,128]{2,1,0:T(4,128)S(1)}, u32[]{:S(2)}, u32[]{:S(2)}) collective-permute-start(f32[31,4,128]{2,1,0:T(4,128)S(1)} %get-tuple-element.46), channel_id=1, source_target_pairs={{0,4},{1,2},{2,1},{3,7},{4,0},{5,6},{6,5},{7,3},{8,12},{9,10},{10,... | collective-permute-start | bytes 190472 | tf_op jit(solution)/shard_map/ppermute | solution.py:478
  9.3 8.1 %collective-permute-start.6 = (f32[33,40,128]{2,1,0:T(8,128)S(1)}, f32[33,40,128]{2,1,0:T(8,128)S(1)}, u32[]{:S(2)}, u32[]{:S(2)}) collective-permute-start(f32[33,40,128]{2,1,0:T(8,128)S(1)} %get-tuple-element.57), channel_id=1, source_target_pairs={{0,4},{1,5},{2,6},{3,7},{4,0},{5,1},{6,2},{7,3},{8,12},{9,13},{10,... | collective-permute-start | bytes 2027528 | tf_op jit(solution)/shard_map/ppermute | solution.py:478
  10.7 5.6 %copy-start = (s32[2,32,128]{2,1,0:T(8,128)S(1)}, s32[2,32,128]{2,1,0:T(8,128)}, u32[]{:S(2)}) copy-start(s32[2,32,128]{2,1,0:T(8,128)} %classes.1) | copy-start | bytes 98308
  10.7 5.6 %copy-start.1 = (f32[8]{0:T(128)S(1)}, f32[8]{0:T(128)}, u32[]{:S(2)}) copy-start(f32[8]{0:T(128)} %eps_table.1) | copy-start | bytes 100
  10.7 5.6 %copy-start.2 = (f32[8]{0:T(128)S(1)}, f32[8]{0:T(128)}, u32[]{:S(2)}) copy-start(f32[8]{0:T(128)} %chi_table.1) | copy-start | bytes 100
  10.7 13.6 %collective-permute-start.4 = (f32[888,128]{1,0:T(8,128)S(1)}, f32[888,128]{1,0:T(8,128)S(1)}, u32[]{:S(2)}, u32[]{:S(2)}) collective-permute-start(f32[888,128]{1,0:T(8,128)S(1)} %get-tuple-element.54), channel_id=1, source_target_pairs={{0,1},{1,0},{2,3},{3,2},{4,8},{5,9},{6,10},{7,11},{8,4},{9,5},{10,... | collective-permute-start | bytes 1363976 | tf_op jit(solution)/shard_map/ppermute | solution.py:478
  13.6 10.7 %collective-permute-start.5 = (f32[432,128]{1,0:T(8,128)S(1)}, f32[432,128]{1,0:T(8,128)S(1)}, u32[]{:S(2)}, u32[]{:S(2)}) collective-permute-start(f32[432,128]{1,0:T(8,128)S(1)} %shard_map.124), channel_id=1, source_target_pairs={{0,1},{1,0},{2,3},{3,2},{4,8},{5,9},{6,10},{7,11},{8,4},{9,5},{10,... | collective-permute-start | bytes 663560 | tf_op jit(solution)/shard_map/ppermute | solution.py:478

commit v6 on v5

--- a/solution.py
+++ b/solution.py
@@ -26,9 +26,6 @@
 HI_AT = {k: i for i, k in enumerate(HI)}
 LO_AT = {k: i for i, k in enumerate(LO) if k}
 NS, NR = len(HI), len(RAW)
-
-FIRST = [(c, p) for p in range(5) for c in ALL] + [(E, 5), (E + 1, 5)]
-SECOND = [(c, p) for p in (5, 6, 7) for c in ALL if (c, p) not in FIRST]
 
 VM = pl.BlockSpec(memory_space=pltpu.VMEM)
 HBM = pl.BlockSpec(memory_space=pltpu.HBM)
@@ -148,23 +145,21 @@
     return eps[plane] if comp == EPS else chi[plane]
 
 
-def load(d, e, h, eps, chi, dv, ev, hv, epsv, chiv, ya, yb, yc, yd, sems):
+def load(d, e, h, eps, chi, dv, ev, hv, epsv, chiv, ya, yb, sems):
     moves = [(a.at[c], b.at[c]) for a, b in ((d, dv), (e, ev), (h, hv)) for c in range(3)] + [(eps, epsv), (chi, chiv)]
     copies = [pltpu.make_async_copy(a, b, sems.at[i]) for i, (a, b) in enumerate(moves)]
     for c in copies:
         c.start()
-    gz, gx, _, last = position()
-    even, first_core = lax.rem(gx, 2) == 0, lax.rem(gz, 2) == 0
+    _, gx, _, last = position()
+    even = lax.rem(gx, 2) == 0
     keep = scalar(jnp.logical_and(gx != 0, gx != last))
-    for c in copies:
-        c.wait()
-    fields = (dv, ev, hv, epsv, chiv)
-    for units, a, b in ((FIRST, ya, yb), (SECOND, yc, yd)):
-        for i, (comp, p) in enumerate(units):
-            v = jnp.where(first_core, own(fields, comp, p), own(fields, comp, NZL - 1 - p))
+    for comp in ALL:
+        copies[comp].wait()
+        for p in range(NZL):
+            v = own((dv, ev, hv, epsv, chiv), comp, p)
             low, high = v[:XH], v[NXL - XH :]
-            a[i] = jnp.where(even, high, low)
-            b[i] = jnp.where(even, low, high) * keep
+            ya[comp, p] = jnp.where(even, high, low)
+            yb[comp, p] = jnp.where(even, low, high) * keep
 
 
 def mark(out):
@@ -177,13 +172,10 @@
     grid.sweep(3, range(2, 3), (), put)
 
 
-def lookup(classes, eps_table, chi_table, eps_in, chi_in):
-    for out, table in ((eps_in, eps_table), (chi_in, chi_table)):
-        for k in range(ADVANCE):
-            picked = jnp.zeros((NXL, NY), jnp.float32)
-            for label in range(table.shape[0]):
-                picked = jnp.where(classes[k] == label, table[label], picked)
-            out[k] = picked
+def lookup(classes, table):
+    labels = jnp.arange(table.shape[0], dtype=jnp.int32).reshape(-1, 1, 1, 1)
+    picked = jnp.where(classes[None] == labels, table.reshape(-1, 1, 1, 1), jnp.float32(0.0))
+    return jnp.sum(picked, axis=0)
 
 
 def sent(grid, side, i):
@@ -241,11 +233,14 @@
     return rows(jnp.where(even, a, b), jnp.where(even, b, a))
 
 
-def edges(d, e, h, eps, chi, ra, rb, inside, cross, sd, se, sh, slo, tiles):
+def edges(d, e, h, eps, chi, ra, rb, inside, xt, sd, se, sh, slo, cross):
     fields = (d, e, h, eps, chi)
     gz, _, last, _ = position()
     keep = scalar(jnp.logical_and(gz != 0, gz != last))
     half = halo_row() < XH
+    for comp in ALL:
+        for p in range(NZL):
+            xt[comp, p] = joined(ra[comp, p], rb[comp, p])
 
     def pack(grid, side):
         for i, unit in enumerate(side):
@@ -258,51 +253,50 @@
 
     @pl.when(lax.rem(gz, 2) == 0)
     def _():
-        at = {k: i for i, k in enumerate(FIRST)}
-        for i in range(len(FIRST)):
-            tiles[i] = joined(ra[i], rb[i])
-        grid = edge_grid(inside[...], fields, lambda comp, p: tiles[at[(comp, p)]])
+        grid = edge_grid(inside[...], fields, lambda comp, p: xt[comp, p])
         early(grid, lambda c, p, v, n: grid.put((sd, se, sh)[c // 3], (c % 3, p), c, p, v, n))
         pack(grid, HI)
 
     @pl.when(lax.rem(gz, 2) == 1)
     def _():
-        at = {(c, NZL - 1 - p): i for i, (c, p) in enumerate(FIRST) if p < 2}
-        for i in at.values():
-            tiles[i] = joined(ra[i], rb[i])
-        grid = edge_grid(inside[...], fields, lambda comp, p: tiles[at[(comp, p)]])
+        grid = edge_grid(inside[...], fields, lambda comp, p: xt[comp, p])
         grid.step_h(1, 6, range(2), lambda c, p, v, n: grid.put(slo, c - H, c, p, v, n))
         pack(grid, LO)
 
 
-def merge(d, e, h, eps, chi, id_, ie, ih, ilo, ra, rb, rc, rd, inside, xt, fd, fe, fh, chip, sd, se, sh, slo):
+def merge(d, e, h, eps, chi, id_, ie, ih, ilo, xt, sd, se, sh, slo, inside, fd, fe, fh, chip, td, te, th, tlo):
     fields = (d, e, h, eps, chi)
-    gz, _, _, _ = position()
-    first_core = lax.rem(gz, 2) == 0
-    for units, a, b in ((FIRST, ra, rb), (SECOND, rc, rd)):
-        for i, (comp, p) in enumerate(units):
-            xt[comp, jnp.where(first_core, p, NZL - 1 - p)] = joined(a[i], b[i])
-    thin = edge_grid(inside[...], fields, lambda comp, p: xt[comp, p])
-    thin.step_h(1, 6, range(2), lambda c, p, v, n: thin.put(slo, c - H, c, p, v, n))
-    early(thin, lambda c, p, v, n: thin.put((sd, se, sh)[c // 3], (c % 3, p), c, p, v, n))
     half = halo_row() < XH
 
     def merged(v, w):
         return rows(jnp.where(half, w[16:24], v[0:8]), v[8:24], jnp.where(half, v[24:32], w[0:8]), w[8:16])
 
-    grid = Grid(ROWS, None, None)
-    hold_own(grid, fields, xt)
-    for k, (v, w, ref) in enumerate(((id_, sd, fd), (ie, se, fe), (ih, sh, fh))):
-        for p in EARLY[k]:
-            for c in range(3):
-                grid.put(ref, (c, p), 3 * k + c, p, merged(v[c, p], w[c, p]), 1)
-    for c in range(2):
-        grid.hold(H + c, 6, functools.partial(lambda a: merged(ilo[a], slo[a]), c))
-    for i in range(NS):
-        v = sent(grid, HI, i)
-        if i < len(LO) and LO[i]:
-            v = jnp.where(first_core, sent(grid, LO, i), v)
-        chip[i] = v
+    def join(sides, side):
+        grid = Grid(ROWS, None, None)
+        hold_own(grid, fields, xt)
+        for k, (v, w, ref) in enumerate(((id_, sides[0], fd), (ie, sides[1], fe), (ih, sides[2], fh))):
+            for p in EARLY[k]:
+                for c in range(3):
+                    grid.put(ref, (c, p), 3 * k + c, p, merged(v[c, p], w[c, p]), 1)
+        for c in range(2):
+            grid.hold(H + c, 6, functools.partial(lambda a: merged(ilo[a], tlo[a]), c))
+        for i, unit in enumerate(side):
+            if unit:
+                chip[i] = grid.get(*unit)
+
+    gz, _, _, _ = position()
+
+    @pl.when(lax.rem(gz, 2) == 0)
+    def _():
+        grid = edge_grid(inside[...], fields, lambda comp, p: xt[comp, p])
+        grid.step_h(1, 6, range(2), lambda c, p, v, n: grid.put(tlo, c - H, c, p, v, n))
+        join((sd, se, sh), LO)
+
+    @pl.when(lax.rem(gz, 2) == 1)
+    def _():
+        grid = edge_grid(inside[...], fields, lambda comp, p: xt[comp, p])
+        early(grid, lambda c, p, v, n: grid.put((td, te, th)[c // 3], (c % 3, p), c, p, v, n))
+        join((td, te, th), HI)
 
 
 def full_grid():
@@ -358,8 +352,7 @@
     grid.sweep(4, (3,), (), put)
 
 
-def complete(own_refs, xt, frames, more, above, below, scratch, outs, sems, coming):
-    fields = own_refs
+def complete(fields, xt, frames, more, above, below, state, staged, media, coming, done):
     grid = full_grid()
     hold_own(grid, fields, xt)
     hold_frames(grid, frames, EARLY)
@@ -369,13 +362,6 @@
             for (comp, p), i in at.items():
                 level = (p + (H <= comp < EPS)) if shift > 0 else int(p == 6)
                 grid.hold(comp, p + shift, functools.partial(side, i), level)
-    state, staged = scratch[:3], scratch[3:6]
-    copies = []
-
-    def send(o):
-        for k in range(3):
-            copies.append(pltpu.make_async_copy(staged[k].at[:, pl.ds(o, 1)], outs[k].at[:, pl.ds(o, 1)], sems.at[k, o]))
-            copies[-1].start()
 
     def put(c, p, v, n):
         k = c // 3
@@ -393,7 +379,8 @@
                     for c in range(3):
                         staged[2][c, p - ADVANCE] = grid.get(H + c, p, STEPS)[:NXL]
                 grid.step_de(STEPS, p, put)
-                send(p - ADVANCE)
+                for k in range(3):
+                    done(k, p - ADVANCE, 1)
 
     if below is not None:
         grid.sweep(1, (-1,), (-1, 0), put)
@@ -401,51 +388,43 @@
         grid.sweep(3, (0, 1), (1, 2), put)
         last_sweep((1, 2), (2, 3))
     if above is not None:
-        for k, (comp, new) in enumerate(((EPS, coming and coming[0]), (CHI, coming and coming[1]))):
+        for k, comp in enumerate((EPS, CHI)):
             for o in range(ADVANCE):
                 v = grid.get(comp, NZL + o)[:NXL]
-                if new is not None:
+                if coming is not None:
                     gz, _, last, _ = position()
-                    v = jnp.where(gz == last, new[o], v)
-                scratch[6 + k][o] = v
-            copies.append(pltpu.make_async_copy(scratch[6 + k], outs[3 + k].at[pl.ds(NZL - ADVANCE, ADVANCE)], sems.at[3, k]))
-            copies[-1].start()
+                    v = jnp.where(gz == last, coming[k][o], v)
+                media[k][o] = v
+            done(3 + k, KEPT, ADVANCE)
         grid.sweep(1, (7,), (7, 8), put)
         grid.sweep(2, range(6, 9), range(6, 10), put)
         grid.sweep(3, range(5, 10), range(5, 11), put)
         last_sweep(range(4, 10), range(4, 10))
-    for c in copies:
-        c.wait()
-
-
-def near(d, e, h, eps, chi, xt, fd, fe, fh, gd, ge, gh, cc, d_out, e_out, h_out, eps_out, chi_out, *rest):
-    *scratch, sems = rest
-    fields, frames, more = (d, e, h, eps, chi), (fd, fe, fh), (gd, ge, gh)
-    outs = (d_out, e_out, h_out, eps_out, chi_out)
+
+
+KEPT = NZL - ADVANCE
+LOW, HIGH = (0, 2), (2, 6)
+
+
+def near(d, e, h, eps, chi, xt, fd, fe, fh, gd, ge, gh, cc, nd, ne, nh, neps, nchi, *state):
+    given = (d, e, h, eps, chi), xt, (fd, fe, fh), (gd, ge, gh)
     gz, _, _, _ = position()
-    keep = NZL - ADVANCE
-    media = [
-        pltpu.make_async_copy(a.at[pl.ds(ADVANCE, keep)], b.at[pl.ds(0, keep)], sems.at[3, 2 + k])
-        for k, (a, b) in enumerate(((eps, eps_out), (chi, chi_out)))
-    ]
-    for c in media:
-        c.start()
+
+    def done(k, o, n):
+        pass
 
     @pl.when(lax.rem(gz, 2) == 0)
     def _():
-        complete(fields, xt, frames, more, lambda i: cc[i], None, scratch, outs, sems, None)
+        complete(*given, lambda i: cc[i], None, state, (nd, ne, nh), (neps, nchi), None, done)
 
     @pl.when(lax.rem(gz, 2) == 1)
     def _():
-        complete(fields, xt, frames, more, None, lambda i: cc[i], scratch, outs, sems, None)
-
-    for c in media:
-        c.wait()
-
-
-def far(d, e, h, eps, chi, xt, fd, fe, fh, gd, ge, gh, ca, cb, eps_in, chi_in, *rest):
-    outs, scratch, sems = rest[5:10], rest[10:-1], rest[-1]
-    fields, frames, more = (d, e, h, eps, chi), (fd, fe, fh), (gd, ge, gh)
+        complete(*given, None, lambda i: cc[i], state, (nd, ne, nh), (neps, nchi), None, done)
+
+
+def far(d, e, h, eps, chi, xt, fd, fe, fh, gd, ge, gh, ca, cb, eps_in, chi_in, nd, ne, nh, neps, nchi, *rest):
+    outs, state, staged, media, sems = rest[:5], rest[5:8], rest[8:11], rest[11:13], rest[13]
+    given = (d, e, h, eps, chi), xt, (fd, fe, fh), (gd, ge, gh)
     half = halo_row() < XH
     gz, _, _, _ = position()
 
@@ -454,13 +433,37 @@
         x = ca[24 * NS + 8 * i : 24 * NS + 8 * i + 8] if i < NR else cb[8 * (NS + i - NR) : 8 * (NS + i - NR) + 8]
         return rows(jnp.where(half, x, m), ca[24 * i + 8 : 24 * i + 24], jnp.where(half, m, x), cb[8 * i : 8 * i + 8])
 
+    def run(above, below, made, new_media):
+        copies = []
+
+        def send(source, target):
+            copies.append(pltpu.make_async_copy(source, target, sems.at[len(copies)]))
+            copies[-1].start()
+
+        def done(k, o, n):
+            if k < 3:
+                send(staged[k].at[:, pl.ds(o, n)], outs[k].at[:, pl.ds(o, n)])
+            else:
+                send(media[k - 3], outs[k].at[pl.ds(o, n)])
+
+        o, n = made
+        for a, b in zip((nd, ne, nh), outs):
+            send(a.at[:, pl.ds(o, n)], b.at[:, pl.ds(o, n)])
+        for a, b in zip((eps, chi), outs[3:]):
+            send(a.at[pl.ds(ADVANCE, KEPT)], b.at[pl.ds(0, KEPT)])
+        for a, b in zip(new_media, outs[3:]):
+            send(a, b.at[pl.ds(KEPT, ADVANCE)])
+        complete(*given, above, below, state, staged, media, (eps_in, chi_in), done)
+        for c in copies:
+            c.wait()
+
     @pl.when(lax.rem(gz, 2) == 0)
     def _():
-        complete(fields, xt, frames, more, None, cross, scratch, outs, sems, None)
+        run(None, cross, HIGH, (neps, nchi))
 
     @pl.when(lax.rem(gz, 2) == 1)
     def _():
-        complete(fields, xt, frames, more, cross, None, scratch, outs, sems, (eps_in, chi_in))
+        run(cross, None, LOW, ())
 
 
 def swapped(shard, axis, first):
@@ -492,11 +495,11 @@
 
 def on_device(d_field, e_field, h_field, permittivity, kerr_coeff, classes, eps_table, chi_table):
     field, medium = shape(3, NZL, NXL, NY), shape(NZL, NXL, NY)
-    one, two = shape(len(FIRST), XH, NY), shape(len(SECOND), XH, NY)
-    *fields, ya, yb, yc, yd = call(
+    halo = shape(11, NZL, XH, NY)
+    *fields, ya, yb = call(
         load,
         [pltpu.with_memory_space_constraint(a, pltpu.HBM) for a in (d_field, e_field, h_field, permittivity, kerr_coeff)],
-        (field, field, field, medium, medium, one, one, two, two),
+        (field, field, field, medium, medium, halo, halo),
         [pltpu.SemaphoreType.DMA((11,))],
         specs=[HBM] * 5,
     )
@@ -504,39 +507,35 @@
     lo = shape(2, NXL, NY)
     *inside, za = call(inner, fields, (*[shape(3, 5, NXL, NY)] * 3, lo, shape(24 * NS + 8 * NR, NY)))
     ca = swapped(za, "gz", 1)
-    rc, rd = swapped(yc, "gx", 0), swapped(yd, "gx", 1)
     (edge,) = call(mark, [], (shape(8, NY),))
-    thin = [pltpu.VMEM((3, 5, EDGE, NY), jnp.float32)] * 3 + [pltpu.VMEM((2, EDGE, NY), jnp.float32)]
-    (zb,) = call(
+    thin = [(3, 5, EDGE, NY)] * 3 + [(2, EDGE, NY)]
+    xt, *outside, zb = call(
         edges,
         [*fields, ra, rb, edge],
-        (shape(8 * (NS + NS - NR), NY),),
-        [*thin, pltpu.VMEM((len(FIRST), 8, NY), jnp.float32)],
+        (shape(11, NZL, 8, NY), *[shape(*t) for t in thin], shape(8 * (NS + NS - NR), NY)),
     )
     cb = swapped(zb, "gz", 1)
-    coming = call(lookup, [classes, eps_table, chi_table], (shape(ADVANCE, NXL, NY),) * 2, specs=[VM, SM, SM])
-    frames = [shape(3, 5, ROWS, NY)] * 3
-    xt, *frames, zc = call(
-        merge, [*fields, *inside, ra, rb, rc, rd, edge], (shape(11, NZL, 8, NY), *frames, shape(NS, ROWS, NY)), thin
+    coming = lookup(classes, eps_table), lookup(classes, chi_table)
+    *frames, zc = call(
+        merge,
+        [*fields, *inside, xt, *outside, edge],
+        (*[shape(3, 5, ROWS, NY)] * 3, shape(NS, ROWS, NY)),
+        [pltpu.VMEM(t, jnp.float32) for t in thin],
     )
     cc = swapped(zc, "gz", 0)
     more = call(middle, [*fields, xt, *frames], (shape(3, 7, ROWS, NY),) * 3)
-    scratch = [pltpu.VMEM((3, 13, ROWS, NY), jnp.float32)] * 3 + [pltpu.VMEM((3, NZL, NXL, NY), jnp.float32)] * 3
-    scratch += [pltpu.VMEM((ADVANCE, NXL, NY), jnp.float32)] * 2 + [pltpu.SemaphoreType.DMA((4, NZL))]
+    state = [pltpu.VMEM((3, 13, ROWS, NY), jnp.float32)] * 3
     given = [*fields, xt, *frames, *more]
-    results = (field, field, field, medium, medium)
-    outs = call(near, [*given, cc], results, scratch, vmem=16, out=HBM)
-    given += [ca, cb, *coming]
-    n = len(given)
+    two = (ADVANCE, NXL, NY)
+    made = call(near, [*given, cc], (field, field, field, shape(*two), shape(*two)), state, vmem=16)
+    staged = [pltpu.VMEM(field.shape, jnp.float32)] * 3 + [pltpu.VMEM(two, jnp.float32)] * 2
     return call(
         far,
-        [*given, *outs],
-        results,
-        scratch,
+        [*given, ca, cb, *coming, *made],
+        (field, field, field, medium, medium),
+        [*state, *staged, pltpu.SemaphoreType.DMA((32,))],
         vmem=16,
-        specs=[VM] * n + [HBM] * 5,
         out=HBM,
-        aliases={n + k: k for k in range(5)},
     )
 
 

time: 26.8 us -> 26.6 us (level)
  waiting for transfers between devices: 7.61 us -> 10.8 us
  Pallas kernels: 7.34 us -> 5.69 us
  starting transfers between devices: 10.7 us -> 9.09 us
    ppermute x7 -> x5, waiting for transfers between devices: 7.61 us -> 10.8 us  [swapped(): return lax.ppermute(shard, ('gz', 'gx'), moves)]
    pallas_call x9 -> x8, Pallas kernels: 7.34 us -> 5.69 us  [call(): pl.pallas_call(body, out_shape=out_shape, in_specs=[VM] * len(inputs) if...]
    ppermute x7 -> x5, starting transfers between devices: 10.7 us -> 9.09 us  [swapped(): return lax.ppermute(shard, ('gz', 'gx'), moves)]
  transfers between devices with their start and end apart: 7 -> 5, of which waited for: 3 -> 3; matrix products, arithmetic and copies ran while one was open for 0% -> 0% of each run, Pallas kernels for 12% -> 6%
where the time goes in v6:
time: 26.6 us; the launch traced here: 26.4 us
  waiting for transfers between devices  10.8 us (41%)
  starting transfers between devices  9.09 us (34%)
  Pallas kernels  5.69 us (21%)
  between operations  0.69 us (3%)
    ppermute x5, waiting for transfers between devices, swapped(): return lax.ppermute(shard, ('gz', 'gx'), moves)  10.8 us
    ppermute x5, starting transfers between devices, swapped(): return lax.ppermute(shard, ('gz', 'gx'), moves)  9.09 us
    pallas_call x8, Pallas kernels, call(): pl.pallas_call(body, out_shape=out_shape, in_specs=[VM] * len(inputs) if...  5.69 us
  transfers between devices with their start and end apart: 5, of which 3 were waited for; matrix products, arithmetic and copies ran while one was open for 0% of the time, Pallas kernels for 6%

profile of v6, /device:TPU:111, one launch (start us, length us, event | category | flops | bytes accessed | tf_op | source)
XLA Modules:
  0.0 26.4 jit_solution(156829403115604446)
XLA Ops:
  0.6 1.5 %shard_map.119 = (f32[3,8,32,128]{3,2,1,0:T(8,128)S(1)}, f32[3,8,32,128]{3,2,1,0:T(8,128)S(1)}, f32[3,8,32,128]{3,2,1,0:T(8,128)S(1)}, f32[8,32,128]{2,1,0:T(8,1...) custom-call(f32[3,8,32,128]{3,2,1,0:T(8,128)} %d.1, ...), custom_call_target="tpu_custom_call" | custom-call | tf_op jit(solution)/shard_map/pallas_call | solution.py:485
  2.1 0.3 collective-permute-start
  2.4 2.1 %collective-permute-start.1 = (f32[11,8,4,128]{3,2,1,0:T(4,128)S(1)}, f32[11,8,4,128]{3,2,1,0:T(4,128)S(1)}, u32[]{:S(2)}, u32[]{:S(2)}) collective-permute-start(f32[11,8,4,128]{3,2,1,0:T(4,128)S(1)} %get-tuple-element.41), channel_id=1, source_target_pairs={{0,4},{1,2},{2,1},{3,7},{4,0},{5,6},{6,5},{7,3},{8,12},{9,10},{10,... | collective-permute-start | bytes 540680 | tf_op jit(solution)/shard_map/ppermute | solution.py:481
  4.5 0.5 %shard_map.122 = (f32[3,5,32,128]{3,2,1,0:T(8,128)S(1)}, f32[3,5,32,128]{3,2,1,0:T(8,128)S(1)}, f32[3,5,32,128]{3,2,1,0:T(8,128)S(1)}, f32[2,32,128]{2,1,0:T(8,128)S(1)}, f32[888,128]{1,0:T(8,128)S(1)}) custom-call(f32[3,8,32,128]{3,2,1,0:T(8,128)S(1)} %get-tuple-element.35.d, f32[3,8,32,128]{3,2,1,0:T(8,128)S(1)} %get-tuple-element.36.e, ...), custom_call_target="tpu_custom_call" | custom-call | tf_op jit(solution)/shard_map/pallas_call | solution.py:485
  5.0 2.7 %collective-permute-done.ra = f32[11,8,4,128]{3,2,1,0:T(4,128)S(1)} collective-permute-done((f32[11,8,4,128]{3,2,1,0:T(4,128)S(1)}, f32[11,8,4,128]{3,2,1,0:T(4,128)S(1)}, u32[]{:S(2)}, u32[]{:S(2)}) %collective-permute-start) | collective-permute-done | bytes 180256 | tf_op jit(solution)/shard_map/ppermute | solution.py:481
  7.7 0.8 %collective-permute-done.1.rb = f32[11,8,4,128]{3,2,1,0:T(4,128)S(1)} collective-permute-done((f32[11,8,4,128]{3,2,1,0:T(4,128)S(1)}, f32[11,8,4,128]{3,2,1,0:T(4,128)S(1)}, u32[]{:S(2)}, u32[]{:S(2)}) %collective-permute-start.1) | collective-permute-done | bytes 180256 | tf_op jit(solution)/shard_map/ppermute | solution.py:481
  8.5 0.1 shard_map.121
  8.6 0.0 copy-start
  8.6 0.5 %shard_map.123 = (f32[3,5,40,128]{3,2,1,0:T(8,128)S(1)}, f32[3,5,40,128]{3,2,1,0:T(8,128)S(1)}, f32[3,5,40,128]{3,2,1,0:T(8,128)S(1)}, f32[33,40,128]{2,1,0:T(8,128)S(1)}) custom-call(f32[3,8,32,128]{3,2,1,0:T(8,128)S(1)} %get-tuple-element.35.d, f32[3,8,32,128]{3,2,1,0:T(8,128)S(1)} %get-tuple-element.36.e, f32[3,8,32,128]{3,2,1,0:T(8,128)S(1)} %get-tuple-element.37.h, ...), custom_call_target="tpu_custom_call" | custom-call | tf_op jit(solution)/shard_map/pallas_call | solution.py:485
  9.1 1.6 %collective-permute-start.4 = (f32[33,40,128]{2,1,0:T(8,128)S(1)}, f32[33,40,128]{2,1,0:T(8,128)S(1)}, u32[]{:S(2)}, u32[]{:S(2)}) collective-permute-start(f32[33,40,128]{2,1,0:T(8,128)S(1)} %get-tuple-element.59), channel_id=1, source_target_pairs={{0,4},{1,5},{2,6},{3,7},{4,0},{5,1},{6,2},{7,3},{8,12},{9,13},{10,... | collective-permute-start | bytes 2027528 | tf_op jit(solution)/shard_map/ppermute | solution.py:481
  10.8 0.0 copy-start.1
  10.8 0.0 copy-start.2
  10.8 2.8 %collective-permute-start.2 = (f32[888,128]{1,0:T(8,128)S(1)}, f32[888,128]{1,0:T(8,128)S(1)}, u32[]{:S(2)}, u32[]{:S(2)}) collective-permute-start(f32[888,128]{1,0:T(8,128)S(1)} %get-tuple-element.57), channel_id=1, source_target_pairs={{0,1},{1,0},{2,3},{3,2},{4,8},{5,9},{6,10},{7,11},{8,4},{9,5},{10,... | collective-permute-start | bytes 1363976 | tf_op jit(solution)/shard_map/ppermute | solution.py:481
  13.5 2.3 %collective-permute-start.3 = (f32[432,128]{1,0:T(8,128)S(1)}, f32[432,128]{1,0:T(8,128)S(1)}, u32[]{:S(2)}, u32[]{:S(2)}) collective-permute-start(f32[432,128]{1,0:T(8,128)S(1)} %get-tuple-element.58), channel_id=1, source_target_pairs={{0,1},{1,0},{2,3},{3,2},{4,8},{5,9},{6,10},{7,11},{8,4},{9,5},{10,... | collective-permute-start | bytes 663560 | tf_op jit(solution)/shard_map/ppermute | solution.py:481
  15.8 0.0 copy-done
  15.8 0.0 copy-done.1
  15.8 0.0 copy-done.2
  15.8 0.1 select_reduce_fusion
  16.0 0.5 %shard_map.124 = (f32[3,7,40,128]{3,2,1,0:T(8,128)S(1)}, f32[3,7,40,128]{3,2,1,0:T(8,128)S(1)}, f32[3,7,40,128]{3,2,1,0:T(8,128)S(1)}) custom-call(f32[3,8,32,128]{3,2,1,0:T(8,128)S(1)} %get-tuple-element.35.d, f32[3,8,32,128]{3,2,1,0:T(8,128)S(1)} %get-tuple-element.36.e, f32[3,8,32,128]{3,2,1,0:T(8,128)S(1)} %get-tuple-element.37.h, ...), custom_call_target="tpu_custom_call" | custom-call | tf_op jit(solution)/shard_map/pallas_call | solution.py:485
  16.5 0.0 collective-permute-done.4.cc
  16.5 0.6 %shard_map.125 = (f32[3,8,32,128]{3,2,1,0:T(8,128)S(1)}, f32[3,8,32,128]{3,2,1,0:T(8,128)S(1)}, f32[3,8,32,128]{3,2,1,0:T(8,128)S(1)}, f32[2,32,128]{2,1,0:T(8,128)S(1)}, f32[2,32,128]{2,1,0:T(8,128)S(1)}) custom-call(f32[3,8,32,128]{3,2,1,0:T(8,128)S(1)} %get-tuple-element.35.d, f32[3,8,32,128]{3,2,1,0:T(8,128)S(1)} %get-tuple-element.36.e, ...), custom_call_target="tpu_custom_call" | custom-call | tf_op jit(solution)/shard_map/pallas_call | solution.py:485
  17.0 7.3 %collective-permute-done.3.cb = f32[432,128]{1,0:T(8,128)S(1)} collective-permute-done((f32[432,128]{1,0:T(8,128)S(1)}, f32[432,128]{1,0:T(8,128)S(1)}, u32[]{:S(2)}, u32[]{:S(2)}) %collective-permute-start.3) | collective-permute-done | bytes 221216 | tf_op jit(solution)/shard_map/ppermute | solution.py:481
  24.3 0.0 collective-permute-done.2.ca
  24.3 2.1 %shard_map.126 = (f32[3,8,32,128]{3,2,1,0:T(8,128)}, f32[3,8,32,128]{3,2,1,0:T(8,128)}, f32[3,8,32,128]{3,2,1,0:T(8,128)}, f32[8,32,128]{2,1,0:T(8,128)}, f32[8,32,128]{2,1,0:T(8,128)}) custom-call(f32[3,8,32,128]{3,2,1,0:T(8,128)S(1)} %get-tuple-element.35.d, f32[3,8,32,128]{3,2,1,0:T(8,128)S(1)} %get-tuple-element.36.e, ...), custom_call_target="tpu_custom_call" | custom-call | tf_op jit(solution)/shard_map/pallas_call | solution.py:485
  (1 shorter events, 0.0 us)
Async XLA Ops:
  2.1 5.5 %collective-permute-start = (f32[11,8,4,128]{3,2,1,0:T(4,128)S(1)}, f32[11,8,4,128]{3,2,1,0:T(4,128)S(1)}, u32[]{:S(2)}, u32[]{:S(2)}) collective-permute-start(f32[11,8,4,128]{3,2,1,0:T(4,128)S(1)} %get-tuple-element.40), channel_id=1, source_target_pairs={{0,1},{1,0},{2,3},{3,2},{4,5},{5,4},{6,7},{7,6},{8,9},{9,8},{10,11... | collective-permute-start | bytes 540680 | tf_op jit(solution)/shard_map/ppermute | solution.py:481
  2.4 6.1 %collective-permute-start.1 = (f32[11,8,4,128]{3,2,1,0:T(4,128)S(1)}, f32[11,8,4,128]{3,2,1,0:T(4,128)S(1)}, u32[]{:S(2)}, u32[]{:S(2)}) collective-permute-start(f32[11,8,4,128]{3,2,1,0:T(4,128)S(1)} %get-tuple-element.41), channel_id=1, source_target_pairs={{0,4},{1,2},{2,1},{3,7},{4,0},{5,6},{6,5},{7,3},{8,12},{9,10},{10,... | collective-permute-start | bytes 540680 | tf_op jit(solution)/shard_map/ppermute | solution.py:481
  8.6 7.2 %copy-start = (s32[2,32,128]{2,1,0:T(8,128)S(1)}, s32[2,32,128]{2,1,0:T(8,128)}, u32[]{:S(2)}) copy-start(s32[2,32,128]{2,1,0:T(8,128)} %param.13) | copy-start | bytes 98308
  9.1 7.3 %collective-permute-start.4 = (f32[33,40,128]{2,1,0:T(8,128)S(1)}, f32[33,40,128]{2,1,0:T(8,128)S(1)}, u32[]{:S(2)}, u32[]{:S(2)}) collective-permute-start(f32[33,40,128]{2,1,0:T(8,128)S(1)} %get-tuple-element.59), channel_id=1, source_target_pairs={{0,4},{1,5},{2,6},{3,7},{4,0},{5,1},{6,2},{7,3},{8,12},{9,13},{10,... | collective-permute-start | bytes 2027528 | tf_op jit(solution)/shard_map/ppermute | solution.py:481
  10.8 5.1 %copy-start.1 = (f32[8]{0:T(128)S(1)}, f32[8]{0:T(128)}, u32[]{:S(2)}) copy-start(f32[8]{0:T(128)} %param.15) | copy-start | bytes 100
  10.8 5.1 %copy-start.2 = (f32[8]{0:T(128)S(1)}, f32[8]{0:T(128)}, u32[]{:S(2)}) copy-start(f32[8]{0:T(128)} %param.14) | copy-start | bytes 100
  10.8 13.6 %collective-permute-start.2 = (f32[888,128]{1,0:T(8,128)S(1)}, f32[888,128]{1,0:T(8,128)S(1)}, u32[]{:S(2)}, u32[]{:S(2)}) collective-permute-start(f32[888,128]{1,0:T(8,128)S(1)} %get-tuple-element.57), channel_id=1, source_target_pairs={{0,1},{1,0},{2,3},{3,2},{4,8},{5,9},{6,10},{7,11},{8,4},{9,5},{10,... | collective-permute-start | bytes 1363976 | tf_op jit(solution)/shard_map/ppermute | solution.py:481
  13.5 10.8 %collective-permute-start.3 = (f32[432,128]{1,0:T(8,128)S(1)}, f32[432,128]{1,0:T(8,128)S(1)}, u32[]{:S(2)}, u32[]{:S(2)}) collective-permute-start(f32[432,128]{1,0:T(8,128)S(1)} %get-tuple-element.58), channel_id=1, source_target_pairs={{0,1},{1,0},{2,3},{3,2},{4,8},{5,9},{6,10},{7,11},{8,4},{9,5},{10,... | collective-permute-start | bytes 663560 | tf_op jit(solution)/shard_map/ppermute | solution.py:481

commit v7 on v6

--- a/solution.py
+++ b/solution.py
@@ -20,11 +20,13 @@
 ROWS = NXL + 2 * XH
 EDGE = 24
 
-RAW = [(c, 0) for c in range(H)] + [(c, p) for p in range(3) for c in (EPS, CHI)]
-HI = RAW + [(H + c, 0) for c in range(3)] + [(c, p) for p in (1, 2) for c in range(EPS)]
-LO = [(c, 7) for c in ALL] + [None, (H, 6), (H + 1, 6)]
+DP, HP, INV = 11, 14, 17
+RAW = [(E + c, 0) for c in range(3)] + [(c, p) for p in range(3) for c in (EPS, CHI)]
+HI = RAW + [(DP + c, p) for p in range(3) for c in range(3)] + [(HP + c, p) for p in range(2) for c in range(3)]
+HI += [(INV, 1), (INV, 2)]
+LO = [(c, 7) for c in ALL] + [(H, 6), (H + 1, 6)]
 HI_AT = {k: i for i, k in enumerate(HI)}
-LO_AT = {k: i for i, k in enumerate(LO) if k}
+LO_AT = {k: i for i, k in enumerate(LO)}
 NS, NR = len(HI), len(RAW)
 
 VM = pl.BlockSpec(memory_space=pltpu.VMEM)
@@ -92,6 +94,12 @@
     def step_h(self, n, p, comps, put):
         f = self.factor(p)
         ex, ey, ez = (self.get(E + c, p, n - 1) for c in range(3))
+        if self.level.get((HP, p)) == n:
+            hx, hy, hz = (self.get(HP + c, p) for c in range(3))
+            put(H, p, hx - f * ((self.next_y(ez) - ez) + ey), n)
+            put(H + 1, p, hy + f * (ex + (self.next_x(ez) - ez)), n)
+            put(H + 2, p, hz - f * ((self.next_x(ey) - ey) - (self.next_y(ex) - ex)), n)
+            return
         new = {}
         if 0 in comps:
             eyn = self.get(E + 1, p + 1, n - 1)
@@ -104,21 +112,47 @@
         for c, curl in new.items():
             put(H + c, p, self.get(H + c, p, n - 1) - f * curl, n)
 
+    def medium(self, p):
+        eps, fill = self.get(EPS, p), self.fill(p)
+        return eps if fill is None else eps + fill, self.get(CHI, p)
+
+    def first_inverse(self, n, p):
+        ex, ey, ez = (self.get(E + c, p, n) for c in range(3))
+        eps, chi = self.medium(p)
+        return 1.0 / (eps + chi * (ex * ex + ey * ey + ez * ez))
+
+    def derive(self):
+        out = {}
+        for p in range(3):
+            f, n = self.factor(p), p + 1
+            hx, hy, hz = (self.get(H + c, p, n) for c in range(3))
+            dx, dy, dz = (self.get(D + c, p, n - 1) for c in range(3))
+            out[(DP, p)] = dx + f * ((hz - self.prev_y(hz)) - hy)
+            out[(DP + 1, p)] = dy + f * (hx - (hz - self.prev_x(hz)))
+            out[(DP + 2, p)] = dz + f * ((hy - self.prev_x(hy)) - (hx - self.prev_y(hx)))
+            if p < 2:
+                out[(HP, p)] = hx + f * self.get(E + 1, p + 1, n)
+                out[(HP + 1, p)] = hy - f * self.get(E, p + 1, n)
+                out[(HP + 2, p)] = hz
+            if p > 0:
+                out[(INV, p)] = self.first_inverse(n - 1, p)
+        return out
+
     def step_de(self, n, p, put):
         f = self.factor(p)
-        hx, hy, hz = (self.get(H + c, p, n) for c in range(3))
         hxp, hyp = (self.get(H + c, p - 1, n) for c in range(2))
-        dx = self.get(D, p, n - 1) + f * ((hz - self.prev_y(hz)) - (hy - hyp))
-        dy = self.get(D + 1, p, n - 1) + f * ((hx - hxp) - (hz - self.prev_x(hz)))
-        dz = self.get(D + 2, p, n - 1) + f * ((hy - self.prev_x(hy)) - (hx - self.prev_y(hx)))
-        ex, ey, ez = (self.get(E + c, p, n - 1) for c in range(3))
-        eps, chi = self.get(EPS, p), self.get(CHI, p)
-        fill = self.fill(p)
-        if fill is not None:
-            eps = eps + fill
+        if self.level.get((DP, p)) == n:
+            dx, dy, dz = (self.get(DP + c, p) for c in range(3))
+            dx, dy = dx + f * hyp, dy - f * hxp
+        else:
+            hx, hy, hz = (self.get(H + c, p, n) for c in range(3))
+            dx = self.get(D, p, n - 1) + f * ((hz - self.prev_y(hz)) - (hy - hyp))
+            dy = self.get(D + 1, p, n - 1) + f * ((hx - hxp) - (hz - self.prev_x(hz)))
+            dz = self.get(D + 2, p, n - 1) + f * ((hy - self.prev_x(hy)) - (hx - self.prev_y(hx)))
+        eps, chi = self.medium(p)
+        inverse = self.get(INV, p) if self.level.get((INV, p)) == n else self.first_inverse(n - 1, p)
         if n == STEPS:
-            dx, dy, dz, ex, ey, ez, eps, chi = (v[:NXL] for v in (dx, dy, dz, ex, ey, ez, eps, chi))
-        inverse = 1.0 / (eps + chi * (ex * ex + ey * ey + ez * ez))
+            dx, dy, dz, eps, chi, inverse = (v[:NXL] for v in (dx, dy, dz, eps, chi, inverse))
         squares = chi * (dx * dx + dy * dy + dz * dz)
         for _ in range(KERR - 1):
             inverse = 1.0 / (eps + squares * (inverse * inverse))
@@ -178,9 +212,9 @@
     return jnp.sum(picked, axis=0)
 
 
-def sent(grid, side, i):
-    comp, plane = side[i]
-    return grid.get(comp, plane)
+def payload(grid, side):
+    made = grid.derive() if side is HI else {}
+    return [made[k] if k in made else grid.get(*k) for k in side]
 
 
 def inner(d, e, h, eps, chi, fd, fe, fh, lo, out):
@@ -200,10 +234,10 @@
     first_core = lax.rem(gz, 2) == 0
     keep = scalar(jnp.logical_and(gz != 0, gz != last))
     half = halo_row() < XH
-    for i in range(NS):
-        v = sent(grid, HI, i)
-        if i < len(LO) and LO[i]:
-            v = jnp.where(first_core, v, sent(grid, LO, i))
+    low = payload(grid, LO)
+    for i, v in enumerate(payload(grid, HI)):
+        if i < len(LO):
+            v = jnp.where(first_core, v, low[i])
         v = v * keep
         out[24 * i : 24 * i + 8] = jnp.where(half, v[24:32], v[0:8])
         out[24 * i + 8 : 24 * i + 24] = v[8:24]
@@ -243,13 +277,12 @@
             xt[comp, p] = joined(ra[comp, p], rb[comp, p])
 
     def pack(grid, side):
-        for i, unit in enumerate(side):
-            if unit:
-                v = grid.get(*unit) * keep
-                cross[8 * i : 8 * i + 8] = v[8:16]
-                if i >= NR:
-                    at = 8 * (NS + i - NR)
-                    cross[at : at + 8] = jnp.where(half, v[16:24], v[0:8])
+        for i, v in enumerate(payload(grid, side)):
+            v = v * keep
+            cross[8 * i : 8 * i + 8] = v[8:16]
+            if i >= NR:
+                at = 8 * (NS + i - NR)
+                cross[at : at + 8] = jnp.where(half, v[16:24], v[0:8])
 
     @pl.when(lax.rem(gz, 2) == 0)
     def _():
@@ -272,17 +305,16 @@
         return rows(jnp.where(half, w[16:24], v[0:8]), v[8:24], jnp.where(half, v[24:32], w[0:8]), w[8:16])
 
     def join(sides, side):
-        grid = Grid(ROWS, None, None)
+        grid = full_grid()
         hold_own(grid, fields, xt)
         for k, (v, w, ref) in enumerate(((id_, sides[0], fd), (ie, sides[1], fe), (ih, sides[2], fh))):
-            for p in EARLY[k]:
+            for p, level in EARLY[k].items():
                 for c in range(3):
-                    grid.put(ref, (c, p), 3 * k + c, p, merged(v[c, p], w[c, p]), 1)
+                    grid.put(ref, (c, p), 3 * k + c, p, merged(v[c, p], w[c, p]), level)
         for c in range(2):
             grid.hold(H + c, 6, functools.partial(lambda a: merged(ilo[a], tlo[a]), c))
-        for i, unit in enumerate(side):
-            if unit:
-                chip[i] = grid.get(*unit)
+        for i, v in enumerate(payload(grid, side)):
+            chip[i] = v
 
     gz, _, _, _ = position()
 
@@ -360,7 +392,9 @@
     for side, at, shift in ((above, HI_AT, NZL), (below, LO_AT, -NZL)):
         if side is not None:
             for (comp, p), i in at.items():
-                level = (p + (H <= comp < EPS)) if shift > 0 else int(p == 6)
+                level = int(p == 6)
+                if comp >= DP:
+                    level = p + 2 if HP <= comp < INV else p + 1
                 grid.hold(comp, p + shift, functools.partial(side, i), level)
 
     def put(c, p, v, n):

time: 26.6 us -> 25.1 us (0.944)
  waiting for transfers between devices: 10.8 us -> 9.17 us
    ppermute x5, waiting for transfers between devices: 10.8 us -> 9.17 us  [swapped(): return lax.ppermute(shard, ('gz', 'gx'), moves)]
  transfers between devices with their start and end apart: 5 -> 5, of which waited for: 3 -> 4; matrix products, arithmetic and copies ran while one was open for 0% -> 0% of each run, Pallas kernels for 6% -> 6%
where the time goes in v7:
time: 25.1 us; the launch traced here: 24.8 us
  waiting for transfers between devices  9.17 us (37%)
  starting transfers between devices  9.08 us (36%)
  Pallas kernels  5.77 us (23%)
  between operations  0.7 us (3%)
    ppermute x5, waiting for transfers between devices, swapped(): return lax.ppermute(shard, ('gz', 'gx'), moves)  9.17 us
    ppermute x5, starting transfers between devices, swapped(): return lax.ppermute(shard, ('gz', 'gx'), moves)  9.08 us
    pallas_call x8, Pallas kernels, call(): pl.pallas_call(body, out_shape=out_shape, in_specs=[VM] * len(inputs) if...  5.77 us
  transfers between devices with their start and end apart: 5, of which 4 were waited for; matrix products, arithmetic and copies ran while one was open for 0% of the time, Pallas kernels for 6%

profile of v7, /device:TPU:111, one launch (start us, length us, event | category | flops | bytes accessed | tf_op | source)
XLA Modules:
  0.0 24.8 jit_solution(10521266288060970406)
XLA Ops:
  0.6 1.5 %shard_map.119 = (f32[3,8,32,128]{3,2,1,0:T(8,128)S(1)}, f32[3,8,32,128]{3,2,1,0:T(8,128)S(1)}, f32[3,8,32,128]{3,2,1,0:T(8,128)S(1)}, f32[8,32,128]{2,1,0:T(8,1...) custom-call(f32[3,8,32,128]{3,2,1,0:T(8,128)} %d.1, ...), custom_call_target="tpu_custom_call" | custom-call | tf_op jit(solution)/shard_map/pallas_call | solution.py:519
  2.1 0.3 %collective-permute-start = (f32[11,8,4,128]{3,2,1,0:T(4,128)S(1)}, f32[11,8,4,128]{3,2,1,0:T(4,128)S(1)}, u32[]{:S(2)}, u32[]{:S(2)}) collective-permute-start(f32[11,8,4,128]{3,2,1,0:T(4,128)S(1)} %get-tuple-element.40), channel_id=1, source_target_pairs={{0,1},{1,0},{2,3},{3,2},{4,5},{5,4},{6,7},{7,6},{8,9},{9,8},{10,11... | collective-permute-start | bytes 540680 | tf_op jit(solution)/shard_map/ppermute | solution.py:515
  2.4 2.1 %collective-permute-start.1 = (f32[11,8,4,128]{3,2,1,0:T(4,128)S(1)}, f32[11,8,4,128]{3,2,1,0:T(4,128)S(1)}, u32[]{:S(2)}, u32[]{:S(2)}) collective-permute-start(f32[11,8,4,128]{3,2,1,0:T(4,128)S(1)} %get-tuple-element.41), channel_id=1, source_target_pairs={{0,4},{1,2},{2,1},{3,7},{4,0},{5,6},{6,5},{7,3},{8,12},{9,10},{10,... | collective-permute-start | bytes 540680 | tf_op jit(solution)/shard_map/ppermute | solution.py:515
  4.5 0.5 %shard_map.122 = (f32[3,5,32,128]{3,2,1,0:T(8,128)S(1)}, f32[3,5,32,128]{3,2,1,0:T(8,128)S(1)}, f32[3,5,32,128]{3,2,1,0:T(8,128)S(1)}, f32[2,32,128]{2,1,0:T(8,128)S(1)}, f32[696,128]{1,0:T(8,128)S(1)}) custom-call(f32[3,8,32,128]{3,2,1,0:T(8,128)S(1)} %get-tuple-element.35.d, f32[3,8,32,128]{3,2,1,0:T(8,128)S(1)} %get-tuple-element.36.e, ...), custom_call_target="tpu_custom_call" | custom-call | tf_op jit(solution)/shard_map/pallas_call | solution.py:519
  5.1 2.6 %collective-permute-done.ra = f32[11,8,4,128]{3,2,1,0:T(4,128)S(1)} collective-permute-done((f32[11,8,4,128]{3,2,1,0:T(4,128)S(1)}, f32[11,8,4,128]{3,2,1,0:T(4,128)S(1)}, u32[]{:S(2)}, u32[]{:S(2)}) %collective-permute-start) | collective-permute-done | bytes 180256 | tf_op jit(solution)/shard_map/ppermute | solution.py:515
  7.7 0.8 %collective-permute-done.1.rb = f32[11,8,4,128]{3,2,1,0:T(4,128)S(1)} collective-permute-done((f32[11,8,4,128]{3,2,1,0:T(4,128)S(1)}, f32[11,8,4,128]{3,2,1,0:T(4,128)S(1)}, u32[]{:S(2)}, u32[]{:S(2)}) %collective-permute-start.1) | collective-permute-done | bytes 180256 | tf_op jit(solution)/shard_map/ppermute | solution.py:515
  8.5 0.1 shard_map.121
  8.6 0.0 copy-start
  8.6 0.5 %shard_map.123 = (f32[3,5,40,128]{3,2,1,0:T(8,128)S(1)}, f32[3,5,40,128]{3,2,1,0:T(8,128)S(1)}, f32[3,5,40,128]{3,2,1,0:T(8,128)S(1)}, f32[26,40,128]{2,1,0:T(8,128)S(1)}) custom-call(f32[3,8,32,128]{3,2,1,0:T(8,128)S(1)} %get-tuple-element.35.d, f32[3,8,32,128]{3,2,1,0:T(8,128)S(1)} %get-tuple-element.36.e, f32[3,8,32,128]{3,2,1,0:T(8,128)S(1)} %get-tuple-element.37.h, ...), custom_call_target="tpu_custom_call" | custom-call | tf_op jit(solution)/shard_map/pallas_call | solution.py:519
  9.2 1.6 %collective-permute-start.4 = (f32[26,40,128]{2,1,0:T(8,128)S(1)}, f32[26,40,128]{2,1,0:T(8,128)S(1)}, u32[]{:S(2)}, u32[]{:S(2)}) collective-permute-start(f32[26,40,128]{2,1,0:T(8,128)S(1)} %get-tuple-element.59), channel_id=1, source_target_pairs={{0,4},{1,5},{2,6},{3,7},{4,0},{5,1},{6,2},{7,3},{8,12},{9,13},{10,... | collective-permute-start | bytes 1597448 | tf_op jit(solution)/shard_map/ppermute | solution.py:515
  10.8 0.0 copy-start.1
  10.8 0.0 copy-start.2
  10.8 2.8 %collective-permute-start.2 = (f32[696,128]{1,0:T(8,128)S(1)}, f32[696,128]{1,0:T(8,128)S(1)}, u32[]{:S(2)}, u32[]{:S(2)}) collective-permute-start(f32[696,128]{1,0:T(8,128)S(1)} %get-tuple-element.57), channel_id=1, source_target_pairs={{0,1},{1,0},{2,3},{3,2},{4,8},{5,9},{6,10},{7,11},{8,4},{9,5},{10,... | collective-permute-start | bytes 1069064 | tf_op jit(solution)/shard_map/ppermute | solution.py:515
  13.6 2.3 %collective-permute-start.3 = (f32[344,128]{1,0:T(8,128)S(1)}, f32[344,128]{1,0:T(8,128)S(1)}, u32[]{:S(2)}, u32[]{:S(2)}) collective-permute-start(f32[344,128]{1,0:T(8,128)S(1)} %get-tuple-element.58), channel_id=1, source_target_pairs={{0,1},{1,0},{2,3},{3,2},{4,8},{5,9},{6,10},{7,11},{8,4},{9,5},{10,... | collective-permute-start | bytes 528392 | tf_op jit(solution)/shard_map/ppermute | solution.py:515
  15.9 0.0 copy-done
  15.9 0.0 copy-done.1
  15.9 0.0 copy-done.2
  15.9 0.1 select_reduce_fusion
  16.0 0.5 %shard_map.124 = (f32[3,7,40,128]{3,2,1,0:T(8,128)S(1)}, f32[3,7,40,128]{3,2,1,0:T(8,128)S(1)}, f32[3,7,40,128]{3,2,1,0:T(8,128)S(1)}) custom-call(f32[3,8,32,128]{3,2,1,0:T(8,128)S(1)} %get-tuple-element.35.d, f32[3,8,32,128]{3,2,1,0:T(8,128)S(1)} %get-tuple-element.36.e, f32[3,8,32,128]{3,2,1,0:T(8,128)S(1)} %get-tuple-element.37.h, ...), custom_call_target="tpu_custom_call" | custom-call | tf_op jit(solution)/shard_map/pallas_call | solution.py:519
  16.5 0.0 collective-permute-done.4.cc
  16.5 0.6 %shard_map.125 = (f32[3,8,32,128]{3,2,1,0:T(8,128)S(1)}, f32[3,8,32,128]{3,2,1,0:T(8,128)S(1)}, f32[3,8,32,128]{3,2,1,0:T(8,128)S(1)}, f32[2,32,128]{2,1,0:T(8,128)S(1)}, f32[2,32,128]{2,1,0:T(8,128)S(1)}) custom-call(f32[3,8,32,128]{3,2,1,0:T(8,128)S(1)} %get-tuple-element.35.d, f32[3,8,32,128]{3,2,1,0:T(8,128)S(1)} %get-tuple-element.36.e, ...), custom_call_target="tpu_custom_call" | custom-call | tf_op jit(solution)/shard_map/pallas_call | solution.py:519
  17.1 3.8 %collective-permute-done.2.ca = f32[696,128]{1,0:T(8,128)S(1)} collective-permute-done((f32[696,128]{1,0:T(8,128)S(1)}, f32[696,128]{1,0:T(8,128)S(1)}, u32[]{:S(2)}, u32[]{:S(2)}) %collective-permute-start.2) | collective-permute-done | bytes 356384 | tf_op jit(solution)/shard_map/ppermute | solution.py:515
  21.0 1.9 %collective-permute-done.3.cb = f32[344,128]{1,0:T(8,128)S(1)} collective-permute-done((f32[344,128]{1,0:T(8,128)S(1)}, f32[344,128]{1,0:T(8,128)S(1)}, u32[]{:S(2)}, u32[]{:S(2)}) %collective-permute-start.3) | collective-permute-done | bytes 176160 | tf_op jit(solution)/shard_map/ppermute | solution.py:515
  22.8 2.0 %shard_map.126 = (f32[3,8,32,128]{3,2,1,0:T(8,128)}, f32[3,8,32,128]{3,2,1,0:T(8,128)}, f32[3,8,32,128]{3,2,1,0:T(8,128)}, f32[8,32,128]{2,1,0:T(8,128)}, f32[8,32,128]{2,1,0:T(8,128)}) custom-call(f32[3,8,32,128]{3,2,1,0:T(8,128)S(1)} %get-tuple-element.35.d, f32[3,8,32,128]{3,2,1,0:T(8,128)S(1)} %get-tuple-element.36.e, ...), custom_call_target="tpu_custom_call" | custom-call | tf_op jit(solution)/shard_map/pallas_call | solution.py:519
  (1 shorter events, 0.0 us)
Async XLA Ops:
  2.1 5.5 %collective-permute-start = (f32[11,8,4,128]{3,2,1,0:T(4,128)S(1)}, f32[11,8,4,128]{3,2,1,0:T(4,128)S(1)}, u32[]{:S(2)}, u32[]{:S(2)}) collective-permute-start(f32[11,8,4,128]{3,2,1,0:T(4,128)S(1)} %get-tuple-element.40), channel_id=1, source_target_pairs={{0,1},{1,0},{2,3},{3,2},{4,5},{5,4},{6,7},{7,6},{8,9},{9,8},{10,11... | collective-permute-start | bytes 540680 | tf_op jit(solution)/shard_map/ppermute | solution.py:515
  2.4 6.1 %collective-permute-start.1 = (f32[11,8,4,128]{3,2,1,0:T(4,128)S(1)}, f32[11,8,4,128]{3,2,1,0:T(4,128)S(1)}, u32[]{:S(2)}, u32[]{:S(2)}) collective-permute-start(f32[11,8,4,128]{3,2,1,0:T(4,128)S(1)} %get-tuple-element.41), channel_id=1, source_target_pairs={{0,4},{1,2},{2,1},{3,7},{4,0},{5,6},{6,5},{7,3},{8,12},{9,10},{10,... | collective-permute-start | bytes 540680 | tf_op jit(solution)/shard_map/ppermute | solution.py:515
  8.6 7.3 %copy-start = (s32[2,32,128]{2,1,0:T(8,128)S(1)}, s32[2,32,128]{2,1,0:T(8,128)}, u32[]{:S(2)}) copy-start(s32[2,32,128]{2,1,0:T(8,128)} %param.13) | copy-start | bytes 98308
  9.2 7.3 %collective-permute-start.4 = (f32[26,40,128]{2,1,0:T(8,128)S(1)}, f32[26,40,128]{2,1,0:T(8,128)S(1)}, u32[]{:S(2)}, u32[]{:S(2)}) collective-permute-start(f32[26,40,128]{2,1,0:T(8,128)S(1)} %get-tuple-element.59), channel_id=1, source_target_pairs={{0,4},{1,5},{2,6},{3,7},{4,0},{5,1},{6,2},{7,3},{8,12},{9,13},{10,... | collective-permute-start | bytes 1597448 | tf_op jit(solution)/shard_map/ppermute | solution.py:515
  10.8 5.1 %copy-start.1 = (f32[8]{0:T(128)S(1)}, f32[8]{0:T(128)}, u32[]{:S(2)}) copy-start(f32[8]{0:T(128)} %param.15) | copy-start | bytes 100
  10.8 5.1 %copy-start.2 = (f32[8]{0:T(128)S(1)}, f32[8]{0:T(128)}, u32[]{:S(2)}) copy-start(f32[8]{0:T(128)} %param.14) | copy-start | bytes 100
  10.8 10.1 %collective-permute-start.2 = (f32[696,128]{1,0:T(8,128)S(1)}, f32[696,128]{1,0:T(8,128)S(1)}, u32[]{:S(2)}, u32[]{:S(2)}) collective-permute-start(f32[696,128]{1,0:T(8,128)S(1)} %get-tuple-element.57), channel_id=1, source_target_pairs={{0,1},{1,0},{2,3},{3,2},{4,8},{5,9},{6,10},{7,11},{8,4},{9,5},{10,... | collective-permute-start | bytes 1069064 | tf_op jit(solution)/shard_map/ppermute | solution.py:515
  13.6 9.2 %collective-permute-start.3 = (f32[344,128]{1,0:T(8,128)S(1)}, f32[344,128]{1,0:T(8,128)S(1)}, u32[]{:S(2)}, u32[]{:S(2)}) collective-permute-start(f32[344,128]{1,0:T(8,128)S(1)} %get-tuple-element.58), channel_id=1, source_target_pairs={{0,1},{1,0},{2,3},{3,2},{4,8},{5,9},{6,10},{7,11},{8,4},{9,5},{10,... | collective-permute-start | bytes 528392 | tf_op jit(solution)/shard_map/ppermute | solution.py:515

commit v8 on v7

--- a/solution.py
+++ b/solution.py
@@ -28,6 +28,10 @@
 HI_AT = {k: i for i, k in enumerate(HI)}
 LO_AT = {k: i for i, k in enumerate(LO)}
 NS, NR = len(HI), len(RAW)
+
+FOUR, THREE = (E, E + 1, E + 2, H + 1, H + 2), (D, D + 1, D + 2, H, EPS, CHI)
+NF = len(FOUR) * NZL * 4
+NHALO = NF + len(THREE) * NZL * 3
 
 VM = pl.BlockSpec(memory_space=pltpu.VMEM)
 HBM = pl.BlockSpec(memory_space=pltpu.HBM)
@@ -179,21 +183,35 @@
     return eps[plane] if comp == EPS else chi[plane]
 
 
-def load(d, e, h, eps, chi, dv, ev, hv, epsv, chiv, ya, yb, sems):
-    moves = [(a.at[c], b.at[c]) for a, b in ((d, dv), (e, ev), (h, hv)) for c in range(3)] + [(eps, epsv), (chi, chiv)]
-    copies = [pltpu.make_async_copy(a, b, sems.at[i]) for i, (a, b) in enumerate(moves)]
-    for c in copies:
-        c.start()
+def halo_slot(comp, p):
+    if comp in FOUR:
+        return (FOUR.index(comp) * NZL + p) * 4, 4
+    return NF + (THREE.index(comp) * NZL + p) * 3, 3
+
+
+def load(d, e, h, eps, chi, ya, yb, held, sems):
+    parts = [r.at[c] for r in (d, e, h) for c in range(3)] + [eps, chi]
+    copies = [
+        [
+            pltpu.make_async_copy(r.at[:, pl.ds(at, 8)], held.at[comp, :, pl.ds(k * 8, 8)], sems.at[comp, k])
+            for k, at in enumerate((0, NXL - 8))
+        ]
+        for comp, r in enumerate(parts)
+    ]
+    for pair in copies:
+        for c in pair:
+            c.start()
     _, gx, _, last = position()
     even = lax.rem(gx, 2) == 0
     keep = scalar(jnp.logical_and(gx != 0, gx != last))
     for comp in ALL:
-        copies[comp].wait()
+        for c in copies[comp]:
+            c.wait()
         for p in range(NZL):
-            v = own((dv, ev, hv, epsv, chiv), comp, p)
-            low, high = v[:XH], v[NXL - XH :]
-            ya[comp, p] = jnp.where(even, high, low)
-            yb[comp, p] = jnp.where(even, low, high) * keep
+            at, n = halo_slot(comp, p)
+            low, high = held[comp, p, 0:n], held[comp, p, 16 - n : 16]
+            ya[at : at + n] = jnp.where(even, high, low)
+            yb[at : at + n] = jnp.where(even, low, high) * keep
 
 
 def mark(out):
@@ -261,10 +279,15 @@
     return grid
 
 
-def joined(a, b):
+def joined(a, b, comp, p):
     _, gx, _, _ = position()
     even = lax.rem(gx, 2) == 0
-    return rows(jnp.where(even, a, b), jnp.where(even, b, a))
+    at, n = halo_slot(comp, p)
+    a, b = a[at : at + n], b[at : at + n]
+    above, below = jnp.where(even, a, b), jnp.where(even, b, a)
+    if n == 4:
+        return rows(above, below)
+    return rows(above, above[2:3], below[0:1], below)
 
 
 def edges(d, e, h, eps, chi, ra, rb, inside, xt, sd, se, sh, slo, cross):
@@ -274,7 +297,7 @@
     half = halo_row() < XH
     for comp in ALL:
         for p in range(NZL):
-            xt[comp, p] = joined(ra[comp, p], rb[comp, p])
+            xt[comp, p] = joined(ra, rb, comp, p)
 
     def pack(grid, side):
         for i, v in enumerate(payload(grid, side)):
@@ -437,28 +460,47 @@
 
 
 KEPT = NZL - ADVANCE
-LOW, HIGH = (0, 2), (2, 6)
-
-
-def near(d, e, h, eps, chi, xt, fd, fe, fh, gd, ge, gh, cc, nd, ne, nh, neps, nchi, *state):
+
+
+def run(given, above, below, coming, outs, scratch, also=()):
+    state, staged, media, sems = scratch[:3], scratch[3:6], scratch[6:8], scratch[8]
+    copies = []
+
+    def send(source, target):
+        copies.append(pltpu.make_async_copy(source, target, sems.at[len(copies)]))
+        copies[-1].start()
+
+    def done(k, o, n):
+        if k < 3:
+            send(staged[k].at[:, pl.ds(o, n)], outs[k].at[:, pl.ds(o, n)])
+        else:
+            send(media[k - 3], outs[k].at[pl.ds(o, n)])
+
+    for a, b in also:
+        send(a, b)
+    complete(*given, above, below, state, staged, media, coming, done)
+    for c in copies:
+        c.wait()
+
+
+def near(d, e, h, eps, chi, xt, fd, fe, fh, gd, ge, gh, cc, *rest):
     given = (d, e, h, eps, chi), xt, (fd, fe, fh), (gd, ge, gh)
+    outs, scratch = rest[:5], rest[5:]
+    also = [(a.at[pl.ds(ADVANCE, KEPT)], b.at[pl.ds(0, KEPT)]) for a, b in ((eps, outs[3]), (chi, outs[4]))]
     gz, _, _, _ = position()
 
-    def done(k, o, n):
-        pass
-
     @pl.when(lax.rem(gz, 2) == 0)
     def _():
-        complete(*given, lambda i: cc[i], None, state, (nd, ne, nh), (neps, nchi), None, done)
+        run(given, lambda i: cc[i], None, None, outs, scratch, also)
 
     @pl.when(lax.rem(gz, 2) == 1)
     def _():
-        complete(*given, None, lambda i: cc[i], state, (nd, ne, nh), (neps, nchi), None, done)
-
-
-def far(d, e, h, eps, chi, xt, fd, fe, fh, gd, ge, gh, ca, cb, eps_in, chi_in, nd, ne, nh, neps, nchi, *rest):
-    outs, state, staged, media, sems = rest[:5], rest[5:8], rest[8:11], rest[11:13], rest[13]
+        run(given, None, lambda i: cc[i], None, outs, scratch, also)
+
+
+def far(d, e, h, eps, chi, xt, fd, fe, fh, gd, ge, gh, ca, cb, eps_in, chi_in, *rest):
     given = (d, e, h, eps, chi), xt, (fd, fe, fh), (gd, ge, gh)
+    outs, scratch = rest[5:10], rest[10:]
     half = halo_row() < XH
     gz, _, _, _ = position()
 
@@ -467,37 +509,13 @@
         x = ca[24 * NS + 8 * i : 24 * NS + 8 * i + 8] if i < NR else cb[8 * (NS + i - NR) : 8 * (NS + i - NR) + 8]
         return rows(jnp.where(half, x, m), ca[24 * i + 8 : 24 * i + 24], jnp.where(half, m, x), cb[8 * i : 8 * i + 8])
 
-    def run(above, below, made, new_media):
-        copies = []
-
-        def send(source, target):
-            copies.append(pltpu.make_async_copy(source, target, sems.at[len(copies)]))
-            copies[-1].start()
-
-        def done(k, o, n):
-            if k < 3:
-                send(staged[k].at[:, pl.ds(o, n)], outs[k].at[:, pl.ds(o, n)])
-            else:
-                send(media[k - 3], outs[k].at[pl.ds(o, n)])
-
-        o, n = made
-        for a, b in zip((nd, ne, nh), outs):
-            send(a.at[:, pl.ds(o, n)], b.at[:, pl.ds(o, n)])
-        for a, b in zip((eps, chi), outs[3:]):
-            send(a.at[pl.ds(ADVANCE, KEPT)], b.at[pl.ds(0, KEPT)])
-        for a, b in zip(new_media, outs[3:]):
-            send(a, b.at[pl.ds(KEPT, ADVANCE)])
-        complete(*given, above, below, state, staged, media, (eps_in, chi_in), done)
-        for c in copies:
-            c.wait()
-
     @pl.when(lax.rem(gz, 2) == 0)
     def _():
-        run(None, cross, HIGH, (neps, nchi))
+        run(given, None, cross, None, outs, scratch)
 
     @pl.when(lax.rem(gz, 2) == 1)
     def _():
-        run(cross, None, LOW, ())
+        run(given, cross, None, (eps_in, chi_in), outs, scratch)
 
 
 def swapped(shard, axis, first):
@@ -529,12 +547,13 @@
 
 def on_device(d_field, e_field, h_field, permittivity, kerr_coeff, classes, eps_table, chi_table):
     field, medium = shape(3, NZL, NXL, NY), shape(NZL, NXL, NY)
-    halo = shape(11, NZL, XH, NY)
-    *fields, ya, yb = call(
+    fields = [d_field, e_field, h_field, permittivity, kerr_coeff]
+    halo = shape(NHALO, NY)
+    ya, yb = call(
         load,
-        [pltpu.with_memory_space_constraint(a, pltpu.HBM) for a in (d_field, e_field, h_field, permittivity, kerr_coeff)],
-        (field, field, field, medium, medium, halo, halo),
-        [pltpu.SemaphoreType.DMA((11,))],
+        [pltpu.with_memory_space_constraint(a, pltpu.HBM) for a in fields],
+        (halo, halo),
+        [pltpu.VMEM((11, NZL, 16, NY), jnp.float32), pltpu.SemaphoreType.DMA((11, 2))],
         specs=[HBM] * 5,
     )
     ra, rb = swapped(ya, "gx", 0), swapped(yb, "gx", 1)
@@ -561,15 +580,21 @@
     state = [pltpu.VMEM((3, 13, ROWS, NY), jnp.float32)] * 3
     given = [*fields, xt, *frames, *more]
     two = (ADVANCE, NXL, NY)
-    made = call(near, [*given, cc], (field, field, field, shape(*two), shape(*two)), state, vmem=16)
-    staged = [pltpu.VMEM(field.shape, jnp.float32)] * 3 + [pltpu.VMEM(two, jnp.float32)] * 2
+    results = (field, field, field, medium, medium)
+    scratch = state + [pltpu.VMEM(field.shape, jnp.float32)] * 3 + [pltpu.VMEM(two, jnp.float32)] * 2
+    scratch += [pltpu.SemaphoreType.DMA((32,))]
+    outs = call(near, [*given, cc], results, scratch, vmem=16, out=HBM)
+    given += [ca, cb, *coming]
+    n = len(given)
     return call(
         far,
-        [*given, ca, cb, *coming, *made],
-        (field, field, field, medium, medium),
-        [*state, *staged, pltpu.SemaphoreType.DMA((32,))],
+        [*given, *outs],
+        results,
+        scratch,
         vmem=16,
+        specs=[VM] * n + [HBM] * 5,
         out=HBM,
+        aliases={n + k: k for k in range(5)},
     )
 
 

time: 25.1 us -> 24.5 us (0.976)
  waiting for transfers between devices: 9.17 us -> 7.64 us
  Pallas kernels: 5.77 us -> 6.64 us
    ppermute x5, waiting for transfers between devices: 9.17 us -> 7.64 us  [swapped(): return lax.ppermute(shard, ('gz', 'gx'), moves)]
    pallas_call x8, Pallas kernels: 5.77 us -> 6.64 us  [call(): pl.pallas_call(body, out_shape=out_shape, in_specs=[VM] * len(inputs) if...]
  transfers between devices with their start and end apart: 5 -> 5, of which waited for: 4 -> 3; matrix products, arithmetic and copies ran while one was open for 0% -> 0% of each run, Pallas kernels for 6% -> 11%
where the time goes in v8:
time: 24.5 us; the launch traced here: 24.3 us
  starting transfers between devices  9.08 us (37%)
  waiting for transfers between devices  7.64 us (31%)
  Pallas kernels  6.64 us (27%)
  between operations  0.76 us (3%)
    ppermute x5, starting transfers between devices, swapped(): return lax.ppermute(shard, ('gz', 'gx'), moves)  9.08 us
    ppermute x5, waiting for transfers between devices, swapped(): return lax.ppermute(shard, ('gz', 'gx'), moves)  7.64 us
    pallas_call x8, Pallas kernels, call(): pl.pallas_call(body, out_shape=out_shape, in_specs=[VM] * len(inputs) if...  6.64 us
  transfers between devices with their start and end apart: 5, of which 3 were waited for; matrix products, arithmetic and copies ran while one was open for 0% of the time, Pallas kernels for 11%

profile of v8, /device:TPU:111, one launch (start us, length us, event | category | flops | bytes accessed | tf_op | source)
XLA Modules:
  0.0 24.3 jit_solution(18283818282964301513)
XLA Ops:
  0.6 0.0 copy-start.4
  0.6 0.0 copy-start.3
  0.7 0.0 copy-start.2
  0.7 0.0 copy-start.1
  0.7 0.0 copy-start
  0.7 1.4 %shard_map.119 = (f32[304,128]{1,0:T(8,128)S(1)}, f32[304,128]{1,0:T(8,128)S(1)}) custom-call(f32[3,8,32,128]{3,2,1,0:T(8,128)} %d.13, f32[3,8,32,128]{3,2,1,0:T(8,128)} %e.13, f32[3,8,32,128]{3,2,1,0:T(8,128)} %h.13, f32[8,32,128]{2,1,0:T(8,128)} %eps.13, f32[8,32,128]{2,1,0:T(8,128)} %chi.13), custom_call_target="tpu_custom_call" | custom-call | tf_op jit(solution)/shard_map/pallas_call | solution.py:537
  2.1 0.3 %collective-permute-start = (f32[304,128]{1,0:T(8,128)S(1)}, f32[304,128]{1,0:T(8,128)S(1)}, u32[]{:S(2)}, u32[]{:S(2)}) collective-permute-start(f32[304,128]{1,0:T(8,128)S(1)} %get-tuple-element.30), channel_id=1, source_target_pairs={{0,1},{1,0},{2,3},{3,2},{4,5},{5,4},{6,7},{7,6},{8,9},{9,8},{10,11... | collective-permute-start | bytes 466952 | tf_op jit(solution)/shard_map/ppermute | solution.py:533
  2.3 2.1 %collective-permute-start.1 = (f32[304,128]{1,0:T(8,128)S(1)}, f32[304,128]{1,0:T(8,128)S(1)}, u32[]{:S(2)}, u32[]{:S(2)}) collective-permute-start(f32[304,128]{1,0:T(8,128)S(1)} %get-tuple-element.31), channel_id=1, source_target_pairs={{0,4},{1,2},{2,1},{3,7},{4,0},{5,6},{6,5},{7,3},{8,12},{9,10},{10,... | collective-permute-start | bytes 466952 | tf_op jit(solution)/shard_map/ppermute | solution.py:533
  4.5 0.0 copy-done.4
  4.5 0.0 copy-done.3
  4.5 0.0 copy-done.2
  4.5 0.0 copy-done.1
  4.5 0.0 copy-done
  4.5 0.5 %shard_map.122 = (f32[3,5,32,128]{3,2,1,0:T(8,128)S(1)}, f32[3,5,32,128]{3,2,1,0:T(8,128)S(1)}, f32[3,5,32,128]{3,2,1,0:T(8,128)S(1)}, f32[2,32,128]{2,1,0:T(8,128)S(1)}, f32[696,128]{1,0:T(8,128)S(1)}) custom-call(f32[3,8,32,128]{3,2,1,0:T(8,128)S(1)} %copy-done, f32[3,8,32,128]{3,2,1,0:T(8,128)S(1)} %copy-done.1, f32[3,8,32,128]{3,2,1,0:T(8,128)S(1)} %copy-done.2, ...), custom_call_target="tpu_custom_call" | custom-call | tf_op jit(solution)/shard_map/pallas_call | solution.py:537
  5.0 2.0 %collective-permute-done.ra = f32[304,128]{1,0:T(8,128)S(1)} collective-permute-done((f32[304,128]{1,0:T(8,128)S(1)}, f32[304,128]{1,0:T(8,128)S(1)}, u32[]{:S(2)}, u32[]{:S(2)}) %collective-permute-start) | collective-permute-done | bytes 155680 | tf_op jit(solution)/shard_map/ppermute | solution.py:533
  7.1 0.8 %collective-permute-done.1.rb = f32[304,128]{1,0:T(8,128)S(1)} collective-permute-done((f32[304,128]{1,0:T(8,128)S(1)}, f32[304,128]{1,0:T(8,128)S(1)}, u32[]{:S(2)}, u32[]{:S(2)}) %collective-permute-start.1) | collective-permute-done | bytes 155680 | tf_op jit(solution)/shard_map/ppermute | solution.py:533
  7.9 0.2 shard_map.121
  8.0 0.0 copy-start.5
  8.1 0.5 %shard_map.123 = (f32[3,5,40,128]{3,2,1,0:T(8,128)S(1)}, f32[3,5,40,128]{3,2,1,0:T(8,128)S(1)}, f32[3,5,40,128]{3,2,1,0:T(8,128)S(1)}, f32[26,40,128]{2,1,0:T(8,128)S(1)}) custom-call(f32[3,8,32,128]{3,2,1,0:T(8,128)S(1)} %copy-done, f32[3,8,32,128]{3,2,1,0:T(8,128)S(1)} %copy-done.1, f32[3,8,32,128]{3,2,1,0:T(8,128)S(1)} %copy-done.2, ...), custom_call_target="tpu_custom_call" | custom-call | tf_op jit(solution)/shard_map/pallas_call | solution.py:537
  8.6 1.6 %collective-permute-start.4 = (f32[26,40,128]{2,1,0:T(8,128)S(1)}, f32[26,40,128]{2,1,0:T(8,128)S(1)}, u32[]{:S(2)}, u32[]{:S(2)}) collective-permute-start(f32[26,40,128]{2,1,0:T(8,128)S(1)} %get-tuple-element.49), channel_id=1, source_target_pairs={{0,4},{1,5},{2,6},{3,7},{4,0},{5,1},{6,2},{7,3},{8,12},{9,13},{10,... | collective-permute-start | bytes 1597448 | tf_op jit(solution)/shard_map/ppermute | solution.py:533
  10.2 2.8 %collective-permute-start.2 = (f32[696,128]{1,0:T(8,128)S(1)}, f32[696,128]{1,0:T(8,128)S(1)}, u32[]{:S(2)}, u32[]{:S(2)}) collective-permute-start(f32[696,128]{1,0:T(8,128)S(1)} %get-tuple-element.47), channel_id=1, source_target_pairs={{0,1},{1,0},{2,3},{3,2},{4,8},{5,9},{6,10},{7,11},{8,4},{9,5},{10,... | collective-permute-start | bytes 1069064 | tf_op jit(solution)/shard_map/ppermute | solution.py:533
  13.0 2.3 %collective-permute-start.3 = (f32[344,128]{1,0:T(8,128)S(1)}, f32[344,128]{1,0:T(8,128)S(1)}, u32[]{:S(2)}, u32[]{:S(2)}) collective-permute-start(f32[344,128]{1,0:T(8,128)S(1)} %get-tuple-element.48), channel_id=1, source_target_pairs={{0,1},{1,0},{2,3},{3,2},{4,8},{5,9},{6,10},{7,11},{8,4},{9,5},{10,... | collective-permute-start | bytes 528392 | tf_op jit(solution)/shard_map/ppermute | solution.py:533
  15.3 0.0 copy-done.5
  15.3 0.0 copy-done.6
  15.3 0.0 copy-done.7
  15.3 0.1 select_reduce_fusion
  15.4 0.5 %shard_map.124 = (f32[3,7,40,128]{3,2,1,0:T(8,128)S(1)}, f32[3,7,40,128]{3,2,1,0:T(8,128)S(1)}, f32[3,7,40,128]{3,2,1,0:T(8,128)S(1)}) custom-call(f32[3,8,32,128]{3,2,1,0:T(8,128)S(1)} %copy-done, f32[3,8,32,128]{3,2,1,0:T(8,128)S(1)} %copy-done.1, f32[3,8,32,128]{3,2,1,0:T(8,128)S(1)} %copy-done.2, f32[8,32,128]{2,1,0:T(8,128)S(1)} %copy-done.3, ...), custom_call_target="tpu_custom_call" | custom-call | tf_op jit(solution)/shard_map/pallas_call | solution.py:537
  15.9 0.0 collective-permute-done.4.cc
  15.9 1.5 %shard_map.125 = (f32[3,8,32,128]{3,2,1,0:T(8,128)}, f32[3,8,32,128]{3,2,1,0:T(8,128)}, f32[3,8,32,128]{3,2,1,0:T(8,128)}, f32[8,32,128]{2,1,0:T(8,128)}, f32[8,32,128]{2,1,0:T(8,128)}) custom-call(f32[3,8,32,128]{3,2,1,0:T(8,128)S(1)} %copy-done, f32[3,8,32,128]{3,2,1,0:T(8,128)S(1)} %copy-done.1, f32[3,8,32,128]{3,2,1,0:T(8,128)S(1)} %copy-done.2, ...), custom_call_target="tpu_custom_call" | custom-call | tf_op jit(solution)/shard_map/pallas_call | solution.py:537
  17.5 4.8 %collective-permute-done.3.cb = f32[344,128]{1,0:T(8,128)S(1)} collective-permute-done((f32[344,128]{1,0:T(8,128)S(1)}, f32[344,128]{1,0:T(8,128)S(1)}, u32[]{:S(2)}, u32[]{:S(2)}) %collective-permute-start.3) | collective-permute-done | bytes 176160 | tf_op jit(solution)/shard_map/ppermute | solution.py:533
  22.3 0.0 collective-permute-done.2.ca
  22.3 2.0 %shard_map.126 = (f32[3,8,32,128]{3,2,1,0:T(8,128)}, f32[3,8,32,128]{3,2,1,0:T(8,128)}, f32[3,8,32,128]{3,2,1,0:T(8,128)}, f32[8,32,128]{2,1,0:T(8,128)}, f32[8,32,128]{2,1,0:T(8,128)}) custom-call(f32[3,8,32,128]{3,2,1,0:T(8,128)S(1)} %copy-done, ...), custom_call_target="tpu_custom_call", output_to_operand_aliasing={{0}: (16, {}), {1}: (17, {}), {2}: (18, {}), {3}: (19, {}),... | custom-call | tf_op jit(solution)/shard_map/pallas_call | solution.py:537
  (3 shorter events, 0.0 us)
Async XLA Ops:
  0.6 3.8 %copy-start.4 = (f32[8,32,128]{2,1,0:T(8,128)S(1)}, f32[8,32,128]{2,1,0:T(8,128)}, u32[]{:S(2)}) copy-start(f32[8,32,128]{2,1,0:T(8,128)} %chi.13) | copy-start | bytes 393220
  0.6 3.8 %copy-start.3 = (f32[8,32,128]{2,1,0:T(8,128)S(1)}, f32[8,32,128]{2,1,0:T(8,128)}, u32[]{:S(2)}) copy-start(f32[8,32,128]{2,1,0:T(8,128)} %eps.13) | copy-start | bytes 393220
  0.7 3.8 %copy-start.2 = (f32[3,8,32,128]{3,2,1,0:T(8,128)S(1)}, f32[3,8,32,128]{3,2,1,0:T(8,128)}, u32[]{:S(2)}) copy-start(f32[3,8,32,128]{3,2,1,0:T(8,128)} %h.13) | copy-start | bytes 1179652
  0.7 3.8 %copy-start.1 = (f32[3,8,32,128]{3,2,1,0:T(8,128)S(1)}, f32[3,8,32,128]{3,2,1,0:T(8,128)}, u32[]{:S(2)}) copy-start(f32[3,8,32,128]{3,2,1,0:T(8,128)} %e.13) | copy-start | bytes 1179652
  0.7 3.8 %copy-start = (f32[3,8,32,128]{3,2,1,0:T(8,128)S(1)}, f32[3,8,32,128]{3,2,1,0:T(8,128)}, u32[]{:S(2)}) copy-start(f32[3,8,32,128]{3,2,1,0:T(8,128)} %d.13) | copy-start | bytes 1179652
  2.1 5.0 %collective-permute-start = (f32[304,128]{1,0:T(8,128)S(1)}, f32[304,128]{1,0:T(8,128)S(1)}, u32[]{:S(2)}, u32[]{:S(2)}) collective-permute-start(f32[304,128]{1,0:T(8,128)S(1)} %get-tuple-element.30), channel_id=1, source_target_pairs={{0,1},{1,0},{2,3},{3,2},{4,5},{5,4},{6,7},{7,6},{8,9},{9,8},{10,11... | collective-permute-start | bytes 466952 | tf_op jit(solution)/shard_map/ppermute | solution.py:533
  2.3 5.6 %collective-permute-start.1 = (f32[304,128]{1,0:T(8,128)S(1)}, f32[304,128]{1,0:T(8,128)S(1)}, u32[]{:S(2)}, u32[]{:S(2)}) collective-permute-start(f32[304,128]{1,0:T(8,128)S(1)} %get-tuple-element.31), channel_id=1, source_target_pairs={{0,4},{1,2},{2,1},{3,7},{4,0},{5,6},{6,5},{7,3},{8,12},{9,10},{10,... | collective-permute-start | bytes 466952 | tf_op jit(solution)/shard_map/ppermute | solution.py:533
  8.0 7.3 %copy-start.5 = (s32[2,32,128]{2,1,0:T(8,128)S(1)}, s32[2,32,128]{2,1,0:T(8,128)}, u32[]{:S(2)}) copy-start(s32[2,32,128]{2,1,0:T(8,128)} %param.13) | copy-start | bytes 98308
  8.6 7.3 %collective-permute-start.4 = (f32[26,40,128]{2,1,0:T(8,128)S(1)}, f32[26,40,128]{2,1,0:T(8,128)S(1)}, u32[]{:S(2)}, u32[]{:S(2)}) collective-permute-start(f32[26,40,128]{2,1,0:T(8,128)S(1)} %get-tuple-element.49), channel_id=1, source_target_pairs={{0,4},{1,5},{2,6},{3,7},{4,0},{5,1},{6,2},{7,3},{8,12},{9,13},{10,... | collective-permute-start | bytes 1597448 | tf_op jit(solution)/shard_map/ppermute | solution.py:533
  10.2 5.1 %copy-start.6 = (f32[8]{0:T(128)S(1)}, f32[8]{0:T(128)}, u32[]{:S(2)}) copy-start(f32[8]{0:T(128)} %param.15) | copy-start | bytes 100
  10.2 5.1 %copy-start.7 = (f32[8]{0:T(128)S(1)}, f32[8]{0:T(128)}, u32[]{:S(2)}) copy-start(f32[8]{0:T(128)} %param.14) | copy-start | bytes 100
  10.2 12.0 %collective-permute-start.2 = (f32[696,128]{1,0:T(8,128)S(1)}, f32[696,128]{1,0:T(8,128)S(1)}, u32[]{:S(2)}, u32[]{:S(2)}) collective-permute-start(f32[696,128]{1,0:T(8,128)S(1)} %get-tuple-element.47), channel_id=1, source_target_pairs={{0,1},{1,0},{2,3},{3,2},{4,8},{5,9},{6,10},{7,11},{8,4},{9,5},{10,... | collective-permute-start | bytes 1069064 | tf_op jit(solution)/shard_map/ppermute | solution.py:533
  13.0 9.2 %collective-permute-start.3 = (f32[344,128]{1,0:T(8,128)S(1)}, f32[344,128]{1,0:T(8,128)S(1)}, u32[]{:S(2)}, u32[]{:S(2)}) collective-permute-start(f32[344,128]{1,0:T(8,128)S(1)} %get-tuple-element.48), channel_id=1, source_target_pairs={{0,1},{1,0},{2,3},{3,2},{4,8},{5,9},{6,10},{7,11},{8,4},{9,5},{10,... | collective-permute-start | bytes 528392 | tf_op jit(solution)/shard_map/ppermute | solution.py:533

commit v9 on v8

--- a/solution.py
+++ b/solution.py
@@ -24,10 +24,31 @@
 RAW = [(E + c, 0) for c in range(3)] + [(c, p) for p in range(3) for c in (EPS, CHI)]
 HI = RAW + [(DP + c, p) for p in range(3) for c in range(3)] + [(HP + c, p) for p in range(2) for c in range(3)]
 HI += [(INV, 1), (INV, 2)]
-LO = [(c, 7) for c in ALL] + [(H, 6), (H + 1, 6)]
+HI_ROWS = {8: range(8), 6: (0, 1, 2, 5, 6, 7), 4: (0, 1, 6, 7), 2: (0, 7)}
+LO_ROWS = {8: range(8), 6: (0, 1, 2, 3, 6, 7), 4: (0, 1, 2, 7), 2: ()}
+
+
+def slot_rows(comp, p):
+    if (comp, p) == (E, 0):
+        return 8
+    level = p + (HP <= comp < INV)
+    return 6 - 2 * p if comp < HP or comp >= INV else 6 - 2 * (level - 1)
+
+
+WIDTH = [slot_rows(*k) for k in HI]
+HALO_AT = [sum(WIDTH[:i]) for i in range(len(HI))]
+LO = [None] * len(HI)
+_wide = [i for i, n in enumerate(WIDTH) if n >= 6]
+_thin = [i for i, n in enumerate(WIDTH) if n == 4]
+for _k in [(E + c, 7) for c in range(3)] + [(H + c, 7) for c in range(3)]:
+    LO[_wide.pop(0)] = _k
+for _k in [(D + c, 7) for c in range(3)] + [(EPS, 7), (CHI, 7), (H, 6), (H + 1, 6)]:
+    LO[_thin.pop(0)] = _k
 HI_AT = {k: i for i, k in enumerate(HI)}
-LO_AT = {k: i for i, k in enumerate(LO)}
+LO_AT = {k: i for i, k in enumerate(LO) if k}
 NS, NR = len(HI), len(RAW)
+NEW_AT = -(-sum(WIDTH) // 8) * 8
+LATE = NEW_AT + 8 * (NS - NR)
 
 FOUR, THREE = (E, E + 1, E + 2, H + 1, H + 2), (D, D + 1, D + 2, H, EPS, CHI)
 NF = len(FOUR) * NZL * 4
@@ -232,7 +253,7 @@
 
 def payload(grid, side):
     made = grid.derive() if side is HI else {}
-    return [made[k] if k in made else grid.get(*k) for k in side]
+    return [k and (made[k] if k in made else grid.get(*k)) for k in side]
 
 
 def inner(d, e, h, eps, chi, fd, fe, fh, lo, out):
@@ -254,7 +275,7 @@
     half = halo_row() < XH
     low = payload(grid, LO)
     for i, v in enumerate(payload(grid, HI)):
-        if i < len(LO):
+        if low[i] is not None:
             v = jnp.where(first_core, v, low[i])
         v = v * keep
         out[24 * i : 24 * i + 8] = jnp.where(half, v[24:32], v[0:8])
@@ -299,25 +320,36 @@
         for p in range(NZL):
             xt[comp, p] = joined(ra, rb, comp, p)
 
-    def pack(grid, side):
+    def pack(grid, side, chosen):
         for i, v in enumerate(payload(grid, side)):
+            if v is None:
+                continue
             v = v * keep
-            cross[8 * i : 8 * i + 8] = v[8:16]
+            at, n = HALO_AT[i], WIDTH[i]
+            runs = []
+            for r in chosen[n]:
+                if runs and runs[-1][1] == r:
+                    runs[-1][1] = r + 1
+                else:
+                    runs.append([r, r + 1])
+            for a, b in runs:
+                cross[at : at + b - a] = v[8 + a : 8 + b]
+                at += b - a
             if i >= NR:
-                at = 8 * (NS + i - NR)
+                at = NEW_AT + 8 * (i - NR)
                 cross[at : at + 8] = jnp.where(half, v[16:24], v[0:8])
 
     @pl.when(lax.rem(gz, 2) == 0)
     def _():
         grid = edge_grid(inside[...], fields, lambda comp, p: xt[comp, p])
         early(grid, lambda c, p, v, n: grid.put((sd, se, sh)[c // 3], (c % 3, p), c, p, v, n))
-        pack(grid, HI)
+        pack(grid, HI, HI_ROWS)
 
     @pl.when(lax.rem(gz, 2) == 1)
     def _():
         grid = edge_grid(inside[...], fields, lambda comp, p: xt[comp, p])
         grid.step_h(1, 6, range(2), lambda c, p, v, n: grid.put(slo, c - H, c, p, v, n))
-        pack(grid, LO)
+        pack(grid, LO, LO_ROWS)
 
 
 def merge(d, e, h, eps, chi, id_, ie, ih, ilo, xt, sd, se, sh, slo, inside, fd, fe, fh, chip, td, te, th, tlo):
@@ -337,7 +369,8 @@
         for c in range(2):
             grid.hold(H + c, 6, functools.partial(lambda a: merged(ilo[a], tlo[a]), c))
         for i, v in enumerate(payload(grid, side)):
-            chip[i] = v
+            if v is not None:
+                chip[i] = v
 
     gz, _, _, _ = position()
 
@@ -504,18 +537,23 @@
     half = halo_row() < XH
     gz, _, _, _ = position()
 
-    def cross(i):
+    def cross(chosen, i):
         m = ca[24 * i : 24 * i + 8]
-        x = ca[24 * NS + 8 * i : 24 * NS + 8 * i + 8] if i < NR else cb[8 * (NS + i - NR) : 8 * (NS + i - NR) + 8]
-        return rows(jnp.where(half, x, m), ca[24 * i + 8 : 24 * i + 24], jnp.where(half, m, x), cb[8 * i : 8 * i + 8])
+        x = ca[24 * NS + 8 * i : 24 * NS + 8 * i + 8] if i < NR else cb[NEW_AT + 8 * (i - NR) : NEW_AT + 8 * (i - NR) + 8]
+        at, kept = HALO_AT[i], list(chosen[WIDTH[i]])
+        v = cb[at : at + WIDTH[i]]
+        if len(kept) < 8:
+            near_row = [max([k for k in kept if k <= r], default=kept[0]) for r in range(8)]
+            v = rows(*[v[kept.index(k) : kept.index(k) + 1] for k in near_row])
+        return rows(jnp.where(half, x, m), ca[24 * i + 8 : 24 * i + 24], jnp.where(half, m, x), v)
 
     @pl.when(lax.rem(gz, 2) == 0)
     def _():
-        run(given, None, cross, None, outs, scratch)
+        run(given, None, functools.partial(cross, LO_ROWS), None, outs, scratch)
 
     @pl.when(lax.rem(gz, 2) == 1)
     def _():
-        run(given, cross, None, (eps_in, chi_in), outs, scratch)
+        run(given, functools.partial(cross, HI_ROWS), None, (eps_in, chi_in), outs, scratch)
 
 
 def swapped(shard, axis, first):
@@ -563,9 +601,7 @@
     (edge,) = call(mark, [], (shape(8, NY),))
     thin = [(3, 5, EDGE, NY)] * 3 + [(2, EDGE, NY)]
     xt, *outside, zb = call(
-        edges,
-        [*fields, ra, rb, edge],
-        (shape(11, NZL, 8, NY), *[shape(*t) for t in thin], shape(8 * (NS + NS - NR), NY)),
+        edges, [*fields, ra, rb, edge], (shape(11, NZL, 8, NY), *[shape(*t) for t in thin], shape(LATE, NY))
     )
     cb = swapped(zb, "gz", 1)
     coming = lookup(classes, eps_table), lookup(classes, chi_table)

time: 24.5 us -> 24.1 us (0.984)
  waiting for transfers between devices: 7.64 us -> 7.16 us
    ppermute x5, waiting for transfers between devices: 7.64 us -> 7.16 us  [swapped(): return lax.ppermute(shard, ('gz', 'gx'), moves)]
where the time goes in v9:
time: 24.1 us; the launch traced here: 23.8 us
  starting transfers between devices  9.1 us (38%)
  waiting for transfers between devices  7.16 us (30%)
  Pallas kernels  6.64 us (28%)
  between operations  0.75 us (3%)
    ppermute x5, starting transfers between devices, swapped(): return lax.ppermute(shard, ('gz', 'gx'), moves)  9.1 us
    ppermute x5, waiting for transfers between devices, swapped(): return lax.ppermute(shard, ('gz', 'gx'), moves)  7.16 us
    pallas_call x8, Pallas kernels, call(): pl.pallas_call(body, out_shape=out_shape, in_specs=[VM] * len(inputs) if...  6.64 us
  transfers between devices with their start and end apart: 5, of which 3 were waited for; matrix products, arithmetic and copies ran while one was open for 0% of the time, Pallas kernels for 11%

profile of v9, /device:TPU:111, one launch (start us, length us, event | category | flops | bytes accessed | tf_op | source)
XLA Modules:
  0.0 23.8 jit_solution(5218546269698172340)
XLA Ops:
  0.6 0.0 copy-start.4
  0.6 0.0 copy-start.3
  0.7 0.0 copy-start.2
  0.7 0.0 copy-start.1
  0.7 0.0 copy-start
  0.7 1.4 %shard_map.119 = (f32[304,128]{1,0:T(8,128)S(1)}, f32[304,128]{1,0:T(8,128)S(1)}) custom-call(f32[3,8,32,128]{3,2,1,0:T(8,128)} %d.13, f32[3,8,32,128]{3,2,1,0:T(8,128)} %e.13, f32[3,8,32,128]{3,2,1,0:T(8,128)} %h.13, f32[8,32,128]{2,1,0:T(8,128)} %eps.13, f32[8,32,128]{2,1,0:T(8,128)} %chi.13), custom_call_target="tpu_custom_call" | custom-call | tf_op jit(solution)/shard_map/pallas_call | solution.py:575
  2.1 0.3 %collective-permute-start = (f32[304,128]{1,0:T(8,128)S(1)}, f32[304,128]{1,0:T(8,128)S(1)}, u32[]{:S(2)}, u32[]{:S(2)}) collective-permute-start(f32[304,128]{1,0:T(8,128)S(1)} %get-tuple-element.30), channel_id=1, source_target_pairs={{0,1},{1,0},{2,3},{3,2},{4,5},{5,4},{6,7},{7,6},{8,9},{9,8},{10,11... | collective-permute-start | bytes 466952 | tf_op jit(solution)/shard_map/ppermute | solution.py:571
  2.3 2.1 %collective-permute-start.1 = (f32[304,128]{1,0:T(8,128)S(1)}, f32[304,128]{1,0:T(8,128)S(1)}, u32[]{:S(2)}, u32[]{:S(2)}) collective-permute-start(f32[304,128]{1,0:T(8,128)S(1)} %get-tuple-element.31), channel_id=1, source_target_pairs={{0,4},{1,2},{2,1},{3,7},{4,0},{5,6},{6,5},{7,3},{8,12},{9,10},{10,... | collective-permute-start | bytes 466952 | tf_op jit(solution)/shard_map/ppermute | solution.py:571
  4.5 0.0 copy-done.4
  4.5 0.0 copy-done.3
  4.5 0.0 copy-done.2
  4.5 0.0 copy-done.1
  4.5 0.0 copy-done
  4.5 0.5 %shard_map.122 = (f32[3,5,32,128]{3,2,1,0:T(8,128)S(1)}, f32[3,5,32,128]{3,2,1,0:T(8,128)S(1)}, f32[3,5,32,128]{3,2,1,0:T(8,128)S(1)}, f32[2,32,128]{2,1,0:T(8,128)S(1)}, f32[696,128]{1,0:T(8,128)S(1)}) custom-call(f32[3,8,32,128]{3,2,1,0:T(8,128)S(1)} %copy-done, f32[3,8,32,128]{3,2,1,0:T(8,128)S(1)} %copy-done.1, f32[3,8,32,128]{3,2,1,0:T(8,128)S(1)} %copy-done.2, ...), custom_call_target="tpu_custom_call" | custom-call | tf_op jit(solution)/shard_map/pallas_call | solution.py:575
  5.0 2.0 %collective-permute-done.ra = f32[304,128]{1,0:T(8,128)S(1)} collective-permute-done((f32[304,128]{1,0:T(8,128)S(1)}, f32[304,128]{1,0:T(8,128)S(1)}, u32[]{:S(2)}, u32[]{:S(2)}) %collective-permute-start) | collective-permute-done | bytes 155680 | tf_op jit(solution)/shard_map/ppermute | solution.py:571
  7.1 0.8 %collective-permute-done.1.rb = f32[304,128]{1,0:T(8,128)S(1)} collective-permute-done((f32[304,128]{1,0:T(8,128)S(1)}, f32[304,128]{1,0:T(8,128)S(1)}, u32[]{:S(2)}, u32[]{:S(2)}) %collective-permute-start.1) | collective-permute-done | bytes 155680 | tf_op jit(solution)/shard_map/ppermute | solution.py:571
  7.9 0.2 shard_map.121
  8.0 0.0 copy-start.5
  8.1 0.5 %shard_map.123 = (f32[3,5,40,128]{3,2,1,0:T(8,128)S(1)}, f32[3,5,40,128]{3,2,1,0:T(8,128)S(1)}, f32[3,5,40,128]{3,2,1,0:T(8,128)S(1)}, f32[26,40,128]{2,1,0:T(8,128)S(1)}) custom-call(f32[3,8,32,128]{3,2,1,0:T(8,128)S(1)} %copy-done, f32[3,8,32,128]{3,2,1,0:T(8,128)S(1)} %copy-done.1, f32[3,8,32,128]{3,2,1,0:T(8,128)S(1)} %copy-done.2, ...), custom_call_target="tpu_custom_call" | custom-call | tf_op jit(solution)/shard_map/pallas_call | solution.py:575
  8.6 1.7 %collective-permute-start.4 = (f32[26,40,128]{2,1,0:T(8,128)S(1)}, f32[26,40,128]{2,1,0:T(8,128)S(1)}, u32[]{:S(2)}, u32[]{:S(2)}) collective-permute-start(f32[26,40,128]{2,1,0:T(8,128)S(1)} %get-tuple-element.49), channel_id=1, source_target_pairs={{0,4},{1,5},{2,6},{3,7},{4,0},{5,1},{6,2},{7,3},{8,12},{9,13},{10,... | collective-permute-start | bytes 1597448 | tf_op jit(solution)/shard_map/ppermute | solution.py:571
  10.2 2.8 %collective-permute-start.2 = (f32[696,128]{1,0:T(8,128)S(1)}, f32[696,128]{1,0:T(8,128)S(1)}, u32[]{:S(2)}, u32[]{:S(2)}) collective-permute-start(f32[696,128]{1,0:T(8,128)S(1)} %get-tuple-element.47), channel_id=1, source_target_pairs={{0,1},{1,0},{2,3},{3,2},{4,8},{5,9},{6,10},{7,11},{8,4},{9,5},{10,... | collective-permute-start | bytes 1069064 | tf_op jit(solution)/shard_map/ppermute | solution.py:571
  13.0 2.3 %collective-permute-start.3 = (f32[256,128]{1,0:T(8,128)S(1)}, f32[256,128]{1,0:T(8,128)S(1)}, u32[]{:S(2)}, u32[]{:S(2)}) collective-permute-start(f32[256,128]{1,0:T(8,128)S(1)} %get-tuple-element.48), channel_id=1, source_target_pairs={{0,1},{1,0},{2,3},{3,2},{4,8},{5,9},{6,10},{7,11},{8,4},{9,5},{10,... | collective-permute-start | bytes 393224 | tf_op jit(solution)/shard_map/ppermute | solution.py:571
  15.3 0.0 copy-done.5
  15.3 0.0 copy-done.6
  15.3 0.0 copy-done.7
  15.3 0.1 select_reduce_fusion
  15.4 0.5 %shard_map.124 = (f32[3,7,40,128]{3,2,1,0:T(8,128)S(1)}, f32[3,7,40,128]{3,2,1,0:T(8,128)S(1)}, f32[3,7,40,128]{3,2,1,0:T(8,128)S(1)}) custom-call(f32[3,8,32,128]{3,2,1,0:T(8,128)S(1)} %copy-done, f32[3,8,32,128]{3,2,1,0:T(8,128)S(1)} %copy-done.1, f32[3,8,32,128]{3,2,1,0:T(8,128)S(1)} %copy-done.2, f32[8,32,128]{2,1,0:T(8,128)S(1)} %copy-done.3, ...), custom_call_target="tpu_custom_call" | custom-call | tf_op jit(solution)/shard_map/pallas_call | solution.py:575
  15.9 0.0 collective-permute-done.4.cc
  16.0 1.5 %shard_map.125 = (f32[3,8,32,128]{3,2,1,0:T(8,128)}, f32[3,8,32,128]{3,2,1,0:T(8,128)}, f32[3,8,32,128]{3,2,1,0:T(8,128)}, f32[8,32,128]{2,1,0:T(8,128)}, f32[8,32,128]{2,1,0:T(8,128)}) custom-call(f32[3,8,32,128]{3,2,1,0:T(8,128)S(1)} %copy-done, f32[3,8,32,128]{3,2,1,0:T(8,128)S(1)} %copy-done.1, f32[3,8,32,128]{3,2,1,0:T(8,128)S(1)} %copy-done.2, ...), custom_call_target="tpu_custom_call" | custom-call | tf_op jit(solution)/shard_map/pallas_call | solution.py:575
  17.5 4.3 %collective-permute-done.3.cb = f32[256,128]{1,0:T(8,128)S(1)} collective-permute-done((f32[256,128]{1,0:T(8,128)S(1)}, f32[256,128]{1,0:T(8,128)S(1)}, u32[]{:S(2)}, u32[]{:S(2)}) %collective-permute-start.3) | collective-permute-done | bytes 131104 | tf_op jit(solution)/shard_map/ppermute | solution.py:571
  21.8 0.0 collective-permute-done.2.ca
  21.8 2.0 %shard_map.126 = (f32[3,8,32,128]{3,2,1,0:T(8,128)}, f32[3,8,32,128]{3,2,1,0:T(8,128)}, f32[3,8,32,128]{3,2,1,0:T(8,128)}, f32[8,32,128]{2,1,0:T(8,128)}, f32[8,32,128]{2,1,0:T(8,128)}) custom-call(f32[3,8,32,128]{3,2,1,0:T(8,128)S(1)} %copy-done, ...), custom_call_target="tpu_custom_call", output_to_operand_aliasing={{0}: (16, {}), {1}: (17, {}), {2}: (18, {}), {3}: (19, {}),... | custom-call | tf_op jit(solution)/shard_map/pallas_call | solution.py:575
  (3 shorter events, 0.0 us)
Async XLA Ops:
  0.6 3.8 %copy-start.4 = (f32[8,32,128]{2,1,0:T(8,128)S(1)}, f32[8,32,128]{2,1,0:T(8,128)}, u32[]{:S(2)}) copy-start(f32[8,32,128]{2,1,0:T(8,128)} %chi.13) | copy-start | bytes 393220
  0.6 3.8 %copy-start.3 = (f32[8,32,128]{2,1,0:T(8,128)S(1)}, f32[8,32,128]{2,1,0:T(8,128)}, u32[]{:S(2)}) copy-start(f32[8,32,128]{2,1,0:T(8,128)} %eps.13) | copy-start | bytes 393220
  0.7 3.8 %copy-start.2 = (f32[3,8,32,128]{3,2,1,0:T(8,128)S(1)}, f32[3,8,32,128]{3,2,1,0:T(8,128)}, u32[]{:S(2)}) copy-start(f32[3,8,32,128]{3,2,1,0:T(8,128)} %h.13) | copy-start | bytes 1179652
  0.7 3.8 %copy-start.1 = (f32[3,8,32,128]{3,2,1,0:T(8,128)S(1)}, f32[3,8,32,128]{3,2,1,0:T(8,128)}, u32[]{:S(2)}) copy-start(f32[3,8,32,128]{3,2,1,0:T(8,128)} %e.13) | copy-start | bytes 1179652
  0.7 3.8 %copy-start = (f32[3,8,32,128]{3,2,1,0:T(8,128)S(1)}, f32[3,8,32,128]{3,2,1,0:T(8,128)}, u32[]{:S(2)}) copy-start(f32[3,8,32,128]{3,2,1,0:T(8,128)} %d.13) | copy-start | bytes 1179652
  2.1 5.0 %collective-permute-start = (f32[304,128]{1,0:T(8,128)S(1)}, f32[304,128]{1,0:T(8,128)S(1)}, u32[]{:S(2)}, u32[]{:S(2)}) collective-permute-start(f32[304,128]{1,0:T(8,128)S(1)} %get-tuple-element.30), channel_id=1, source_target_pairs={{0,1},{1,0},{2,3},{3,2},{4,5},{5,4},{6,7},{7,6},{8,9},{9,8},{10,11... | collective-permute-start | bytes 466952 | tf_op jit(solution)/shard_map/ppermute | solution.py:571
  2.3 5.6 %collective-permute-start.1 = (f32[304,128]{1,0:T(8,128)S(1)}, f32[304,128]{1,0:T(8,128)S(1)}, u32[]{:S(2)}, u32[]{:S(2)}) collective-permute-start(f32[304,128]{1,0:T(8,128)S(1)} %get-tuple-element.31), channel_id=1, source_target_pairs={{0,4},{1,2},{2,1},{3,7},{4,0},{5,6},{6,5},{7,3},{8,12},{9,10},{10,... | collective-permute-start | bytes 466952 | tf_op jit(solution)/shard_map/ppermute | solution.py:571
  8.0 7.3 %copy-start.5 = (s32[2,32,128]{2,1,0:T(8,128)S(1)}, s32[2,32,128]{2,1,0:T(8,128)}, u32[]{:S(2)}) copy-start(s32[2,32,128]{2,1,0:T(8,128)} %param.13) | copy-start | bytes 98308
  8.6 7.4 %collective-permute-start.4 = (f32[26,40,128]{2,1,0:T(8,128)S(1)}, f32[26,40,128]{2,1,0:T(8,128)S(1)}, u32[]{:S(2)}, u32[]{:S(2)}) collective-permute-start(f32[26,40,128]{2,1,0:T(8,128)S(1)} %get-tuple-element.49), channel_id=1, source_target_pairs={{0,4},{1,5},{2,6},{3,7},{4,0},{5,1},{6,2},{7,3},{8,12},{9,13},{10,... | collective-permute-start | bytes 1597448 | tf_op jit(solution)/shard_map/ppermute | solution.py:571
  10.2 5.1 %copy-start.6 = (f32[8]{0:T(128)S(1)}, f32[8]{0:T(128)}, u32[]{:S(2)}) copy-start(f32[8]{0:T(128)} %param.15) | copy-start | bytes 100
  10.2 5.1 %copy-start.7 = (f32[8]{0:T(128)S(1)}, f32[8]{0:T(128)}, u32[]{:S(2)}) copy-start(f32[8]{0:T(128)} %param.14) | copy-start | bytes 100
  10.2 11.5 %collective-permute-start.2 = (f32[696,128]{1,0:T(8,128)S(1)}, f32[696,128]{1,0:T(8,128)S(1)}, u32[]{:S(2)}, u32[]{:S(2)}) collective-permute-start(f32[696,128]{1,0:T(8,128)S(1)} %get-tuple-element.47), channel_id=1, source_target_pairs={{0,1},{1,0},{2,3},{3,2},{4,8},{5,9},{6,10},{7,11},{8,4},{9,5},{10,... | collective-permute-start | bytes 1069064 | tf_op jit(solution)/shard_map/ppermute | solution.py:571
  13.0 8.8 %collective-permute-start.3 = (f32[256,128]{1,0:T(8,128)S(1)}, f32[256,128]{1,0:T(8,128)S(1)}, u32[]{:S(2)}, u32[]{:S(2)}) collective-permute-start(f32[256,128]{1,0:T(8,128)S(1)} %get-tuple-element.48), channel_id=1, source_target_pairs={{0,1},{1,0},{2,3},{3,2},{4,8},{5,9},{6,10},{7,11},{8,4},{9,5},{10,... | collective-permute-start | bytes 393224 | tf_op jit(solution)/shard_map/ppermute | solution.py:571

commit v10 on v9

--- a/solution.py
+++ b/solution.py
@@ -210,29 +210,23 @@
     return NF + (THREE.index(comp) * NZL + p) * 3, 3
 
 
-def load(d, e, h, eps, chi, ya, yb, held, sems):
-    parts = [r.at[c] for r in (d, e, h) for c in range(3)] + [eps, chi]
-    copies = [
-        [
-            pltpu.make_async_copy(r.at[:, pl.ds(at, 8)], held.at[comp, :, pl.ds(k * 8, 8)], sems.at[comp, k])
-            for k, at in enumerate((0, NXL - 8))
-        ]
-        for comp, r in enumerate(parts)
-    ]
-    for pair in copies:
-        for c in pair:
-            c.start()
+def load(d, e, h, eps, chi, dv, ev, hv, epsv, chiv, ya, yb, sems):
+    held = (dv, ev, hv, epsv, chiv)
+    copies = [pltpu.make_async_copy(a, b, sems.at[i]) for i, (a, b) in enumerate(zip((d, e, h, eps, chi), held))]
+    for c in copies:
+        c.start()
     _, gx, _, last = position()
     even = lax.rem(gx, 2) == 0
     keep = scalar(jnp.logical_and(gx != 0, gx != last))
-    for comp in ALL:
-        for c in copies[comp]:
-            c.wait()
-        for p in range(NZL):
-            at, n = halo_slot(comp, p)
-            low, high = held[comp, p, 0:n], held[comp, p, 16 - n : 16]
-            ya[at : at + n] = jnp.where(even, high, low)
-            yb[at : at + n] = jnp.where(even, low, high) * keep
+    for comps, copy in zip((range(D, E), range(E, H), range(H, EPS), (EPS,), (CHI,)), copies):
+        copy.wait()
+        for comp in comps:
+            for p in range(NZL):
+                at, n = halo_slot(comp, p)
+                v = own(held, comp, p)
+                low, high = v[0:n], v[NXL - n :]
+                ya[at : at + n] = jnp.where(even, high, low)
+                yb[at : at + n] = jnp.where(even, low, high) * keep
 
 
 def mark(out):
@@ -415,11 +409,11 @@
             grid.hold(comp, p, functools.partial(lambda c, q: rows(own(fields, c, q), xt[c, q]), comp, p))
 
 
-def hold_frames(grid, refs, levels):
+def hold_frames(grid, refs, levels, size=ROWS):
     for k, ref in enumerate(refs):
         for p, level in levels[k].items():
             for c in range(3):
-                grid.hold(3 * k + c, p, functools.partial(lambda r, a, b: r[a, b], ref, c, p), level)
+                grid.hold(3 * k + c, p, functools.partial(lambda r, a, b: r[a, b, 0:size], ref, c, p), level)
 
 
 EARLY = ({1: 1, 2: 2, 3: 2, 4: 1}, {1: 1, 2: 2, 3: 2, 4: 1}, {0: 1, 1: 2, 2: 3, 3: 2, 4: 1})
@@ -440,100 +434,120 @@
     grid.sweep(4, (3,), (), put)
 
 
-def complete(fields, xt, frames, more, above, below, state, staged, media, coming, done):
-    grid = full_grid()
-    hold_own(grid, fields, xt)
-    hold_frames(grid, frames, EARLY)
-    hold_frames(grid, more, MIDDLE)
-    for side, at, shift in ((above, HI_AT, NZL), (below, LO_AT, -NZL)):
-        if side is not None:
-            for (comp, p), i in at.items():
-                level = int(p == 6)
-                if comp >= DP:
-                    level = p + 2 if HP <= comp < INV else p + 1
-                grid.hold(comp, p + shift, functools.partial(side, i), level)
-
-    def put(c, p, v, n):
-        k = c // 3
-        if n == STEPS and p >= ADVANCE:
-            staged[k][c % 3, p - ADVANCE] = v[:NXL]
-        if n < STEPS or k == 2:
-            grid.put(state[k], (c % 3, p + 2), c, p, v, n)
-
-    def last_sweep(h_planes, de_planes):
-        for p in sorted(set(h_planes) | set(de_planes)):
-            if p in h_planes:
-                grid.step_h(STEPS, p, range(3), put)
-            if p in de_planes:
-                if p not in h_planes:
-                    for c in range(3):
-                        staged[2][c, p - ADVANCE] = grid.get(H + c, p, STEPS)[:NXL]
-                grid.step_de(STEPS, p, put)
-                for k in range(3):
-                    done(k, p - ADVANCE, 1)
-
-    if below is not None:
+def hold_side(grid, high, read):
+    at, shift = (HI_AT, NZL) if high else (LO_AT, -NZL)
+    for (comp, p), i in at.items():
+        level = int(p == 6)
+        if comp >= DP:
+            level = p + 2 if HP <= comp < INV else p + 1
+        grid.hold(comp, p + shift, functools.partial(read, i), level)
+
+
+def chain(grid, high, put, keep, done=lambda o: None):
+    if high:
+        grid.sweep(1, (7,), (7, 8), put)
+        grid.sweep(2, range(6, 9), range(6, 10), put)
+        grid.sweep(3, range(5, 10), range(5, 11), put)
+        h_planes, de_planes = range(4, 10), range(4, 10)
+    else:
         grid.sweep(1, (-1,), (-1, 0), put)
         grid.sweep(2, (-1, 0), (0, 1), put)
         grid.sweep(3, (0, 1), (1, 2), put)
-        last_sweep((1, 2), (2, 3))
-    if above is not None:
-        for k, comp in enumerate((EPS, CHI)):
-            for o in range(ADVANCE):
-                v = grid.get(comp, NZL + o)[:NXL]
-                if coming is not None:
-                    gz, _, last, _ = position()
-                    v = jnp.where(gz == last, coming[k][o], v)
-                media[k][o] = v
-            done(3 + k, KEPT, ADVANCE)
-        grid.sweep(1, (7,), (7, 8), put)
-        grid.sweep(2, range(6, 9), range(6, 10), put)
-        grid.sweep(3, range(5, 10), range(5, 11), put)
-        last_sweep(range(4, 10), range(4, 10))
+        h_planes, de_planes = (1, 2), (2, 3)
+    for p in sorted(set(h_planes) | set(de_planes)):
+        if p in h_planes:
+            grid.step_h(STEPS, p, range(3), put)
+        if p in de_planes:
+            if p not in h_planes:
+                for c in range(3):
+                    keep(c, p - ADVANCE, grid.get(H + c, p, STEPS))
+            grid.step_de(STEPS, p, put)
+            done(p - ADVANCE)
 
 
 KEPT = NZL - ADVANCE
 
 
-def run(given, above, below, coming, outs, scratch, also=()):
-    state, staged, media, sems = scratch[:3], scratch[3:6], scratch[6:8], scratch[8]
-    copies = []
-
-    def send(source, target):
-        copies.append(pltpu.make_async_copy(source, target, sems.at[len(copies)]))
-        copies[-1].start()
-
-    def done(k, o, n):
-        if k < 3:
-            send(staged[k].at[:, pl.ds(o, n)], outs[k].at[:, pl.ds(o, n)])
-        else:
-            send(media[k - 3], outs[k].at[pl.ds(o, n)])
-
-    for a, b in also:
-        send(a, b)
-    complete(*given, above, below, state, staged, media, coming, done)
-    for c in copies:
-        c.wait()
-
-
-def near(d, e, h, eps, chi, xt, fd, fe, fh, gd, ge, gh, cc, *rest):
-    given = (d, e, h, eps, chi), xt, (fd, fe, fh), (gd, ge, gh)
-    outs, scratch = rest[:5], rest[5:]
-    also = [(a.at[pl.ds(ADVANCE, KEPT)], b.at[pl.ds(0, KEPT)]) for a, b in ((eps, outs[3]), (chi, outs[4]))]
+def near(d, e, h, eps, chi, xt, fd, fe, fh, gd, ge, gh, cc, nd, ne, nh, neps, nchi, *state):
     gz, _, _, _ = position()
 
-    @pl.when(lax.rem(gz, 2) == 0)
-    def _():
-        run(given, lambda i: cc[i], None, None, outs, scratch, also)
-
-    @pl.when(lax.rem(gz, 2) == 1)
-    def _():
-        run(given, None, lambda i: cc[i], None, outs, scratch, also)
-
-
-def far(d, e, h, eps, chi, xt, fd, fe, fh, gd, ge, gh, ca, cb, eps_in, chi_in, *rest):
-    given = (d, e, h, eps, chi), xt, (fd, fe, fh), (gd, ge, gh)
-    outs, scratch = rest[5:10], rest[10:]
+    def side(high):
+        grid = full_grid()
+        hold_own(grid, (d, e, h, eps, chi), xt)
+        hold_frames(grid, (fd, fe, fh), EARLY)
+        hold_frames(grid, (gd, ge, gh), MIDDLE)
+        hold_side(grid, high, lambda i: cc[i])
+
+        def put(c, p, v, n):
+            k = c // 3
+            if n == STEPS and p >= ADVANCE:
+                (nd, ne, nh)[k][c % 3, p - ADVANCE] = v[:NXL]
+            if n < STEPS or k == 2:
+                grid.put(state[k], (c % 3, p + 2), c, p, v, n)
+
+        def keep(c, o, v):
+            nh[c, o] = v[:NXL]
+
+        chain(grid, high, put, keep)
+        if high:
+            for out, comp in ((neps, EPS), (nchi, CHI)):
+                for o in range(ADVANCE):
+                    out[o] = grid.get(comp, NZL + o)[:NXL]
+
+    pl.when(lax.rem(gz, 2) == 0)(lambda: side(True))
+    pl.when(lax.rem(gz, 2) == 1)(lambda: side(False))
+
+
+def ahead(d, e, h, eps, chi, fd, fe, fh, gd, ge, gh, ca, eps_in, chi_in, ie, ih, od, oe, oh, oeps, ochi, sd):
+    gz, _, last, _ = position()
+    half = halo_row() < XH
+
+    def read(i):
+        m = ca[24 * i : 24 * i + 8]
+        x = ca[24 * NS + 8 * i : 24 * NS + 8 * i + 8] if i < NR else m
+        return rows(jnp.where(half, x, m), ca[24 * i + 8 : 24 * i + 24], jnp.where(half, m, x))
+
+    def side(high):
+        z = scalar(gz != last) if high else scalar(gz != 0)
+
+        def own_plane(p):
+            return 0 <= p < NZL
+
+        grid = Grid(NXL, lambda p: HALF if own_plane(p) else HALF * z, lambda p: None if own_plane(p) else 1.0 - z)
+        for comp in ALL:
+            for p in range(NZL):
+                grid.hold(comp, p, functools.partial(own, (d, e, h, eps, chi), comp, p))
+        hold_frames(grid, (fd, fe, fh), EARLY, NXL)
+        hold_frames(grid, (gd, ge, gh), MIDDLE, NXL)
+        hold_side(grid, high, read)
+
+        def put(c, p, v, n):
+            k = c // 3
+            if n == STEPS and p >= ADVANCE:
+                (od, oe, oh)[k][c % 3, p - ADVANCE] = v
+            if k == 2:
+                grid.put(ih, (n - 1, c % 3, p + 2), c, p, v, n)
+            elif n < STEPS and k == 1:
+                grid.put(ie, (n - 1, c % 3, p + 2), c, p, v, n)
+            elif n < STEPS:
+                grid.put(sd, (c % 3, p + 2), c, p, v, n)
+
+        def keep(c, o, v):
+            oh[c, o] = v
+
+        chain(grid, high, put, keep)
+        if high:
+            for out, comp, new in ((oeps, EPS, eps_in), (ochi, CHI, chi_in)):
+                for o in range(ADVANCE):
+                    out[o] = jnp.where(gz == last, new[o], grid.get(comp, NZL + o))
+
+    pl.when(lax.rem(gz, 2) == 0)(lambda: side(False))
+    pl.when(lax.rem(gz, 2) == 1)(lambda: side(True))
+
+
+def far(d, e, h, eps, chi, xt, fd, fe, fh, gd, ge, gh, ca, cb, *rest):
+    nd, ne, nh, neps, nchi, ie, ih, od, oe, oh, oeps, ochi = rest[:12]
+    outs, state, edge, sems = rest[12:17], rest[17:20], rest[20:23], rest[23]
     half = halo_row() < XH
     gz, _, _, _ = position()
 
@@ -547,13 +561,59 @@
             v = rows(*[v[kept.index(k) : kept.index(k) + 1] for k in near_row])
         return rows(jnp.where(half, x, m), ca[24 * i + 8 : 24 * i + 24], jnp.where(half, m, x), v)
 
-    @pl.when(lax.rem(gz, 2) == 0)
-    def _():
-        run(given, None, functools.partial(cross, LO_ROWS), None, outs, scratch)
-
-    @pl.when(lax.rem(gz, 2) == 1)
-    def _():
-        run(given, functools.partial(cross, HI_ROWS), None, (eps_in, chi_in), outs, scratch)
+    def side(high):
+        copies = []
+
+        def send(source, target):
+            copies.append(pltpu.make_async_copy(source, target, sems.at[len(copies)]))
+            copies[-1].start()
+
+        here, there = (pl.ds(ADVANCE, KEPT), pl.ds(0, ADVANCE)) if high else (pl.ds(0, ADVANCE), pl.ds(ADVANCE, KEPT))
+        middle_rows = pl.ds(8, 16)
+        for a, b, out in zip((nd, ne, nh), (od, oe, oh), outs):
+            send(a.at[:, there], out.at[:, there])
+            send(b.at[:, here, middle_rows], out.at[:, here, middle_rows])
+        for a, new, out in zip((eps, chi), (oeps, ochi) if high else (neps, nchi), outs[3:]):
+            send(a.at[pl.ds(ADVANCE, KEPT)], out.at[pl.ds(0, KEPT)])
+            send(new, out.at[pl.ds(KEPT, ADVANCE)])
+
+        grid = full_grid()
+        hold_own(grid, (d, e, h, eps, chi), xt)
+        hold_frames(grid, (fd, fe, fh), EARLY)
+        hold_frames(grid, (gd, ge, gh), MIDDLE)
+        hold_side(grid, high, functools.partial(cross, HI_ROWS if high else LO_ROWS))
+        none = jnp.zeros((16, NY), jnp.float32)
+
+        def result(k, c, o, v):
+            edge[k][c, o, 0:8] = v[0:8]
+            edge[k][c, o, 8:16] = v[24:32]
+
+        def put(c, p, v, n):
+            k, at = c // 3, (c % 3, p + 2)
+            if n == STEPS and p >= ADVANCE:
+                result(k, c % 3, p - ADVANCE, v)
+            if n < STEPS or k == 2:
+                ref, inner_ref = state[k], (None, ie, ih)[k]
+                ref[(*at, slice(0, 8))] = v[0:8]
+                ref[(*at, slice(8, 24))] = v[24:40]
+
+                def read():
+                    mid = none if inner_ref is None else inner_ref[(n - 1, *at, slice(8, 24))]
+                    return rows(ref[(*at, slice(0, 8))], mid, ref[(*at, slice(8, 24))])
+
+                grid.hold(c, p, read, n)
+
+        def done(o):
+            for k in range(3):
+                for a, b in ((0, 0), (8, 24)):
+                    send(edge[k].at[:, pl.ds(o, 1), pl.ds(a, 8)], outs[k].at[:, pl.ds(o, 1), pl.ds(b, 8)])
+
+        chain(grid, high, put, functools.partial(result, 2), done)
+        for c in copies:
+            c.wait()
+
+    pl.when(lax.rem(gz, 2) == 0)(lambda: side(False))
+    pl.when(lax.rem(gz, 2) == 1)(lambda: side(True))
 
 
 def swapped(shard, axis, first):
@@ -585,13 +645,12 @@
 
 def on_device(d_field, e_field, h_field, permittivity, kerr_coeff, classes, eps_table, chi_table):
     field, medium = shape(3, NZL, NXL, NY), shape(NZL, NXL, NY)
-    fields = [d_field, e_field, h_field, permittivity, kerr_coeff]
     halo = shape(NHALO, NY)
-    ya, yb = call(
+    *fields, ya, yb = call(
         load,
-        [pltpu.with_memory_space_constraint(a, pltpu.HBM) for a in fields],
-        (halo, halo),
-        [pltpu.VMEM((11, NZL, 16, NY), jnp.float32), pltpu.SemaphoreType.DMA((11, 2))],
+        [pltpu.with_memory_space_constraint(a, pltpu.HBM) for a in (d_field, e_field, h_field, permittivity, kerr_coeff)],
+        (field, field, field, medium, medium, halo, halo),
+        [pltpu.SemaphoreType.DMA((5,))],
         specs=[HBM] * 5,
     )
     ra, rb = swapped(ya, "gx", 0), swapped(yb, "gx", 1)
@@ -614,23 +673,24 @@
     cc = swapped(zc, "gz", 0)
     more = call(middle, [*fields, xt, *frames], (shape(3, 7, ROWS, NY),) * 3)
     state = [pltpu.VMEM((3, 13, ROWS, NY), jnp.float32)] * 3
-    given = [*fields, xt, *frames, *more]
-    two = (ADVANCE, NXL, NY)
-    results = (field, field, field, medium, medium)
-    scratch = state + [pltpu.VMEM(field.shape, jnp.float32)] * 3 + [pltpu.VMEM(two, jnp.float32)] * 2
-    scratch += [pltpu.SemaphoreType.DMA((32,))]
-    outs = call(near, [*given, cc], results, scratch, vmem=16, out=HBM)
-    given += [ca, cb, *coming]
-    n = len(given)
+    two = shape(ADVANCE, NXL, NY)
+    made = call(near, [*fields, xt, *frames, *more, cc], (field, field, field, two, two), state, vmem=16)
+    levels = shape(STEPS - 1, 3, 13, NXL, NY), shape(STEPS, 3, 13, NXL, NY)
+    inside = call(
+        ahead,
+        [*fields, *frames, *more, ca, *coming],
+        (*levels, field, field, field, two, two),
+        [pltpu.VMEM((3, 13, NXL, NY), jnp.float32)],
+        vmem=16,
+    )
+    thin = [pltpu.VMEM((3, 13, EDGE, NY), jnp.float32)] * 3 + [pltpu.VMEM((3, NZL, 16, NY), jnp.float32)] * 3
     return call(
         far,
-        [*given, *outs],
-        results,
-        scratch,
+        [*fields, xt, *frames, *more, ca, cb, *made, *inside],
+        (field, field, field, medium, medium),
+        [*thin, pltpu.SemaphoreType.DMA((48,))],
         vmem=16,
-        specs=[VM] * n + [HBM] * 5,
         out=HBM,
-        aliases={n + k: k for k in range(5)},
     )
 
 

time: 24.1 us -> 23.9 us (level)
    pallas_call x8 -> x9, Pallas kernels: 6.64 us -> 6.42 us  [call(): pl.pallas_call(body, out_shape=out_shape, in_specs=[VM] * len(inputs) if...]
  transfers between devices with their start and end apart: 5 -> 5, of which waited for: 3 -> 3; matrix products, arithmetic and copies ran while one was open for 0% -> 0% of each run, Pallas kernels for 11% -> 10%
where the time goes in v10:
time: 23.9 us; the launch traced here: 23.7 us
  starting transfers between devices  9.1 us (38%)
  waiting for transfers between devices  7.31 us (31%)
  Pallas kernels  6.42 us (27%)
  between operations  0.72 us (3%)
    ppermute x5, starting transfers between devices, swapped(): return lax.ppermute(shard, ('gz', 'gx'), moves)  9.1 us
    ppermute x5, waiting for transfers between devices, swapped(): return lax.ppermute(shard, ('gz', 'gx'), moves)  7.31 us
    pallas_call x9, Pallas kernels, call(): pl.pallas_call(body, out_shape=out_shape, in_specs=[VM] * len(inputs) if...  6.42 us
  transfers between devices with their start and end apart: 5, of which 3 were waited for; matrix products, arithmetic and copies ran while one was open for 0% of the time, Pallas kernels for 10%

profile of v10, /device:TPU:111, one launch (start us, length us, event | category | flops | bytes accessed | tf_op | source)
XLA Modules:
  0.0 23.7 jit_solution(12658845638702887735)
XLA Ops:
  0.6 1.4 %shard_map.119 = (f32[3,8,32,128]{3,2,1,0:T(8,128)S(1)}, f32[3,8,32,128]{3,2,1,0:T(8,128)S(1)}, f32[3,8,32,128]{3,2,1,0:T(8,128)S(1)}, f32[8,32,128]{2,1,0:T(8,1...) custom-call(f32[3,8,32,128]{3,2,1,0:T(8,128)} %d.1, f32[3,8,32,128]{3,2,1,0:T(8,128)} %e.1, ...), custom_call_target="tpu_custom_call" | custom-call | tf_op jit(solution)/shard_map/pallas_call | solution.py:635
  2.0 0.3 %collective-permute-start = (f32[304,128]{1,0:T(8,128)S(1)}, f32[304,128]{1,0:T(8,128)S(1)}, u32[]{:S(2)}, u32[]{:S(2)}) collective-permute-start(f32[304,128]{1,0:T(8,128)S(1)} %get-tuple-element.47), channel_id=1, source_target_pairs={{0,1},{1,0},{2,3},{3,2},{4,5},{5,4},{6,7},{7,6},{8,9},{9,8},{10,11... | collective-permute-start | bytes 466952 | tf_op jit(solution)/shard_map/ppermute | solution.py:631
  2.2 2.1 %collective-permute-start.1 = (f32[304,128]{1,0:T(8,128)S(1)}, f32[304,128]{1,0:T(8,128)S(1)}, u32[]{:S(2)}, u32[]{:S(2)}) collective-permute-start(f32[304,128]{1,0:T(8,128)S(1)} %get-tuple-element.48), channel_id=1, source_target_pairs={{0,4},{1,2},{2,1},{3,7},{4,0},{5,6},{6,5},{7,3},{8,12},{9,10},{10,... | collective-permute-start | bytes 466952 | tf_op jit(solution)/shard_map/ppermute | solution.py:631
  4.4 0.5 %shard_map.122 = (f32[3,5,32,128]{3,2,1,0:T(8,128)S(1)}, f32[3,5,32,128]{3,2,1,0:T(8,128)S(1)}, f32[3,5,32,128]{3,2,1,0:T(8,128)S(1)}, f32[2,32,128]{2,1,0:T(8,128)S(1)}, f32[696,128]{1,0:T(8,128)S(1)}) custom-call(f32[3,8,32,128]{3,2,1,0:T(8,128)S(1)} %get-tuple-element.42.d, f32[3,8,32,128]{3,2,1,0:T(8,128)S(1)} %get-tuple-element.43.e, ...), custom_call_target="tpu_custom_call" | custom-call | tf_op jit(solution)/shard_map/pallas_call | solution.py:635
  4.9 0.0 copy-start
  4.9 0.0 copy-start.1
  4.9 0.0 copy-start.2
  5.0 2.0 %collective-permute-done.ra = f32[304,128]{1,0:T(8,128)S(1)} collective-permute-done((f32[304,128]{1,0:T(8,128)S(1)}, f32[304,128]{1,0:T(8,128)S(1)}, u32[]{:S(2)}, u32[]{:S(2)}) %collective-permute-start) | collective-permute-done | bytes 155680 | tf_op jit(solution)/shard_map/ppermute | solution.py:631
  7.0 0.8 %collective-permute-done.1.rb = f32[304,128]{1,0:T(8,128)S(1)} collective-permute-done((f32[304,128]{1,0:T(8,128)S(1)}, f32[304,128]{1,0:T(8,128)S(1)}, u32[]{:S(2)}, u32[]{:S(2)}) %collective-permute-start.1) | collective-permute-done | bytes 155680 | tf_op jit(solution)/shard_map/ppermute | solution.py:631
  7.8 0.2 shard_map.121
  8.0 0.5 %shard_map.123 = (f32[3,5,40,128]{3,2,1,0:T(8,128)S(1)}, f32[3,5,40,128]{3,2,1,0:T(8,128)S(1)}, f32[3,5,40,128]{3,2,1,0:T(8,128)S(1)}, f32[26,40,128]{2,1,0:T(8,128)S(1)}) custom-call(f32[3,8,32,128]{3,2,1,0:T(8,128)S(1)} %get-tuple-element.42.d, f32[3,8,32,128]{3,2,1,0:T(8,128)S(1)} %get-tuple-element.43.e, f32[3,8,32,128]{3,2,1,0:T(8,128)S(1)} %get-tuple-element.44.h, ...), custom_call_target="tpu_custom_call" | custom-call | tf_op jit(solution)/shard_map/pallas_call | solution.py:635
  8.5 1.7 %collective-permute-start.4 = (f32[26,40,128]{2,1,0:T(8,128)S(1)}, f32[26,40,128]{2,1,0:T(8,128)S(1)}, u32[]{:S(2)}, u32[]{:S(2)}) collective-permute-start(f32[26,40,128]{2,1,0:T(8,128)S(1)} %get-tuple-element.66), channel_id=1, source_target_pairs={{0,4},{1,5},{2,6},{3,7},{4,0},{5,1},{6,2},{7,3},{8,12},{9,13},{10,... | collective-permute-start | bytes 1597448 | tf_op jit(solution)/shard_map/ppermute | solution.py:631
  10.2 2.8 %collective-permute-start.2 = (f32[696,128]{1,0:T(8,128)S(1)}, f32[696,128]{1,0:T(8,128)S(1)}, u32[]{:S(2)}, u32[]{:S(2)}) collective-permute-start(f32[696,128]{1,0:T(8,128)S(1)} %get-tuple-element.64), channel_id=1, source_target_pairs={{0,1},{1,0},{2,3},{3,2},{4,8},{5,9},{6,10},{7,11},{8,4},{9,5},{10,... | collective-permute-start | bytes 1069064 | tf_op jit(solution)/shard_map/ppermute | solution.py:631
  12.9 2.3 %collective-permute-start.3 = (f32[256,128]{1,0:T(8,128)S(1)}, f32[256,128]{1,0:T(8,128)S(1)}, u32[]{:S(2)}, u32[]{:S(2)}) collective-permute-start(f32[256,128]{1,0:T(8,128)S(1)} %get-tuple-element.65), channel_id=1, source_target_pairs={{0,1},{1,0},{2,3},{3,2},{4,8},{5,9},{6,10},{7,11},{8,4},{9,5},{10,... | collective-permute-start | bytes 393224 | tf_op jit(solution)/shard_map/ppermute | solution.py:631
  15.2 0.0 copy-done
  15.2 0.0 copy-done.1
  15.2 0.0 copy-done.2
  15.2 0.1 select_reduce_fusion
  15.3 0.5 %shard_map.124 = (f32[3,7,40,128]{3,2,1,0:T(8,128)S(1)}, f32[3,7,40,128]{3,2,1,0:T(8,128)S(1)}, f32[3,7,40,128]{3,2,1,0:T(8,128)S(1)}) custom-call(f32[3,8,32,128]{3,2,1,0:T(8,128)S(1)} %get-tuple-element.42.d, f32[3,8,32,128]{3,2,1,0:T(8,128)S(1)} %get-tuple-element.43.e, f32[3,8,32,128]{3,2,1,0:T(8,128)S(1)} %get-tuple-element.44.h, ...), custom_call_target="tpu_custom_call" | custom-call | tf_op jit(solution)/shard_map/pallas_call | solution.py:635
  15.8 4.4 %collective-permute-done.2.ca = f32[696,128]{1,0:T(8,128)S(1)} collective-permute-done((f32[696,128]{1,0:T(8,128)S(1)}, f32[696,128]{1,0:T(8,128)S(1)}, u32[]{:S(2)}, u32[]{:S(2)}) %collective-permute-start.2) | collective-permute-done | bytes 356384 | tf_op jit(solution)/shard_map/ppermute | solution.py:631
  20.3 0.9 %shard_map.126 = (f32[3,3,13,32,128]{4,3,2,1,0:T(8,128)S(1)}, f32[4,3,13,32,128]{4,3,2,1,0:T(8,128)S(1)}, f32[3,8,32,128]{3,2,1,0:T(8,128)S(1)}, f32[3,8,32,128]...) custom-call(f32[3,8,32,128]{3,2,1,0:T(8,128)S(1)} %get-tuple-element.42.d, ...), custom_call_target="tpu_custom_call" | custom-call | tf_op jit(solution)/shard_map/pallas_call | solution.py:635
  21.2 0.0 collective-permute-done.4.cc
  21.2 0.6 %shard_map.125 = (f32[3,8,32,128]{3,2,1,0:T(8,128)S(1)}, f32[3,8,32,128]{3,2,1,0:T(8,128)S(1)}, f32[3,8,32,128]{3,2,1,0:T(8,128)S(1)}, f32[2,32,128]{2,1,0:T(8,128)S(1)}, f32[2,32,128]{2,1,0:T(8,128)S(1)}) custom-call(f32[3,8,32,128]{3,2,1,0:T(8,128)S(1)} %get-tuple-element.42.d, f32[3,8,32,128]{3,2,1,0:T(8,128)S(1)} %get-tuple-element.43.e, ...), custom_call_target="tpu_custom_call" | custom-call | tf_op jit(solution)/shard_map/pallas_call | solution.py:635
  21.8 0.0 collective-permute-done.3.cb
  21.8 1.9 %shard_map.127 = (f32[3,8,32,128]{3,2,1,0:T(8,128)}, f32[3,8,32,128]{3,2,1,0:T(8,128)}, f32[3,8,32,128]{3,2,1,0:T(8,128)}, f32[8,32,128]{2,1,0:T(8,128)}, f32[8,32,128]{2,1,0:T(8,128)}) custom-call(f32[3,8,32,128]{3,2,1,0:T(8,128)S(1)} %get-tuple-element.42.d, f32[3,8,32,128]{3,2,1,0:T(8,128)S(1)} %get-tuple-element.43.e, ...), custom_call_target="tpu_custom_call" | custom-call | tf_op jit(solution)/shard_map/pallas_call | solution.py:635
  (1 shorter events, 0.0 us)
Async XLA Ops:
  2.0 5.0 %collective-permute-start = (f32[304,128]{1,0:T(8,128)S(1)}, f32[304,128]{1,0:T(8,128)S(1)}, u32[]{:S(2)}, u32[]{:S(2)}) collective-permute-start(f32[304,128]{1,0:T(8,128)S(1)} %get-tuple-element.47), channel_id=1, source_target_pairs={{0,1},{1,0},{2,3},{3,2},{4,5},{5,4},{6,7},{7,6},{8,9},{9,8},{10,11... | collective-permute-start | bytes 466952 | tf_op jit(solution)/shard_map/ppermute | solution.py:631
  2.2 5.6 %collective-permute-start.1 = (f32[304,128]{1,0:T(8,128)S(1)}, f32[304,128]{1,0:T(8,128)S(1)}, u32[]{:S(2)}, u32[]{:S(2)}) collective-permute-start(f32[304,128]{1,0:T(8,128)S(1)} %get-tuple-element.48), channel_id=1, source_target_pairs={{0,4},{1,2},{2,1},{3,7},{4,0},{5,6},{6,5},{7,3},{8,12},{9,10},{10,... | collective-permute-start | bytes 466952 | tf_op jit(solution)/shard_map/ppermute | solution.py:631
  4.9 10.3 %copy-start = (s32[2,32,128]{2,1,0:T(8,128)S(1)}, s32[2,32,128]{2,1,0:T(8,128)}, u32[]{:S(2)}) copy-start(s32[2,32,128]{2,1,0:T(8,128)} %param.13) | copy-start | bytes 98308
  4.9 10.3 %copy-start.1 = (f32[8]{0:T(128)S(1)}, f32[8]{0:T(128)}, u32[]{:S(2)}) copy-start(f32[8]{0:T(128)} %param.15) | copy-start | bytes 100
  4.9 10.3 %copy-start.2 = (f32[8]{0:T(128)S(1)}, f32[8]{0:T(128)}, u32[]{:S(2)}) copy-start(f32[8]{0:T(128)} %param.14) | copy-start | bytes 100
  8.5 12.7 %collective-permute-start.4 = (f32[26,40,128]{2,1,0:T(8,128)S(1)}, f32[26,40,128]{2,1,0:T(8,128)S(1)}, u32[]{:S(2)}, u32[]{:S(2)}) collective-permute-start(f32[26,40,128]{2,1,0:T(8,128)S(1)} %get-tuple-element.66), channel_id=1, source_target_pairs={{0,4},{1,5},{2,6},{3,7},{4,0},{5,1},{6,2},{7,3},{8,12},{9,13},{10,... | collective-permute-start | bytes 1597448 | tf_op jit(solution)/shard_map/ppermute | solution.py:631
  10.2 10.1 %collective-permute-start.2 = (f32[696,128]{1,0:T(8,128)S(1)}, f32[696,128]{1,0:T(8,128)S(1)}, u32[]{:S(2)}, u32[]{:S(2)}) collective-permute-start(f32[696,128]{1,0:T(8,128)S(1)} %get-tuple-element.64), channel_id=1, source_target_pairs={{0,1},{1,0},{2,3},{3,2},{4,8},{5,9},{6,10},{7,11},{8,4},{9,5},{10,... | collective-permute-start | bytes 1069064 | tf_op jit(solution)/shard_map/ppermute | solution.py:631
  12.9 8.9 %collective-permute-start.3 = (f32[256,128]{1,0:T(8,128)S(1)}, f32[256,128]{1,0:T(8,128)S(1)}, u32[]{:S(2)}, u32[]{:S(2)}) collective-permute-start(f32[256,128]{1,0:T(8,128)S(1)} %get-tuple-element.65), channel_id=1, source_target_pairs={{0,1},{1,0},{2,3},{3,2},{4,8},{5,9},{6,10},{7,11},{8,4},{9,5},{10,... | collective-permute-start | bytes 393224 | tf_op jit(solution)/shard_map/ppermute | solution.py:631

commit v11 on v10

--- a/solution.py
+++ b/solution.py
@@ -498,7 +498,8 @@
     pl.when(lax.rem(gz, 2) == 1)(lambda: side(False))
 
 
-def ahead(d, e, h, eps, chi, fd, fe, fh, gd, ge, gh, ca, eps_in, chi_in, ie, ih, od, oe, oh, oeps, ochi, sd):
+def ahead(d, e, h, eps, chi, fd, fe, fh, gd, ge, gh, ca, eps_in, chi_in, nd, ne, nh, neps, nchi, *rest):
+    outs, (ie, ih, od, oe, oh, oeps, ochi, sd, sems) = rest[:5], rest[5:]
     gz, _, last, _ = position()
     half = halo_row() < XH
 
@@ -508,6 +509,14 @@
         return rows(jnp.where(half, x, m), ca[24 * i + 8 : 24 * i + 24], jnp.where(half, m, x))
 
     def side(high):
+        there = pl.ds(0, ADVANCE) if high else pl.ds(ADVANCE, KEPT)
+        moves = [(a.at[:, there], b.at[:, there]) for a, b in zip((nd, ne, nh), outs)]
+        moves += [(a.at[pl.ds(ADVANCE, KEPT)], b.at[pl.ds(0, KEPT)]) for a, b in zip((eps, chi), outs[3:])]
+        if not high:
+            moves += [(a, b.at[pl.ds(KEPT, ADVANCE)]) for a, b in zip((neps, nchi), outs[3:])]
+        copies = [pltpu.make_async_copy(a, b, sems.at[i]) for i, (a, b) in enumerate(moves)]
+        for c in copies:
+            c.start()
         z = scalar(gz != last) if high else scalar(gz != 0)
 
         def own_plane(p):
@@ -540,13 +549,15 @@
             for out, comp, new in ((oeps, EPS, eps_in), (ochi, CHI, chi_in)):
                 for o in range(ADVANCE):
                     out[o] = jnp.where(gz == last, new[o], grid.get(comp, NZL + o))
+        for c in copies:
+            c.wait()
 
     pl.when(lax.rem(gz, 2) == 0)(lambda: side(False))
     pl.when(lax.rem(gz, 2) == 1)(lambda: side(True))
 
 
 def far(d, e, h, eps, chi, xt, fd, fe, fh, gd, ge, gh, ca, cb, *rest):
-    nd, ne, nh, neps, nchi, ie, ih, od, oe, oh, oeps, ochi = rest[:12]
+    ie, ih, od, oe, oh, oeps, ochi = rest[:7]
     outs, state, edge, sems = rest[12:17], rest[17:20], rest[20:23], rest[23]
     half = halo_row() < XH
     gz, _, _, _ = position()
@@ -568,14 +579,12 @@
             copies.append(pltpu.make_async_copy(source, target, sems.at[len(copies)]))
             copies[-1].start()
 
-        here, there = (pl.ds(ADVANCE, KEPT), pl.ds(0, ADVANCE)) if high else (pl.ds(0, ADVANCE), pl.ds(ADVANCE, KEPT))
-        middle_rows = pl.ds(8, 16)
-        for a, b, out in zip((nd, ne, nh), (od, oe, oh), outs):
-            send(a.at[:, there], out.at[:, there])
-            send(b.at[:, here, middle_rows], out.at[:, here, middle_rows])
-        for a, new, out in zip((eps, chi), (oeps, ochi) if high else (neps, nchi), outs[3:]):
-            send(a.at[pl.ds(ADVANCE, KEPT)], out.at[pl.ds(0, KEPT)])
-            send(new, out.at[pl.ds(KEPT, ADVANCE)])
+        here = pl.ds(ADVANCE, KEPT) if high else pl.ds(0, ADVANCE)
+        for a, out in zip((od, oe, oh), outs):
+            send(a.at[:, here, pl.ds(8, 16)], out.at[:, here, pl.ds(8, 16)])
+        if high:
+            for a, out in zip((oeps, ochi), outs[3:]):
+                send(a, out.at[pl.ds(KEPT, ADVANCE)])
 
         grid = full_grid()
         hold_own(grid, (d, e, h, eps, chi), xt)
@@ -636,7 +645,7 @@
         body,
         out_shape=out_shape,
         in_specs=[VM] * len(inputs) if specs is None else specs,
-        out_specs=jax.tree.map(lambda _: out, out_shape),
+        out_specs=out if isinstance(out, tuple) else (out,) * len(out_shape),
         input_output_aliases=aliases or {},
         scratch_shapes=list(scratch),
         compiler_params=pltpu.CompilerParams(vmem_limit_bytes=vmem << 20),
@@ -676,21 +685,27 @@
     two = shape(ADVANCE, NXL, NY)
     made = call(near, [*fields, xt, *frames, *more, cc], (field, field, field, two, two), state, vmem=16)
     levels = shape(STEPS - 1, 3, 13, NXL, NY), shape(STEPS, 3, 13, NXL, NY)
-    inside = call(
+    results = (field, field, field, medium, medium)
+    *outs, ie, ih, od, oe, oh, oeps, ochi = call(
         ahead,
-        [*fields, *frames, *more, ca, *coming],
-        (*levels, field, field, field, two, two),
-        [pltpu.VMEM((3, 13, NXL, NY), jnp.float32)],
+        [*fields, *frames, *more, ca, *coming, *made],
+        (*results, *levels, field, field, field, two, two),
+        [pltpu.VMEM((3, 13, NXL, NY), jnp.float32), pltpu.SemaphoreType.DMA((8,))],
         vmem=16,
+        out=(HBM,) * 5 + (VM,) * 7,
     )
     thin = [pltpu.VMEM((3, 13, EDGE, NY), jnp.float32)] * 3 + [pltpu.VMEM((3, NZL, 16, NY), jnp.float32)] * 3
+    given = [*fields, xt, *frames, *more, ca, cb, ie, ih, od, oe, oh, oeps, ochi]
+    n = len(given)
     return call(
         far,
-        [*fields, xt, *frames, *more, ca, cb, *made, *inside],
-        (field, field, field, medium, medium),
+        [*given, *outs],
+        results,
         [*thin, pltpu.SemaphoreType.DMA((48,))],
         vmem=16,
+        specs=[VM] * n + [HBM] * 5,
         out=HBM,
+        aliases={n + k: k for k in range(5)},
     )
 
 

time: 23.9 us -> 24.1 us (level)
  Pallas kernels: 6.42 us -> 7.15 us
  waiting for transfers between devices: 7.31 us -> 6.72 us
    pallas_call x9, Pallas kernels: 6.42 us -> 7.15 us  [call(): pl.pallas_call(body, out_shape=out_shape, in_specs=[VM] * len(inputs) if...]
    ppermute x5, waiting for transfers between devices: 7.31 us -> 6.72 us  [swapped(): return lax.ppermute(shard, ('gz', 'gx'), moves)]
  transfers between devices with their start and end apart: 5 -> 5, of which waited for: 3 -> 3; matrix products, arithmetic and copies ran while one was open for 0% -> 0% of each run, Pallas kernels for 10% -> 14%
where the time goes in v11:
time: 24.1 us; the launch traced here: 23.8 us
  starting transfers between devices  9.1 us (38%)
  Pallas kernels  7.15 us (30%)
  waiting for transfers between devices  6.72 us (28%)
  between operations  0.72 us (3%)
    ppermute x5, starting transfers between devices, swapped(): return lax.ppermute(shard, ('gz', 'gx'), moves)  9.1 us
    pallas_call x9, Pallas kernels, call(): pl.pallas_call(body, out_shape=out_shape, in_specs=[VM] * len(inputs) if...  7.15 us
    ppermute x5, waiting for transfers between devices, swapped(): return lax.ppermute(shard, ('gz', 'gx'), moves)  6.72 us
  transfers between devices with their start and end apart: 5, of which 3 were waited for; matrix products, arithmetic and copies ran while one was open for 0% of the time, Pallas kernels for 14%

profile of v11, /device:TPU:111, one launch (start us, length us, event | category | flops | bytes accessed | tf_op | source)
XLA Modules:
  0.0 23.8 jit_solution(8969433481889810326)
XLA Ops:
  0.6 1.4 %shard_map.119 = (f32[3,8,32,128]{3,2,1,0:T(8,128)S(1)}, f32[3,8,32,128]{3,2,1,0:T(8,128)S(1)}, f32[3,8,32,128]{3,2,1,0:T(8,128)S(1)}, f32[8,32,128]{2,1,0:T(8,1...) custom-call(f32[3,8,32,128]{3,2,1,0:T(8,128)} %d.1, f32[3,8,32,128]{3,2,1,0:T(8,128)} %e.1, ...), custom_call_target="tpu_custom_call" | custom-call | tf_op jit(solution)/shard_map/pallas_call | solution.py:644
  2.0 0.3 %collective-permute-start = (f32[304,128]{1,0:T(8,128)S(1)}, f32[304,128]{1,0:T(8,128)S(1)}, u32[]{:S(2)}, u32[]{:S(2)}) collective-permute-start(f32[304,128]{1,0:T(8,128)S(1)} %get-tuple-element.52), channel_id=1, source_target_pairs={{0,1},{1,0},{2,3},{3,2},{4,5},{5,4},{6,7},{7,6},{8,9},{9,8},{10,11... | collective-permute-start | bytes 466952 | tf_op jit(solution)/shard_map/ppermute | solution.py:640
  2.2 2.1 %collective-permute-start.1 = (f32[304,128]{1,0:T(8,128)S(1)}, f32[304,128]{1,0:T(8,128)S(1)}, u32[]{:S(2)}, u32[]{:S(2)}) collective-permute-start(f32[304,128]{1,0:T(8,128)S(1)} %get-tuple-element.53), channel_id=1, source_target_pairs={{0,4},{1,2},{2,1},{3,7},{4,0},{5,6},{6,5},{7,3},{8,12},{9,10},{10,... | collective-permute-start | bytes 466952 | tf_op jit(solution)/shard_map/ppermute | solution.py:640
  4.4 0.5 %shard_map.122 = (f32[3,5,32,128]{3,2,1,0:T(8,128)S(1)}, f32[3,5,32,128]{3,2,1,0:T(8,128)S(1)}, f32[3,5,32,128]{3,2,1,0:T(8,128)S(1)}, f32[2,32,128]{2,1,0:T(8,128)S(1)}, f32[696,128]{1,0:T(8,128)S(1)}) custom-call(f32[3,8,32,128]{3,2,1,0:T(8,128)S(1)} %get-tuple-element.47.d, f32[3,8,32,128]{3,2,1,0:T(8,128)S(1)} %get-tuple-element.48.e, ...), custom_call_target="tpu_custom_call" | custom-call | tf_op jit(solution)/shard_map/pallas_call | solution.py:644
  4.9 0.0 copy-start
  4.9 0.0 copy-start.1
  4.9 0.0 copy-start.2
  5.0 2.0 %collective-permute-done.ra = f32[304,128]{1,0:T(8,128)S(1)} collective-permute-done((f32[304,128]{1,0:T(8,128)S(1)}, f32[304,128]{1,0:T(8,128)S(1)}, u32[]{:S(2)}, u32[]{:S(2)}) %collective-permute-start) | collective-permute-done | bytes 155680 | tf_op jit(solution)/shard_map/ppermute | solution.py:640
  7.0 0.8 %collective-permute-done.1.rb = f32[304,128]{1,0:T(8,128)S(1)} collective-permute-done((f32[304,128]{1,0:T(8,128)S(1)}, f32[304,128]{1,0:T(8,128)S(1)}, u32[]{:S(2)}, u32[]{:S(2)}) %collective-permute-start.1) | collective-permute-done | bytes 155680 | tf_op jit(solution)/shard_map/ppermute | solution.py:640
  7.8 0.2 shard_map.121
  8.0 0.5 %shard_map.123 = (f32[3,5,40,128]{3,2,1,0:T(8,128)S(1)}, f32[3,5,40,128]{3,2,1,0:T(8,128)S(1)}, f32[3,5,40,128]{3,2,1,0:T(8,128)S(1)}, f32[26,40,128]{2,1,0:T(8,128)S(1)}) custom-call(f32[3,8,32,128]{3,2,1,0:T(8,128)S(1)} %get-tuple-element.47.d, f32[3,8,32,128]{3,2,1,0:T(8,128)S(1)} %get-tuple-element.48.e, f32[3,8,32,128]{3,2,1,0:T(8,128)S(1)} %get-tuple-element.49.h, ...), custom_call_target="tpu_custom_call" | custom-call | tf_op jit(solution)/shard_map/pallas_call | solution.py:644
  8.5 1.7 %collective-permute-start.4 = (f32[26,40,128]{2,1,0:T(8,128)S(1)}, f32[26,40,128]{2,1,0:T(8,128)S(1)}, u32[]{:S(2)}, u32[]{:S(2)}) collective-permute-start(f32[26,40,128]{2,1,0:T(8,128)S(1)} %get-tuple-element.71), channel_id=1, source_target_pairs={{0,4},{1,5},{2,6},{3,7},{4,0},{5,1},{6,2},{7,3},{8,12},{9,13},{10,... | collective-permute-start | bytes 1597448 | tf_op jit(solution)/shard_map/ppermute | solution.py:640
  10.2 2.8 %collective-permute-start.2 = (f32[696,128]{1,0:T(8,128)S(1)}, f32[696,128]{1,0:T(8,128)S(1)}, u32[]{:S(2)}, u32[]{:S(2)}) collective-permute-start(f32[696,128]{1,0:T(8,128)S(1)} %get-tuple-element.69), channel_id=1, source_target_pairs={{0,1},{1,0},{2,3},{3,2},{4,8},{5,9},{6,10},{7,11},{8,4},{9,5},{10,... | collective-permute-start | bytes 1069064 | tf_op jit(solution)/shard_map/ppermute | solution.py:640
  12.9 2.3 %collective-permute-start.3 = (f32[256,128]{1,0:T(8,128)S(1)}, f32[256,128]{1,0:T(8,128)S(1)}, u32[]{:S(2)}, u32[]{:S(2)}) collective-permute-start(f32[256,128]{1,0:T(8,128)S(1)} %get-tuple-element.70), channel_id=1, source_target_pairs={{0,1},{1,0},{2,3},{3,2},{4,8},{5,9},{6,10},{7,11},{8,4},{9,5},{10,... | collective-permute-start | bytes 393224 | tf_op jit(solution)/shard_map/ppermute | solution.py:640
  15.2 0.0 copy-done
  15.2 0.0 copy-done.1
  15.2 0.0 copy-done.2
  15.2 0.1 select_reduce_fusion
  15.3 0.5 %shard_map.124 = (f32[3,7,40,128]{3,2,1,0:T(8,128)S(1)}, f32[3,7,40,128]{3,2,1,0:T(8,128)S(1)}, f32[3,7,40,128]{3,2,1,0:T(8,128)S(1)}) custom-call(f32[3,8,32,128]{3,2,1,0:T(8,128)S(1)} %get-tuple-element.47.d, f32[3,8,32,128]{3,2,1,0:T(8,128)S(1)} %get-tuple-element.48.e, f32[3,8,32,128]{3,2,1,0:T(8,128)S(1)} %get-tuple-element.49.h, ...), custom_call_target="tpu_custom_call" | custom-call | tf_op jit(solution)/shard_map/pallas_call | solution.py:644
  15.9 0.0 collective-permute-done.4.cc
  15.9 0.6 %shard_map.125 = (f32[3,8,32,128]{3,2,1,0:T(8,128)S(1)}, f32[3,8,32,128]{3,2,1,0:T(8,128)S(1)}, f32[3,8,32,128]{3,2,1,0:T(8,128)S(1)}, f32[2,32,128]{2,1,0:T(8,128)S(1)}, f32[2,32,128]{2,1,0:T(8,128)S(1)}) custom-call(f32[3,8,32,128]{3,2,1,0:T(8,128)S(1)} %get-tuple-element.47.d, f32[3,8,32,128]{3,2,1,0:T(8,128)S(1)} %get-tuple-element.48.e, ...), custom_call_target="tpu_custom_call" | custom-call | tf_op jit(solution)/shard_map/pallas_call | solution.py:644
  16.4 3.8 %collective-permute-done.2.ca = f32[696,128]{1,0:T(8,128)S(1)} collective-permute-done((f32[696,128]{1,0:T(8,128)S(1)}, f32[696,128]{1,0:T(8,128)S(1)}, u32[]{:S(2)}, u32[]{:S(2)}) %collective-permute-start.2) | collective-permute-done | bytes 356384 | tf_op jit(solution)/shard_map/ppermute | solution.py:640
  20.3 1.6 %shard_map.126 = (f32[3,8,32,128]{3,2,1,0:T(8,128)}, f32[3,8,32,128]{3,2,1,0:T(8,128)}, f32[3,8,32,128]{3,2,1,0:T(8,128)}, f32[8,32,128]{2,1,0:T(8,128)}, f32[8,...) custom-call(f32[3,8,32,128]{3,2,1,0:T(8,128)S(1)} %get-tuple-element, ...), custom_call_target="tpu_custom_call" | custom-call | tf_op jit(solution)/shard_map/pallas_call | solution.py:644
  21.9 0.0 collective-permute-done.3.cb
  21.9 1.9 %shard_map.127 = (f32[3,8,32,128]{3,2,1,0:T(8,128)}, f32[3,8,32,128]{3,2,1,0:T(8,128)}, f32[3,8,32,128]{3,2,1,0:T(8,128)}, f32[8,32,128]{2,1,0:T(8,128)}, f32[8,32,128]{2,1,0:T(8,128)}) custom-call(f32[3,8,32,128]{3,2,1,0:T(8,128)S(1)} %get-tuple-element.47.d, ...), custom_call_target="tpu_custom_call", output_to_operand_aliasing={{0}: (21, {}), {1}: (22, {}), {2}: (23, {}), {3}: (24, {}),... | custom-call | tf_op jit(solution)/shard_map/pallas_call | solution.py:644
  (1 shorter events, 0.0 us)
Async XLA Ops:
  2.0 5.0 %collective-permute-start = (f32[304,128]{1,0:T(8,128)S(1)}, f32[304,128]{1,0:T(8,128)S(1)}, u32[]{:S(2)}, u32[]{:S(2)}) collective-permute-start(f32[304,128]{1,0:T(8,128)S(1)} %get-tuple-element.52), channel_id=1, source_target_pairs={{0,1},{1,0},{2,3},{3,2},{4,5},{5,4},{6,7},{7,6},{8,9},{9,8},{10,11... | collective-permute-start | bytes 466952 | tf_op jit(solution)/shard_map/ppermute | solution.py:640
  2.2 5.6 %collective-permute-start.1 = (f32[304,128]{1,0:T(8,128)S(1)}, f32[304,128]{1,0:T(8,128)S(1)}, u32[]{:S(2)}, u32[]{:S(2)}) collective-permute-start(f32[304,128]{1,0:T(8,128)S(1)} %get-tuple-element.53), channel_id=1, source_target_pairs={{0,4},{1,2},{2,1},{3,7},{4,0},{5,6},{6,5},{7,3},{8,12},{9,10},{10,... | collective-permute-start | bytes 466952 | tf_op jit(solution)/shard_map/ppermute | solution.py:640
  4.9 10.3 %copy-start = (s32[2,32,128]{2,1,0:T(8,128)S(1)}, s32[2,32,128]{2,1,0:T(8,128)}, u32[]{:S(2)}) copy-start(s32[2,32,128]{2,1,0:T(8,128)} %param.13) | copy-start | bytes 98308
  4.9 10.3 %copy-start.1 = (f32[8]{0:T(128)S(1)}, f32[8]{0:T(128)}, u32[]{:S(2)}) copy-start(f32[8]{0:T(128)} %param.15) | copy-start | bytes 100
  4.9 10.3 %copy-start.2 = (f32[8]{0:T(128)S(1)}, f32[8]{0:T(128)}, u32[]{:S(2)}) copy-start(f32[8]{0:T(128)} %param.14) | copy-start | bytes 100
  8.5 7.4 %collective-permute-start.4 = (f32[26,40,128]{2,1,0:T(8,128)S(1)}, f32[26,40,128]{2,1,0:T(8,128)S(1)}, u32[]{:S(2)}, u32[]{:S(2)}) collective-permute-start(f32[26,40,128]{2,1,0:T(8,128)S(1)} %get-tuple-element.71), channel_id=1, source_target_pairs={{0,4},{1,5},{2,6},{3,7},{4,0},{5,1},{6,2},{7,3},{8,12},{9,13},{10,... | collective-permute-start | bytes 1597448 | tf_op jit(solution)/shard_map/ppermute | solution.py:640
  10.2 10.1 %collective-permute-start.2 = (f32[696,128]{1,0:T(8,128)S(1)}, f32[696,128]{1,0:T(8,128)S(1)}, u32[]{:S(2)}, u32[]{:S(2)}) collective-permute-start(f32[696,128]{1,0:T(8,128)S(1)} %get-tuple-element.69), channel_id=1, source_target_pairs={{0,1},{1,0},{2,3},{3,2},{4,8},{5,9},{6,10},{7,11},{8,4},{9,5},{10,... | collective-permute-start | bytes 1069064 | tf_op jit(solution)/shard_map/ppermute | solution.py:640
  12.9 9.0 %collective-permute-start.3 = (f32[256,128]{1,0:T(8,128)S(1)}, f32[256,128]{1,0:T(8,128)S(1)}, u32[]{:S(2)}, u32[]{:S(2)}) collective-permute-start(f32[256,128]{1,0:T(8,128)S(1)} %get-tuple-element.70), channel_id=1, source_target_pairs={{0,1},{1,0},{2,3},{3,2},{4,8},{5,9},{6,10},{7,11},{8,4},{9,5},{10,... | collective-permute-start | bytes 393224 | tf_op jit(solution)/shard_map/ppermute | solution.py:640

commit v12 on v10

--- a/solution.py
+++ b/solution.py
@@ -547,7 +547,7 @@
 
 def far(d, e, h, eps, chi, xt, fd, fe, fh, gd, ge, gh, ca, cb, *rest):
     nd, ne, nh, neps, nchi, ie, ih, od, oe, oh, oeps, ochi = rest[:12]
-    outs, state, edge, sems = rest[12:17], rest[17:20], rest[20:23], rest[23]
+    outs, state, staged, sems = rest[12:17], rest[17:20], rest[20:23], rest[23]
     half = halo_row() < XH
     gz, _, _, _ = position()
 
@@ -568,11 +568,9 @@
             copies.append(pltpu.make_async_copy(source, target, sems.at[len(copies)]))
             copies[-1].start()
 
-        here, there = (pl.ds(ADVANCE, KEPT), pl.ds(0, ADVANCE)) if high else (pl.ds(0, ADVANCE), pl.ds(ADVANCE, KEPT))
-        middle_rows = pl.ds(8, 16)
-        for a, b, out in zip((nd, ne, nh), (od, oe, oh), outs):
+        there = pl.ds(0, ADVANCE) if high else pl.ds(ADVANCE, KEPT)
+        for a, out in zip((nd, ne, nh), outs):
             send(a.at[:, there], out.at[:, there])
-            send(b.at[:, here, middle_rows], out.at[:, here, middle_rows])
         for a, new, out in zip((eps, chi), (oeps, ochi) if high else (neps, nchi), outs[3:]):
             send(a.at[pl.ds(ADVANCE, KEPT)], out.at[pl.ds(0, KEPT)])
             send(new, out.at[pl.ds(KEPT, ADVANCE)])
@@ -585,8 +583,9 @@
         none = jnp.zeros((16, NY), jnp.float32)
 
         def result(k, c, o, v):
-            edge[k][c, o, 0:8] = v[0:8]
-            edge[k][c, o, 8:16] = v[24:32]
+            staged[k][c, o, 0:8] = v[0:8]
+            staged[k][c, o, 8:24] = (od, oe, oh)[k][c, o, 8:24]
+            staged[k][c, o, 24:32] = v[24:32]
 
         def put(c, p, v, n):
             k, at = c // 3, (c % 3, p + 2)
@@ -604,9 +603,11 @@
                 grid.hold(c, p, read, n)
 
         def done(o):
-            for k in range(3):
-                for a, b in ((0, 0), (8, 24)):
-                    send(edge[k].at[:, pl.ds(o, 1), pl.ds(a, 8)], outs[k].at[:, pl.ds(o, 1), pl.ds(b, 8)])
+            batch = {4: 3, 7: 3, 1: 2}.get(o)
+            if batch:
+                some = pl.ds(o + 1 - batch, batch)
+                for k in range(3):
+                    send(staged[k].at[:, some], outs[k].at[:, some])
 
         chain(grid, high, put, functools.partial(result, 2), done)
         for c in copies:
@@ -683,7 +684,7 @@
         [pltpu.VMEM((3, 13, NXL, NY), jnp.float32)],
         vmem=16,
     )
-    thin = [pltpu.VMEM((3, 13, EDGE, NY), jnp.float32)] * 3 + [pltpu.VMEM((3, NZL, 16, NY), jnp.float32)] * 3
+    thin = [pltpu.VMEM((3, 13, EDGE, NY), jnp.float32)] * 3 + [pltpu.VMEM(field.shape, jnp.float32)] * 3
     return call(
         far,
         [*fields, xt, *frames, *more, ca, cb, *made, *inside],

time: 23.9 us -> 24.3 us (1.017)
  Pallas kernels: 6.42 us -> 6.73 us
    pallas_call x9, Pallas kernels: 6.42 us -> 6.73 us  [call(): pl.pallas_call(body, out_shape=out_shape, in_specs=[VM] * len(inputs) if...]
where the time goes in v12:
time: 24.3 us; the launch traced here: 24 us
  starting transfers between devices  9.1 us (37%)
  waiting for transfers between devices  7.31 us (30%)
  Pallas kernels  6.73 us (28%)
  between operations  0.72 us (3%)
    ppermute x5, starting transfers between devices, swapped(): return lax.ppermute(shard, ('gz', 'gx'), moves)  9.1 us
    ppermute x5, waiting for transfers between devices, swapped(): return lax.ppermute(shard, ('gz', 'gx'), moves)  7.31 us
    pallas_call x9, Pallas kernels, call(): pl.pallas_call(body, out_shape=out_shape, in_specs=[VM] * len(inputs) if...  6.73 us
  transfers between devices with their start and end apart: 5, of which 3 were waited for; matrix products, arithmetic and copies ran while one was open for 0% of the time, Pallas kernels for 10%

profile of v12, /device:TPU:111, one launch (start us, length us, event | category | flops | bytes accessed | tf_op | source)
XLA Modules:
  0.0 24.0 jit_solution(14324784248160992224)
XLA Ops:
  0.6 1.4 %shard_map.119 = (f32[3,8,32,128]{3,2,1,0:T(8,128)S(1)}, f32[3,8,32,128]{3,2,1,0:T(8,128)S(1)}, f32[3,8,32,128]{3,2,1,0:T(8,128)S(1)}, f32[8,32,128]{2,1,0:T(8,1...) custom-call(f32[3,8,32,128]{3,2,1,0:T(8,128)} %d.1, f32[3,8,32,128]{3,2,1,0:T(8,128)} %e.1, ...), custom_call_target="tpu_custom_call" | custom-call | tf_op jit(solution)/shard_map/pallas_call | solution.py:636
  2.0 0.3 %collective-permute-start = (f32[304,128]{1,0:T(8,128)S(1)}, f32[304,128]{1,0:T(8,128)S(1)}, u32[]{:S(2)}, u32[]{:S(2)}) collective-permute-start(f32[304,128]{1,0:T(8,128)S(1)} %get-tuple-element.47), channel_id=1, source_target_pairs={{0,1},{1,0},{2,3},{3,2},{4,5},{5,4},{6,7},{7,6},{8,9},{9,8},{10,11... | collective-permute-start | bytes 466952 | tf_op jit(solution)/shard_map/ppermute | solution.py:632
  2.2 2.1 %collective-permute-start.1 = (f32[304,128]{1,0:T(8,128)S(1)}, f32[304,128]{1,0:T(8,128)S(1)}, u32[]{:S(2)}, u32[]{:S(2)}) collective-permute-start(f32[304,128]{1,0:T(8,128)S(1)} %get-tuple-element.48), channel_id=1, source_target_pairs={{0,4},{1,2},{2,1},{3,7},{4,0},{5,6},{6,5},{7,3},{8,12},{9,10},{10,... | collective-permute-start | bytes 466952 | tf_op jit(solution)/shard_map/ppermute | solution.py:632
  4.4 0.5 %shard_map.122 = (f32[3,5,32,128]{3,2,1,0:T(8,128)S(1)}, f32[3,5,32,128]{3,2,1,0:T(8,128)S(1)}, f32[3,5,32,128]{3,2,1,0:T(8,128)S(1)}, f32[2,32,128]{2,1,0:T(8,128)S(1)}, f32[696,128]{1,0:T(8,128)S(1)}) custom-call(f32[3,8,32,128]{3,2,1,0:T(8,128)S(1)} %get-tuple-element.42.d, f32[3,8,32,128]{3,2,1,0:T(8,128)S(1)} %get-tuple-element.43.e, ...), custom_call_target="tpu_custom_call" | custom-call | tf_op jit(solution)/shard_map/pallas_call | solution.py:636
  4.9 0.0 copy-start
  4.9 0.0 copy-start.1
  4.9 0.0 copy-start.2
  5.0 2.0 %collective-permute-done.ra = f32[304,128]{1,0:T(8,128)S(1)} collective-permute-done((f32[304,128]{1,0:T(8,128)S(1)}, f32[304,128]{1,0:T(8,128)S(1)}, u32[]{:S(2)}, u32[]{:S(2)}) %collective-permute-start) | collective-permute-done | bytes 155680 | tf_op jit(solution)/shard_map/ppermute | solution.py:632
  7.0 0.8 %collective-permute-done.1.rb = f32[304,128]{1,0:T(8,128)S(1)} collective-permute-done((f32[304,128]{1,0:T(8,128)S(1)}, f32[304,128]{1,0:T(8,128)S(1)}, u32[]{:S(2)}, u32[]{:S(2)}) %collective-permute-start.1) | collective-permute-done | bytes 155680 | tf_op jit(solution)/shard_map/ppermute | solution.py:632
  7.8 0.2 shard_map.121
  8.0 0.5 %shard_map.123 = (f32[3,5,40,128]{3,2,1,0:T(8,128)S(1)}, f32[3,5,40,128]{3,2,1,0:T(8,128)S(1)}, f32[3,5,40,128]{3,2,1,0:T(8,128)S(1)}, f32[26,40,128]{2,1,0:T(8,128)S(1)}) custom-call(f32[3,8,32,128]{3,2,1,0:T(8,128)S(1)} %get-tuple-element.42.d, f32[3,8,32,128]{3,2,1,0:T(8,128)S(1)} %get-tuple-element.43.e, f32[3,8,32,128]{3,2,1,0:T(8,128)S(1)} %get-tuple-element.44.h, ...), custom_call_target="tpu_custom_call" | custom-call | tf_op jit(solution)/shard_map/pallas_call | solution.py:636
  8.5 1.7 %collective-permute-start.4 = (f32[26,40,128]{2,1,0:T(8,128)S(1)}, f32[26,40,128]{2,1,0:T(8,128)S(1)}, u32[]{:S(2)}, u32[]{:S(2)}) collective-permute-start(f32[26,40,128]{2,1,0:T(8,128)S(1)} %get-tuple-element.66), channel_id=1, source_target_pairs={{0,4},{1,5},{2,6},{3,7},{4,0},{5,1},{6,2},{7,3},{8,12},{9,13},{10,... | collective-permute-start | bytes 1597448 | tf_op jit(solution)/shard_map/ppermute | solution.py:632
  10.2 2.8 %collective-permute-start.2 = (f32[696,128]{1,0:T(8,128)S(1)}, f32[696,128]{1,0:T(8,128)S(1)}, u32[]{:S(2)}, u32[]{:S(2)}) collective-permute-start(f32[696,128]{1,0:T(8,128)S(1)} %get-tuple-element.64), channel_id=1, source_target_pairs={{0,1},{1,0},{2,3},{3,2},{4,8},{5,9},{6,10},{7,11},{8,4},{9,5},{10,... | collective-permute-start | bytes 1069064 | tf_op jit(solution)/shard_map/ppermute | solution.py:632
  12.9 2.3 %collective-permute-start.3 = (f32[256,128]{1,0:T(8,128)S(1)}, f32[256,128]{1,0:T(8,128)S(1)}, u32[]{:S(2)}, u32[]{:S(2)}) collective-permute-start(f32[256,128]{1,0:T(8,128)S(1)} %get-tuple-element.65), channel_id=1, source_target_pairs={{0,1},{1,0},{2,3},{3,2},{4,8},{5,9},{6,10},{7,11},{8,4},{9,5},{10,... | collective-permute-start | bytes 393224 | tf_op jit(solution)/shard_map/ppermute | solution.py:632
  15.2 0.0 copy-done
  15.2 0.0 copy-done.1
  15.2 0.0 copy-done.2
  15.2 0.1 select_reduce_fusion
  15.3 0.5 %shard_map.124 = (f32[3,7,40,128]{3,2,1,0:T(8,128)S(1)}, f32[3,7,40,128]{3,2,1,0:T(8,128)S(1)}, f32[3,7,40,128]{3,2,1,0:T(8,128)S(1)}) custom-call(f32[3,8,32,128]{3,2,1,0:T(8,128)S(1)} %get-tuple-element.42.d, f32[3,8,32,128]{3,2,1,0:T(8,128)S(1)} %get-tuple-element.43.e, f32[3,8,32,128]{3,2,1,0:T(8,128)S(1)} %get-tuple-element.44.h, ...), custom_call_target="tpu_custom_call" | custom-call | tf_op jit(solution)/shard_map/pallas_call | solution.py:636
  15.8 4.4 %collective-permute-done.2.ca = f32[696,128]{1,0:T(8,128)S(1)} collective-permute-done((f32[696,128]{1,0:T(8,128)S(1)}, f32[696,128]{1,0:T(8,128)S(1)}, u32[]{:S(2)}, u32[]{:S(2)}) %collective-permute-start.2) | collective-permute-done | bytes 356384 | tf_op jit(solution)/shard_map/ppermute | solution.py:632
  20.3 0.9 %shard_map.126 = (f32[3,3,13,32,128]{4,3,2,1,0:T(8,128)S(1)}, f32[4,3,13,32,128]{4,3,2,1,0:T(8,128)S(1)}, f32[3,8,32,128]{3,2,1,0:T(8,128)S(1)}, f32[3,8,32,128]...) custom-call(f32[3,8,32,128]{3,2,1,0:T(8,128)S(1)} %get-tuple-element.42.d, ...), custom_call_target="tpu_custom_call" | custom-call | tf_op jit(solution)/shard_map/pallas_call | solution.py:636
  21.2 0.0 collective-permute-done.4.cc
  21.2 0.6 %shard_map.125 = (f32[3,8,32,128]{3,2,1,0:T(8,128)S(1)}, f32[3,8,32,128]{3,2,1,0:T(8,128)S(1)}, f32[3,8,32,128]{3,2,1,0:T(8,128)S(1)}, f32[2,32,128]{2,1,0:T(8,128)S(1)}, f32[2,32,128]{2,1,0:T(8,128)S(1)}) custom-call(f32[3,8,32,128]{3,2,1,0:T(8,128)S(1)} %get-tuple-element.42.d, f32[3,8,32,128]{3,2,1,0:T(8,128)S(1)} %get-tuple-element.43.e, ...), custom_call_target="tpu_custom_call" | custom-call | tf_op jit(solution)/shard_map/pallas_call | solution.py:636
  21.8 0.0 collective-permute-done.3.cb
  21.8 2.2 %shard_map.127 = (f32[3,8,32,128]{3,2,1,0:T(8,128)}, f32[3,8,32,128]{3,2,1,0:T(8,128)}, f32[3,8,32,128]{3,2,1,0:T(8,128)}, f32[8,32,128]{2,1,0:T(8,128)}, f32[8,32,128]{2,1,0:T(8,128)}) custom-call(f32[3,8,32,128]{3,2,1,0:T(8,128)S(1)} %get-tuple-element.42.d, f32[3,8,32,128]{3,2,1,0:T(8,128)S(1)} %get-tuple-element.43.e, ...), custom_call_target="tpu_custom_call" | custom-call | tf_op jit(solution)/shard_map/pallas_call | solution.py:636
  (1 shorter events, 0.0 us)
Async XLA Ops:
  2.0 5.0 %collective-permute-start = (f32[304,128]{1,0:T(8,128)S(1)}, f32[304,128]{1,0:T(8,128)S(1)}, u32[]{:S(2)}, u32[]{:S(2)}) collective-permute-start(f32[304,128]{1,0:T(8,128)S(1)} %get-tuple-element.47), channel_id=1, source_target_pairs={{0,1},{1,0},{2,3},{3,2},{4,5},{5,4},{6,7},{7,6},{8,9},{9,8},{10,11... | collective-permute-start | bytes 466952 | tf_op jit(solution)/shard_map/ppermute | solution.py:632
  2.2 5.6 %collective-permute-start.1 = (f32[304,128]{1,0:T(8,128)S(1)}, f32[304,128]{1,0:T(8,128)S(1)}, u32[]{:S(2)}, u32[]{:S(2)}) collective-permute-start(f32[304,128]{1,0:T(8,128)S(1)} %get-tuple-element.48), channel_id=1, source_target_pairs={{0,4},{1,2},{2,1},{3,7},{4,0},{5,6},{6,5},{7,3},{8,12},{9,10},{10,... | collective-permute-start | bytes 466952 | tf_op jit(solution)/shard_map/ppermute | solution.py:632
  4.9 10.3 %copy-start = (s32[2,32,128]{2,1,0:T(8,128)S(1)}, s32[2,32,128]{2,1,0:T(8,128)}, u32[]{:S(2)}) copy-start(s32[2,32,128]{2,1,0:T(8,128)} %param.13) | copy-start | bytes 98308
  4.9 10.3 %copy-start.1 = (f32[8]{0:T(128)S(1)}, f32[8]{0:T(128)}, u32[]{:S(2)}) copy-start(f32[8]{0:T(128)} %param.15) | copy-start | bytes 100
  4.9 10.3 %copy-start.2 = (f32[8]{0:T(128)S(1)}, f32[8]{0:T(128)}, u32[]{:S(2)}) copy-start(f32[8]{0:T(128)} %param.14) | copy-start | bytes 100
  8.5 12.7 %collective-permute-start.4 = (f32[26,40,128]{2,1,0:T(8,128)S(1)}, f32[26,40,128]{2,1,0:T(8,128)S(1)}, u32[]{:S(2)}, u32[]{:S(2)}) collective-permute-start(f32[26,40,128]{2,1,0:T(8,128)S(1)} %get-tuple-element.66), channel_id=1, source_target_pairs={{0,4},{1,5},{2,6},{3,7},{4,0},{5,1},{6,2},{7,3},{8,12},{9,13},{10,... | collective-permute-start | bytes 1597448 | tf_op jit(solution)/shard_map/ppermute | solution.py:632
  10.2 10.1 %collective-permute-start.2 = (f32[696,128]{1,0:T(8,128)S(1)}, f32[696,128]{1,0:T(8,128)S(1)}, u32[]{:S(2)}, u32[]{:S(2)}) collective-permute-start(f32[696,128]{1,0:T(8,128)S(1)} %get-tuple-element.64), channel_id=1, source_target_pairs={{0,1},{1,0},{2,3},{3,2},{4,8},{5,9},{6,10},{7,11},{8,4},{9,5},{10,... | collective-permute-start | bytes 1069064 | tf_op jit(solution)/shard_map/ppermute | solution.py:632
  12.9 8.9 %collective-permute-start.3 = (f32[256,128]{1,0:T(8,128)S(1)}, f32[256,128]{1,0:T(8,128)S(1)}, u32[]{:S(2)}, u32[]{:S(2)}) collective-permute-start(f32[256,128]{1,0:T(8,128)S(1)} %get-tuple-element.65), channel_id=1, source_target_pairs={{0,1},{1,0},{2,3},{3,2},{4,8},{5,9},{6,10},{7,11},{8,4},{9,5},{10,... | collective-permute-start | bytes 393224 | tf_op jit(solution)/shard_map/ppermute | solution.py:632

commit v13 on v10

--- a/solution.py
+++ b/solution.py
@@ -46,9 +46,19 @@
     LO[_thin.pop(0)] = _k
 HI_AT = {k: i for i, k in enumerate(HI)}
 LO_AT = {k: i for i, k in enumerate(LO) if k}
-NS, NR = len(HI), len(RAW)
-NEW_AT = -(-sum(WIDTH) // 8) * 8
-LATE = NEW_AT + 8 * (NS - NR)
+NS = len(HI)
+
+
+def late_rows(comp, p):
+    if comp < DP:
+        return 0
+    return p if comp == INV else p + 1
+
+
+LATE_N = [late_rows(*k) for k in HI]
+EARLY_AT = [24 * NS + sum(8 - 2 * n for n in LATE_N[:i]) for i in range(NS + 1)]
+LATE_AT = [sum(WIDTH) + sum(2 * n for n in LATE_N[:i]) for i in range(NS + 1)]
+EARLY_ROWS, LATE_ROWS = (-(-at[-1] // 8) * 8 for at in (EARLY_AT, LATE_AT))
 
 FOUR, THREE = (E, E + 1, E + 2, H + 1, H + 2), (D, D + 1, D + 2, H, EPS, CHI)
 NF = len(FOUR) * NZL * 4
@@ -274,8 +284,8 @@
         v = v * keep
         out[24 * i : 24 * i + 8] = jnp.where(half, v[24:32], v[0:8])
         out[24 * i + 8 : 24 * i + 24] = v[8:24]
-        if i < NR:
-            out[24 * NS + 8 * i : 24 * NS + 8 * i + 8] = jnp.where(half, v[0:8], v[24:32])
+        n = LATE_N[i]
+        out[EARLY_AT[i] : EARLY_AT[i + 1]] = jnp.where(half, v[0:8], v[24:32])[n : 8 - n]
 
 
 def edge_grid(inside, fields, tile):
@@ -329,9 +339,11 @@
             for a, b in runs:
                 cross[at : at + b - a] = v[8 + a : 8 + b]
                 at += b - a
-            if i >= NR:
-                at = NEW_AT + 8 * (i - NR)
-                cross[at : at + 8] = jnp.where(half, v[16:24], v[0:8])
+            n = LATE_N[i]
+            if n:
+                at = LATE_AT[i]
+                cross[at : at + n] = v[16 : 16 + n]
+                cross[at + n : at + 2 * n] = v[8 - n : 8]
 
     @pl.when(lax.rem(gz, 2) == 0)
     def _():
@@ -504,7 +516,7 @@
 
     def read(i):
         m = ca[24 * i : 24 * i + 8]
-        x = ca[24 * NS + 8 * i : 24 * NS + 8 * i + 8] if i < NR else m
+        x = m if LATE_N[i] else ca[EARLY_AT[i] : EARLY_AT[i + 1]]
         return rows(jnp.where(half, x, m), ca[24 * i + 8 : 24 * i + 24], jnp.where(half, m, x))
 
     def side(high):
@@ -553,7 +565,9 @@
 
     def cross(chosen, i):
         m = ca[24 * i : 24 * i + 8]
-        x = ca[24 * NS + 8 * i : 24 * NS + 8 * i + 8] if i < NR else cb[NEW_AT + 8 * (i - NR) : NEW_AT + 8 * (i - NR) + 8]
+        x, n = ca[EARLY_AT[i] : EARLY_AT[i + 1]], LATE_N[i]
+        if n:
+            x = rows(cb[LATE_AT[i] : LATE_AT[i] + n], x, cb[LATE_AT[i] + n : LATE_AT[i] + 2 * n])
         at, kept = HALO_AT[i], list(chosen[WIDTH[i]])
         v = cb[at : at + WIDTH[i]]
         if len(kept) < 8:
@@ -655,12 +669,12 @@
     )
     ra, rb = swapped(ya, "gx", 0), swapped(yb, "gx", 1)
     lo = shape(2, NXL, NY)
-    *inside, za = call(inner, fields, (*[shape(3, 5, NXL, NY)] * 3, lo, shape(24 * NS + 8 * NR, NY)))
+    *inside, za = call(inner, fields, (*[shape(3, 5, NXL, NY)] * 3, lo, shape(EARLY_ROWS, NY)))
     ca = swapped(za, "gz", 1)
     (edge,) = call(mark, [], (shape(8, NY),))
     thin = [(3, 5, EDGE, NY)] * 3 + [(2, EDGE, NY)]
     xt, *outside, zb = call(
-        edges, [*fields, ra, rb, edge], (shape(11, NZL, 8, NY), *[shape(*t) for t in thin], shape(LATE, NY))
+        edges, [*fields, ra, rb, edge], (shape(11, NZL, 8, NY), *[shape(*t) for t in thin], shape(LATE_ROWS, NY))
     )
     cb = swapped(zb, "gz", 1)
     coming = lookup(classes, eps_table), lookup(classes, chi_table)

time: 23.9 us -> 24.4 us (1.021)
  waiting for transfers between devices: 7.31 us -> 7.74 us
    ppermute x5, waiting for transfers between devices: 7.31 us -> 7.74 us  [swapped(): return lax.ppermute(shard, ('gz', 'gx'), moves)]
where the time goes in v13:
time: 24.4 us; the launch traced here: 24.1 us
  starting transfers between devices  9.1 us (37%)
  waiting for transfers between devices  7.74 us (32%)
  Pallas kernels  6.42 us (26%)
  between operations  0.72 us (3%)
    ppermute x5, starting transfers between devices, swapped(): return lax.ppermute(shard, ('gz', 'gx'), moves)  9.1 us
    ppermute x5, waiting for transfers between devices, swapped(): return lax.ppermute(shard, ('gz', 'gx'), moves)  7.74 us
    pallas_call x9, Pallas kernels, call(): pl.pallas_call(body, out_shape=out_shape, in_specs=[VM] * len(inputs) if...  6.42 us
  transfers between devices with their start and end apart: 5, of which 3 were waited for; matrix products, arithmetic and copies ran while one was open for 0% of the time, Pallas kernels for 10%

profile of v13, /device:TPU:111, one launch (start us, length us, event | category | flops | bytes accessed | tf_op | source)
XLA Modules:
  0.0 24.1 jit_solution(3165096939302073807)
XLA Ops:
  0.6 1.4 %shard_map.119 = (f32[3,8,32,128]{3,2,1,0:T(8,128)S(1)}, f32[3,8,32,128]{3,2,1,0:T(8,128)S(1)}, f32[3,8,32,128]{3,2,1,0:T(8,128)S(1)}, f32[8,32,128]{2,1,0:T(8,1...) custom-call(f32[3,8,32,128]{3,2,1,0:T(8,128)} %d.1, f32[3,8,32,128]{3,2,1,0:T(8,128)} %e.1, ...), custom_call_target="tpu_custom_call" | custom-call | tf_op jit(solution)/shard_map/pallas_call | solution.py:649
  2.0 0.3 %collective-permute-start = (f32[304,128]{1,0:T(8,128)S(1)}, f32[304,128]{1,0:T(8,128)S(1)}, u32[]{:S(2)}, u32[]{:S(2)}) collective-permute-start(f32[304,128]{1,0:T(8,128)S(1)} %get-tuple-element.47), channel_id=1, source_target_pairs={{0,1},{1,0},{2,3},{3,2},{4,5},{5,4},{6,7},{7,6},{8,9},{9,8},{10,11... | collective-permute-start | bytes 466952 | tf_op jit(solution)/shard_map/ppermute | solution.py:645
  2.2 2.1 %collective-permute-start.1 = (f32[304,128]{1,0:T(8,128)S(1)}, f32[304,128]{1,0:T(8,128)S(1)}, u32[]{:S(2)}, u32[]{:S(2)}) collective-permute-start(f32[304,128]{1,0:T(8,128)S(1)} %get-tuple-element.48), channel_id=1, source_target_pairs={{0,4},{1,2},{2,1},{3,7},{4,0},{5,6},{6,5},{7,3},{8,12},{9,10},{10,... | collective-permute-start | bytes 466952 | tf_op jit(solution)/shard_map/ppermute | solution.py:645
  4.4 0.5 %shard_map.122 = (f32[3,5,32,128]{3,2,1,0:T(8,128)S(1)}, f32[3,5,32,128]{3,2,1,0:T(8,128)S(1)}, f32[3,5,32,128]{3,2,1,0:T(8,128)S(1)}, f32[2,32,128]{2,1,0:T(8,128)S(1)}, f32[776,128]{1,0:T(8,128)S(1)}) custom-call(f32[3,8,32,128]{3,2,1,0:T(8,128)S(1)} %get-tuple-element.42.d, f32[3,8,32,128]{3,2,1,0:T(8,128)S(1)} %get-tuple-element.43.e, ...), custom_call_target="tpu_custom_call" | custom-call | tf_op jit(solution)/shard_map/pallas_call | solution.py:649
  4.9 0.0 copy-start
  4.9 0.0 copy-start.1
  4.9 0.0 copy-start.2
  5.0 2.0 %collective-permute-done.ra = f32[304,128]{1,0:T(8,128)S(1)} collective-permute-done((f32[304,128]{1,0:T(8,128)S(1)}, f32[304,128]{1,0:T(8,128)S(1)}, u32[]{:S(2)}, u32[]{:S(2)}) %collective-permute-start) | collective-permute-done | bytes 155680 | tf_op jit(solution)/shard_map/ppermute | solution.py:645
  7.0 0.8 %collective-permute-done.1.rb = f32[304,128]{1,0:T(8,128)S(1)} collective-permute-done((f32[304,128]{1,0:T(8,128)S(1)}, f32[304,128]{1,0:T(8,128)S(1)}, u32[]{:S(2)}, u32[]{:S(2)}) %collective-permute-start.1) | collective-permute-done | bytes 155680 | tf_op jit(solution)/shard_map/ppermute | solution.py:645
  7.8 0.2 shard_map.121
  8.0 0.5 %shard_map.123 = (f32[3,5,40,128]{3,2,1,0:T(8,128)S(1)}, f32[3,5,40,128]{3,2,1,0:T(8,128)S(1)}, f32[3,5,40,128]{3,2,1,0:T(8,128)S(1)}, f32[26,40,128]{2,1,0:T(8,128)S(1)}) custom-call(f32[3,8,32,128]{3,2,1,0:T(8,128)S(1)} %get-tuple-element.42.d, f32[3,8,32,128]{3,2,1,0:T(8,128)S(1)} %get-tuple-element.43.e, f32[3,8,32,128]{3,2,1,0:T(8,128)S(1)} %get-tuple-element.44.h, ...), custom_call_target="tpu_custom_call" | custom-call | tf_op jit(solution)/shard_map/pallas_call | solution.py:649
  8.5 1.7 %collective-permute-start.4 = (f32[26,40,128]{2,1,0:T(8,128)S(1)}, f32[26,40,128]{2,1,0:T(8,128)S(1)}, u32[]{:S(2)}, u32[]{:S(2)}) collective-permute-start(f32[26,40,128]{2,1,0:T(8,128)S(1)} %get-tuple-element.66), channel_id=1, source_target_pairs={{0,4},{1,5},{2,6},{3,7},{4,0},{5,1},{6,2},{7,3},{8,12},{9,13},{10,... | collective-permute-start | bytes 1597448 | tf_op jit(solution)/shard_map/ppermute | solution.py:645
  10.2 2.8 %collective-permute-start.2 = (f32[776,128]{1,0:T(8,128)S(1)}, f32[776,128]{1,0:T(8,128)S(1)}, u32[]{:S(2)}, u32[]{:S(2)}) collective-permute-start(f32[776,128]{1,0:T(8,128)S(1)} %get-tuple-element.64), channel_id=1, source_target_pairs={{0,1},{1,0},{2,3},{3,2},{4,8},{5,9},{6,10},{7,11},{8,4},{9,5},{10,... | collective-permute-start | bytes 1191944 | tf_op jit(solution)/shard_map/ppermute | solution.py:645
  12.9 2.3 %collective-permute-start.3 = (f32[176,128]{1,0:T(8,128)S(1)}, f32[176,128]{1,0:T(8,128)S(1)}, u32[]{:S(2)}, u32[]{:S(2)}) collective-permute-start(f32[176,128]{1,0:T(8,128)S(1)} %get-tuple-element.65), channel_id=1, source_target_pairs={{0,1},{1,0},{2,3},{3,2},{4,8},{5,9},{6,10},{7,11},{8,4},{9,5},{10,... | collective-permute-start | bytes 270344 | tf_op jit(solution)/shard_map/ppermute | solution.py:645
  15.2 0.0 copy-done
  15.2 0.0 copy-done.1
  15.2 0.0 copy-done.2
  15.2 0.1 select_reduce_fusion
  15.3 0.5 %shard_map.124 = (f32[3,7,40,128]{3,2,1,0:T(8,128)S(1)}, f32[3,7,40,128]{3,2,1,0:T(8,128)S(1)}, f32[3,7,40,128]{3,2,1,0:T(8,128)S(1)}) custom-call(f32[3,8,32,128]{3,2,1,0:T(8,128)S(1)} %get-tuple-element.42.d, f32[3,8,32,128]{3,2,1,0:T(8,128)S(1)} %get-tuple-element.43.e, f32[3,8,32,128]{3,2,1,0:T(8,128)S(1)} %get-tuple-element.44.h, ...), custom_call_target="tpu_custom_call" | custom-call | tf_op jit(solution)/shard_map/pallas_call | solution.py:649
  15.8 4.9 %collective-permute-done.2.ca = f32[776,128]{1,0:T(8,128)S(1)} collective-permute-done((f32[776,128]{1,0:T(8,128)S(1)}, f32[776,128]{1,0:T(8,128)S(1)}, u32[]{:S(2)}, u32[]{:S(2)}) %collective-permute-start.2) | collective-permute-done | bytes 397344 | tf_op jit(solution)/shard_map/ppermute | solution.py:645
  20.7 0.9 %shard_map.126 = (f32[3,3,13,32,128]{4,3,2,1,0:T(8,128)S(1)}, f32[4,3,13,32,128]{4,3,2,1,0:T(8,128)S(1)}, f32[3,8,32,128]{3,2,1,0:T(8,128)S(1)}, f32[3,8,32,128]...) custom-call(f32[3,8,32,128]{3,2,1,0:T(8,128)S(1)} %get-tuple-element.42.d, ...), custom_call_target="tpu_custom_call" | custom-call | tf_op jit(solution)/shard_map/pallas_call | solution.py:649
  21.6 0.0 collective-permute-done.4.cc
  21.6 0.6 %shard_map.125 = (f32[3,8,32,128]{3,2,1,0:T(8,128)S(1)}, f32[3,8,32,128]{3,2,1,0:T(8,128)S(1)}, f32[3,8,32,128]{3,2,1,0:T(8,128)S(1)}, f32[2,32,128]{2,1,0:T(8,128)S(1)}, f32[2,32,128]{2,1,0:T(8,128)S(1)}) custom-call(f32[3,8,32,128]{3,2,1,0:T(8,128)S(1)} %get-tuple-element.42.d, f32[3,8,32,128]{3,2,1,0:T(8,128)S(1)} %get-tuple-element.43.e, ...), custom_call_target="tpu_custom_call" | custom-call | tf_op jit(solution)/shard_map/pallas_call | solution.py:649
  22.2 0.0 collective-permute-done.3.cb
  22.2 1.9 %shard_map.127 = (f32[3,8,32,128]{3,2,1,0:T(8,128)}, f32[3,8,32,128]{3,2,1,0:T(8,128)}, f32[3,8,32,128]{3,2,1,0:T(8,128)}, f32[8,32,128]{2,1,0:T(8,128)}, f32[8,32,128]{2,1,0:T(8,128)}) custom-call(f32[3,8,32,128]{3,2,1,0:T(8,128)S(1)} %get-tuple-element.42.d, f32[3,8,32,128]{3,2,1,0:T(8,128)S(1)} %get-tuple-element.43.e, ...), custom_call_target="tpu_custom_call" | custom-call | tf_op jit(solution)/shard_map/pallas_call | solution.py:649
  (1 shorter events, 0.0 us)
Async XLA Ops:
  2.0 5.0 %collective-permute-start = (f32[304,128]{1,0:T(8,128)S(1)}, f32[304,128]{1,0:T(8,128)S(1)}, u32[]{:S(2)}, u32[]{:S(2)}) collective-permute-start(f32[304,128]{1,0:T(8,128)S(1)} %get-tuple-element.47), channel_id=1, source_target_pairs={{0,1},{1,0},{2,3},{3,2},{4,5},{5,4},{6,7},{7,6},{8,9},{9,8},{10,11... | collective-permute-start | bytes 466952 | tf_op jit(solution)/shard_map/ppermute | solution.py:645
  2.2 5.6 %collective-permute-start.1 = (f32[304,128]{1,0:T(8,128)S(1)}, f32[304,128]{1,0:T(8,128)S(1)}, u32[]{:S(2)}, u32[]{:S(2)}) collective-permute-start(f32[304,128]{1,0:T(8,128)S(1)} %get-tuple-element.48), channel_id=1, source_target_pairs={{0,4},{1,2},{2,1},{3,7},{4,0},{5,6},{6,5},{7,3},{8,12},{9,10},{10,... | collective-permute-start | bytes 466952 | tf_op jit(solution)/shard_map/ppermute | solution.py:645
  4.9 10.3 %copy-start = (s32[2,32,128]{2,1,0:T(8,128)S(1)}, s32[2,32,128]{2,1,0:T(8,128)}, u32[]{:S(2)}) copy-start(s32[2,32,128]{2,1,0:T(8,128)} %param.13) | copy-start | bytes 98308
  4.9 10.3 %copy-start.1 = (f32[8]{0:T(128)S(1)}, f32[8]{0:T(128)}, u32[]{:S(2)}) copy-start(f32[8]{0:T(128)} %param.15) | copy-start | bytes 100
  4.9 10.3 %copy-start.2 = (f32[8]{0:T(128)S(1)}, f32[8]{0:T(128)}, u32[]{:S(2)}) copy-start(f32[8]{0:T(128)} %param.14) | copy-start | bytes 100
  8.5 13.1 %collective-permute-start.4 = (f32[26,40,128]{2,1,0:T(8,128)S(1)}, f32[26,40,128]{2,1,0:T(8,128)S(1)}, u32[]{:S(2)}, u32[]{:S(2)}) collective-permute-start(f32[26,40,128]{2,1,0:T(8,128)S(1)} %get-tuple-element.66), channel_id=1, source_target_pairs={{0,4},{1,5},{2,6},{3,7},{4,0},{5,1},{6,2},{7,3},{8,12},{9,13},{10,... | collective-permute-start | bytes 1597448 | tf_op jit(solution)/shard_map/ppermute | solution.py:645
  10.2 10.6 %collective-permute-start.2 = (f32[776,128]{1,0:T(8,128)S(1)}, f32[776,128]{1,0:T(8,128)S(1)}, u32[]{:S(2)}, u32[]{:S(2)}) collective-permute-start(f32[776,128]{1,0:T(8,128)S(1)} %get-tuple-element.64), channel_id=1, source_target_pairs={{0,1},{1,0},{2,3},{3,2},{4,8},{5,9},{6,10},{7,11},{8,4},{9,5},{10,... | collective-permute-start | bytes 1191944 | tf_op jit(solution)/shard_map/ppermute | solution.py:645
  12.9 9.3 %collective-permute-start.3 = (f32[176,128]{1,0:T(8,128)S(1)}, f32[176,128]{1,0:T(8,128)S(1)}, u32[]{:S(2)}, u32[]{:S(2)}) collective-permute-start(f32[176,128]{1,0:T(8,128)S(1)} %get-tuple-element.65), channel_id=1, source_target_pairs={{0,1},{1,0},{2,3},{3,2},{4,8},{5,9},{6,10},{7,11},{8,4},{9,5},{10,... | collective-permute-start | bytes 270344 | tf_op jit(solution)/shard_map/ppermute | solution.py:645

commit v14 on v13

--- a/solution.py
+++ b/solution.py
@@ -52,6 +52,8 @@
 def late_rows(comp, p):
     if comp < DP:
         return 0
+    if comp < HP:
+        return 4
     return p if comp == INV else p + 1
 
 
@@ -285,7 +287,8 @@
         out[24 * i : 24 * i + 8] = jnp.where(half, v[24:32], v[0:8])
         out[24 * i + 8 : 24 * i + 24] = v[8:24]
         n = LATE_N[i]
-        out[EARLY_AT[i] : EARLY_AT[i + 1]] = jnp.where(half, v[0:8], v[24:32])[n : 8 - n]
+        if n < 4:
+            out[EARLY_AT[i] : EARLY_AT[i + 1]] = jnp.where(half, v[0:8], v[24:32])[n : 8 - n]
 
 
 def edge_grid(inside, fields, tile):
@@ -455,17 +458,16 @@
         grid.hold(comp, p + shift, functools.partial(read, i), level)
 
 
-def chain(grid, high, put, keep, done=lambda o: None):
+def stages(grid, high, put, keep, done=lambda o: None):
     if high:
-        grid.sweep(1, (7,), (7, 8), put)
-        grid.sweep(2, range(6, 9), range(6, 10), put)
-        grid.sweep(3, range(5, 10), range(5, 11), put)
+        first = ((7,), (7, 8)), (range(6, 9), range(6, 10)), (range(5, 10), range(5, 11))
         h_planes, de_planes = range(4, 10), range(4, 10)
     else:
-        grid.sweep(1, (-1,), (-1, 0), put)
-        grid.sweep(2, (-1, 0), (0, 1), put)
-        grid.sweep(3, (0, 1), (1, 2), put)
+        first = ((-1,), (-1, 0)), ((-1, 0), (0, 1)), ((0, 1), (1, 2))
         h_planes, de_planes = (1, 2), (2, 3)
+    for n, (hs, des) in enumerate(first, 1):
+        grid.sweep(n, hs, des, put)
+        yield n
     for p in sorted(set(h_planes) | set(de_planes)):
         if p in h_planes:
             grid.step_h(STEPS, p, range(3), put)
@@ -475,42 +477,52 @@
                     keep(c, p - ADVANCE, grid.get(H + c, p, STEPS))
             grid.step_de(STEPS, p, put)
             done(p - ADVANCE)
+    yield STEPS
+
+
+def chain(*args):
+    for _ in stages(*args):
+        pass
 
 
 KEPT = NZL - ADVANCE
+
+
+def near_side(given, high, cc, made, state):
+    fields, xt, frames, more = given
+    grid = full_grid()
+    hold_own(grid, fields, xt)
+    hold_frames(grid, frames, EARLY)
+    hold_frames(grid, more, MIDDLE)
+    hold_side(grid, high, lambda i: cc[i])
+
+    def put(c, p, v, n):
+        k = c // 3
+        if n == STEPS and p >= ADVANCE:
+            made[k][c % 3, p - ADVANCE] = v[:NXL]
+        if n < STEPS or k == 2:
+            grid.put(state[k], (c % 3, p + 2), c, p, v, n)
+
+    def keep(c, o, v):
+        made[2][c, o] = v[:NXL]
+
+    return grid, stages(grid, high, put, keep)
 
 
 def near(d, e, h, eps, chi, xt, fd, fe, fh, gd, ge, gh, cc, nd, ne, nh, neps, nchi, *state):
     gz, _, _, _ = position()
 
-    def side(high):
-        grid = full_grid()
-        hold_own(grid, (d, e, h, eps, chi), xt)
-        hold_frames(grid, (fd, fe, fh), EARLY)
-        hold_frames(grid, (gd, ge, gh), MIDDLE)
-        hold_side(grid, high, lambda i: cc[i])
-
-        def put(c, p, v, n):
-            k = c // 3
-            if n == STEPS and p >= ADVANCE:
-                (nd, ne, nh)[k][c % 3, p - ADVANCE] = v[:NXL]
-            if n < STEPS or k == 2:
-                grid.put(state[k], (c % 3, p + 2), c, p, v, n)
-
-        def keep(c, o, v):
-            nh[c, o] = v[:NXL]
-
-        chain(grid, high, put, keep)
-        if high:
-            for out, comp in ((neps, EPS), (nchi, CHI)):
-                for o in range(ADVANCE):
-                    out[o] = grid.get(comp, NZL + o)[:NXL]
-
-    pl.when(lax.rem(gz, 2) == 0)(lambda: side(True))
-    pl.when(lax.rem(gz, 2) == 1)(lambda: side(False))
-
-
-def ahead(d, e, h, eps, chi, fd, fe, fh, gd, ge, gh, ca, eps_in, chi_in, ie, ih, od, oe, oh, oeps, ochi, sd):
+    @pl.when(lax.rem(gz, 2) == 0)
+    def _():
+        grid, parts = near_side(((d, e, h, eps, chi), xt, (fd, fe, fh), (gd, ge, gh)), True, cc, (nd, ne, nh), state)
+        for _ in parts:
+            pass
+        for out, comp in ((neps, EPS), (nchi, CHI)):
+            for o in range(ADVANCE):
+                out[o] = grid.get(comp, NZL + o)[:NXL]
+
+
+def ahead(d, e, h, eps, chi, xt, fd, fe, fh, gd, ge, gh, ca, cc, eps_in, chi_in, ie, ih, od, oe, oh, oeps, ochi, sd, *state):
     gz, _, last, _ = position()
     half = halo_row() < XH
 
@@ -547,7 +559,14 @@
         def keep(c, o, v):
             oh[c, o] = v
 
-        chain(grid, high, put, keep)
+        parts = stages(grid, high, put, keep)
+        if high:
+            _, others = near_side(((d, e, h, eps, chi), xt, (fd, fe, fh), (gd, ge, gh)), False, cc, (od, oe, oh), state)
+            for _ in zip(others, parts):
+                pass
+        else:
+            for _ in parts:
+                pass
         if high:
             for out, comp, new in ((oeps, EPS, eps_in), (ochi, CHI, chi_in)):
                 for o in range(ADVANCE):
@@ -565,9 +584,11 @@
 
     def cross(chosen, i):
         m = ca[24 * i : 24 * i + 8]
-        x, n = ca[EARLY_AT[i] : EARLY_AT[i + 1]], LATE_N[i]
+        n = LATE_N[i]
+        parts = [ca[EARLY_AT[i] : EARLY_AT[i + 1]]] if n < 4 else []
         if n:
-            x = rows(cb[LATE_AT[i] : LATE_AT[i] + n], x, cb[LATE_AT[i] + n : LATE_AT[i] + 2 * n])
+            parts = [cb[LATE_AT[i] : LATE_AT[i] + n], *parts, cb[LATE_AT[i] + n : LATE_AT[i] + 2 * n]]
+        x = rows(*parts)
         at, kept = HALO_AT[i], list(chosen[WIDTH[i]])
         v = cb[at : at + WIDTH[i]]
         if len(kept) < 8:
@@ -584,7 +605,7 @@
 
         here, there = (pl.ds(ADVANCE, KEPT), pl.ds(0, ADVANCE)) if high else (pl.ds(0, ADVANCE), pl.ds(ADVANCE, KEPT))
         middle_rows = pl.ds(8, 16)
-        for a, b, out in zip((nd, ne, nh), (od, oe, oh), outs):
+        for a, b, out in zip((od, oe, oh) if high else (nd, ne, nh), (od, oe, oh), outs):
             send(a.at[:, there], out.at[:, there])
             send(b.at[:, here, middle_rows], out.at[:, here, middle_rows])
         for a, new, out in zip((eps, chi), (oeps, ochi) if high else (neps, nchi), outs[3:]):
@@ -692,9 +713,9 @@
     levels = shape(STEPS - 1, 3, 13, NXL, NY), shape(STEPS, 3, 13, NXL, NY)
     inside = call(
         ahead,
-        [*fields, *frames, *more, ca, *coming],
+        [*fields, xt, *frames, *more, ca, cc, *coming],
         (*levels, field, field, field, two, two),
-        [pltpu.VMEM((3, 13, NXL, NY), jnp.float32)],
+        [pltpu.VMEM((3, 13, NXL, NY), jnp.float32), *state],
         vmem=16,
     )
     thin = [pltpu.VMEM((3, 13, EDGE, NY), jnp.float32)] * 3 + [pltpu.VMEM((3, NZL, 16, NY), jnp.float32)] * 3

time: 24.4 us -> 23.8 us (0.975)
  Pallas kernels: 6.42 us -> 6.05 us
    pallas_call x9, Pallas kernels: 6.42 us -> 6.05 us  [call(): pl.pallas_call(body, out_shape=out_shape, in_specs=[VM] * len(inputs) if...]
  transfers between devices with their start and end apart: 5 -> 5, of which waited for: 3 -> 4; matrix products, arithmetic and copies ran while one was open for 0% -> 0% of each run, Pallas kernels for 10% -> 9%
where the time goes in v14:
time: 23.8 us; the launch traced here: 23.5 us
  starting transfers between devices  9.1 us (38%)
  waiting for transfers between devices  7.54 us (32%)
  Pallas kernels  6.05 us (25%)
  between operations  0.72 us (3%)
    ppermute x5, starting transfers between devices, swapped(): return lax.ppermute(shard, ('gz', 'gx'), moves)  9.1 us
    ppermute x5, waiting for transfers between devices, swapped(): return lax.ppermute(shard, ('gz', 'gx'), moves)  7.54 us
    pallas_call x9, Pallas kernels, call(): pl.pallas_call(body, out_shape=out_shape, in_specs=[VM] * len(inputs) if...  6.05 us
  transfers between devices with their start and end apart: 5, of which 4 were waited for; matrix products, arithmetic and copies ran while one was open for 0% of the time, Pallas kernels for 9%

profile of v14, /device:TPU:111, one launch (start us, length us, event | category | flops | bytes accessed | tf_op | source)
XLA Modules:
  0.0 23.5 jit_solution(1141540000905458341)
XLA Ops:
  0.6 1.4 %shard_map.119 = (f32[3,8,32,128]{3,2,1,0:T(8,128)S(1)}, f32[3,8,32,128]{3,2,1,0:T(8,128)S(1)}, f32[3,8,32,128]{3,2,1,0:T(8,128)S(1)}, f32[8,32,128]{2,1,0:T(8,1...) custom-call(f32[3,8,32,128]{3,2,1,0:T(8,128)} %d.1, f32[3,8,32,128]{3,2,1,0:T(8,128)} %e.1, ...), custom_call_target="tpu_custom_call" | custom-call | tf_op jit(solution)/shard_map/pallas_call | solution.py:670
  2.0 0.3 %collective-permute-start = (f32[304,128]{1,0:T(8,128)S(1)}, f32[304,128]{1,0:T(8,128)S(1)}, u32[]{:S(2)}, u32[]{:S(2)}) collective-permute-start(f32[304,128]{1,0:T(8,128)S(1)} %get-tuple-element.47), channel_id=1, source_target_pairs={{0,1},{1,0},{2,3},{3,2},{4,5},{5,4},{6,7},{7,6},{8,9},{9,8},{10,11... | collective-permute-start | bytes 466952 | tf_op jit(solution)/shard_map/ppermute | solution.py:666
  2.2 2.1 %collective-permute-start.1 = (f32[304,128]{1,0:T(8,128)S(1)}, f32[304,128]{1,0:T(8,128)S(1)}, u32[]{:S(2)}, u32[]{:S(2)}) collective-permute-start(f32[304,128]{1,0:T(8,128)S(1)} %get-tuple-element.48), channel_id=1, source_target_pairs={{0,4},{1,2},{2,1},{3,7},{4,0},{5,6},{6,5},{7,3},{8,12},{9,10},{10,... | collective-permute-start | bytes 466952 | tf_op jit(solution)/shard_map/ppermute | solution.py:666
  4.4 0.5 %shard_map.122 = (f32[3,5,32,128]{3,2,1,0:T(8,128)S(1)}, f32[3,5,32,128]{3,2,1,0:T(8,128)S(1)}, f32[3,5,32,128]{3,2,1,0:T(8,128)S(1)}, f32[2,32,128]{2,1,0:T(8,128)S(1)}, f32[736,128]{1,0:T(8,128)S(1)}) custom-call(f32[3,8,32,128]{3,2,1,0:T(8,128)S(1)} %get-tuple-element.42.d, f32[3,8,32,128]{3,2,1,0:T(8,128)S(1)} %get-tuple-element.43.e, ...), custom_call_target="tpu_custom_call" | custom-call | tf_op jit(solution)/shard_map/pallas_call | solution.py:670
  4.9 0.0 copy-start
  4.9 0.0 copy-start.1
  4.9 0.0 copy-start.2
  5.0 2.0 %collective-permute-done.ra = f32[304,128]{1,0:T(8,128)S(1)} collective-permute-done((f32[304,128]{1,0:T(8,128)S(1)}, f32[304,128]{1,0:T(8,128)S(1)}, u32[]{:S(2)}, u32[]{:S(2)}) %collective-permute-start) | collective-permute-done | bytes 155680 | tf_op jit(solution)/shard_map/ppermute | solution.py:666
  7.0 0.8 %collective-permute-done.1.rb = f32[304,128]{1,0:T(8,128)S(1)} collective-permute-done((f32[304,128]{1,0:T(8,128)S(1)}, f32[304,128]{1,0:T(8,128)S(1)}, u32[]{:S(2)}, u32[]{:S(2)}) %collective-permute-start.1) | collective-permute-done | bytes 155680 | tf_op jit(solution)/shard_map/ppermute | solution.py:666
  7.8 0.2 shard_map.121
  8.0 0.5 %shard_map.123 = (f32[3,5,40,128]{3,2,1,0:T(8,128)S(1)}, f32[3,5,40,128]{3,2,1,0:T(8,128)S(1)}, f32[3,5,40,128]{3,2,1,0:T(8,128)S(1)}, f32[26,40,128]{2,1,0:T(8,128)S(1)}) custom-call(f32[3,8,32,128]{3,2,1,0:T(8,128)S(1)} %get-tuple-element.42.d, f32[3,8,32,128]{3,2,1,0:T(8,128)S(1)} %get-tuple-element.43.e, f32[3,8,32,128]{3,2,1,0:T(8,128)S(1)} %get-tuple-element.44.h, ...), custom_call_target="tpu_custom_call" | custom-call | tf_op jit(solution)/shard_map/pallas_call | solution.py:670
  8.5 1.7 %collective-permute-start.4 = (f32[26,40,128]{2,1,0:T(8,128)S(1)}, f32[26,40,128]{2,1,0:T(8,128)S(1)}, u32[]{:S(2)}, u32[]{:S(2)}) collective-permute-start(f32[26,40,128]{2,1,0:T(8,128)S(1)} %get-tuple-element.66), channel_id=1, source_target_pairs={{0,4},{1,5},{2,6},{3,7},{4,0},{5,1},{6,2},{7,3},{8,12},{9,13},{10,... | collective-permute-start | bytes 1597448 | tf_op jit(solution)/shard_map/ppermute | solution.py:666
  10.2 2.8 %collective-permute-start.2 = (f32[736,128]{1,0:T(8,128)S(1)}, f32[736,128]{1,0:T(8,128)S(1)}, u32[]{:S(2)}, u32[]{:S(2)}) collective-permute-start(f32[736,128]{1,0:T(8,128)S(1)} %get-tuple-element.64), channel_id=1, source_target_pairs={{0,1},{1,0},{2,3},{3,2},{4,8},{5,9},{6,10},{7,11},{8,4},{9,5},{10,... | collective-permute-start | bytes 1130504 | tf_op jit(solution)/shard_map/ppermute | solution.py:666
  12.9 2.3 %collective-permute-start.3 = (f32[216,128]{1,0:T(8,128)S(1)}, f32[216,128]{1,0:T(8,128)S(1)}, u32[]{:S(2)}, u32[]{:S(2)}) collective-permute-start(f32[216,128]{1,0:T(8,128)S(1)} %get-tuple-element.65), channel_id=1, source_target_pairs={{0,1},{1,0},{2,3},{3,2},{4,8},{5,9},{6,10},{7,11},{8,4},{9,5},{10,... | collective-permute-start | bytes 331784 | tf_op jit(solution)/shard_map/ppermute | solution.py:666
  15.2 0.0 copy-done
  15.2 0.0 copy-done.1
  15.2 0.0 copy-done.2
  15.2 0.1 select_reduce_fusion
  15.3 0.5 %shard_map.124 = (f32[3,7,40,128]{3,2,1,0:T(8,128)S(1)}, f32[3,7,40,128]{3,2,1,0:T(8,128)S(1)}, f32[3,7,40,128]{3,2,1,0:T(8,128)S(1)}) custom-call(f32[3,8,32,128]{3,2,1,0:T(8,128)S(1)} %get-tuple-element.42.d, f32[3,8,32,128]{3,2,1,0:T(8,128)S(1)} %get-tuple-element.43.e, f32[3,8,32,128]{3,2,1,0:T(8,128)S(1)} %get-tuple-element.44.h, ...), custom_call_target="tpu_custom_call" | custom-call | tf_op jit(solution)/shard_map/pallas_call | solution.py:670
  15.8 0.0 collective-permute-done.4.cc
  15.9 4.6 %collective-permute-done.2.ca = f32[736,128]{1,0:T(8,128)S(1)} collective-permute-done((f32[736,128]{1,0:T(8,128)S(1)}, f32[736,128]{1,0:T(8,128)S(1)}, u32[]{:S(2)}, u32[]{:S(2)}) %collective-permute-start.2) | collective-permute-done | bytes 376864 | tf_op jit(solution)/shard_map/ppermute | solution.py:666
  20.5 1.1 %shard_map.126 = (f32[3,3,13,32,128]{4,3,2,1,0:T(8,128)S(1)}, f32[4,3,13,32,128]{4,3,2,1,0:T(8,128)S(1)}, f32[3,8,32,128]{3,2,1,0:T(8,128)S(1)}, f32[3,8,32,128]...) custom-call(f32[3,8,32,128]{3,2,1,0:T(8,128)S(1)} %get-tuple-element.42.d, ...), custom_call_target="tpu_custom_call" | custom-call | tf_op jit(solution)/shard_map/pallas_call | solution.py:670
  21.6 0.1 collective-permute-done.3.cb
  21.7 1.8 %shard_map.127 = (f32[3,8,32,128]{3,2,1,0:T(8,128)}, f32[3,8,32,128]{3,2,1,0:T(8,128)}, f32[3,8,32,128]{3,2,1,0:T(8,128)}, f32[8,32,128]{2,1,0:T(8,128)}, f32[8,32,128]{2,1,0:T(8,128)}) custom-call(f32[3,8,32,128]{3,2,1,0:T(8,128)S(1)} %get-tuple-element.42.d, f32[3,8,32,128]{3,2,1,0:T(8,128)S(1)} %get-tuple-element.43.e, ...), custom_call_target="tpu_custom_call" | custom-call | tf_op jit(solution)/shard_map/pallas_call | solution.py:670
  (2 shorter events, 0.0 us)
Async XLA Ops:
  2.0 5.0 %collective-permute-start = (f32[304,128]{1,0:T(8,128)S(1)}, f32[304,128]{1,0:T(8,128)S(1)}, u32[]{:S(2)}, u32[]{:S(2)}) collective-permute-start(f32[304,128]{1,0:T(8,128)S(1)} %get-tuple-element.47), channel_id=1, source_target_pairs={{0,1},{1,0},{2,3},{3,2},{4,5},{5,4},{6,7},{7,6},{8,9},{9,8},{10,11... | collective-permute-start | bytes 466952 | tf_op jit(solution)/shard_map/ppermute | solution.py:666
  2.2 5.6 %collective-permute-start.1 = (f32[304,128]{1,0:T(8,128)S(1)}, f32[304,128]{1,0:T(8,128)S(1)}, u32[]{:S(2)}, u32[]{:S(2)}) collective-permute-start(f32[304,128]{1,0:T(8,128)S(1)} %get-tuple-element.48), channel_id=1, source_target_pairs={{0,4},{1,2},{2,1},{3,7},{4,0},{5,6},{6,5},{7,3},{8,12},{9,10},{10,... | collective-permute-start | bytes 466952 | tf_op jit(solution)/shard_map/ppermute | solution.py:666
  4.9 10.3 %copy-start = (s32[2,32,128]{2,1,0:T(8,128)S(1)}, s32[2,32,128]{2,1,0:T(8,128)}, u32[]{:S(2)}) copy-start(s32[2,32,128]{2,1,0:T(8,128)} %param.13) | copy-start | bytes 98308
  4.9 10.3 %copy-start.1 = (f32[8]{0:T(128)S(1)}, f32[8]{0:T(128)}, u32[]{:S(2)}) copy-start(f32[8]{0:T(128)} %param.15) | copy-start | bytes 100
  4.9 10.3 %copy-start.2 = (f32[8]{0:T(128)S(1)}, f32[8]{0:T(128)}, u32[]{:S(2)}) copy-start(f32[8]{0:T(128)} %param.14) | copy-start | bytes 100
  8.5 7.3 %collective-permute-start.4 = (f32[26,40,128]{2,1,0:T(8,128)S(1)}, f32[26,40,128]{2,1,0:T(8,128)S(1)}, u32[]{:S(2)}, u32[]{:S(2)}) collective-permute-start(f32[26,40,128]{2,1,0:T(8,128)S(1)} %get-tuple-element.66), channel_id=1, source_target_pairs={{0,4},{1,5},{2,6},{3,7},{4,0},{5,1},{6,2},{7,3},{8,12},{9,13},{10,... | collective-permute-start | bytes 1597448 | tf_op jit(solution)/shard_map/ppermute | solution.py:666
  10.2 10.3 %collective-permute-start.2 = (f32[736,128]{1,0:T(8,128)S(1)}, f32[736,128]{1,0:T(8,128)S(1)}, u32[]{:S(2)}, u32[]{:S(2)}) collective-permute-start(f32[736,128]{1,0:T(8,128)S(1)} %get-tuple-element.64), channel_id=1, source_target_pairs={{0,1},{1,0},{2,3},{3,2},{4,8},{5,9},{6,10},{7,11},{8,4},{9,5},{10,... | collective-permute-start | bytes 1130504 | tf_op jit(solution)/shard_map/ppermute | solution.py:666
  12.9 8.8 %collective-permute-start.3 = (f32[216,128]{1,0:T(8,128)S(1)}, f32[216,128]{1,0:T(8,128)S(1)}, u32[]{:S(2)}, u32[]{:S(2)}) collective-permute-start(f32[216,128]{1,0:T(8,128)S(1)} %get-tuple-element.65), channel_id=1, source_target_pairs={{0,1},{1,0},{2,3},{3,2},{4,8},{5,9},{6,10},{7,11},{8,4},{9,5},{10,... | collective-permute-start | bytes 331784 | tf_op jit(solution)/shard_map/ppermute | solution.py:666

commit v15 on v14

--- a/solution.py
+++ b/solution.py
@@ -262,33 +262,41 @@
     return [k and (made[k] if k in made else grid.get(*k)) for k in side]
 
 
-def inner(d, e, h, eps, chi, fd, fe, fh, lo, out):
-    fields = (d, e, h, eps, chi)
+def inner(fields, side, fd, fe, fh, lo, out):
     grid = Grid(NXL, lambda p: HALF, lambda p: None)
     for comp in ALL:
         for p in range(NZL):
             grid.hold(comp, p, functools.partial(own, fields, comp, p))
     grid.step_h(1, 6, range(2), lambda c, p, v, n: grid.put(lo, c - H, c, p, v, n))
-
-    def put(c, p, v, n):
-        ref = (fd, fe, fh)[c // 3]
-        grid.put(ref, (c % 3, p), c, p, v, n)
-
-    early(grid, put)
+    early(grid, lambda c, p, v, n: grid.put((fd, fe, fh)[c // 3], (c % 3, p), c, p, v, n))
     gz, _, last, _ = position()
-    first_core = lax.rem(gz, 2) == 0
     keep = scalar(jnp.logical_and(gz != 0, gz != last))
     half = halo_row() < XH
-    low = payload(grid, LO)
-    for i, v in enumerate(payload(grid, HI)):
-        if low[i] is not None:
-            v = jnp.where(first_core, v, low[i])
+    for i, v in enumerate(payload(grid, side)):
+        if v is None:
+            continue
         v = v * keep
         out[24 * i : 24 * i + 8] = jnp.where(half, v[24:32], v[0:8])
         out[24 * i + 8 : 24 * i + 24] = v[8:24]
         n = LATE_N[i]
         if n < 4:
             out[EARLY_AT[i] : EARLY_AT[i + 1]] = jnp.where(half, v[0:8], v[24:32])[n : 8 - n]
+
+
+def sooner(d, e, h, eps, chi, *out):
+    gz, _, _, _ = position()
+    pl.when(lax.rem(gz, 2) == 1)(lambda: inner((d, e, h, eps, chi), LO, *out))
+
+
+def later(d, e, h, eps, chi, *refs):
+    had, out = refs[:5], refs[5:]
+    gz, _, _, _ = position()
+    pl.when(lax.rem(gz, 2) == 0)(lambda: inner((d, e, h, eps, chi), HI, *out))
+
+    @pl.when(lax.rem(gz, 2) == 1)
+    def _():
+        for a, b in zip(had, out):
+            b[...] = a[...]
 
 
 def edge_grid(inside, fields, tile):
@@ -688,9 +696,10 @@
         [pltpu.SemaphoreType.DMA((5,))],
         specs=[HBM] * 5,
     )
+    kinds = (*[shape(3, 5, NXL, NY)] * 3, shape(2, NXL, NY), shape(EARLY_ROWS, NY))
+    had = call(sooner, fields, kinds)
     ra, rb = swapped(ya, "gx", 0), swapped(yb, "gx", 1)
-    lo = shape(2, NXL, NY)
-    *inside, za = call(inner, fields, (*[shape(3, 5, NXL, NY)] * 3, lo, shape(EARLY_ROWS, NY)))
+    *inside, za = call(later, [*fields, *had], kinds)
     ca = swapped(za, "gz", 1)
     (edge,) = call(mark, [], (shape(8, NY),))
     thin = [(3, 5, EDGE, NY)] * 3 + [(2, EDGE, NY)]

time: 23.8 us -> 23.8 us (level)
    pallas_call x9 -> x10, Pallas kernels: 6.05 us -> 6.05 us  [call(): pl.pallas_call(body, out_shape=out_shape, in_specs=[VM] * len(inputs) if...]
where the time goes in v15:
time: 23.8 us; the launch traced here: 23.5 us
  starting transfers between devices  9.11 us (38%)
  waiting for transfers between devices  7.53 us (32%)
  Pallas kernels  6.05 us (25%)
  between operations  0.72 us (3%)
    ppermute x5, starting transfers between devices, swapped(): return lax.ppermute(shard, ('gz', 'gx'), moves)  9.11 us
    ppermute x5, waiting for transfers between devices, swapped(): return lax.ppermute(shard, ('gz', 'gx'), moves)  7.53 us
    pallas_call x10, Pallas kernels, call(): pl.pallas_call(body, out_shape=out_shape, in_specs=[VM] * len(inputs) if...  6.05 us
  transfers between devices with their start and end apart: 5, of which 4 were waited for; matrix products, arithmetic and copies ran while one was open for 0% of the time, Pallas kernels for 9%

profile of v15, /device:TPU:111, one launch (start us, length us, event | category | flops | bytes accessed | tf_op | source)
XLA Modules:
  0.0 23.5 jit_solution(12739701354489030176)
XLA Ops:
  0.6 1.4 %shard_map.119 = (f32[3,8,32,128]{3,2,1,0:T(8,128)S(1)}, f32[3,8,32,128]{3,2,1,0:T(8,128)S(1)}, f32[3,8,32,128]{3,2,1,0:T(8,128)S(1)}, f32[8,32,128]{2,1,0:T(8,1...) custom-call(f32[3,8,32,128]{3,2,1,0:T(8,128)} %d.1, f32[3,8,32,128]{3,2,1,0:T(8,128)} %e.1, ...), custom_call_target="tpu_custom_call" | custom-call | tf_op jit(solution)/shard_map/pallas_call | solution.py:678
  2.0 0.3 %collective-permute-start = (f32[304,128]{1,0:T(8,128)S(1)}, f32[304,128]{1,0:T(8,128)S(1)}, u32[]{:S(2)}, u32[]{:S(2)}) collective-permute-start(f32[304,128]{1,0:T(8,128)S(1)} %get-tuple-element.52), channel_id=1, source_target_pairs={{0,1},{1,0},{2,3},{3,2},{4,5},{5,4},{6,7},{7,6},{8,9},{9,8},{10,11... | collective-permute-start | bytes 466952 | tf_op jit(solution)/shard_map/ppermute | solution.py:674
  2.2 2.1 %collective-permute-start.1 = (f32[304,128]{1,0:T(8,128)S(1)}, f32[304,128]{1,0:T(8,128)S(1)}, u32[]{:S(2)}, u32[]{:S(2)}) collective-permute-start(f32[304,128]{1,0:T(8,128)S(1)} %get-tuple-element.53), channel_id=1, source_target_pairs={{0,4},{1,2},{2,1},{3,7},{4,0},{5,6},{6,5},{7,3},{8,12},{9,10},{10,... | collective-permute-start | bytes 466952 | tf_op jit(solution)/shard_map/ppermute | solution.py:674
  4.4 0.4 %shard_map.122 = (f32[3,5,32,128]{3,2,1,0:T(8,128)S(1)}, f32[3,5,32,128]{3,2,1,0:T(8,128)S(1)}, f32[3,5,32,128]{3,2,1,0:T(8,128)S(1)}, f32[2,32,128]{2,1,0:T(8,128)S(1)}, f32[736,128]{1,0:T(8,128)S(1)}) custom-call(f32[3,8,32,128]{3,2,1,0:T(8,128)S(1)} %get-tuple-element.47.d, f32[3,8,32,128]{3,2,1,0:T(8,128)S(1)} %get-tuple-element.48.e, ...), custom_call_target="tpu_custom_call" | custom-call | tf_op jit(solution)/shard_map/pallas_call | solution.py:678
  4.8 0.1 shard_map.123
  4.9 0.0 copy-start
  4.9 0.0 copy-start.1
  5.0 0.0 copy-start.2
  5.0 2.0 %collective-permute-done.ra = f32[304,128]{1,0:T(8,128)S(1)} collective-permute-done((f32[304,128]{1,0:T(8,128)S(1)}, f32[304,128]{1,0:T(8,128)S(1)}, u32[]{:S(2)}, u32[]{:S(2)}) %collective-permute-start) | collective-permute-done | bytes 155680 | tf_op jit(solution)/shard_map/ppermute | solution.py:674
  7.0 0.8 %collective-permute-done.1.rb = f32[304,128]{1,0:T(8,128)S(1)} collective-permute-done((f32[304,128]{1,0:T(8,128)S(1)}, f32[304,128]{1,0:T(8,128)S(1)}, u32[]{:S(2)}, u32[]{:S(2)}) %collective-permute-start.1) | collective-permute-done | bytes 155680 | tf_op jit(solution)/shard_map/ppermute | solution.py:674
  7.8 0.2 shard_map.121
  8.0 0.5 %shard_map.124 = (f32[3,5,40,128]{3,2,1,0:T(8,128)S(1)}, f32[3,5,40,128]{3,2,1,0:T(8,128)S(1)}, f32[3,5,40,128]{3,2,1,0:T(8,128)S(1)}, f32[26,40,128]{2,1,0:T(8,128)S(1)}) custom-call(f32[3,8,32,128]{3,2,1,0:T(8,128)S(1)} %get-tuple-element.47.d, f32[3,8,32,128]{3,2,1,0:T(8,128)S(1)} %get-tuple-element.48.e, f32[3,8,32,128]{3,2,1,0:T(8,128)S(1)} %get-tuple-element.49.h, ...), custom_call_target="tpu_custom_call" | custom-call | tf_op jit(solution)/shard_map/pallas_call | solution.py:678
  8.5 1.7 %collective-permute-start.4 = (f32[26,40,128]{2,1,0:T(8,128)S(1)}, f32[26,40,128]{2,1,0:T(8,128)S(1)}, u32[]{:S(2)}, u32[]{:S(2)}) collective-permute-start(f32[26,40,128]{2,1,0:T(8,128)S(1)} %get-tuple-element.76), channel_id=1, source_target_pairs={{0,4},{1,5},{2,6},{3,7},{4,0},{5,1},{6,2},{7,3},{8,12},{9,13},{10,... | collective-permute-start | bytes 1597448 | tf_op jit(solution)/shard_map/ppermute | solution.py:674
  10.2 2.8 %collective-permute-start.2 = (f32[736,128]{1,0:T(8,128)S(1)}, f32[736,128]{1,0:T(8,128)S(1)}, u32[]{:S(2)}, u32[]{:S(2)}) collective-permute-start(f32[736,128]{1,0:T(8,128)S(1)} %get-tuple-element.74), channel_id=1, source_target_pairs={{0,1},{1,0},{2,3},{3,2},{4,8},{5,9},{6,10},{7,11},{8,4},{9,5},{10,... | collective-permute-start | bytes 1130504 | tf_op jit(solution)/shard_map/ppermute | solution.py:674
  12.9 2.3 %collective-permute-start.3 = (f32[216,128]{1,0:T(8,128)S(1)}, f32[216,128]{1,0:T(8,128)S(1)}, u32[]{:S(2)}, u32[]{:S(2)}) collective-permute-start(f32[216,128]{1,0:T(8,128)S(1)} %get-tuple-element.75), channel_id=1, source_target_pairs={{0,1},{1,0},{2,3},{3,2},{4,8},{5,9},{6,10},{7,11},{8,4},{9,5},{10,... | collective-permute-start | bytes 331784 | tf_op jit(solution)/shard_map/ppermute | solution.py:674
  15.2 0.0 copy-done
  15.2 0.0 copy-done.1
  15.2 0.0 copy-done.2
  15.2 0.1 select_reduce_fusion
  15.3 0.5 %shard_map.125 = (f32[3,7,40,128]{3,2,1,0:T(8,128)S(1)}, f32[3,7,40,128]{3,2,1,0:T(8,128)S(1)}, f32[3,7,40,128]{3,2,1,0:T(8,128)S(1)}) custom-call(f32[3,8,32,128]{3,2,1,0:T(8,128)S(1)} %get-tuple-element.47.d, f32[3,8,32,128]{3,2,1,0:T(8,128)S(1)} %get-tuple-element.48.e, f32[3,8,32,128]{3,2,1,0:T(8,128)S(1)} %get-tuple-element.49.h, ...), custom_call_target="tpu_custom_call" | custom-call | tf_op jit(solution)/shard_map/pallas_call | solution.py:678
  15.9 0.0 collective-permute-done.4.cc
  15.9 4.6 %collective-permute-done.2.ca = f32[736,128]{1,0:T(8,128)S(1)} collective-permute-done((f32[736,128]{1,0:T(8,128)S(1)}, f32[736,128]{1,0:T(8,128)S(1)}, u32[]{:S(2)}, u32[]{:S(2)}) %collective-permute-start.2) | collective-permute-done | bytes 376864 | tf_op jit(solution)/shard_map/ppermute | solution.py:674
  20.5 1.1 %shard_map.127 = (f32[3,3,13,32,128]{4,3,2,1,0:T(8,128)S(1)}, f32[4,3,13,32,128]{4,3,2,1,0:T(8,128)S(1)}, f32[3,8,32,128]{3,2,1,0:T(8,128)S(1)}, f32[3,8,32,128]...) custom-call(f32[3,8,32,128]{3,2,1,0:T(8,128)S(1)} %get-tuple-element.47.d, ...), custom_call_target="tpu_custom_call" | custom-call | tf_op jit(solution)/shard_map/pallas_call | solution.py:678
  21.6 0.1 collective-permute-done.3.cb
  21.7 1.8 %shard_map.128 = (f32[3,8,32,128]{3,2,1,0:T(8,128)}, f32[3,8,32,128]{3,2,1,0:T(8,128)}, f32[3,8,32,128]{3,2,1,0:T(8,128)}, f32[8,32,128]{2,1,0:T(8,128)}, f32[8,32,128]{2,1,0:T(8,128)}) custom-call(f32[3,8,32,128]{3,2,1,0:T(8,128)S(1)} %get-tuple-element.47.d, f32[3,8,32,128]{3,2,1,0:T(8,128)S(1)} %get-tuple-element.48.e, ...), custom_call_target="tpu_custom_call" | custom-call | tf_op jit(solution)/shard_map/pallas_call | solution.py:678
  (2 shorter events, 0.0 us)
Async XLA Ops:
  2.0 5.0 %collective-permute-start = (f32[304,128]{1,0:T(8,128)S(1)}, f32[304,128]{1,0:T(8,128)S(1)}, u32[]{:S(2)}, u32[]{:S(2)}) collective-permute-start(f32[304,128]{1,0:T(8,128)S(1)} %get-tuple-element.52), channel_id=1, source_target_pairs={{0,1},{1,0},{2,3},{3,2},{4,5},{5,4},{6,7},{7,6},{8,9},{9,8},{10,11... | collective-permute-start | bytes 466952 | tf_op jit(solution)/shard_map/ppermute | solution.py:674
  2.2 5.6 %collective-permute-start.1 = (f32[304,128]{1,0:T(8,128)S(1)}, f32[304,128]{1,0:T(8,128)S(1)}, u32[]{:S(2)}, u32[]{:S(2)}) collective-permute-start(f32[304,128]{1,0:T(8,128)S(1)} %get-tuple-element.53), channel_id=1, source_target_pairs={{0,4},{1,2},{2,1},{3,7},{4,0},{5,6},{6,5},{7,3},{8,12},{9,10},{10,... | collective-permute-start | bytes 466952 | tf_op jit(solution)/shard_map/ppermute | solution.py:674
  4.9 10.3 %copy-start = (s32[2,32,128]{2,1,0:T(8,128)S(1)}, s32[2,32,128]{2,1,0:T(8,128)}, u32[]{:S(2)}) copy-start(s32[2,32,128]{2,1,0:T(8,128)} %param.13) | copy-start | bytes 98308
  4.9 10.3 %copy-start.1 = (f32[8]{0:T(128)S(1)}, f32[8]{0:T(128)}, u32[]{:S(2)}) copy-start(f32[8]{0:T(128)} %param.15) | copy-start | bytes 100
  5.0 10.3 %copy-start.2 = (f32[8]{0:T(128)S(1)}, f32[8]{0:T(128)}, u32[]{:S(2)}) copy-start(f32[8]{0:T(128)} %param.14) | copy-start | bytes 100
  8.5 7.3 %collective-permute-start.4 = (f32[26,40,128]{2,1,0:T(8,128)S(1)}, f32[26,40,128]{2,1,0:T(8,128)S(1)}, u32[]{:S(2)}, u32[]{:S(2)}) collective-permute-start(f32[26,40,128]{2,1,0:T(8,128)S(1)} %get-tuple-element.76), channel_id=1, source_target_pairs={{0,4},{1,5},{2,6},{3,7},{4,0},{5,1},{6,2},{7,3},{8,12},{9,13},{10,... | collective-permute-start | bytes 1597448 | tf_op jit(solution)/shard_map/ppermute | solution.py:674
  10.2 10.3 %collective-permute-start.2 = (f32[736,128]{1,0:T(8,128)S(1)}, f32[736,128]{1,0:T(8,128)S(1)}, u32[]{:S(2)}, u32[]{:S(2)}) collective-permute-start(f32[736,128]{1,0:T(8,128)S(1)} %get-tuple-element.74), channel_id=1, source_target_pairs={{0,1},{1,0},{2,3},{3,2},{4,8},{5,9},{6,10},{7,11},{8,4},{9,5},{10,... | collective-permute-start | bytes 1130504 | tf_op jit(solution)/shard_map/ppermute | solution.py:674
  12.9 8.8 %collective-permute-start.3 = (f32[216,128]{1,0:T(8,128)S(1)}, f32[216,128]{1,0:T(8,128)S(1)}, u32[]{:S(2)}, u32[]{:S(2)}) collective-permute-start(f32[216,128]{1,0:T(8,128)S(1)} %get-tuple-element.75), channel_id=1, source_target_pairs={{0,1},{1,0},{2,3},{3,2},{4,8},{5,9},{6,10},{7,11},{8,4},{9,5},{10,... | collective-permute-start | bytes 331784 | tf_op jit(solution)/shard_map/ppermute | solution.py:674

commit v16 on v14

--- a/solution.py
+++ b/solution.py
@@ -60,11 +60,11 @@
 LATE_N = [late_rows(*k) for k in HI]
 EARLY_AT = [24 * NS + sum(8 - 2 * n for n in LATE_N[:i]) for i in range(NS + 1)]
 LATE_AT = [sum(WIDTH) + sum(2 * n for n in LATE_N[:i]) for i in range(NS + 1)]
-EARLY_ROWS, LATE_ROWS = (-(-at[-1] // 8) * 8 for at in (EARLY_AT, LATE_AT))
+EARLY_ROWS, LATE_ROWS = (-(-at[-1] // 8) * 8 + 8 for at in (EARLY_AT, LATE_AT))
 
 FOUR, THREE = (E, E + 1, E + 2, H + 1, H + 2), (D, D + 1, D + 2, H, EPS, CHI)
-NF = len(FOUR) * NZL * 4
-NHALO = NF + len(THREE) * NZL * 3
+NF = 8 + len(FOUR) * NZL * 4
+NHALO = NF + len(THREE) * NZL * 3 + 8
 
 VM = pl.BlockSpec(memory_space=pltpu.VMEM)
 HBM = pl.BlockSpec(memory_space=pltpu.HBM)
@@ -218,7 +218,7 @@
 
 def halo_slot(comp, p):
     if comp in FOUR:
-        return (FOUR.index(comp) * NZL + p) * 4, 4
+        return 8 + (FOUR.index(comp) * NZL + p) * 4, 4
     return NF + (THREE.index(comp) * NZL + p) * 3, 3
 
 

time: 23.8 us -> 24.1 us (1.013)
  waiting for transfers between devices: 7.54 us -> 7.8 us
    ppermute x5, waiting for transfers between devices: 7.54 us -> 7.8 us  [swapped(): return lax.ppermute(shard, ('gz', 'gx'), moves)]
where the time goes in v16:
time: 24.1 us; the launch traced here: 23.8 us
  starting transfers between devices  9.1 us (38%)
  waiting for transfers between devices  7.8 us (32%)
  Pallas kernels  6.04 us (25%)
  between operations  0.72 us (3%)
    ppermute x5, starting transfers between devices, swapped(): return lax.ppermute(shard, ('gz', 'gx'), moves)  9.1 us
    ppermute x5, waiting for transfers between devices, swapped(): return lax.ppermute(shard, ('gz', 'gx'), moves)  7.8 us
    pallas_call x9, Pallas kernels, call(): pl.pallas_call(body, out_shape=out_shape, in_specs=[VM] * len(inputs) if...  6.04 us
  transfers between devices with their start and end apart: 5, of which 4 were waited for; matrix products, arithmetic and copies ran while one was open for 0% of the time, Pallas kernels for 9%

profile of v16, /device:TPU:111, one launch (start us, length us, event | category | flops | bytes accessed | tf_op | source)
XLA Modules:
  0.0 23.8 jit_solution(16688845477619917724)
XLA Ops:
  0.6 1.4 %shard_map.119 = (f32[3,8,32,128]{3,2,1,0:T(8,128)S(1)}, f32[3,8,32,128]{3,2,1,0:T(8,128)S(1)}, f32[3,8,32,128]{3,2,1,0:T(8,128)S(1)}, f32[8,32,128]{2,1,0:T(8,1...) custom-call(f32[3,8,32,128]{3,2,1,0:T(8,128)} %d.1, f32[3,8,32,128]{3,2,1,0:T(8,128)} %e.1, ...), custom_call_target="tpu_custom_call" | custom-call | tf_op jit(solution)/shard_map/pallas_call | solution.py:670
  2.0 0.3 %collective-permute-start = (f32[320,128]{1,0:T(8,128)S(1)}, f32[320,128]{1,0:T(8,128)S(1)}, u32[]{:S(2)}, u32[]{:S(2)}) collective-permute-start(f32[320,128]{1,0:T(8,128)S(1)} %get-tuple-element.47), channel_id=1, source_target_pairs={{0,1},{1,0},{2,3},{3,2},{4,5},{5,4},{6,7},{7,6},{8,9},{9,8},{10,11... | collective-permute-start | bytes 491528 | tf_op jit(solution)/shard_map/ppermute | solution.py:666
  2.2 2.1 %collective-permute-start.1 = (f32[320,128]{1,0:T(8,128)S(1)}, f32[320,128]{1,0:T(8,128)S(1)}, u32[]{:S(2)}, u32[]{:S(2)}) collective-permute-start(f32[320,128]{1,0:T(8,128)S(1)} %get-tuple-element.48), channel_id=1, source_target_pairs={{0,4},{1,2},{2,1},{3,7},{4,0},{5,6},{6,5},{7,3},{8,12},{9,10},{10,... | collective-permute-start | bytes 491528 | tf_op jit(solution)/shard_map/ppermute | solution.py:666
  4.4 0.5 %shard_map.122 = (f32[3,5,32,128]{3,2,1,0:T(8,128)S(1)}, f32[3,5,32,128]{3,2,1,0:T(8,128)S(1)}, f32[3,5,32,128]{3,2,1,0:T(8,128)S(1)}, f32[2,32,128]{2,1,0:T(8,128)S(1)}, f32[744,128]{1,0:T(8,128)S(1)}) custom-call(f32[3,8,32,128]{3,2,1,0:T(8,128)S(1)} %get-tuple-element.42.d, f32[3,8,32,128]{3,2,1,0:T(8,128)S(1)} %get-tuple-element.43.e, ...), custom_call_target="tpu_custom_call" | custom-call | tf_op jit(solution)/shard_map/pallas_call | solution.py:670
  4.9 0.0 copy-start
  4.9 0.0 copy-start.1
  4.9 0.0 copy-start.2
  5.0 2.2 %collective-permute-done.ra = f32[320,128]{1,0:T(8,128)S(1)} collective-permute-done((f32[320,128]{1,0:T(8,128)S(1)}, f32[320,128]{1,0:T(8,128)S(1)}, u32[]{:S(2)}, u32[]{:S(2)}) %collective-permute-start) | collective-permute-done | bytes 163872 | tf_op jit(solution)/shard_map/ppermute | solution.py:666
  7.2 0.8 %collective-permute-done.1.rb = f32[320,128]{1,0:T(8,128)S(1)} collective-permute-done((f32[320,128]{1,0:T(8,128)S(1)}, f32[320,128]{1,0:T(8,128)S(1)}, u32[]{:S(2)}, u32[]{:S(2)}) %collective-permute-start.1) | collective-permute-done | bytes 163872 | tf_op jit(solution)/shard_map/ppermute | solution.py:666
  8.0 0.2 shard_map.121
  8.2 0.5 %shard_map.123 = (f32[3,5,40,128]{3,2,1,0:T(8,128)S(1)}, f32[3,5,40,128]{3,2,1,0:T(8,128)S(1)}, f32[3,5,40,128]{3,2,1,0:T(8,128)S(1)}, f32[26,40,128]{2,1,0:T(8,128)S(1)}) custom-call(f32[3,8,32,128]{3,2,1,0:T(8,128)S(1)} %get-tuple-element.42.d, f32[3,8,32,128]{3,2,1,0:T(8,128)S(1)} %get-tuple-element.43.e, f32[3,8,32,128]{3,2,1,0:T(8,128)S(1)} %get-tuple-element.44.h, ...), custom_call_target="tpu_custom_call" | custom-call | tf_op jit(solution)/shard_map/pallas_call | solution.py:670
  8.7 1.7 %collective-permute-start.4 = (f32[26,40,128]{2,1,0:T(8,128)S(1)}, f32[26,40,128]{2,1,0:T(8,128)S(1)}, u32[]{:S(2)}, u32[]{:S(2)}) collective-permute-start(f32[26,40,128]{2,1,0:T(8,128)S(1)} %get-tuple-element.66), channel_id=1, source_target_pairs={{0,4},{1,5},{2,6},{3,7},{4,0},{5,1},{6,2},{7,3},{8,12},{9,13},{10,... | collective-permute-start | bytes 1597448 | tf_op jit(solution)/shard_map/ppermute | solution.py:666
  10.3 2.8 %collective-permute-start.2 = (f32[744,128]{1,0:T(8,128)S(1)}, f32[744,128]{1,0:T(8,128)S(1)}, u32[]{:S(2)}, u32[]{:S(2)}) collective-permute-start(f32[744,128]{1,0:T(8,128)S(1)} %get-tuple-element.64), channel_id=1, source_target_pairs={{0,1},{1,0},{2,3},{3,2},{4,8},{5,9},{6,10},{7,11},{8,4},{9,5},{10,... | collective-permute-start | bytes 1142792 | tf_op jit(solution)/shard_map/ppermute | solution.py:666
  13.1 2.3 %collective-permute-start.3 = (f32[224,128]{1,0:T(8,128)S(1)}, f32[224,128]{1,0:T(8,128)S(1)}, u32[]{:S(2)}, u32[]{:S(2)}) collective-permute-start(f32[224,128]{1,0:T(8,128)S(1)} %get-tuple-element.65), channel_id=1, source_target_pairs={{0,1},{1,0},{2,3},{3,2},{4,8},{5,9},{6,10},{7,11},{8,4},{9,5},{10,... | collective-permute-start | bytes 344072 | tf_op jit(solution)/shard_map/ppermute | solution.py:666
  15.4 0.0 copy-done
  15.4 0.0 copy-done.1
  15.4 0.0 copy-done.2
  15.4 0.1 select_reduce_fusion
  15.5 0.5 %shard_map.124 = (f32[3,7,40,128]{3,2,1,0:T(8,128)S(1)}, f32[3,7,40,128]{3,2,1,0:T(8,128)S(1)}, f32[3,7,40,128]{3,2,1,0:T(8,128)S(1)}) custom-call(f32[3,8,32,128]{3,2,1,0:T(8,128)S(1)} %get-tuple-element.42.d, f32[3,8,32,128]{3,2,1,0:T(8,128)S(1)} %get-tuple-element.43.e, f32[3,8,32,128]{3,2,1,0:T(8,128)S(1)} %get-tuple-element.44.h, ...), custom_call_target="tpu_custom_call" | custom-call | tf_op jit(solution)/shard_map/pallas_call | solution.py:670
  16.0 0.0 collective-permute-done.4.cc
  16.1 4.7 %collective-permute-done.2.ca = f32[744,128]{1,0:T(8,128)S(1)} collective-permute-done((f32[744,128]{1,0:T(8,128)S(1)}, f32[744,128]{1,0:T(8,128)S(1)}, u32[]{:S(2)}, u32[]{:S(2)}) %collective-permute-start.2) | collective-permute-done | bytes 380960 | tf_op jit(solution)/shard_map/ppermute | solution.py:666
  20.7 1.1 %shard_map.126 = (f32[3,3,13,32,128]{4,3,2,1,0:T(8,128)S(1)}, f32[4,3,13,32,128]{4,3,2,1,0:T(8,128)S(1)}, f32[3,8,32,128]{3,2,1,0:T(8,128)S(1)}, f32[3,8,32,128]...) custom-call(f32[3,8,32,128]{3,2,1,0:T(8,128)S(1)} %get-tuple-element.42.d, ...), custom_call_target="tpu_custom_call" | custom-call | tf_op jit(solution)/shard_map/pallas_call | solution.py:670
  21.9 0.1 collective-permute-done.3.cb
  22.0 1.8 %shard_map.127 = (f32[3,8,32,128]{3,2,1,0:T(8,128)}, f32[3,8,32,128]{3,2,1,0:T(8,128)}, f32[3,8,32,128]{3,2,1,0:T(8,128)}, f32[8,32,128]{2,1,0:T(8,128)}, f32[8,32,128]{2,1,0:T(8,128)}) custom-call(f32[3,8,32,128]{3,2,1,0:T(8,128)S(1)} %get-tuple-element.42.d, f32[3,8,32,128]{3,2,1,0:T(8,128)S(1)} %get-tuple-element.43.e, ...), custom_call_target="tpu_custom_call" | custom-call | tf_op jit(solution)/shard_map/pallas_call | solution.py:670
  (2 shorter events, 0.0 us)
Async XLA Ops:
  2.0 5.2 %collective-permute-start = (f32[320,128]{1,0:T(8,128)S(1)}, f32[320,128]{1,0:T(8,128)S(1)}, u32[]{:S(2)}, u32[]{:S(2)}) collective-permute-start(f32[320,128]{1,0:T(8,128)S(1)} %get-tuple-element.47), channel_id=1, source_target_pairs={{0,1},{1,0},{2,3},{3,2},{4,5},{5,4},{6,7},{7,6},{8,9},{9,8},{10,11... | collective-permute-start | bytes 491528 | tf_op jit(solution)/shard_map/ppermute | solution.py:666
  2.2 5.8 %collective-permute-start.1 = (f32[320,128]{1,0:T(8,128)S(1)}, f32[320,128]{1,0:T(8,128)S(1)}, u32[]{:S(2)}, u32[]{:S(2)}) collective-permute-start(f32[320,128]{1,0:T(8,128)S(1)} %get-tuple-element.48), channel_id=1, source_target_pairs={{0,4},{1,2},{2,1},{3,7},{4,0},{5,6},{6,5},{7,3},{8,12},{9,10},{10,... | collective-permute-start | bytes 491528 | tf_op jit(solution)/shard_map/ppermute | solution.py:666
  4.9 10.5 %copy-start = (s32[2,32,128]{2,1,0:T(8,128)S(1)}, s32[2,32,128]{2,1,0:T(8,128)}, u32[]{:S(2)}) copy-start(s32[2,32,128]{2,1,0:T(8,128)} %param.13) | copy-start | bytes 98308
  4.9 10.5 %copy-start.1 = (f32[8]{0:T(128)S(1)}, f32[8]{0:T(128)}, u32[]{:S(2)}) copy-start(f32[8]{0:T(128)} %param.15) | copy-start | bytes 100
  4.9 10.5 %copy-start.2 = (f32[8]{0:T(128)S(1)}, f32[8]{0:T(128)}, u32[]{:S(2)}) copy-start(f32[8]{0:T(128)} %param.14) | copy-start | bytes 100
  8.7 7.3 %collective-permute-start.4 = (f32[26,40,128]{2,1,0:T(8,128)S(1)}, f32[26,40,128]{2,1,0:T(8,128)S(1)}, u32[]{:S(2)}, u32[]{:S(2)}) collective-permute-start(f32[26,40,128]{2,1,0:T(8,128)S(1)} %get-tuple-element.66), channel_id=1, source_target_pairs={{0,4},{1,5},{2,6},{3,7},{4,0},{5,1},{6,2},{7,3},{8,12},{9,13},{10,... | collective-permute-start | bytes 1597448 | tf_op jit(solution)/shard_map/ppermute | solution.py:666
  10.3 10.4 %collective-permute-start.2 = (f32[744,128]{1,0:T(8,128)S(1)}, f32[744,128]{1,0:T(8,128)S(1)}, u32[]{:S(2)}, u32[]{:S(2)}) collective-permute-start(f32[744,128]{1,0:T(8,128)S(1)} %get-tuple-element.64), channel_id=1, source_target_pairs={{0,1},{1,0},{2,3},{3,2},{4,8},{5,9},{6,10},{7,11},{8,4},{9,5},{10,... | collective-permute-start | bytes 1142792 | tf_op jit(solution)/shard_map/ppermute | solution.py:666
  13.1 8.9 %collective-permute-start.3 = (f32[224,128]{1,0:T(8,128)S(1)}, f32[224,128]{1,0:T(8,128)S(1)}, u32[]{:S(2)}, u32[]{:S(2)}) collective-permute-start(f32[224,128]{1,0:T(8,128)S(1)} %get-tuple-element.65), channel_id=1, source_target_pairs={{0,1},{1,0},{2,3},{3,2},{4,8},{5,9},{6,10},{7,11},{8,4},{9,5},{10,... | collective-permute-start | bytes 344072 | tf_op jit(solution)/shard_map/ppermute | solution.py:666
